TPU v7x, 32 devices: a whole 2x2x4 slice. The times are simulated.
32 devices in a mesh: dp: 8 (over z, y), mp: 4 (over x, core).
Axes of the slice: x: 2, y: 2, z: 4, core: 2. Of those that a mesh axis runs over, the one named last changes fastest.
Arguments:
- tokens: bfloat16 [16384, 1024], P('dp'), may hold values from -6 to 6
- cotangent: bfloat16 [16384, 1024], P('dp'), may hold values from -6 to 6
- group_ids: int32 [16384], P('dp'), may hold values from 0 to 15
- pre_gain: bfloat16 [1024], replicated, may hold values from 0.5 to 1.5
- pre_shift: bfloat16 [1024], replicated, may hold values from -1.25 to 1.25
- frozen_triple_weight: bfloat16 [1024, 3, 1024], P('dp', None, 'mp'), may hold values from -0.1875 to 0.1875
- frozen_triple_bias: bfloat16 [3, 1024], P(None, 'mp'), may hold values from -1.25 to 1.25
- out_weight: bfloat16 [1024, 1024], P('mp', 'dp'), may hold values from -0.75 to 0.75
- out_bias: bfloat16 [1024], replicated, may hold values from -1.25 to 1.25
- mid_gain: bfloat16 [1024], replicated, may hold values from 0.099609375 to 1.8984375
- mid_shift: bfloat16 [1024], replicated, may hold values from -1.25 to 1.25
- fc_weight: bfloat16 [1024, 4096], P('dp', 'mp'), may hold values from -0.1875 to 0.1875
- fc_bias: bfloat16 [4096], P('mp'), may hold values from -1.25 to 1.25
- proj_weight: bfloat16 [4096, 1024], P('mp', 'dp'), may hold values from -0.09375 to 0.09375
- proj_bias: bfloat16 [1024], P('mp'), may hold values from -1.25 to 1.25
- down_master: float32 [2, 4, 1024], replicated, may hold values from -0.1875 to 0.1875
- up_master: float32 [2, 4, 1024], P(None, None, 'mp'), may hold values from -0.1875 to 0.1875
- down_first: float32 [2, 4, 1024], replicated, as said below
- down_second: float32 [2, 4, 1024], replicated, as said below
- up_first: float32 [2, 4, 1024], P(None, None, 'mp'), as said below
- up_second: float32 [2, 4, 1024], P(None, None, 'mp'), as said below
- learn_rate: float32 [], replicated, may hold values from 0.02 to 0.04
Outputs:
- output: bfloat16 [16384, 1024], P('dp', 'mp')
- input_grad: bfloat16 [16384, 1024], P('dp', 'mp')
- down_new: float32 [2, 4, 1024], replicated
- down_moment: float32 [2, 4, 1024], replicated
- down_square: float32 [2, 4, 1024], replicated
- down_copy: bfloat16 [2, 4, 1024], replicated
- up_new: float32 [2, 4, 1024], P(None, None, 'mp')
- up_moment: float32 [2, 4, 1024], P(None, None, 'mp')
- up_square: float32 [2, 4, 1024], P(None, None, 'mp')
- up_copy: bfloat16 [2, 4, 1024], P(None, None, 'mp')
Inputs may be any that keep to these rules, and one draw needn't show every extreme that they name: `down_first`: first moments of the down maps, of both signs. `down_second`: second moments of the down maps, positive. `up_first`: first moments of the up maps, of both signs. `up_second`: second moments of the up maps, positive.
All inputs are finite; a program needn't handle non-finite values.
Results may differ from a plain program's by a relative error of at most 0.02.
Values may be sent and summed in bfloat16 or wider, within the bound.
No kernel may reach another device: no remote copies, remote signals or barrier semaphores. Data moves between devices by JAX's collectives and lax.ppermute only.
A program may use at most 192 MiB of HBM per device.

v0:
```python
import jax
import jax.numpy as jnp
from jax import lax
from jax.sharding import PartitionSpec as P

HEAD_DIM = 64
ADAPTER_RANK = 4
GROUPS = 16
STEP = 3
MICRO = 2


ADAPTER_SCALE = 8.0
NORM_EPS = 1e-05
MASKED = -1e30
BETA_ONE = 0.5
BETA_TWO = 0.5
ADAM_EPS = 1e-08
DECAY = 0.01


def layer_stats(values):
    center = values - jnp.mean(values, axis=-1, keepdims=True)
    spread = jnp.mean(center * center, axis=-1, keepdims=True)
    scaler = lax.rsqrt(spread + NORM_EPS)
    return (center * scaler, scaler)


def norm_back(normal_hat, scaler, scaled_grad):
    first_mean = jnp.mean(scaled_grad, axis=-1, keepdims=True)
    second_mean = jnp.mean(scaled_grad * normal_hat, axis=-1, keepdims=True)
    return scaler * (scaled_grad - first_mean - normal_hat * second_mean)


def gelu_tanh(values):
    return jax.nn.gelu(values, approximate=True)


def fetch_frozen(frozen_triple_weight, fc_weight, out_weight, proj_weight):
    return (
        lax.all_gather(frozen_triple_weight, "dp", axis=0, tiled=True),
        lax.all_gather(fc_weight, "dp", axis=0, tiled=True),
        lax.all_gather(out_weight, "dp", axis=1, tiled=True),
        lax.all_gather(proj_weight, "dp", axis=1, tiled=True),
    )


def score_block(query_part, key_heads, start, block_rows, key_count):
    score_scale = HEAD_DIM ** (-0.5)
    scores = (
        jnp.einsum("qhd,khd->hqk", query_part, key_heads, preferred_element_type=jnp.float32)
        * score_scale
    )
    allowed = (start + jnp.arange(block_rows, dtype=jnp.int32))[:, None] >= jnp.arange(
        key_count, dtype=jnp.int32
    )[None, :]
    return jnp.where(allowed[None], scores, MASKED)


def attend(queries, key_rows, value_rows):
    length, col_width = queries.shape
    head_count = col_width // HEAD_DIM
    block_rows = min(512, length)
    query_heads = queries.reshape(length, head_count, HEAD_DIM)
    key_heads = key_rows.reshape(length, head_count, HEAD_DIM)
    value_heads = value_rows.reshape(length, head_count, HEAD_DIM)
    mixed_parts = []
    logsum_parts = []
    for index in range(length // block_rows):
        start = index * block_rows
        stop = start + block_rows
        query_part = query_heads[start:stop]
        scores = score_block(query_part, key_heads[:stop], start, block_rows, stop)
        row_top = jnp.max(scores, axis=-1, keepdims=True)
        exp_terms = jnp.exp(scores - row_top)
        row_total = jnp.sum(exp_terms, axis=-1, keepdims=True)
        probs = (exp_terms / row_total).astype(jnp.bfloat16)
        mixed = jnp.einsum(
            "hqk,khd->qhd", probs, value_heads[:stop], preferred_element_type=jnp.float32
        )
        mixed_parts.append(mixed.reshape(block_rows, col_width))
        logsum_parts.append((row_top + jnp.log(row_total))[..., 0])
    return (jnp.concatenate(mixed_parts, axis=0), logsum_parts)


def attend_back(queries, key_rows, value_rows, logsum, mixed_grad):
    length, col_width = queries.shape
    head_count = col_width // HEAD_DIM
    block_rows = min(512, length)
    score_scale = HEAD_DIM ** (-0.5)
    query_heads = queries.reshape(length, head_count, HEAD_DIM)
    key_heads = key_rows.reshape(length, head_count, HEAD_DIM)
    value_heads = value_rows.reshape(length, head_count, HEAD_DIM)
    grad_heads = mixed_grad.reshape(length, head_count, HEAD_DIM)
    key_acc = jnp.zeros((length, head_count, HEAD_DIM), jnp.float32)
    value_acc = jnp.zeros((length, head_count, HEAD_DIM), jnp.float32)
    query_parts = []
    for index in range(length // block_rows):
        start = index * block_rows
        stop = start + block_rows
        query_part = query_heads[start:stop]
        grad_part = grad_heads[start:stop]
        key_part = key_heads[:stop]
        scores = score_block(query_part, key_part, start, block_rows, stop)
        probs = jnp.exp(scores - logsum[index][:, :, None])
        prob_grad = jnp.einsum(
            "qhd,khd->hqk", grad_part, value_heads[:stop], preferred_element_type=jnp.float32
        )
        inner = jnp.sum(prob_grad * probs, axis=-1, keepdims=True)
        score_grad = (probs * (prob_grad - inner)).astype(jnp.bfloat16)
        query_grad = (
            jnp.einsum("hqk,khd->qhd", score_grad, key_part, preferred_element_type=jnp.float32)
            * score_scale
        )
        key_acc = key_acc.at[:stop].add(
            jnp.einsum("hqk,qhd->khd", score_grad, query_part, preferred_element_type=jnp.float32)
            * score_scale
        )
        value_acc = value_acc.at[:stop].add(
            jnp.einsum(
                "hqk,qhd->khd",
                probs.astype(jnp.bfloat16),
                grad_part,
                preferred_element_type=jnp.float32,
            )
        )
        query_parts.append(query_grad.reshape(block_rows, col_width))
    return (
        jnp.concatenate(query_parts, axis=0),
        key_acc.reshape(length, col_width),
        value_acc.reshape(length, col_width),
    )


def adam_update(master, first, second, grad, step_value, learn_rate):
    new_first = BETA_ONE * first + (1.0 - BETA_ONE) * grad
    new_second = BETA_TWO * second + (1.0 - BETA_TWO) * grad * grad
    fix_one = 1.0 - jnp.power(jnp.float32(BETA_ONE), step_value)
    fix_two = 1.0 - jnp.power(jnp.float32(BETA_TWO), step_value)
    update = new_first / fix_one / (jnp.sqrt(new_second / fix_two) + ADAM_EPS)
    new_master = master - learn_rate * (update + DECAY * master)
    return (new_master, new_first, new_second)


def on_device(
    tokens,
    cotangent,
    group_ids,
    pre_gain,
    pre_shift,
    frozen_triple_weight,
    frozen_triple_bias,
    out_weight,
    out_bias,
    mid_gain,
    mid_shift,
    fc_weight,
    fc_bias,
    proj_weight,
    proj_bias,
    down_master,
    up_master,
    down_first,
    down_second,
    up_first,
    up_second,
    learn_rate,
):
    tok_dev = tokens.shape[0]
    model_width = tokens.shape[1]
    length = tok_dev // MICRO
    shard_width = model_width // lax.axis_size("mp")
    shard_start = lax.axis_index("mp") * shard_width
    pre_gain_f = pre_gain.astype(jnp.float32)
    pre_shift_f = pre_shift.astype(jnp.float32)
    mid_gain_f = mid_gain.astype(jnp.float32)
    mid_shift_f = mid_shift.astype(jnp.float32)
    out_bias_f = out_bias.astype(jnp.float32)
    fc_bias_f = fc_bias.astype(jnp.float32)
    proj_bias_f = proj_bias.astype(jnp.float32)
    bias_flat = frozen_triple_bias.astype(jnp.float32).reshape(-1)
    onehot = group_ids[:, None] == jnp.arange(GROUPS, dtype=jnp.int32)[None, :]
    local_counts = jnp.sum(onehot.astype(jnp.int32), axis=0)
    totals = lax.psum(local_counts, "dp").astype(jnp.float32)
    own_count = jnp.sum(jnp.where(onehot, totals[None, :], jnp.float32(0.0)), axis=1)
    token_weight = jnp.float32(tok_dev * lax.axis_size("dp")) / (GROUPS * own_count)
    down_low = down_master.astype(jnp.bfloat16).reshape(2 * ADAPTER_RANK, model_width)
    raise_reduced = up_master.astype(jnp.bfloat16)
    grad_down = jnp.zeros((2 * ADAPTER_RANK, model_width), jnp.float32)
    raise_gradient = jnp.zeros(up_master.shape, jnp.float32)
    output_parts = []
    input_parts = []
    for micro_index in range(MICRO):
        current = fetch_frozen(frozen_triple_weight, fc_weight, out_weight, proj_weight)
        qkv_full, fc_full, out_full, proj_full = current
        qkv_flat = qkv_full.reshape(model_width, -1)
        head_width = qkv_flat.shape[1] // 3
        row_start = micro_index * length
        rows_f = lax.dynamic_slice_in_dim(tokens, row_start, length, 0).astype(jnp.float32)
        pre_hat, pre_scale = layer_stats(rows_f)
        normed = (pre_hat * pre_gain_f + pre_shift_f).astype(jnp.bfloat16)
        mixed_proj = jnp.dot(normed, qkv_flat, preferred_element_type=jnp.float32) + bias_flat
        bottleneck = jnp.einsum(
            "td,rd->tr", normed, down_low, preferred_element_type=jnp.float32
        ).astype(jnp.bfloat16)
        queries = (
            mixed_proj[:, :head_width]
            + ADAPTER_SCALE
            * jnp.dot(
                bottleneck[:, :ADAPTER_RANK], raise_reduced[0], preferred_element_type=jnp.float32
            )
        ).astype(jnp.bfloat16)
        key_rows = mixed_proj[:, head_width : 2 * head_width].astype(jnp.bfloat16)
        value_rows = (
            mixed_proj[:, 2 * head_width :]
            + ADAPTER_SCALE
            * jnp.dot(
                bottleneck[:, ADAPTER_RANK:], raise_reduced[1], preferred_element_type=jnp.float32
            )
        ).astype(jnp.bfloat16)
        attended, logsum = attend(queries, key_rows, value_rows)
        attended_low = attended.astype(jnp.bfloat16)
        head_term = jnp.dot(attended_low, out_full, preferred_element_type=jnp.float32).astype(
            jnp.bfloat16
        )
        attn_sum = lax.psum(head_term, "mp").astype(jnp.float32)
        hidden = rows_f + attn_sum + out_bias_f
        mid_hat, mid_scale = layer_stats(hidden)
        normed_mid = (mid_hat * mid_gain_f + mid_shift_f).astype(jnp.bfloat16)
        pre_act = jnp.dot(normed_mid, fc_full, preferred_element_type=jnp.float32) + fc_bias_f
        active, gelu_pullback = jax.vjp(gelu_tanh, pre_act)
        unit_part = jnp.dot(
            active.astype(jnp.bfloat16), proj_full, preferred_element_type=jnp.float32
        ).astype(jnp.bfloat16)
        unit_share = lax.psum_scatter(unit_part, "mp", scatter_dimension=1, tiled=True).astype(
            jnp.float32
        )
        hidden_share = lax.dynamic_slice_in_dim(hidden, shard_start, shard_width, 1)
        output_parts.append((hidden_share + unit_share + proj_bias_f).astype(jnp.bfloat16))
        weight_rows = lax.dynamic_slice_in_dim(token_weight, row_start, length, 0)
        out_grad = (
            lax.dynamic_slice_in_dim(cotangent, row_start, length, 0).astype(jnp.float32)
            * weight_rows[:, None]
        )
        out_low = out_grad.astype(jnp.bfloat16)
        active_grad = jnp.einsum(
            "td,fd->tf", out_low, proj_full, preferred_element_type=jnp.float32
        )
        pre_grad = gelu_pullback(active_grad)[0].astype(jnp.bfloat16)
        mid_part = jnp.einsum(
            "tf,df->td", pre_grad, fc_full, preferred_element_type=jnp.float32
        ).astype(jnp.bfloat16)
        mid_grad = lax.psum(mid_part, "mp").astype(jnp.float32)
        hidden_grad = out_grad + norm_back(mid_hat, mid_scale, mid_gain_f * mid_grad)
        hidden_low = hidden_grad.astype(jnp.bfloat16)
        attended_grad = jnp.einsum(
            "td,hd->th", hidden_low, out_full, preferred_element_type=jnp.float32
        ).astype(jnp.bfloat16)
        query_grad, key_grad, value_grad = attend_back(
            queries, key_rows, value_rows, logsum, attended_grad
        )
        query_low = query_grad.astype(jnp.bfloat16)
        key_low = key_grad.astype(jnp.bfloat16)
        value_low = value_grad.astype(jnp.bfloat16)
        proj_grad = jnp.concatenate([query_low, key_low, value_low], axis=1)
        in_part = jnp.einsum("tc,dc->td", proj_grad, qkv_flat, preferred_element_type=jnp.float32)
        bottleneck_gradient = ADAPTER_SCALE * jnp.concatenate(
            [
                jnp.einsum(
                    "tc,rc->tr", query_low, raise_reduced[0], preferred_element_type=jnp.float32
                ),
                jnp.einsum(
                    "tc,rc->tr", value_low, raise_reduced[1], preferred_element_type=jnp.float32
                ),
            ],
            axis=1,
        )
        latent_low = bottleneck_gradient.astype(jnp.bfloat16)
        in_part = (
            in_part + jnp.dot(latent_low, down_low, preferred_element_type=jnp.float32)
        ).astype(jnp.bfloat16)
        grad_down = grad_down + jnp.einsum(
            "tr,td->rd", latent_low, normed, preferred_element_type=jnp.float32
        )
        raise_gradient = raise_gradient + ADAPTER_SCALE * jnp.stack(
            [
                jnp.einsum(
                    "tr,tc->rc",
                    bottleneck[:, :ADAPTER_RANK],
                    query_low,
                    preferred_element_type=jnp.float32,
                ),
                jnp.einsum(
                    "tr,tc->rc",
                    bottleneck[:, ADAPTER_RANK:],
                    value_low,
                    preferred_element_type=jnp.float32,
                ),
            ],
            axis=0,
        )
        hidden_grad_share = lax.dynamic_slice_in_dim(hidden_grad, shard_start, shard_width, 1)
        in_grad = lax.psum(in_part, "mp").astype(jnp.float32)
        full_grad = norm_back(pre_hat, pre_scale, pre_gain_f * in_grad)
        input_parts.append(
            (
                hidden_grad_share + lax.dynamic_slice_in_dim(full_grad, shard_start, shard_width, 1)
            ).astype(jnp.bfloat16)
        )
    output = jnp.concatenate(output_parts, axis=0)
    input_grad = jnp.concatenate(input_parts, axis=0)
    down_grad = lax.psum(grad_down, ("dp", "mp")).reshape(down_master.shape)
    up_grad = lax.psum(raise_gradient, "dp")
    step_value = jnp.float32(STEP)
    down_new, down_moment, down_square = adam_update(
        down_master, down_first, down_second, down_grad, step_value, learn_rate
    )
    up_new, up_moment, up_square = adam_update(
        up_master, up_first, up_second, up_grad, step_value, learn_rate
    )
    return (
        output,
        input_grad,
        down_new,
        down_moment,
        down_square,
        down_new.astype(jnp.bfloat16),
        up_new,
        up_moment,
        up_square,
        up_new.astype(jnp.bfloat16),
    )


def solution(mesh):
    return jax.shard_map(
        on_device,
        mesh=mesh,
        in_specs=(
            P("dp", None),
            P("dp", None),
            P("dp"),
            P(),
            P(),
            P("dp", None, "mp"),
            P(None, "mp"),
            P("mp", "dp"),
            P(),
            P(),
            P(),
            P("dp", "mp"),
            P("mp"),
            P("mp", "dp"),
            P("mp"),
            P(),
            P(None, None, "mp"),
            P(),
            P(),
            P(None, None, "mp"),
            P(None, None, "mp"),
            P(),
        ),
        out_specs=(
            P("dp", "mp"),
            P("dp", "mp"),
            P(),
            P(),
            P(),
            P(),
            P(None, None, "mp"),
            P(None, None, "mp"),
            P(None, None, "mp"),
            P(None, None, "mp"),
        ),
        check_vma=False,
    )
```

profile of v0, /device:TPU:0, one launch (start us, length us, event | category | flops | bytes accessed | tf_op | source)
XLA Modules:
  0.0 567.4 jit_solution(7739182990013695754)
XLA Ops:
  18.8 30.6 %all_gather.17 = bf16[256,1024]{1,0:T(8,128)(2,1)S(1)} all-gather(bf16[256,128]{1,0:T(8,128)(2,1)S(1)} %copy-done.62), channel_id=1, replica_groups=mesh['dp'=8,'mp'=4] {'dp'}, dimensions={1}, use_global_device_ids=true | all-gather | bytes 589824 | tf_op jit(solution)/shard_map/all_gather | solution.py:43
  50.6 4.4 fusion.4
  57.6 5.4 all-gather.4.cloned.1.call-done
  97.7 9.5 %psum.65 = s32[16]{0:T(128)S(1)} all-reduce(s32[16]{0:T(128)S(1)} %convert_reduce_fusion.2), channel_id=1, replica_groups=mesh['dp'=8,'mp'=4] {'dp'}, use_global_device_ids=true, to_apply=%region_21.22 | all-reduce | flops 16 | bytes 128 | tf_op jit(solution)/shard_map/psum | solution.py:184
  107.4 73.4 %all-reduce.15.cloned.1.call-done = (bf16[1024,1024]{1,0:T(8,128)(2,1)}, bf16[1024,1024]{1,0:T(8,128)(2,1)}) async-done(((bf16[1024,1024]{1,0:T(8,128)(2,1)}, bf16[1024,1024]{1,0:T(8,128)(2,1)}), (bf16[1024,1024]{1,0:T(8,128)(2,1)}, bf16[1024,1024]{1,0:T(8,128)(2,1)})) %all-reduce.15.cloned.1.call-update) | async-done | bytes 4194320 | tf_op jit(solution)/shard_map/psum | solution.py:226
  188.2 44.4 %all-gather.6.cloned.1.call-done = bf16[1024,1024]{1,0:T(8,128)(2,1)} async-done(((bf16[128,1024]{1,0:T(8,128)(2,1)}), bf16[1024,1024]{1,0:T(8,128)(2,1)}) %all-gather.6.cloned.1.call-update) | async-done | bytes 2097168 | tf_op jit(solution)/shard_map/all_gather | solution.py:42
  232.6 7.4 %fusion.46 = f32[1024,1024]{1,0:T(8,128)} fusion(bf16[1024,1024]{1,0:T(8,128)(2,1)} %all-gather.6.cloned.1.call-done, f32[1024,1024]{1,0:T(8,128)} %copy-done.7, f32[1024]{0:T(1024)S(1)} %convert_element_type.261, f32[1024]{0:T(1024)S(1)} %convert_element_type.260, f32[1024]{0:T(1024)S(1)} %add_rsqrt_fusion.2, f32[1024]{0:T(1024)S(1)} %broadcast_multiply_fusion.10), kind=kOutput, calls=%fused_computation.100 | convolution fusion | flops 2152726528 | bytes 10502144 | tf_op jit(solution)/shard_map/dot_general | solution.py:230
  240.0 4.5 fusion.47
  244.5 39.8 %all-gather.8.cloned.1.call-done = bf16[1024,1024]{1,0:T(8,128)(2,1)} async-done(((bf16[1024,128]{1,0:T(8,128)(2,1)}), bf16[1024,1024]{1,0:T(8,128)(2,1)}) %all-gather.8.cloned.1.call-update) | async-done | bytes 2097168 | tf_op jit(solution)/shard_map/all_gather | solution.py:44
  284.3 10.2 %convolution_convert_fusion.1 = bf16[1024,1024]{1,0:T(8,128)(2,1)} fusion(bf16[1024,1024]{1,0:T(8,128)(2,1)} %all-gather.6.cloned.1.call-done, f32[1024,1024]{1,0:T(8,128)} %fusion.46, bf16[1024,1024]{1,0:T(8,128)(2,1)} %all-gather.8.cloned.1.call-done, f32[1024]{0:T(1024)S(1)} %get-tuple-element.188, f32[1024]{0:T(1024)S(1)} %convert_element_type.263, ...), kind=kOutput, calls=%fused_computation.128 | convolution fusion | flops 4321181696 | bytes 12591104 | tf_op jit(solution)/shard_map/tf,df->td/dot_general | solution.py:250
  294.5 10.2 %convolution_convert_fusion = bf16[1024,1024]{1,0:T(8,128)(2,1)} fusion(bf16[1024,1024]{1,0:T(8,128)(2,1)} %all-gather.6.cloned.1.call-done, f32[1024,1024]{1,0:T(8,128)} %fusion.47, bf16[1024,1024]{1,0:T(8,128)(2,1)} %all-gather.8.cloned.1.call-done, f32[1024]{0:T(1024)S(1)} %get-tuple-element.189, f32[1024]{0:T(1024)S(1)} %convert_element_type.263, ...), kind=kOutput, calls=%fused_computation.127 | convolution fusion | flops 4321181696 | bytes 12591104 | tf_op jit(solution)/shard_map/tf,df->td/dot_general | solution.py:250
  305.0 7.0 %fusion.77 = bf16[1024,1024]{1,0:T(8,128)(2,1)} fusion(bf16[1024,1024]{1,0:T(8,128)(2,1)} %all-gather.8.cloned.1.call-done, f32[1024,1024]{1,0:T(8,128)} %fusion.46, f32[1024]{0:T(1024)S(1)} %convert_element_type.263), kind=kOutput, calls=%fused_computation.126 | convolution fusion | flops 2159017984 | bytes 8392704 | tf_op jit(solution)/shard_map/dot_general | solution.py:232
  313.3 7.1 %fusion.76 = bf16[1024,1024]{1,0:T(8,128)(2,1)} fusion(bf16[1024,1024]{1,0:T(8,128)(2,1)} %all-gather.8.cloned.1.call-done, f32[1024,1024]{1,0:T(8,128)} %fusion.47, f32[1024]{0:T(1024)S(1)} %convert_element_type.263), kind=kOutput, calls=%fused_computation.125 | convolution fusion | flops 2159017984 | bytes 8392704 | tf_op jit(solution)/shard_map/dot_general | solution.py:232
  320.5 68.2 %all-reduce.13.cloned.1.call-done = (bf16[1024,1024]{1,0:T(8,128)(2,1)}, bf16[1024,1024]{1,0:T(8,128)(2,1)}) async-done(((bf16[1024,1024]{1,0:T(8,128)(2,1)}, bf16[1024,1024]{1,0:T(8,128)(2,1)}), (bf16[1024,1024]{1,0:T(8,128)(2,1)}, bf16[1024,1024]{1,0:T(8,128)(2,1)})) %all-reduce.13.cloned.1.call-update) | async-done | bytes 4194320 | tf_op jit(solution)/shard_map/psum | solution.py:253
  388.8 6.0 %fusion.34 = (f32[1024]{0:T(1024)S(1)}, f32[1024]{0:T(1024)S(1)}, f32[1024]{0:T(1024)S(1)}, f32[1024]{0:T(1024)S(1)}) fusion(bf16[1024,1024]{1,0:T(8,128)(2,1)} %get-tuple-element.155, f32[1024]{0:T(1024)S(1)} %convert_element_type.260, f32[1024]{0:T(1024)S(1)} %add_rsqrt_fusion.2, f32[1024,1024]{1,0:T(8,128)} %copy-done.7, ...), kind=kLoop, calls=%fused_computation.73 | loop fusion | flops 14675968 | bytes 12619776 | tf_op jit(solution)/shard_map/reduce_sum | solution.py:30
  397.4 5.4 multiply_add_fusion.1
  413.2 4.3 multiply_reduce_fusion.1
  429.4 4.5 multiply_reduce_fusion
  433.9 4.7 multiply_convert_fusion
  440.7 4.7 multiply_convert_fusion.1
  467.4 21.6 %psum.71 = f32[2,4,256]{2,1,0:T(4,128)S(1)} all-reduce(f32[2,4,256]{2,1,0:T(4,128)S(1)} %fusion.176), channel_id=1, replica_groups=mesh['dp'=8,'mp'=4] {'dp'}, use_global_device_ids=true, to_apply=%region_40.41 | all-reduce | flops 2048 | bytes 16384 | tf_op jit(solution)/shard_map/psum | solution.py:313
  489.0 38.0 %psum.70 = f32[2,4,1024]{2,1,0:T(4,128)S(1)} all-reduce(f32[2,4,1024]{2,1,0:T(4,128)S(1)} %reshape.535), channel_id=1, replica_groups=mesh['dp'=8,'mp'=4] {'dp','mp'}, use_global_device_ids=true, to_apply=%region_39.40 | all-reduce | flops 8192 | bytes 65536 | tf_op jit(solution)/shard_map/psum | solution.py:312
  533.2 16.2 %all-reduce.11.cloned.1.call-done = (bf16[1024,1024]{1,0:T(8,128)(2,1)}, bf16[1024,1024]{1,0:T(8,128)(2,1)}) async-done(((bf16[1024,1024]{1,0:T(8,128)(2,1)}, bf16[1024,1024]{1,0:T(8,128)(2,1)}), (bf16[1024,1024]{1,0:T(8,128)(2,1)}, bf16[1024,1024]{1,0:T(8,128)(2,1)})) %all-reduce.11.cloned.1.call-update) | async-done | bytes 4194320 | tf_op jit(solution)/shard_map/psum | solution.py:303
  549.4 5.7 multiply_reduce_fusion.5
  (301 shorter events, 117.9 us)
Async XLA Ops:
  7.2 55.8 %all-gather.4.cloned.1.call-start = ((), (), s32[]{:S(2)}) async-start(), calls=%async_computation.2 | async-start | bytes 1769472 | tf_op jit(solution)/shard_map/all_gather | solution.py:41
  9.0 171.8 %all-reduce.15.cloned.1.call-start = ((), (), s32[]{:S(2)}) async-start(), calls=%async_computation.9 | async-start | bytes 8388608 | tf_op jit(solution)/shard_map/psum | solution.py:226
  11.2 39.4 %copy-start.67 = (f32[1024]{0:T(1024)}, f32[1024]{0:T(1024)S(1)}, u32[]{:S(2)}) copy-start(f32[1024]{0:T(1024)S(1)} %convert_element_type.247) | copy-start | bytes 12292
  15.5 41.4 %copy-start.45 = (bf16[8,1024]{1,0:T(8,128)(2,1)}, bf16[8,1024]{1,0:T(8,128)(2,1)S(1)}, u32[]{:S(2)}) copy-start(bf16[8,1024]{1,0:T(8,128)(2,1)S(1)} %reshape.522) | copy-start | bytes 49156
  15.5 35.0 %copy-start.2 = (bf16[2048,1024]{1,0:T(8,128)(2,1)S(1)}, bf16[2048,1024]{1,0:T(8,128)(2,1)}, u32[]{:S(2)}) copy-start(bf16[2048,1024]{1,0:T(8,128)(2,1)} %param.46) | copy-start | bytes 12582916
  15.5 39.4 %copy-start.63 = (f32[1024]{0:T(1024)}, f32[1024]{0:T(1024)S(1)}, u32[]{:S(2)}) copy-start(f32[1024]{0:T(1024)S(1)} %get-tuple-element.212) | copy-start | bytes 12292
  15.6 39.4 %copy-start.65 = (f32[1024]{0:T(1024)}, f32[1024]{0:T(1024)S(1)}, u32[]{:S(2)}) copy-start(f32[1024]{0:T(1024)S(1)} %get-tuple-element.213) | copy-start | bytes 12292
  18.8 36.2 %copy-start.58 = (f32[1024]{0:T(1024)}, f32[1024]{0:T(1024)S(1)}, u32[]{:S(2)}) copy-start(f32[1024]{0:T(1024)S(1)} %add_rsqrt_fusion.3) | copy-start | bytes 12292
  18.8 36.2 %copy-start.60 = (f32[1024]{0:T(1024)}, f32[1024]{0:T(1024)S(1)}, u32[]{:S(2)}) copy-start(f32[1024]{0:T(1024)S(1)} %add_rsqrt_fusion.1) | copy-start | bytes 12292
  57.6 13.3 %copy-start.47 = (bf16[1024,8]{0,1:T(8,128)(2,1)}, bf16[1024,8]{0,1:T(8,128)(2,1)S(1)}, u32[]{:S(2)}) copy-start(bf16[1024,8]{0,1:T(8,128)(2,1)S(1)} %convolution_convert_fusion.4) | copy-start | bytes 49156
  67.3 21.3 %copy-start.26 = (bf16[1024,256]{0,1:T(8,128)(2,1)}, bf16[1024,256]{0,1:T(8,128)(2,1)S(1)}, u32[]{:S(2)}) copy-start(bf16[1024,256]{0,1:T(8,128)(2,1)S(1)} %fusion.130) | copy-start | bytes 1572868
  96.4 136.2 %all-gather.6.cloned.1.call-start = ((), (), s32[]{:S(2)}) async-start(), calls=%async_computation.3 | async-start | bytes 2359296 | tf_op jit(solution)/shard_map/all_gather | solution.py:42
  97.1 187.2 %all-gather.8.cloned.1.call-start = ((), (), s32[]{:S(2)}) async-start(), calls=%async_computation.4 | async-start | bytes 2359296 | tf_op jit(solution)/shard_map/all_gather | solution.py:44
  97.7 291.1 %all-reduce.13.cloned.1.call-start = ((), (), s32[]{:S(2)}) async-start(), calls=%async_computation.8 | async-start | bytes 8388608 | tf_op jit(solution)/shard_map/psum | solution.py:253
  304.7 225.2 %reduce-scatter.3.cloned.1.call-start = ((), (), s32[]{:S(2)}) async-start(), calls=%async_computation.5 | async-start | bytes 2621440 | tf_op jit(solution)/shard_map/reduce_scatter | solution.py:235
  312.0 218.0 %reduce-scatter.5.cloned.1.call-start = ((), (), s32[]{:S(2)}) async-start(), calls=%async_computation.6 | async-start | bytes 2621440 | tf_op jit(solution)/shard_map/reduce_scatter | solution.py:235
  320.5 228.9 %all-reduce.11.cloned.1.call-start = ((), (), s32[]{:S(2)}) async-start(), calls=%async_computation.7 | async-start | bytes 8388608 | tf_op jit(solution)/shard_map/psum | solution.py:303
  412.6 16.9 %copy-start.30 = (bf16[512,256]{0,1:T(8,128)(2,1)}, bf16[512,256]{0,1:T(8,128)(2,1)S(1)}, u32[]{:S(2)}) copy-start(bf16[512,256]{0,1:T(8,128)(2,1)S(1)} %get-tuple-element.183) | copy-start | bytes 786436
  461.8 66.7 %copy-start.57 = (f32[2,4,1024]{2,1,0:T(4,128)S(1)}, f32[2,4,1024]{2,1,0:T(4,128)}, u32[]{:S(2)}) copy-start(f32[2,4,1024]{2,1,0:T(4,128)} %param.61) | copy-start | bytes 98308
  465.6 83.8 %copy-start.59 = (f32[1024]{0:T(1024)S(1)}, f32[1024]{0:T(1024)}, u32[]{:S(2)}) copy-start(f32[1024]{0:T(1024)} %copy-done.58) | copy-start | bytes 12292
  465.6 83.8 %copy-start.61 = (f32[1024]{0:T(1024)S(1)}, f32[1024]{0:T(1024)}, u32[]{:S(2)}) copy-start(f32[1024]{0:T(1024)} %copy-done.60) | copy-start | bytes 12292
  465.6 83.7 %copy-start.64 = (f32[1024]{0:T(1024)S(1)}, f32[1024]{0:T(1024)}, u32[]{:S(2)}) copy-start(f32[1024]{0:T(1024)} %copy-done.63) | copy-start | bytes 12292
  465.6 83.7 %copy-start.66 = (f32[1024]{0:T(1024)S(1)}, f32[1024]{0:T(1024)}, u32[]{:S(2)}) copy-start(f32[1024]{0:T(1024)} %copy-done.65) | copy-start | bytes 12292
  465.6 83.7 %copy-start.68 = (f32[1024]{0:T(1024)S(1)}, f32[1024]{0:T(1024)}, u32[]{:S(2)}) copy-start(f32[1024]{0:T(1024)} %copy-done.67) | copy-start | bytes 12292
  (66 other events, 299.9 us)
Sparse Core Ops, SparseCore 0:
  10.6 52.3 all-gather.3
  96.5 84.2 all-reduce.14
  183.2 49.4 all-gather.5
  234.7 49.5 all-gather.7
  304.8 83.8 all-reduce.12
  391.1 31.5 reduce-scatter.2
  425.4 31.4 reduce-scatter.4
  461.9 87.3 all-reduce.10
where the time goes:
time: 571 us; the launch traced here: 567 us
  waiting for transfers between devices  249 us (44%)
  matrix products  113 us (20%)
  blocking collectives  99.7 us (17%)
  other arithmetic  67.9 us (12%)
  local copies, waits for them, and re-layouts  20.8 us (4%)
  between operations  16.5 us (3%)
    psum x1, waiting for transfers between devices, on_device(): attn_sum = lax.psum(head_term, 'mp').astype(jnp.float32)  73.4 us
    psum x1, waiting for transfers between devices, on_device(): mid_grad = lax.psum(mid_part, 'mp').astype(jnp.float32)  68.2 us
    all_gather x1, waiting for transfers between devices, fetch_frozen(): lax.all_gather(fc_weight, 'dp', axis=0, tiled=True)  44.4 us
    all_gather x1, waiting for transfers between devices, fetch_frozen(): lax.all_gather(proj_weight, 'dp', axis=1, tiled=True)  39.8 us
    psum x1, blocking collectives, on_device(): down_grad = lax.psum(grad_down, ('dp', 'mp')).reshape(down_master.shape)  38 us
    all_gather x1, blocking collectives, fetch_frozen(): lax.all_gather(out_weight, 'dp', axis=1, tiled=True)  30.6 us
    psum x1, blocking collectives, on_device(): up_grad = lax.psum(raise_gradient, 'dp')  21.6 us
    dot_general x2, matrix products, on_device(): jnp.einsum('tf,df->td', pre_grad, fc_full, preferred_element_type=jnp.flo...  20.4 us
  transfers between devices with their start and end apart: 8, of which 6 were waited for; matrix products, arithmetic and copies ran while one was open for 22% of the time, Pallas kernels for 0%

commit v1 on v0

--- a/solution.py
+++ b/solution.py
@@ -1,6 +1,8 @@
 import jax
 import jax.numpy as jnp
 from jax import lax
+from jax.experimental import pallas as pl
+from jax.experimental.pallas import tpu as pltpu
 from jax.sharding import PartitionSpec as P
 
 HEAD_DIM = 64
@@ -142,7 +144,7 @@
     return (new_master, new_first, new_second)
 
 
-def on_device(
+def on_device_general(
     tokens,
     cotangent,
     group_ids,
@@ -332,9 +334,882 @@
     )
 
 
+LEN = 1024
+BLK = 256
+LANES = 128
+LOG2E = 1.4426950408889634
+NT = (((1,), (1,)), ((), ()))
+TN = (((0,), (0,)), ((), ()))
+VMEM_LIMIT = 60 << 20
+F32 = jnp.float32
+BF16 = jnp.bfloat16
+AXES = ("dp", "mp")
+ANY = pl.BlockSpec(memory_space=pl.ANY)
+
+
+def cost(flops, nbytes, trans=0):
+    return pl.CostEstimate(flops=int(flops), bytes_accessed=int(nbytes), transcendentals=int(trans))
+
+
+def shape(rows, cols, dtype=BF16):
+    return jax.ShapeDtypeStruct((rows, cols), dtype)
+
+
+def full(rows, cols):
+    return pl.BlockSpec((rows, cols), lambda i, ix: (0, 0))
+
+
+def call(body, name, grid, in_specs, out_specs, out_shape, scratch, est):
+    return pl.pallas_call(
+        body,
+        grid_spec=pltpu.PrefetchScalarGridSpec(
+            num_scalar_prefetch=1,
+            grid=(grid,),
+            in_specs=in_specs,
+            out_specs=out_specs,
+            scratch_shapes=scratch,
+        ),
+        out_shape=out_shape,
+        compiler_params=pltpu.CompilerParams(vmem_limit_bytes=VMEM_LIMIT),
+        cost_estimate=est,
+        name=name,
+    )
+
+
+def hop(value, half_bit, dp_bits):
+    ranks = lax.axis_size("mp") // 2
+    width = lax.axis_size("mp")
+    total = lax.axis_size("dp") * width
+    flip = dp_bits * width + half_bit * ranks
+    return lax.ppermute(value, AXES, [(i, i ^ flip) for i in range(total)])
+
+
+def core_swap(value):
+    total = lax.axis_size("dp") * lax.axis_size("mp")
+    return lax.ppermute(value, AXES, [(i, i ^ 1) for i in range(total)])
+
+
+def after(value, *others):
+    return lax.optimization_barrier((value, *others))[0]
+
+
+def gather_blocks(own, heavy):
+    zs = [hop(own, 0, 2 * c) for c in (1, 2, 3)]
+    far = jnp.stack(zs)
+    x0, y0 = hop(own, 1, 0), hop(own, 0, 1)
+    x3, y3 = hop(far, 1, 0), hop(far, 0, 1)
+    if heavy == "x":
+        d0 = hop(x0, 0, 1)
+        d3 = hop(y3, 1, 0)
+    else:
+        d0 = hop(y0, 1, 0)
+        d3 = hop(x3, 0, 1)
+    found = [(own, None, 0, 0), (x0, None, 1, 0), (y0, None, 0, 1), (d0, None, 1, 1)]
+    for c in (1, 2, 3):
+        found += [(far, c - 1, 0, 2 * c), (x3, c - 1, 1, 2 * c), (y3, c - 1, 0, 2 * c + 1), (d3, c - 1, 1, 2 * c + 1)]
+    return found
+
+
+def operands(found):
+    arrays = []
+    table = []
+    for array, slot, half_bit, dp_bits in found:
+        for k, held in enumerate(arrays):
+            if held is array:
+                break
+        else:
+            k = len(arrays)
+            arrays.append(array)
+        table.append((k, slot, half_bit, dp_bits))
+    return arrays, table
+
+
+def block_of(refs, entry):
+    k, slot, _, _ = entry
+    return refs[k] if slot is None else refs[k].at[slot]
+
+
+def load_all(pairs, sems):
+    copies = [pltpu.make_async_copy(src, dst, sems.at[n]) for n, (src, dst) in enumerate(pairs)]
+    for copy in copies:
+        copy.start()
+    for copy in copies:
+        copy.wait()
+
+
+def at_rows(index, size):
+    return pl.ds(pl.multiple_of(index * size, size), size)
+
+
+def pick(low, value, which):
+    zero = jnp.zeros((), value.dtype)
+    return jnp.where(low, value, zero) if which == 0 else jnp.where(low, zero, value)
+
+
+def row_stats(values):
+    center = values - jnp.mean(values, axis=-1, keepdims=True)
+    scaler = lax.rsqrt(jnp.mean(center * center, axis=-1, keepdims=True) + NORM_EPS)
+    return center * scaler, scaler
+
+
+def token_weights(ids, table):
+    lanes = lax.broadcasted_iota(jnp.int32, (ids.shape[0], LANES), 1)
+    return jnp.sum(jnp.where(ids == lanes, table, 0.0), axis=-1, keepdims=True)
+
+
+def project_heads(idx, tokens, gain, shift, bias, down, up, found):
+    model = tokens.shape[1]
+    arrays, table = operands(found)
+    step_rows, cols = found[0][0].shape
+    part = cols // 3
+    n = len(arrays)
+
+    def body(ix, tok, gain_ref, shift_ref, bias_ref, down_ref, up_ref, *rest):
+        msgs = rest[:n]
+        q_ref, k_ref, v_ref, normed_ref, latent_ref, w, sems = rest[n:]
+
+        @pl.when(pl.program_id(0) == 0)
+        def _():
+            load_all(
+                [(block_of(msgs, e), w.at[e[2], at_rows(ix[0] ^ e[3], step_rows), :]) for e in table],
+                sems,
+            )
+
+        hat, _ = row_stats(tok[...].astype(F32))
+        normed = (hat * gain_ref[...] + shift_ref[...]).astype(BF16)
+        normed_ref[...] = normed
+        latent = lax.dot_general(normed, down_ref[...], NT, preferred_element_type=F32).astype(BF16)
+        latent_ref[...] = latent
+        for a in range(2):
+            r = jnp.dot(normed, w[a], preferred_element_type=F32) + bias_ref[a : a + 1, :]
+            r = r + jnp.dot(latent, up_ref[a], preferred_element_type=F32)
+            for out, s in ((q_ref, 0), (k_ref, 1), (v_ref, 2)):
+                out[:, a * part : (a + 1) * part] = r[:, s * part : (s + 1) * part].astype(BF16)
+
+    row = pl.BlockSpec((BLK, 2 * part), lambda i, ix: (i, 0))
+    blocks = LEN // BLK
+    return call(
+        body,
+        "project_heads",
+        blocks,
+        [
+            pl.BlockSpec((BLK, model), lambda i, ix: (ix[1] * blocks + i, 0)),
+            full(1, model),
+            full(1, model),
+            full(2, cols),
+            full(LANES, model),
+            pl.BlockSpec((2, LANES, cols), lambda i, ix: (0, 0, 0)),
+        ]
+        + [ANY] * n,
+        [row, row, row, pl.BlockSpec((BLK, model), lambda i, ix: (i, 0)), pl.BlockSpec((BLK, LANES), lambda i, ix: (i, 0))],
+        [shape(LEN, 2 * part)] * 3 + [shape(LEN, model), shape(LEN, LANES)],
+        [pltpu.VMEM((2, model, cols), BF16), pltpu.SemaphoreType.DMA((len(table),))],
+        cost(4 * LEN * model * cols, 16 * LEN * model),
+    )(idx, tokens, gain, shift, bias, down, up, *arrays)
+
+
+def attend_fast(queries, key_rows, value_rows):
+    length, width = queries.shape
+    pairs = width // LANES
+
+    def body(q_ref, k_ref, v_ref, o_ref, lse_ref):
+        scale = HEAD_DIM**-0.5 * LOG2E
+        low = lax.broadcasted_iota(jnp.int32, (1, LANES), 1) < HEAD_DIM
+        k = k_ref[...]
+        v = v_ref[...]
+        value_of = [pick(low, v, h) for h in range(2)]
+        for i in range(length // BLK):
+            stop = (i + 1) * BLK
+            qb = q_ref[i * BLK : stop, :]
+            causal = (lax.broadcasted_iota(jnp.int32, (BLK, stop), 0) + i * BLK) >= lax.broadcasted_iota(
+                jnp.int32, (BLK, stop), 1
+            )
+            out = jnp.zeros((BLK, LANES), F32)
+            logs = []
+            for h in range(2):
+                s = lax.dot_general(pick(low, qb, h), k[:stop], NT, preferred_element_type=F32) * scale
+                s = jnp.where(causal, s, MASKED)
+                top = jnp.max(s, axis=-1, keepdims=True)
+                p = jnp.exp2(s - top)
+                total = jnp.sum(p, axis=-1, keepdims=True)
+                probs = (p * (1.0 / total)).astype(BF16)
+                out = out + jnp.dot(probs, value_of[h][:stop], preferred_element_type=F32)
+                logs.append(top + jnp.log2(total))
+            o_ref[i * BLK : stop, :] = out.astype(BF16)
+            both = jnp.where(
+                low, jnp.broadcast_to(logs[0], (BLK, LANES)), jnp.broadcast_to(logs[1], (BLK, LANES))
+            ).T
+            lse_ref[0, 0:1, i * BLK : stop] = both[0:1]
+            lse_ref[0, 1:2, i * BLK : stop] = both[HEAD_DIM : HEAD_DIM + 1]
+
+    spec = pl.BlockSpec((length, LANES), lambda i: (0, i))
+    return pl.pallas_call(
+        body,
+        grid=(pairs,),
+        out_shape=(shape(length, width), jax.ShapeDtypeStruct((pairs, 8, length), F32)),
+        in_specs=[spec] * 3,
+        out_specs=(spec, pl.BlockSpec((1, 8, length), lambda i: (i, 0, 0))),
+        compiler_params=pltpu.CompilerParams(vmem_limit_bytes=VMEM_LIMIT),
+        cost_estimate=cost(8 * length * length * width, 8 * length * width, 2 * pairs * length * length),
+        name="attend",
+    )(queries, key_rows, value_rows)
+
+
+def out_weight_pairs(msgs, table, w, ix, first_row):
+    pairs = []
+    rows, cols = w.shape[0] // 2, LANES
+    for e in table:
+        src = block_of(msgs, e).at[pl.ds(first_row, rows), :]
+        pairs.append((src, w.at[pl.ds(e[2] * rows, rows), at_rows(ix[0] ^ e[3], cols)]))
+    return pairs
+
+
+def attention_out_send(idx, attended, found, first_row):
+    width = attended.shape[1]
+    arrays, table = operands(found)
+    n = len(arrays)
+    model = LANES * len(table) // 2
+    half_blocks = LEN // BLK // 2
+
+    def body(ix, att, *rest):
+        msgs = rest[:n]
+        out, w, sems = rest[n:]
+
+        @pl.when(pl.program_id(0) == 0)
+        def _():
+            load_all(out_weight_pairs(msgs, table, w, ix, first_row), sems)
+
+        out[...] = jnp.dot(att[...], w[...], preferred_element_type=F32).astype(BF16)
+
+    return call(
+        body,
+        "attention_out_send",
+        half_blocks,
+        [pl.BlockSpec((BLK, width), lambda i, ix: ((1 - ix[2]) * half_blocks + i, 0))] + [ANY] * n,
+        pl.BlockSpec((BLK, model), lambda i, ix: (i, 0)),
+        shape(LEN // 2, model),
+        [pltpu.VMEM((width, model), BF16), pltpu.SemaphoreType.DMA((len(table),))],
+        cost(LEN * width * model, 2 * LEN * model),
+    )(idx, attended, *arrays)
+
+
+def attention_out_own(idx, attended, received, tokens, out_bias, gain, shift, found, first_row):
+    width = attended.shape[1]
+    arrays, table = operands(found)
+    n = len(arrays)
+    model = LANES * len(table) // 2
+    half_blocks = LEN // BLK // 2
+
+    def body(ix, att, recv, tok, bias_ref, gain_ref, shift_ref, *rest):
+        msgs = rest[:n]
+        hidden_ref, normed_ref, w, sems = rest[n:]
+
+        @pl.when(pl.program_id(0) == 0)
+        def _():
+            load_all(out_weight_pairs(msgs, table, w, ix, first_row), sems)
+
+        term = jnp.dot(att[...], w[...], preferred_element_type=F32)
+        hidden = tok[...].astype(F32) + term + recv[...].astype(F32) + bias_ref[...]
+        hidden_ref[...] = hidden
+        hat, _ = row_stats(hidden)
+        normed_ref[...] = (hat * gain_ref[...] + shift_ref[...]).astype(BF16)
+
+    row = pl.BlockSpec((BLK, model), lambda i, ix: (i, 0))
+    return call(
+        body,
+        "attention_out_own",
+        half_blocks,
+        [
+            pl.BlockSpec((BLK, width), lambda i, ix: (ix[2] * half_blocks + i, 0)),
+            row,
+            pl.BlockSpec((BLK, model), lambda i, ix: ((2 * ix[1] + ix[2]) * half_blocks + i, 0)),
+            full(1, model),
+            full(1, model),
+            full(1, model),
+        ]
+        + [ANY] * n,
+        [row, row],
+        [shape(LEN // 2, model, F32), shape(LEN // 2, model)],
+        [pltpu.VMEM((width, model), BF16), pltpu.SemaphoreType.DMA((len(table),))],
+        cost(LEN * width * model, 5 * LEN * model),
+    )(idx, attended, received, tokens, out_bias, gain, shift, *arrays)
+
+
+def expand_units(idx, own, other, bias, found):
+    model = own.shape[1]
+    arrays, table = operands(found)
+    n = len(arrays)
+    step_rows, part = found[0][0].shape
+    units = 2 * part
+    half_blocks = LEN // BLK // 2
+    chunk = 512
+    c0 = 0.7978845608028654
+    c1 = 0.044715
+
+    def body(ix, own_ref, other_ref, bias_ref, *rest):
+        msgs = rest[:n]
+        active_ref, slope_ref, w, sems = rest[n:]
+        step = pl.program_id(0)
+
+        @pl.when(step == 0)
+        def _():
+            load_all(
+                [
+                    (block_of(msgs, e), w.at[at_rows(ix[0] ^ e[3], step_rows), pl.ds(e[2] * part, part)])
+                    for e in table
+                ],
+                sems,
+            )
+
+        rows = jnp.where(step < half_blocks, own_ref[...], other_ref[...])
+        for c in range(units // chunk):
+            cols = slice(c * chunk, (c + 1) * chunk)
+            x = jnp.dot(rows, w[:, cols], preferred_element_type=F32) + bias_ref[:, cols]
+            sq = x * x
+            th = jnp.tanh(c0 * x * (1.0 + c1 * sq))
+            left = 0.5 * (1.0 + th)
+            active_ref[:, cols] = (x * left).astype(BF16)
+            slope_ref[:, cols] = (left + 0.5 * x * (1.0 - th * th) * (c0 + (3.0 * c0 * c1) * sq)).astype(BF16)
+
+    row = pl.BlockSpec((BLK, units), lambda i, ix: (i, 0))
+    return call(
+        body,
+        "expand_units",
+        2 * half_blocks,
+        [
+            pl.BlockSpec((BLK, model), lambda i, ix: (jnp.minimum(i, half_blocks - 1), 0)),
+            pl.BlockSpec((BLK, model), lambda i, ix: (jnp.maximum(i - half_blocks, 0), 0)),
+            full(1, units),
+        ]
+        + [ANY] * n,
+        [row, row],
+        [shape(LEN, units)] * 2,
+        [pltpu.VMEM((model, units), BF16), pltpu.SemaphoreType.DMA((len(table),))],
+        cost(2 * LEN * units * model, 6 * LEN * units, LEN * units),
+    )(idx, own, other, bias, *arrays)
+
+
+def proj_pairs(msgs, table, w, ix):
+    rows = w.shape[0] // 2
+    return [
+        (
+            block_of(msgs, e).at[pl.ds(0, rows), :],
+            w.at[pl.ds(e[2] * rows, rows), at_rows(ix[0] ^ e[3], LANES)],
+        )
+        for e in table
+    ]
+
+
+def units_back(idx, mine, cotangent, ids, weight_table, slope, fc_found, proj_found):
+    model = cotangent.shape[1]
+    units = slope.shape[1]
+    fc_arrays, fc_table = operands(fc_found)
+    pj_arrays, pj_table = operands(proj_found)
+    nf, np_ = len(fc_arrays), len(pj_arrays)
+    step_rows, part = fc_found[0][0].shape
+    half_blocks = LEN // BLK // 2
+    chunk = 512
+    first = 0 if mine else half_blocks
+
+    def body(ix, cot, ids_ref, table_ref, slope_ref, *rest):
+        fmsgs, pmsgs = rest[:nf], rest[nf : nf + np_]
+        out, fc_w, pj_w, sems = rest[nf + np_ :]
+
+        @pl.when(pl.program_id(0) == 0)
+        def _():
+            load_all(
+                proj_pairs(pmsgs, pj_table, pj_w, ix)
+                + [
+                    (block_of(fmsgs, e), fc_w.at[at_rows(ix[0] ^ e[3], step_rows), pl.ds(e[2] * part, part)])
+                    for e in fc_table
+                ],
+                sems,
+            )
+
+        weight = token_weights(ids_ref[...], table_ref[...])
+        grad = (cot[...].astype(F32) * weight).astype(BF16)
+        total = jnp.zeros((BLK, model), F32)
+        for c in range(units // chunk):
+            cols = slice(c * chunk, (c + 1) * chunk)
+            up = lax.dot_general(grad, pj_w[cols, :], NT, preferred_element_type=F32)
+            pre = (up * slope_ref[:, cols].astype(F32)).astype(BF16)
+            total = total + lax.dot_general(pre, fc_w[:, cols], NT, preferred_element_type=F32)
+        out[...] = total.astype(out.dtype)
+
+    def token_rows(i, ix):
+        rank = ix[2] if mine else 1 - ix[2]
+        return ((2 * ix[1] + rank) * half_blocks + i, 0)
+
+    return call(
+        body,
+        "units_back_own" if mine else "units_back_send",
+        half_blocks,
+        [
+            pl.BlockSpec((BLK, model), token_rows),
+            pl.BlockSpec((BLK, 1), token_rows),
+            full(1, LANES),
+            pl.BlockSpec((BLK, units), lambda i, ix: (first + i, 0)),
+        ]
+        + [ANY] * (nf + np_),
+        pl.BlockSpec((BLK, model), lambda i, ix: (i, 0)),
+        shape(LEN // 2, model, F32 if mine else BF16),
+        [
+            pltpu.VMEM((model, units), BF16),
+            pltpu.VMEM((units, model), BF16),
+            pltpu.SemaphoreType.DMA((len(fc_table) + len(pj_table),)),
+        ],
+        cost(2 * LEN * units * model, 4 * units * model),
+    )(idx, cotangent, ids, weight_table, slope, *fc_arrays, *pj_arrays)
+
+
+def units_out(idx, mine, active, hidden, proj_found):
+    units = active.shape[1]
+    arrays, table = operands(proj_found)
+    n = len(arrays)
+    model = LANES * len(table) // 2
+    half_blocks = LEN // BLK // 2
+    first = 0 if mine else half_blocks
+
+    def body(ix, act, *rest):
+        extra = rest[:1] if mine else ()
+        rest = rest[len(extra) :]
+        msgs = rest[:n]
+        out, w, sems = rest[n:]
+
+        @pl.when(pl.program_id(0) == 0)
+        def _():
+            load_all(proj_pairs(msgs, table, w, ix), sems)
+
+        term = jnp.dot(act[...], w[...], preferred_element_type=F32)
+        if mine:
+            term = term + extra[0][...]
+        out[...] = term.astype(out.dtype)
+
+    row = pl.BlockSpec((BLK, model), lambda i, ix: (i, 0))
+    return call(
+        body,
+        "units_out_own" if mine else "units_out_send",
+        half_blocks,
+        [pl.BlockSpec((BLK, units), lambda i, ix: (first + i, 0))] + ([row] if mine else []) + [ANY] * n,
+        row,
+        shape(LEN // 2, model, F32 if mine else BF16),
+        [pltpu.VMEM((units, model), BF16), pltpu.SemaphoreType.DMA((len(table),))],
+        cost(LEN * units * model, 4 * units * model),
+    )(idx, active, *((hidden,) if mine else ()), *arrays)
+
+
+def hidden_back(idx, mid_own, mid_recv, cotangent, ids, weight_table, hidden, gain):
+    model = cotangent.shape[1]
+    half_blocks = LEN // BLK // 2
+
+    def body(ix, own, recv, cot, ids_ref, table_ref, hid, gain_ref, grad_ref, low_ref):
+        e = gain_ref[...] * (own[...] + recv[...].astype(F32))
+        hat, scaler = row_stats(hid[...])
+        grad = cot[...].astype(F32) * token_weights(ids_ref[...], table_ref[...])
+        grad = grad + norm_back(hat, scaler, e)
+        grad_ref[...] = grad
+        low_ref[...] = grad.astype(BF16)
+
+    def token_rows(i, ix):
+        return ((2 * ix[1] + ix[2]) * half_blocks + i, 0)
+
+    row = pl.BlockSpec((BLK, model), lambda i, ix: (i, 0))
+    return call(
+        body,
+        "hidden_back",
+        half_blocks,
+        [
+            row,
+            row,
+            pl.BlockSpec((BLK, model), token_rows),
+            pl.BlockSpec((BLK, 1), token_rows),
+            full(1, LANES),
+            row,
+            full(1, model),
+        ],
+        [row, row],
+        [shape(LEN // 2, model, F32), shape(LEN // 2, model)],
+        [],
+        cost(20 * LEN * model, 8 * LEN * model),
+    )(idx, mid_own, mid_recv, cotangent, ids, weight_table, hidden, gain)
+
+
+def attended_back(idx, own, other, found, first_row, width):
+    model = own.shape[1]
+    arrays, table = operands(found)
+    n = len(arrays)
+    half_blocks = LEN // BLK // 2
+
+    def body(ix, own_ref, other_ref, *rest):
+        msgs = rest[:n]
+        out, w, sems = rest[n:]
+        step = pl.program_id(0)
+
+        @pl.when(step == 0)
+        def _():
+            load_all(out_weight_pairs(msgs, table, w, ix, first_row), sems)
+
+        rows = jnp.where(step < half_blocks, own_ref[...], other_ref[...])
+        out[...] = lax.dot_general(rows, w[...], NT, preferred_element_type=F32).astype(BF16)
+
+    def out_rows(i, ix):
+        mine = ix[2] * half_blocks + i
+        return (jnp.where(i < half_blocks, mine, (1 - ix[2]) * half_blocks + i - half_blocks), 0)
+
+    return call(
+        body,
+        "attended_back",
+        2 * half_blocks,
+        [
+            pl.BlockSpec((BLK, model), lambda i, ix: (jnp.minimum(i, half_blocks - 1), 0)),
+            pl.BlockSpec((BLK, model), lambda i, ix: (jnp.maximum(i - half_blocks, 0), 0)),
+        ]
+        + [ANY] * n,
+        pl.BlockSpec((BLK, width), out_rows),
+        shape(LEN, width),
+        [pltpu.VMEM((width, model), BF16), pltpu.SemaphoreType.DMA((len(table),))],
+        cost(2 * LEN * width * model, 4 * LEN * model),
+    )(idx, own, other, *arrays)
+
+
+def attend_back_fast(queries, key_rows, value_rows, mixed, mixed_grad, logsum):
+    length, width = queries.shape
+    pairs = width // LANES
+
+    def body(q_ref, k_ref, v_ref, o_ref, g_ref, lse_ref, dq_ref, dk_ref, dv_ref, dq_acc):
+        scale = HEAD_DIM**-0.5 * LOG2E
+        low = lax.broadcasted_iota(jnp.int32, (1, LANES), 1) < HEAD_DIM
+        q = q_ref[...]
+        g = g_ref[...]
+        qm = [pick(low, q, h) for h in range(2)]
+        gm = [pick(low, g, h) for h in range(2)]
+        prod = (g.astype(F32) * o_ref[...].astype(F32)).T
+        delta = [
+            jnp.sum(prod[:HEAD_DIM], axis=0, keepdims=True),
+            jnp.sum(prod[HEAD_DIM:], axis=0, keepdims=True),
+        ]
+        dq_acc[...] = jnp.zeros_like(dq_acc)
+        for j in range(length // BLK):
+            start = j * BLK
+            stop = start + BLK
+            span = length - start
+            kb = k_ref[start:stop, :]
+            vb = v_ref[start:stop, :]
+            causal = lax.broadcasted_iota(jnp.int32, (BLK, span), 1) >= lax.broadcasted_iota(
+                jnp.int32, (BLK, span), 0
+            )
+            dk = jnp.zeros((BLK, LANES), F32)
+            dv = jnp.zeros((BLK, LANES), F32)
+            for h in range(2):
+                km = pick(low, kb, h)
+                s = lax.dot_general(km, q[start:], NT, preferred_element_type=F32) * scale
+                s = jnp.where(causal, s - lse_ref[0, h : h + 1, start:], MASKED)
+                p = jnp.exp2(s)
+                dp = lax.dot_general(pick(low, vb, h), g[start:], NT, preferred_element_type=F32)
+                ds = (p * (dp - delta[h][:, start:])).astype(BF16)
+                dk = dk + jnp.dot(ds, qm[h][start:], preferred_element_type=F32)
+                dv = dv + jnp.dot(p.astype(BF16), gm[h][start:], preferred_element_type=F32)
+                dq_acc[start:, :] += lax.dot_general(ds, km, TN, preferred_element_type=F32)
+            dk_ref[start:stop, :] = (dk * HEAD_DIM**-0.5).astype(BF16)
+            dv_ref[start:stop, :] = dv.astype(BF16)
+        dq_ref[...] = (dq_acc[...] * HEAD_DIM**-0.5).astype(BF16)
+
+    spec = pl.BlockSpec((length, LANES), lambda i: (0, i))
+    return pl.pallas_call(
+        body,
+        grid=(pairs,),
+        out_shape=(shape(length, width),) * 3,
+        in_specs=[spec] * 5 + [pl.BlockSpec((1, 8, length), lambda i: (i, 0, 0))],
+        out_specs=(spec,) * 3,
+        scratch_shapes=[pltpu.VMEM((length, LANES), F32)],
+        compiler_params=pltpu.CompilerParams(vmem_limit_bytes=VMEM_LIMIT),
+        cost_estimate=cost(20 * length * length * width, 16 * length * width, 2 * pairs * length * length),
+        name="attend_back",
+    )(queries, key_rows, value_rows, mixed, mixed_grad, logsum)
+
+
+def adapter_back(idx, dq, dv, normed, latent, up):
+    model = normed.shape[1]
+    width = dq.shape[1]
+    part = width // 2
+    cols = up.shape[2]
+
+    def body(ix, dq_ref, dv_ref, normed_ref, latent_ref, up_ref, low_ref, down_ref, raise_ref):
+        @pl.when(pl.program_id(0) == 0)
+        def _():
+            down_ref[...] = jnp.zeros_like(down_ref)
+            raise_ref[...] = jnp.zeros_like(raise_ref)
+
+        grad = jnp.zeros((BLK, LANES), F32)
+        latent = latent_ref[...]
+        for a in range(2):
+            for n, ref in ((0, dq_ref), (1, dv_ref)):
+                piece = ref[:, a * part : (a + 1) * part]
+                weight = up_ref[a, :, 2 * n * part : (2 * n + 1) * part]
+                grad = grad + lax.dot_general(piece, weight, NT, preferred_element_type=F32)
+                term = lax.dot_general(latent, piece, TN, preferred_element_type=F32)
+                raise_ref[:, (2 * a + n) * part : (2 * a + n + 1) * part] += term[:8]
+        low = grad.astype(BF16)
+        low_ref[...] = low
+        down_ref[...] += lax.dot_general(low, normed_ref[...], TN, preferred_element_type=F32)[:8]
+
+    row = lambda c: pl.BlockSpec((BLK, c), lambda i, ix: (i, 0))
+    return call(
+        body,
+        "adapter_back",
+        LEN // BLK,
+        [row(width), row(width), row(model), row(LANES), pl.BlockSpec((2, LANES, cols), lambda i, ix: (0, 0, 0))],
+        [row(LANES), full(8, model), full(8, 4 * part)],
+        [shape(LEN, LANES), shape(8, model, F32), shape(8, 4 * part, F32)],
+        [],
+        cost(6 * LEN * model * LANES, 8 * LEN * model),
+    )(idx, dq, dv, normed, latent, up)
+
+
+def heads_back(idx, mine, dq, dk, dv, latent_low, down, found):
+    width = dq.shape[1]
+    part = width // 2
+    model = down.shape[1]
+    arrays, table = operands(found)
+    step_rows, cols = found[0][0].shape
+    n = len(arrays)
+    half_blocks = LEN // BLK // 2
+
+    def body(ix, dq_ref, dk_ref, dv_ref, low_ref, down_ref, *rest):
+        msgs = rest[:n]
+        out, w, sems = rest[n:]
+
+        @pl.when(pl.program_id(0) == 0)
+        def _():
+            load_all(
+                [(block_of(msgs, e), w.at[e[2], at_rows(ix[0] ^ e[3], step_rows), :]) for e in table],
+                sems,
+            )
+
+        total = jnp.dot(low_ref[...], down_ref[...], preferred_element_type=F32)
+        for a in range(2):
+            piece = jnp.concatenate([r[:, a * part : (a + 1) * part] for r in (dq_ref, dk_ref, dv_ref)], axis=1)
+            total = total + lax.dot_general(piece, w[a], NT, preferred_element_type=F32)
+        out[...] = total.astype(out.dtype)
+
+    def rows(i, ix):
+        return ((ix[2] if mine else 1 - ix[2]) * half_blocks + i, 0)
+
+    row = pl.BlockSpec((BLK, width), rows)
+    return call(
+        body,
+        "heads_back_own" if mine else "heads_back_send",
+        half_blocks,
+        [row, row, row, pl.BlockSpec((BLK, LANES), rows), full(LANES, model)] + [ANY] * n,
+        pl.BlockSpec((BLK, model), lambda i, ix: (i, 0)),
+        shape(LEN // 2, model, F32 if mine else BF16),
+        [pltpu.VMEM((2, model, cols), BF16), pltpu.SemaphoreType.DMA((len(table),))],
+        cost(2 * LEN * model * cols, 4 * model * cols),
+    )(idx, dq, dk, dv, latent_low, down, *arrays)
+
+
+def tokens_back(idx, in_own, in_recv, tokens, hidden_grad, gain):
+    model = tokens.shape[1]
+    half_blocks = LEN // BLK // 2
+    parts = 4
+    part = model // parts
+
+    def body(ix, own, recv, tok, hg, gain_ref, *rest):
+        outs, held = rest[:parts], rest[parts]
+        e = gain_ref[...] * (own[...] + recv[...].astype(F32))
+        hat, scaler = row_stats(tok[...].astype(F32))
+        held[...] = (hg[...] + norm_back(hat, scaler, e)).astype(BF16)
+        for k, out in enumerate(outs):
+            out[...] = held[:, at_rows((2 * ix[1] + ix[2]) ^ k, part)]
+
+    row = pl.BlockSpec((BLK, model), lambda i, ix: (i, 0))
+    return call(
+        body,
+        "tokens_back",
+        half_blocks,
+        [row, row, pl.BlockSpec((BLK, model), lambda i, ix: ((2 * ix[1] + ix[2]) * half_blocks + i, 0)), row, full(1, model)],
+        [pl.BlockSpec((BLK, part), lambda i, ix: (i, 0))] * parts,
+        [shape(LEN // 2, part)] * parts,
+        [pltpu.VMEM((BLK, model), BF16)],
+        cost(20 * LEN * model, 8 * LEN * model),
+    )(idx, in_own, in_recv, tokens, hidden_grad, gain)
+
+
+def output_rows(idx, own, recv):
+    model = own.shape[1]
+    half_blocks = LEN // BLK // 2
+    parts = 4
+    part = model // parts
+
+    def body(ix, own_ref, recv_ref, *rest):
+        outs, held = rest[:parts], rest[parts]
+        held[...] = (own_ref[...] + recv_ref[...].astype(F32)).astype(BF16)
+        for k, out in enumerate(outs):
+            out[...] = held[:, at_rows((2 * ix[1] + ix[2]) ^ k, part)]
+
+    row = pl.BlockSpec((BLK, model), lambda i, ix: (i, 0))
+    return call(
+        body,
+        "output_rows",
+        half_blocks,
+        [row, row],
+        [pl.BlockSpec((BLK, part), lambda i, ix: (i, 0))] * parts,
+        [shape(LEN // 2, part)] * parts,
+        [pltpu.VMEM((BLK, model), BF16)],
+        cost(2 * LEN * model, 6 * LEN * model),
+    )(idx, own, recv)
+
+
+def to_features(idx, pieces, bias):
+    pieces = [pieces[0], core_swap(pieces[1]), hop(pieces[2], 1, 0), both_swap(pieces[3])]
+    rows, part = pieces[0].shape
+    parts = len(pieces)
+
+    def body(ix, bias_ref, *rest):
+        outs = rest[parts]
+        for k in range(parts):
+            value = rest[k][...]
+            if bias is not None:
+                value = (value.astype(F32) + bias_ref[...]).astype(BF16)
+            outs[at_rows((2 * ix[1] + ix[2]) ^ k, rows), :] = value
+
+    extra = jnp.zeros((1, part), F32) if bias is None else bias
+    return call(
+        body,
+        "to_features",
+        1,
+        [full(1, part)] + [full(rows, part)] * parts,
+        full(parts * rows, part),
+        shape(parts * rows, part),
+        [],
+        cost(parts * rows * part, 4 * parts * rows * part),
+    )(idx, extra, *pieces)
+
+
+def both_swap(value):
+    total = lax.axis_size("dp") * lax.axis_size("mp")
+    return lax.ppermute(value, AXES, [(i, i ^ 3) for i in range(total)])
+
+
+def on_device_fast(
+    tokens,
+    cotangent,
+    group_ids,
+    pre_gain,
+    pre_shift,
+    frozen_triple_weight,
+    frozen_triple_bias,
+    out_weight,
+    out_bias,
+    mid_gain,
+    mid_shift,
+    fc_weight,
+    fc_bias,
+    proj_weight,
+    proj_bias,
+    down_master,
+    up_master,
+    down_first,
+    down_second,
+    up_first,
+    up_second,
+    learn_rate,
+):
+    tok_dev, model = tokens.shape
+    ranks = lax.axis_size("mp") // 2
+    place = lax.axis_index("mp")
+    idx = jnp.stack([lax.axis_index("dp"), place // ranks, place % ranks]).astype(jnp.int32)
+    line = lambda v: v.astype(F32).reshape(1, -1)
+    step_rows, _, head_part = frozen_triple_weight.shape
+    qkv_own = frozen_triple_weight.reshape(step_rows, 3 * head_part)
+    proj_rows = proj_weight.shape[0]
+    rest_own = jnp.concatenate([proj_weight, out_weight], axis=0)
+    qkv = gather_blocks(qkv_own, "x")
+    rest_own = after(rest_own, qkv[4][0])
+    rest = gather_blocks(rest_own, "y")
+    fc_own = after(fc_weight, rest[4][0])
+    fc = gather_blocks(fc_own, "x")
+    up_low = up_master.astype(BF16).reshape(2 * ADAPTER_RANK, head_part)
+    fc_rows = fc_bias.reshape(-1, head_part)
+    small = jnp.concatenate([frozen_triple_bias, fc_rows, up_low], axis=0)
+    small = jnp.stack([small, hop(small, 1, 0)])
+    bias = small[:, :3].reshape(2, 3 * head_part).astype(F32)
+    fc_line = small[:, 3 : 3 + fc_rows.shape[0]].reshape(1, -1).astype(F32)
+    up_both = small[:, 3 + fc_rows.shape[0] :] * jnp.bfloat16(ADAPTER_SCALE)
+    r = ADAPTER_RANK
+    up = jnp.zeros((2, LANES, 3 * head_part), BF16)
+    up = up.at[:, :r, :head_part].set(up_both[:, :r]).at[:, r : 2 * r, 2 * head_part :].set(up_both[:, r:])
+    down = jnp.zeros((LANES, model), BF16).at[: 2 * r].set(down_master.reshape(2 * r, model).astype(BF16))
+    groups = jnp.arange(LANES, dtype=jnp.int32)[None, :]
+    ids = group_ids[:, None]
+    counts = jnp.sum((ids == groups).astype(jnp.int32), axis=0, keepdims=True)
+    bits = 1
+    while bits < lax.axis_size("dp"):
+        counts = counts + hop(counts, 0, bits)
+        bits *= 2
+    weight_table = F32(tok_dev * lax.axis_size("dp")) / (GROUPS * counts.astype(F32))
+
+    queries, keys, values, normed, latent = project_heads(idx, tokens, line(pre_gain), line(pre_shift), bias, down, up, qkv)
+    mixed, logsum = attend_fast(queries, keys, values)
+    sent = core_swap(attention_out_send(idx, mixed, rest, proj_rows))
+    hidden, normed_mid = attention_out_own(
+        idx, mixed, sent, tokens, line(out_bias), line(mid_gain), line(mid_shift), rest, proj_rows
+    )
+    normed_other = core_swap(normed_mid)
+    active, slope = expand_units(idx, normed_mid, normed_other, fc_line, fc)
+    proj = rest
+    mid_recv = core_swap(units_back(idx, False, cotangent, ids, weight_table, slope, fc, proj))
+    mid_own = units_back(idx, True, cotangent, ids, weight_table, slope, fc, proj)
+    hidden_grad, hidden_low = hidden_back(idx, mid_own, mid_recv, cotangent, ids, weight_table, hidden, line(mid_gain))
+    hidden_other = core_swap(hidden_low)
+    out_recv = core_swap(units_out(idx, False, active, hidden, proj))
+    out_own = units_out(idx, True, active, hidden, proj)
+    mixed_grad = attended_back(idx, hidden_low, hidden_other, rest, proj_rows, mixed.shape[1])
+    dq, dk, dv = attend_back_fast(queries, keys, values, mixed, mixed_grad, logsum)
+    latent_low, down_term, up_term = adapter_back(idx, dq, dv, normed, latent, up)
+    in_recv = core_swap(heads_back(idx, False, dq, dk, dv, latent_low, down, qkv))
+    in_own = heads_back(idx, True, dq, dk, dv, latent_low, down, qkv)
+    output = to_features(idx, output_rows(idx, out_own, out_recv), line(proj_bias))
+    input_grad = to_features(idx, tokens_back(idx, in_own, in_recv, tokens, hidden_grad, line(pre_gain)), None)
+    up_term = up_term.reshape(2 * r, 2, 2, head_part)
+    mine = jnp.concatenate([up_term[:r, 0, 0], up_term[r:, 0, 1]], axis=0)
+    theirs = jnp.concatenate([up_term[:r, 1, 0], up_term[r:, 1, 1]], axis=0)
+    down_sum = down_term + core_swap(down_term)
+    got = hop(jnp.concatenate([down_sum, theirs], axis=1), 1, 0)
+    both = jnp.concatenate([down_sum, mine], axis=1) + got
+    bits = 1
+    while bits < lax.axis_size("dp"):
+        both = both + hop(both, 0, bits)
+        bits *= 2
+    down_grad = both[:, :model].reshape(down_master.shape)
+    up_grad = ADAPTER_SCALE * both[:, model:].reshape(up_master.shape)
+    step_value = jnp.float32(STEP)
+    down_new, down_moment, down_square = adam_update(
+        down_master, down_first, down_second, down_grad, step_value, learn_rate
+    )
+    up_new, up_moment, up_square = adam_update(up_master, up_first, up_second, up_grad, step_value, learn_rate)
+    return (
+        output,
+        input_grad,
+        down_new,
+        down_moment,
+        down_square,
+        down_new.astype(BF16),
+        up_new,
+        up_moment,
+        up_square,
+        up_new.astype(BF16),
+    )
+
+
+def pick_body(mesh):
+    return on_device_fast if mesh.shape["dp"] == 8 and mesh.shape["mp"] == 4 else on_device_general
+
+
 def solution(mesh):
+    body = pick_body(mesh)
     return jax.shard_map(
-        on_device,
+        body,
         mesh=mesh,
         in_specs=(
             P("dp", None),

time: 571 us -> 417 us (0.73)
  Pallas kernels: 0 us -> 161 us
  matrix products: 113 us -> 0 us
  blocking collectives: 99.7 us -> 0 us
  waiting for transfers between devices: 249 us -> 187 us
  other arithmetic: 67.9 us -> 8.52 us
  starting transfers between devices: 0.5 us -> 46.1 us
  between operations: 16.5 us -> 1.91 us
  local copies, waits for them, and re-layouts: 20.8 us -> 12.3 us
    ppermute x0 -> x48, waiting for transfers between devices: none -> 187 us  [the longest x37 176 us: hop(): return lax.ppermute(value, AXES, [(i, i ^ flip) for i in range(total)])]
    pallas_call x0 -> x19, Pallas kernels: none -> 161 us  [the longest x2 25.1 us: units_back(): call(body, 'units_back_own' if mine else 'units_back_send', half_blocks,...]
    psum x3 -> x0, waiting for transfers between devices: 158 us -> none  [the longest x1 73.4 us: on_device(): attn_sum = lax.psum(head_term, 'mp').astype(jnp.float32)]
    dot_general x56 -> x0, matrix products: 113 us -> none  [the longest x2 20.4 us: on_device(): jnp.einsum('tf,df->td', pre_grad, fc_full, preferred_element_type=jnp.flo...]
    all_gather x3 -> x0, waiting for transfers between devices: 89.6 us -> none  [the longest x1 44.4 us: fetch_frozen(): lax.all_gather(fc_weight, 'dp', axis=0, tiled=True)]
    psum x3 -> x0, blocking collectives: 69.1 us -> none  [the longest x1 38 us: on_device(): down_grad = lax.psum(grad_down, ('dp', 'mp')).reshape(down_master.shape)]
    ppermute x0 -> x48, starting transfers between devices: none -> 46.1 us  [the longest x37 42 us: hop(): return lax.ppermute(value, AXES, [(i, i ^ flip) for i in range(total)])]
    all_gather x1 -> x0, blocking collectives: 30.6 us -> none  [fetch_frozen(): lax.all_gather(out_weight, 'dp', axis=1, tiled=True)]
  transfers between devices with their start and end apart: 8 -> 48, of which waited for: 6 -> 24; matrix products, arithmetic and copies ran while one was open for 22% -> 3% of each run, Pallas kernels for 0% -> 27%
where the time goes in v1:
time: 417 us; the launch traced here: 416 us
  waiting for transfers between devices  187 us (45%)
  Pallas kernels  161 us (39%)
  starting transfers between devices  46.1 us (11%)
  local copies, waits for them, and re-layouts  12.3 us (3%)
  other arithmetic  8.52 us (2%)
    ppermute x37, waiting for transfers between devices, hop(): return lax.ppermute(value, AXES, [(i, i ^ flip) for i in range(total)])  176 us
    ppermute x37, starting transfers between devices, hop(): return lax.ppermute(value, AXES, [(i, i ^ flip) for i in range(total)])  42 us
    pallas_call x2, Pallas kernels, units_back(): call(body, 'units_back_own' if mine else 'units_back_send', half_blocks,...  25.1 us
    pallas_call x1, Pallas kernels, attend_back_fast(): pl.pallas_call(body, grid=(pairs,), out_shape=(shape(length, width),) * 3...  19.4 us
    pallas_call x2, Pallas kernels, units_out(): call(body, 'units_out_own' if mine else 'units_out_send', half_blocks, [p...  15.8 us
    pallas_call x1, Pallas kernels, expand_units(): call(body, 'expand_units', 2 * half_blocks, [pl.BlockSpec((BLK, model), l...  15.5 us
    pallas_call x2, Pallas kernels, heads_back(): call(body, 'heads_back_own' if mine else 'heads_back_send', half_blocks,...  14.9 us
    pallas_call x1, Pallas kernels, attend_fast(): pl.pallas_call(body, grid=(pairs,), out_shape=(shape(length, width), jax....  14.6 us
  transfers between devices with their start and end apart: 48, of which 24 were waited for; matrix products, arithmetic and copies ran while one was open for 3% of the time, Pallas kernels for 27%

profile of v1, /device:TPU:0, one launch (start us, length us, event | category | flops | bytes accessed | tf_op | source)
XLA Modules:
  0.0 416.1 jit_solution(14612052346179421311)
XLA Ops:
  13.0 10.8 %collective-permute-done.5 = bf16[128,768]{1,0:T(8,128)(2,1)S(1)} collective-permute-done((bf16[128,768]{1,0:T(8,128)(2,1)S(1)}, bf16[128,768]{1,0:T(8,128)(2,1)S(1)}, u32[]{:S(2)}, u32[]{:S(2)}) %collective-permute-start.5) | collective-permute-done | bytes 196640 | tf_op jit(solution)/shard_map/ppermute | solution.py:384
  29.1 8.2 %collective-permute-done.15 = bf16[1280,128]{1,0:T(8,128)(2,1)S(1)} collective-permute-done((bf16[1280,128]{1,0:T(8,128)(2,1)S(1)}, bf16[1280,128]{1,0:T(8,128)(2,1)S(1)}, u32[]{:S(2)}, u32[]{:S(2)}) %collective-permute-start.15) | collective-permute-done | bytes 327712 | tf_op jit(solution)/shard_map/ppermute | solution.py:384
  37.2 16.2 %collective-permute-done.14 = bf16[1280,128]{1,0:T(8,128)(2,1)S(1)} collective-permute-done((bf16[1280,128]{1,0:T(8,128)(2,1)S(1)}, bf16[1280,128]{1,0:T(8,128)(2,1)S(1)}, u32[]{:S(2)}, u32[]{:S(2)}) %collective-permute-start.14) | collective-permute-done | bytes 327712 | tf_op jit(solution)/shard_map/ppermute | solution.py:384
  58.7 9.7 %collective-permute-done.8.rest_6_ = bf16[3,128,768]{2,1,0:T(8,128)(2,1)} collective-permute-done((bf16[3,128,768]{2,1,0:T(8,128)(2,1)}, bf16[3,128,768]{2,1,0:T(8,128)(2,1)}, u32[]{:S(2)}, u32[]{:S(2)}) %collective-permute-start.8) | collective-permute-done | bytes 589856 | tf_op jit(solution)/shard_map/ppermute | solution.py:384
  72.5 32.5 %collective-permute-done = bf16[15,256]{1,0:T(8,128)(2,1)S(1)} collective-permute-done((bf16[15,256]{1,0:T(8,128)(2,1)S(1)}, bf16[15,256]{1,0:T(8,128)(2,1)S(1)}, u32[]{:S(2)}, u32[]{:S(2)}) %collective-permute-start) | collective-permute-done | bytes 7712 | tf_op jit(solution)/shard_map/ppermute | solution.py:384
  126.1 11.7 %project_heads.1 = (bf16[1024,512]{1,0:T(8,128)(2,1)}, bf16[1024,512]{1,0:T(8,128)(2,1)}, bf16[1024,512]{1,0:T(8,128)(2,1)}, bf16[1024,1024]{1,0:T(8,128)(2,1)}, bf16[1024,128]{1,0:T(8,128)(2,1)}) custom-call(s32[3]{0:T(128)} %pad_add_fusion.ix, bf16[2048,1024]{1,0:T(8,128)(2,1)} %tok.5, f32[1,1024]{1,0:T(1,128)} %bitcast.53, f32[1,1024]{1,0:T(1,128)} %bitcast.59, ...), custom_call_target="tpu_custom_call" | custom-call | flops 3221225472 | bytes 16777216 | tf_op jit(solution)/shard_map/project_heads/pallas_call | solution.py:491
  137.8 14.6 %attend.1 = (bf16[1024,512]{1,0:T(8,128)(2,1)}, f32[4,8,1024]{2,1,0:T(8,128)}) custom-call(bf16[1024,512]{1,0:T(8,128)(2,1)} %get-tuple-element.75.q_ref, bf16[1024,512]{1,0:T(8,128)(2,1)} %get-tuple-element.76.k_ref, bf16[1024,512]{1,0:T(8,128)(2,1)} %get-tuple-element.77.v_ref), custom_call_target="tpu_custom_call" | custom-call | flops 4294967296 | bytes 4194304 | tf_op jit(solution)/shard_map/attend/pallas_call | solution.py:546
  152.4 10.0 %collective-permute-done.18.rest_7_.rest_8_.rest_15_ = bf16[3,1280,128]{2,1,0:T(8,128)(2,1)} collective-permute-done((bf16[3,1280,128]{2,1,0:T(8,128)(2,1)S(1)}, bf16[3,1280,128]{2,1,0:T(8,128)(2,1)}, u32[]{:S(2)}, u32[]{:S(2)}) %collective-permute-start.18) | collective-permute-done | bytes 983072 | tf_op jit(solution)/shard_map/ppermute | solution.py:384
  171.9 6.7 %collective-permute-done.26 = bf16[128,1024]{1,0:T(8,128)(2,1)S(1)} collective-permute-done((bf16[128,1024]{1,0:T(8,128)(2,1)S(1)}, bf16[128,1024]{1,0:T(8,128)(2,1)S(1)}, u32[]{:S(2)}, u32[]{:S(2)}) %collective-permute-start.26) | collective-permute-done | bytes 262176 | tf_op jit(solution)/shard_map/ppermute | solution.py:384
  178.5 13.0 %collective-permute-done.25 = bf16[128,1024]{1,0:T(8,128)(2,1)S(1)} collective-permute-done((bf16[128,1024]{1,0:T(8,128)(2,1)S(1)}, bf16[128,1024]{1,0:T(8,128)(2,1)S(1)}, u32[]{:S(2)}, u32[]{:S(2)}) %collective-permute-start.25) | collective-permute-done | bytes 262176 | tf_op jit(solution)/shard_map/ppermute | solution.py:384
  203.6 7.2 %collective-permute-done.28.rest_6_ = bf16[3,128,1024]{2,1,0:T(8,128)(2,1)S(1)} collective-permute-done((bf16[3,128,1024]{2,1,0:T(8,128)(2,1)S(1)}, bf16[3,128,1024]{2,1,0:T(8,128)(2,1)S(1)}, u32[]{:S(2)}, u32[]{:S(2)}) %collective-permute-start.28) | collective-permute-done | bytes 786464 | tf_op jit(solution)/shard_map/ppermute | solution.py:384
  226.3 18.3 %collective-permute-done.21.rest_1_ = bf16[128,1024]{1,0:T(8,128)(2,1)} collective-permute-done((bf16[128,1024]{1,0:T(8,128)(2,1)S(1)}, bf16[128,1024]{1,0:T(8,128)(2,1)}, u32[]{:S(2)}, u32[]{:S(2)}) %collective-permute-start.21) | collective-permute-done | bytes 262176 | tf_op jit(solution)/shard_map/ppermute | solution.py:384
  246.3 6.5 %collective-permute-done.23.rest_3_ = bf16[128,1024]{1,0:T(8,128)(2,1)} collective-permute-done((bf16[128,1024]{1,0:T(8,128)(2,1)}, bf16[128,1024]{1,0:T(8,128)(2,1)}, u32[]{:S(2)}, u32[]{:S(2)}) %collective-permute-start.23) | collective-permute-done | bytes 262176 | tf_op jit(solution)/shard_map/ppermute | solution.py:384
  253.9 15.5 %expand_units.1 = (bf16[1024,2048]{1,0:T(8,128)(2,1)}, bf16[1024,2048]{1,0:T(8,128)(2,1)}) custom-call(s32[3]{0:T(128)} %pad_add_fusion.ix, bf16[512,1024]{1,0:T(8,128)(2,1)} %get-tuple-element.80.own_ref, bf16[512,1024]{1,0:T(8,128)(2,1)} %collective-permute-done.20.other_ref, f32[1,2048]{1,0:T(1,128)} %reshape.219.bias_ref, bf16[128,1024]{1,0:T(8,128)(2,1)} %rest_0_.2, ...), custom_call_target="tpu_custom_call" | custom-call | flops 4294967296 | bytes 12582912 | tf_op jit(solution)/shard_map/expand_units/pallas_call | solution.py:675
  269.4 12.6 %units_back_send.1 = bf16[512,1024]{1,0:T(8,128)(2,1)} custom-call(s32[3]{0:T(128)} %pad_add_fusion.ix, bf16[2048,1024]{1,0:T(8,128)(2,1)} %cot.5, s32[2048,1]{1,0:T(8,128)} %copy.52.ids_ref, f32[1,128]{1,0:T(1,128)} %multiply_divide_fusion.table_ref, bf16[1024,2048]{1,0:T(8,128)(2,1)} %get-tuple-element.88.slope_ref, bf16[128,1024]{1,0:T(8,128)(2,1)} %rest_0_.2, ...), custom_call_target="tpu_custom_call" | custom-call | flops 4294967296 | bytes 8388608 | tf_op jit(solution)/shard_map/units_back_send/pallas_call | solution.py:743
  282.1 12.5 %units_back_own.1.own = f32[512,1024]{1,0:T(8,128)} custom-call(s32[3]{0:T(128)} %pad_add_fusion.ix, bf16[2048,1024]{1,0:T(8,128)(2,1)} %cot.5, s32[2048,1]{1,0:T(8,128)} %copy.52.ids_ref, f32[1,128]{1,0:T(1,128)} %multiply_divide_fusion.table_ref, bf16[1024,2048]{1,0:T(8,128)(2,1)} %get-tuple-element.88.slope_ref, bf16[128,1024]{1,0:T(8,128)(2,1)} %rest_0_.2, ...), custom_call_target="tpu_custom_call" | custom-call | flops 4294967296 | bytes 8388608 | tf_op jit(solution)/shard_map/units_back_own/pallas_call | solution.py:743
  301.7 7.6 %units_out_send.1 = bf16[512,1024]{1,0:T(8,128)(2,1)} custom-call(s32[3]{0:T(128)} %pad_add_fusion.ix, bf16[1024,2048]{1,0:T(8,128)(2,1)} %get-tuple-element.82.act, bf16[1280,128]{1,0:T(8,128)(2,1)} %copy-done.3, bf16[1280,128]{1,0:T(8,128)(2,1)} %collective-permute-done.10.rest_1_.rest_2_.rest_9_, bf16[1280,128]{1,0:T(8,128)(2,1)} %copy-done.4, ...), custom_call_target="tpu_custom_call" | custom-call | flops 2147483648 | bytes 8388608 | tf_op jit(solution)/shard_map/units_out_send/pallas_call | solution.py:789
  310.4 6.6 %attended_back.1.g_ref = bf16[1024,512]{1,0:T(8,128)(2,1)} custom-call(s32[3]{0:T(128)} %pad_add_fusion.ix, bf16[512,1024]{1,0:T(8,128)(2,1)} %get-tuple-element.89.own_ref, bf16[512,1024]{1,0:T(8,128)(2,1)} %copy-done.15, bf16[1280,128]{1,0:T(8,128)(2,1)} %copy-done.3, bf16[1280,128]{1,0:T(8,128)(2,1)} %collective-permute-done.10.rest_1_.rest_2_.rest_9_, ...), custom_call_target="tpu_custom_call" | custom-call | flops 1073741824 | bytes 4194304 | tf_op jit(solution)/shard_map/attended_back/pallas_call | solution.py:859
  317.0 19.4 %attend_back.1 = (bf16[1024,512]{1,0:T(8,128)(2,1)}, bf16[1024,512]{1,0:T(8,128)(2,1)}, bf16[1024,512]{1,0:T(8,128)(2,1)}) custom-call(bf16[1024,512]{1,0:T(8,128)(2,1)} %get-tuple-element.75.q_ref, bf16[1024,512]{1,0:T(8,128)(2,1)} %get-tuple-element.76.k_ref, bf16[1024,512]{1,0:T(8,128)(2,1)} %get-tuple-element.77.v_ref, ...), custom_call_target="tpu_custom_call" | custom-call | flops 10737418240 | bytes 8388608 | tf_op jit(solution)/shard_map/attend_back/pallas_call | solution.py:918
  336.4 6.2 %adapter_back.1 = (bf16[1024,128]{1,0:T(8,128)(2,1)}, f32[8,1024]{1,0:T(8,128)}, f32[8,1024]{1,0:T(8,128)}) custom-call(s32[3]{0:T(128)} %pad_add_fusion.ix, bf16[1024,512]{1,0:T(8,128)(2,1)} %get-tuple-element.91.dq_ref, bf16[1024,512]{1,0:T(8,128)(2,1)} %get-tuple-element.93.dv_ref, bf16[1024,1024]{1,0:T(8,128)(2,1)} %get-tuple-element.94.normed_ref, ...), custom_call_target="tpu_custom_call" | custom-call | flops 805306368 | bytes 8388608 | tf_op jit(solution)/shard_map/adapter_back/pallas_call | solution.py:957
  342.5 7.5 %heads_back_send.1 = bf16[512,1024]{1,0:T(8,128)(2,1)} custom-call(s32[3]{0:T(128)} %pad_add_fusion.ix, bf16[1024,512]{1,0:T(8,128)(2,1)} %get-tuple-element.91.dq_ref, bf16[1024,512]{1,0:T(8,128)(2,1)} %get-tuple-element.92.dk_ref, bf16[1024,512]{1,0:T(8,128)(2,1)} %get-tuple-element.93.dv_ref, bf16[1024,128]{1,0:T(8,128)(2,1)} %get-tuple-element.96.low_ref, ...), custom_call_target="tpu_custom_call" | custom-call | flops 1610612736 | bytes 3145728 | tf_op jit(solution)/shard_map/heads_back_send/pallas_call | solution.py:999
  354.4 8.2 %units_out_own.1.own_ref = f32[512,1024]{1,0:T(8,128)} custom-call(s32[3]{0:T(128)} %pad_add_fusion.ix, bf16[1024,2048]{1,0:T(8,128)(2,1)} %get-tuple-element.82.act, f32[512,1024]{1,0:T(8,128)} %get-tuple-element.83.rest_0_.hid, bf16[1280,128]{1,0:T(8,128)(2,1)} %copy-done.3, bf16[1280,128]{1,0:T(8,128)(2,1)} %collective-permute-done.10.rest_1_.rest_2_.rest_9_, ...), custom_call_target="tpu_custom_call" | custom-call | flops 2147483648 | bytes 8388608 | tf_op jit(solution)/shard_map/units_out_own/pallas_call | solution.py:789
  385.0 7.4 %heads_back_own.1.own = f32[512,1024]{1,0:T(8,128)} custom-call(s32[3]{0:T(128)} %pad_add_fusion.ix, bf16[1024,512]{1,0:T(8,128)(2,1)} %get-tuple-element.91.dq_ref, bf16[1024,512]{1,0:T(8,128)(2,1)} %get-tuple-element.92.dk_ref, bf16[1024,512]{1,0:T(8,128)(2,1)} %get-tuple-element.93.dv_ref, bf16[1024,128]{1,0:T(8,128)(2,1)} %get-tuple-element.96.low_ref, ...), custom_call_target="tpu_custom_call" | custom-call | flops 1610612736 | bytes 3145728 | tf_op jit(solution)/shard_map/heads_back_own/pallas_call | solution.py:999
  401.9 6.4 %collective-permute-done.41.rest_2_ = bf16[512,256]{1,0:T(8,128)(2,1)S(1)} collective-permute-done((bf16[512,256]{1,0:T(8,128)(2,1)}, bf16[512,256]{1,0:T(8,128)(2,1)S(1)}, u32[]{:S(2)}, u32[]{:S(2)}) %collective-permute-start.41) | collective-permute-done | bytes 262176 | tf_op jit(solution)/shard_map/ppermute | solution.py:384
  (223 shorter events, 139.2 us)
Async XLA Ops:
  7.1 16.7 %collective-permute-start.5 = (bf16[128,768]{1,0:T(8,128)(2,1)S(1)}, bf16[128,768]{1,0:T(8,128)(2,1)S(1)}, u32[]{:S(2)}, u32[]{:S(2)}) collective-permute-start(bf16[128,768]{1,0:T(8,128)(2,1)S(1)} %copy.51.rest_0_), channel_id=1, source_target_pairs={{0,16},{1,17},{2,18},{3,19},{4,20},{5,21},{6,22},{7,23},{8,24},{9,... | collective-permute-start | bytes 589832 | tf_op jit(solution)/shard_map/ppermute | solution.py:384
  7.1 16.7 %collective-permute-start.4 = (bf16[128,768]{1,0:T(8,128)(2,1)S(1)}, bf16[128,768]{1,0:T(8,128)(2,1)S(1)}, u32[]{:S(2)}, u32[]{:S(2)}) collective-permute-start(bf16[128,768]{1,0:T(8,128)(2,1)S(1)} %copy.51.rest_0_), channel_id=1, source_target_pairs={{0,8},{1,9},{2,10},{3,11},{4,12},{5,13},{6,14},{7,15},{8,0},{9,1},... | collective-permute-start | bytes 589832 | tf_op jit(solution)/shard_map/ppermute | solution.py:384
  27.1 26.3 %collective-permute-start.14 = (bf16[1280,128]{1,0:T(8,128)(2,1)S(1)}, bf16[1280,128]{1,0:T(8,128)(2,1)S(1)}, u32[]{:S(2)}, u32[]{:S(2)}) collective-permute-start(bf16[1280,128]{1,0:T(8,128)(2,1)S(1)} %pad_maximum_fusion.3.rest_0_.rest_1_.rest_8_), channel_id=1, source_target_pairs={{0,16},{1,17},{2,18},{3,19},{4,20},{5,21},{6,22},{7,23},{8,24},{9,... | collective-permute-start | bytes 983048 | tf_op jit(solution)/shard_map/ppermute | solution.py:384
  27.1 26.3 %collective-permute-start.13 = (bf16[1280,128]{1,0:T(8,128)(2,1)S(1)}, bf16[1280,128]{1,0:T(8,128)(2,1)S(1)}, u32[]{:S(2)}, u32[]{:S(2)}) collective-permute-start(bf16[1280,128]{1,0:T(8,128)(2,1)S(1)} %pad_maximum_fusion.3.rest_0_.rest_1_.rest_8_), channel_id=1, source_target_pairs={{0,8},{1,9},{2,10},{3,11},{4,12},{5,13},{6,14},{7,15},{8,0},{9,1},... | collective-permute-start | bytes 983048 | tf_op jit(solution)/shard_map/ppermute | solution.py:384
  53.5 65.1 %collective-permute-start.16 = (bf16[3,1280,128]{2,1,0:T(8,128)(2,1)S(1)}, bf16[3,1280,128]{2,1,0:T(8,128)(2,1)S(1)}, u32[]{:S(2)}, u32[]{:S(2)}) collective-permute-start(bf16[3,1280,128]{2,1,0:T(8,128)(2,1)S(1)} %pad_maximum_fusion.rest_4_.rest_5_.rest_12_), channel_id=1, source_target_pairs={{0,2},{1,3},{2,0},{3,1},{4,6},{5,7},{6,4},{7,5},{8,10},{9,11},{10,... | collective-permute-start | bytes 2949128 | tf_op jit(solution)/shard_map/ppermute | solution.py:384
  56.6 49.9 %collective-permute-start.1 = (bf16[128,768]{1,0:T(8,128)(2,1)S(1)}, bf16[128,768]{1,0:T(8,128)(2,1)S(1)}, u32[]{:S(2)}, u32[]{:S(2)}) collective-permute-start(bf16[128,768]{1,0:T(8,128)(2,1)S(1)} %copy.51.rest_0_), channel_id=1, source_target_pairs={{0,2},{1,3},{2,0},{3,1},{4,6},{5,7},{6,4},{7,5},{8,10},{9,11},{10,... | collective-permute-start | bytes 589832 | tf_op jit(solution)/shard_map/ppermute | solution.py:384
  57.2 68.4 %collective-permute-start.7 = (bf16[3,128,768]{2,1,0:T(8,128)(2,1)}, bf16[3,128,768]{2,1,0:T(8,128)(2,1)}, u32[]{:S(2)}, u32[]{:S(2)}) collective-permute-start(bf16[3,128,768]{2,1,0:T(8,128)(2,1)} %pad_maximum_fusion.2.rest_4_), channel_id=1, source_target_pairs={{0,2},{1,3},{2,0},{3,1},{4,6},{5,7},{6,4},{7,5},{8,10},{9,11},{10,... | collective-permute-start | bytes 1769480 | tf_op jit(solution)/shard_map/ppermute | solution.py:384
  68.4 57.7 %collective-permute-start.9 = (bf16[3,128,768]{2,1,0:T(8,128)(2,1)}, bf16[3,128,768]{2,1,0:T(8,128)(2,1)}, u32[]{:S(2)}, u32[]{:S(2)}) collective-permute-start(bf16[3,128,768]{2,1,0:T(8,128)(2,1)} %collective-permute-done.8.rest_6_), channel_id=1, source_target_pairs={{0,2},{1,3},{2,0},{3,1},{4,6},{5,7},{6,4},{7,5},{8,10},{9,11},{10,... | collective-permute-start | bytes 1769480 | tf_op jit(solution)/shard_map/ppermute | solution.py:384
  69.0 36.0 %collective-permute-start = (bf16[15,256]{1,0:T(8,128)(2,1)S(1)}, bf16[15,256]{1,0:T(8,128)(2,1)S(1)}, u32[]{:S(2)}, u32[]{:S(2)}) collective-permute-start(bf16[15,256]{1,0:T(8,128)(2,1)S(1)} %get-tuple-element.119), channel_id=1, source_target_pairs={{0,2},{1,3},{2,0},{3,1},{4,6},{5,7},{6,4},{7,5},{8,10},{9,11},{10,... | collective-permute-start | bytes 23048 | tf_op jit(solution)/shard_map/ppermute | solution.py:384
  117.1 35.3 %collective-permute-start.17 = (bf16[3,1280,128]{2,1,0:T(8,128)(2,1)S(1)}, bf16[3,1280,128]{2,1,0:T(8,128)(2,1)S(1)}, u32[]{:S(2)}, u32[]{:S(2)}) collective-permute-start(bf16[3,1280,128]{2,1,0:T(8,128)(2,1)S(1)} %pad_maximum_fusion.rest_4_.rest_5_.rest_12_), channel_id=1, source_target_pairs={{0,4},{1,5},{2,6},{3,7},{4,0},{5,1},{6,2},{7,3},{8,12},{9,13},{10,... | collective-permute-start | bytes 2949128 | tf_op jit(solution)/shard_map/ppermute | solution.py:384
  118.7 43.8 %collective-permute-start.18 = (bf16[3,1280,128]{2,1,0:T(8,128)(2,1)S(1)}, bf16[3,1280,128]{2,1,0:T(8,128)(2,1)}, u32[]{:S(2)}, u32[]{:S(2)}) collective-permute-start(bf16[3,1280,128]{2,1,0:T(8,128)(2,1)S(1)} %collective-permute-done.16.rest_5_.rest_6_.rest_13_), channel_id=1, source_target_pairs={{0,4},{1,5},{2,6},{3,7},{4,0},{5,1},{6,2},{7,3},{8,12},{9,13},{10,... | collective-permute-start | bytes 2949128 | tf_op jit(solution)/shard_map/ppermute | solution.py:384
  124.1 28.4 %collective-permute-start.10 = (bf16[1280,128]{1,0:T(8,128)(2,1)S(1)}, bf16[1280,128]{1,0:T(8,128)(2,1)}, u32[]{:S(2)}, u32[]{:S(2)}) collective-permute-start(bf16[1280,128]{1,0:T(8,128)(2,1)S(1)} %pad_maximum_fusion.3.rest_0_.rest_1_.rest_8_), channel_id=1, source_target_pairs={{0,2},{1,3},{2,0},{3,1},{4,6},{5,7},{6,4},{7,5},{8,10},{9,11},{10,... | collective-permute-start | bytes 983048 | tf_op jit(solution)/shard_map/ppermute | solution.py:384
  125.6 26.9 %collective-permute-start.12 = (bf16[1280,128]{1,0:T(8,128)(2,1)S(1)}, bf16[1280,128]{1,0:T(8,128)(2,1)}, u32[]{:S(2)}, u32[]{:S(2)}) collective-permute-start(bf16[1280,128]{1,0:T(8,128)(2,1)S(1)} %collective-permute-done.11.rest_2_.rest_3_.rest_10_), channel_id=1, source_target_pairs={{0,2},{1,3},{2,0},{3,1},{4,6},{5,7},{6,4},{7,5},{8,10},{9,11},{10,... | collective-permute-start | bytes 983048 | tf_op jit(solution)/shard_map/ppermute | solution.py:384
  167.3 27.7 %collective-permute-start.19 = (bf16[512,1024]{1,0:T(8,128)(2,1)}, bf16[512,1024]{1,0:T(8,128)(2,1)S(1)}, u32[]{:S(2)}, u32[]{:S(2)}) collective-permute-start(bf16[512,1024]{1,0:T(8,128)(2,1)} %attention_out_send.1), channel_id=1, source_target_pairs={{0,1},{1,0},{2,3},{3,2},{4,5},{5,4},{6,7},{7,6},{8,9},{9,8},{10,11... | collective-permute-start | bytes 3145736 | tf_op jit(solution)/shard_map/ppermute | solution.py:389
  169.4 22.1 %collective-permute-start.25 = (bf16[128,1024]{1,0:T(8,128)(2,1)S(1)}, bf16[128,1024]{1,0:T(8,128)(2,1)S(1)}, u32[]{:S(2)}, u32[]{:S(2)}) collective-permute-start(bf16[128,1024]{1,0:T(8,128)(2,1)S(1)} %copy-done.11), channel_id=1, source_target_pairs={{0,16},{1,17},{2,18},{3,19},{4,20},{5,21},{6,22},{7,23},{8,24},{9,... | collective-permute-start | bytes 786440 | tf_op jit(solution)/shard_map/ppermute | solution.py:384
  169.4 22.1 %collective-permute-start.24 = (bf16[128,1024]{1,0:T(8,128)(2,1)S(1)}, bf16[128,1024]{1,0:T(8,128)(2,1)S(1)}, u32[]{:S(2)}, u32[]{:S(2)}) collective-permute-start(bf16[128,1024]{1,0:T(8,128)(2,1)S(1)} %copy-done.11), channel_id=1, source_target_pairs={{0,8},{1,9},{2,10},{3,11},{4,12},{5,13},{6,14},{7,15},{8,0},{9,1},... | collective-permute-start | bytes 786440 | tf_op jit(solution)/shard_map/ppermute | solution.py:384
  191.6 19.2 %collective-permute-start.28 = (bf16[3,128,1024]{2,1,0:T(8,128)(2,1)S(1)}, bf16[3,128,1024]{2,1,0:T(8,128)(2,1)S(1)}, u32[]{:S(2)}, u32[]{:S(2)}) collective-permute-start(bf16[3,128,1024]{2,1,0:T(8,128)(2,1)S(1)} %pad_maximum_fusion.1.rest_4_), channel_id=1, source_target_pairs={{0,4},{1,5},{2,6},{3,7},{4,0},{5,1},{6,2},{7,3},{8,12},{9,13},{10,... | collective-permute-start | bytes 2359304 | tf_op jit(solution)/shard_map/ppermute | solution.py:384
  202.0 50.8 %collective-permute-start.20 = (bf16[512,1024]{1,0:T(8,128)(2,1)}, bf16[512,1024]{1,0:T(8,128)(2,1)}, u32[]{:S(2)}, u32[]{:S(2)}) collective-permute-start(bf16[512,1024]{1,0:T(8,128)(2,1)} %get-tuple-element.80.own_ref), channel_id=1, source_target_pairs={{0,1},{1,0},{2,3},{3,2},{4,5},{5,4},{6,7},{7,6},{8,9},{9,8},{10,11... | collective-permute-start | bytes 3145736 | tf_op jit(solution)/shard_map/ppermute | solution.py:389
  202.1 50.7 %collective-permute-start.27 = (bf16[3,128,1024]{2,1,0:T(8,128)(2,1)S(1)}, bf16[3,128,1024]{2,1,0:T(8,128)(2,1)S(1)}, u32[]{:S(2)}, u32[]{:S(2)}) collective-permute-start(bf16[3,128,1024]{2,1,0:T(8,128)(2,1)S(1)} %pad_maximum_fusion.1.rest_4_), channel_id=1, source_target_pairs={{0,2},{1,3},{2,0},{3,1},{4,6},{5,7},{6,4},{7,5},{8,10},{9,11},{10,... | collective-permute-start | bytes 2359304 | tf_op jit(solution)/shard_map/ppermute | solution.py:384
  210.8 42.0 %collective-permute-start.29 = (bf16[3,128,1024]{2,1,0:T(8,128)(2,1)S(1)}, bf16[3,128,1024]{2,1,0:T(8,128)(2,1)S(1)}, u32[]{:S(2)}, u32[]{:S(2)}) collective-permute-start(bf16[3,128,1024]{2,1,0:T(8,128)(2,1)S(1)} %collective-permute-done.28.rest_6_), channel_id=1, source_target_pairs={{0,2},{1,3},{2,0},{3,1},{4,6},{5,7},{6,4},{7,5},{8,10},{9,11},{10,... | collective-permute-start | bytes 2359304 | tf_op jit(solution)/shard_map/ppermute | solution.py:384
  212.3 32.3 %collective-permute-start.21 = (bf16[128,1024]{1,0:T(8,128)(2,1)S(1)}, bf16[128,1024]{1,0:T(8,128)(2,1)}, u32[]{:S(2)}, u32[]{:S(2)}) collective-permute-start(bf16[128,1024]{1,0:T(8,128)(2,1)S(1)} %copy-done.11), channel_id=1, source_target_pairs={{0,2},{1,3},{2,0},{3,1},{4,6},{5,7},{6,4},{7,5},{8,10},{9,11},{10,... | collective-permute-start | bytes 786440 | tf_op jit(solution)/shard_map/ppermute | solution.py:384
  224.8 21.5 %collective-permute-start.22 = (bf16[128,1024]{1,0:T(8,128)(2,1)S(1)}, bf16[128,1024]{1,0:T(8,128)(2,1)}, u32[]{:S(2)}, u32[]{:S(2)}) collective-permute-start(bf16[128,1024]{1,0:T(8,128)(2,1)S(1)} %copy-done.11), channel_id=1, source_target_pairs={{0,4},{1,5},{2,6},{3,7},{4,0},{5,1},{6,2},{7,3},{8,12},{9,13},{10,... | collective-permute-start | bytes 786440 | tf_op jit(solution)/shard_map/ppermute | solution.py:384
  309.3 53.3 %collective-permute-start.30 = (bf16[512,1024]{1,0:T(8,128)(2,1)}, bf16[512,1024]{1,0:T(8,128)(2,1)S(1)}, u32[]{:S(2)}, u32[]{:S(2)}) collective-permute-start(bf16[512,1024]{1,0:T(8,128)(2,1)} %units_out_send.1), channel_id=1, source_target_pairs={{0,1},{1,0},{2,3},{3,2},{4,5},{5,4},{6,7},{7,6},{8,9},{9,8},{10,11... | collective-permute-start | bytes 3145736 | tf_op jit(solution)/shard_map/ppermute | solution.py:389
  350.0 42.4 %collective-permute-start.39 = (bf16[512,1024]{1,0:T(8,128)(2,1)}, bf16[512,1024]{1,0:T(8,128)(2,1)S(1)}, u32[]{:S(2)}, u32[]{:S(2)}) collective-permute-start(bf16[512,1024]{1,0:T(8,128)(2,1)} %heads_back_send.1), channel_id=1, source_target_pairs={{0,1},{1,0},{2,3},{3,2},{4,5},{5,4},{6,7},{7,6},{8,9},{9,8},{10,11... | collective-permute-start | bytes 3145736 | tf_op jit(solution)/shard_map/ppermute | solution.py:389
  (66 other events, 1260.3 us)

commit v2 on v0

--- a/solution.py
+++ b/solution.py
@@ -1,6 +1,8 @@
 import jax
 import jax.numpy as jnp
 from jax import lax
+from jax.experimental import pallas as pl
+from jax.experimental.pallas import tpu as pltpu
 from jax.sharding import PartitionSpec as P
 
 HEAD_DIM = 64
@@ -142,7 +144,7 @@
     return (new_master, new_first, new_second)
 
 
-def on_device(
+def on_device_general(
     tokens,
     cotangent,
     group_ids,
@@ -332,9 +334,834 @@
     )
 
 
+LEN = 1024
+BLK = 256
+LANES = 128
+LOG2E = 1.4426950408889634
+NT = (((1,), (1,)), ((), ()))
+TN = (((0,), (0,)), ((), ()))
+VMEM_LIMIT = 60 << 20
+F32 = jnp.float32
+BF16 = jnp.bfloat16
+AXES = ("dp", "mp")
+ANY = pl.BlockSpec(memory_space=pl.ANY)
+
+
+def cost(flops, nbytes, trans=0):
+    return pl.CostEstimate(flops=int(flops), bytes_accessed=int(nbytes), transcendentals=int(trans))
+
+
+def shape(rows, cols, dtype=BF16):
+    return jax.ShapeDtypeStruct((rows, cols), dtype)
+
+
+def full(rows, cols):
+    return pl.BlockSpec((rows, cols), lambda i, ix: (0, 0))
+
+
+def call(body, name, grid, in_specs, out_specs, out_shape, scratch, est):
+    return pl.pallas_call(
+        body,
+        grid_spec=pltpu.PrefetchScalarGridSpec(
+            num_scalar_prefetch=1,
+            grid=(grid,),
+            in_specs=in_specs,
+            out_specs=out_specs,
+            scratch_shapes=scratch,
+        ),
+        out_shape=out_shape,
+        compiler_params=pltpu.CompilerParams(vmem_limit_bytes=VMEM_LIMIT),
+        cost_estimate=est,
+        name=name,
+    )
+
+
+def hop(value, half_bit, dp_bits):
+    ranks = lax.axis_size("mp") // 2
+    width = lax.axis_size("mp")
+    total = lax.axis_size("dp") * width
+    flip = dp_bits * width + half_bit * ranks
+    return lax.ppermute(value, AXES, [(i, i ^ flip) for i in range(total)])
+
+
+def core_swap(value):
+    total = lax.axis_size("dp") * lax.axis_size("mp")
+    return lax.ppermute(value, AXES, [(i, i ^ 1) for i in range(total)])
+
+
+def after(value, *others):
+    return lax.optimization_barrier((value, *others))[0]
+
+
+def inner_z():
+    z = lax.axis_index("dp") // 2
+    return jnp.logical_or(z == 1, z == 2)
+
+
+def z_hop(value, pairs):
+    width = lax.axis_size("mp")
+    perm = []
+    for source, target in pairs:
+        for rest in range(2 * width):
+            perm.append((source * 2 * width + rest, target * 2 * width + rest))
+    return lax.ppermute(value, AXES, perm)
+
+
+MIDDLE = ((1, 2), (2, 1))
+OUTWARD = ((1, 0), (2, 3))
+
+
+def gather_z(own, first):
+    begin = after(own, *first)
+    z1 = hop(begin, 0, 2)
+    m1 = z_hop(begin, MIDDLE)
+    m2 = z_hop(z1, MIDDLE)
+    f1 = z_hop(m1, OUTWARD)
+    f2 = z_hop(m2, OUTWARD)
+    inner = inner_z()
+    near = jnp.stack([own, z1])
+    far = jnp.stack([jnp.where(inner, m2, f1), jnp.where(inner, m1, f2)])
+    return near, far, (z1, m1, m2, f1, f2)
+
+
+def gather_xy(near, far, first_near, first_far):
+    near_b = after(near, *first_near)
+    far_b = after(far, *first_far)
+    x_near, y_near = hop(near_b, 1, 0), hop(near_b, 0, 1)
+    x_far, y_far = hop(far_b, 1, 0), hop(far_b, 0, 1)
+    d_near, d_far = hop(x_near, 0, 1), hop(y_far, 1, 0)
+    found = []
+    for c in (0, 1):
+        for array, half_bit, bit in ((near, 0, 0), (x_near, 1, 0), (y_near, 0, 1), (d_near, 1, 1)):
+            found.append((array, c, half_bit, 2 * c + bit))
+        for array, half_bit, bit in ((far, 0, 0), (x_far, 1, 0), (y_far, 0, 1), (d_far, 1, 1)):
+            found.append((array, c, half_bit, 4 + 2 * c + bit))
+    return found, (x_near, y_near, x_far, y_far, d_near, d_far)
+
+
+def swapped_blocks(found):
+    arrays, table = operands(found)
+    arrays = [core_swap(array) for array in arrays]
+    return [(arrays[e[0]], *e[1:]) for e in table]
+
+
+def operands(found):
+    arrays = []
+    table = []
+    for array, *entry in found:
+        for k, held in enumerate(arrays):
+            if held is array:
+                break
+        else:
+            k = len(arrays)
+            arrays.append(array)
+        table.append((k, *entry))
+    return arrays, table
+
+
+def copies_of(pairs, sems, start=0):
+    return [pltpu.make_async_copy(src, dst, sems.at[start + n]) for n, (src, dst) in enumerate(pairs)]
+
+
+def load_all(pairs, sems):
+    copies = copies_of(pairs, sems)
+    for copy in copies:
+        copy.start()
+    for copy in copies:
+        copy.wait()
+
+
+def at_rows(index, size):
+    return pl.ds(pl.multiple_of(index * size, size), size)
+
+
+def at_lanes(index, size):
+    return pl.ds(pl.multiple_of(index * size, LANES), size)
+
+
+def column_pairs(refs, table, w, ix, first, count, spread):
+    pairs = []
+    for k, slot, half_bit, dp_bits in table:
+        src = refs[k].at[slot, :, pl.ds(first, count)]
+        rows = at_rows(ix[0] ^ dp_bits, src.shape[0])
+        dst = w.at[half_bit, rows, :] if spread else w.at[rows, pl.ds(half_bit * count, count)]
+        pairs.append((src, dst))
+    return pairs
+
+
+def block_pairs(refs, table, w, ix, half_bit, slot_out):
+    return [
+        (refs[k].at[slot], w.at[slot_out, at_rows(ix[0] ^ dp_bits, refs[k].shape[1]), :])
+        for k, slot, a, dp_bits in table
+        if a == half_bit
+    ]
+
+
+def pick(low, value, which):
+    zero = jnp.zeros((), value.dtype)
+    return jnp.where(low, value, zero) if which == 0 else jnp.where(low, zero, value)
+
+
+def row_stats(values):
+    center = values - jnp.mean(values, axis=-1, keepdims=True)
+    scaler = lax.rsqrt(jnp.mean(center * center, axis=-1, keepdims=True) + NORM_EPS)
+    return center * scaler, scaler
+
+
+def token_weights(ids, table):
+    lanes = lax.broadcasted_iota(jnp.int32, (ids.shape[0], LANES), 1)
+    return jnp.sum(jnp.where(ids == lanes, table, 0.0), axis=-1, keepdims=True)
+
+
+def norm_rows(idx, tokens, vec, down):
+    model = tokens.shape[1]
+    blocks = LEN // BLK
+
+    def body(ix, tok, vec_ref, down_ref, normed_ref, latent_ref):
+        hat, _ = row_stats(tok[...].astype(F32))
+        normed = (hat * vec_ref[0:1, :] + vec_ref[1:2, :]).astype(BF16)
+        normed_ref[...] = normed
+        latent_ref[...] = lax.dot_general(normed, down_ref[...], NT, preferred_element_type=F32).astype(BF16)
+
+    row = lambda c: pl.BlockSpec((BLK, c), lambda i, ix: (i, 0))
+    return call(
+        body,
+        "norm_rows",
+        blocks,
+        [pl.BlockSpec((BLK, model), lambda i, ix: (ix[1] * blocks + i, 0)), full(8, model), full(LANES, model)],
+        [row(model), row(LANES)],
+        [shape(LEN, model), shape(LEN, LANES)],
+        [],
+        cost(2 * LEN * model * LANES, 4 * LEN * model),
+    )(idx, tokens, vec, down)
+
+
+def project_heads(idx, normed, latent, bias, up, found):
+    model = normed.shape[1]
+    arrays, table = operands(found)
+    cols = bias.shape[1]
+    part = cols // 3
+    n = len(arrays)
+
+    def body(ix, normed_ref, latent_ref, bias_ref, up_ref, *rest):
+        msgs = rest[:n]
+        q_ref, k_ref, v_ref, w, sems = rest[n:]
+
+        @pl.when(pl.program_id(0) == 0)
+        def _():
+            load_all(column_pairs(msgs, table, w, ix, 0, cols, True), sems)
+
+        for a in range(2):
+            r = jnp.dot(normed_ref[...], w[a], preferred_element_type=F32) + bias_ref[a : a + 1, :]
+            r = r + jnp.dot(latent_ref[...], up_ref[a], preferred_element_type=F32)
+            for out, s in ((q_ref, 0), (k_ref, 1), (v_ref, 2)):
+                out[:, a * part : (a + 1) * part] = r[:, s * part : (s + 1) * part].astype(BF16)
+
+    row = lambda c: pl.BlockSpec((BLK, c), lambda i, ix: (i, 0))
+    return call(
+        body,
+        "project_heads",
+        LEN // BLK,
+        [row(model), row(LANES), full(2, cols), pl.BlockSpec((2, LANES, cols), lambda i, ix: (0, 0, 0))] + [ANY] * n,
+        [row(2 * part)] * 3,
+        [shape(LEN, 2 * part)] * 3,
+        [pltpu.VMEM((2, model, cols), BF16), pltpu.SemaphoreType.DMA((len(table),))],
+        cost(4 * LEN * model * cols, 16 * LEN * model),
+    )(idx, normed, latent, bias, up, *arrays)
+
+
+def attend_fast(queries, key_rows, value_rows):
+    length, width = queries.shape
+    pairs = width // LANES
+
+    def body(q_ref, k_ref, v_ref, o_ref, lse_ref):
+        scale = HEAD_DIM**-0.5 * LOG2E
+        low = lax.broadcasted_iota(jnp.int32, (1, LANES), 1) < HEAD_DIM
+        k = k_ref[...]
+        v = v_ref[...]
+        value_of = [pick(low, v, h) for h in range(2)]
+        for i in range(length // BLK):
+            stop = (i + 1) * BLK
+            qb = q_ref[i * BLK : stop, :]
+            causal = (lax.broadcasted_iota(jnp.int32, (BLK, stop), 0) + i * BLK) >= lax.broadcasted_iota(
+                jnp.int32, (BLK, stop), 1
+            )
+            out = jnp.zeros((BLK, LANES), F32)
+            logs = []
+            for h in range(2):
+                s = lax.dot_general(pick(low, qb, h), k[:stop], NT, preferred_element_type=F32) * scale
+                s = jnp.where(causal, s, MASKED)
+                top = jnp.max(s, axis=-1, keepdims=True)
+                p = jnp.exp2(s - top)
+                total = jnp.sum(p, axis=-1, keepdims=True)
+                probs = (p * (1.0 / total)).astype(BF16)
+                out = out + jnp.dot(probs, value_of[h][:stop], preferred_element_type=F32)
+                logs.append(top + jnp.log2(total))
+            o_ref[i * BLK : stop, :] = out.astype(BF16)
+            both = jnp.where(
+                low, jnp.broadcast_to(logs[0], (BLK, LANES)), jnp.broadcast_to(logs[1], (BLK, LANES))
+            ).T
+            lse_ref[0, 0:1, i * BLK : stop] = both[0:1]
+            lse_ref[0, 1:2, i * BLK : stop] = both[HEAD_DIM : HEAD_DIM + 1]
+
+    spec = pl.BlockSpec((length, LANES), lambda i: (0, i))
+    return pl.pallas_call(
+        body,
+        grid=(pairs,),
+        out_shape=(shape(length, width), jax.ShapeDtypeStruct((pairs, 8, length), F32)),
+        in_specs=[spec] * 3,
+        out_specs=(spec, pl.BlockSpec((1, 8, length), lambda i: (i, 0, 0))),
+        compiler_params=pltpu.CompilerParams(vmem_limit_bytes=VMEM_LIMIT),
+        cost_estimate=cost(8 * length * length * width, 8 * length * width, 2 * pairs * length * length),
+        name="attend",
+    )(queries, key_rows, value_rows)
+
+
+def attention_out_send(idx, attended, found, first):
+    width = attended.shape[1]
+    arrays, table = operands(found)
+    n = len(arrays)
+    model = LANES * lax.axis_size("dp")
+    half_blocks = LEN // BLK // 2
+
+    def body(ix, att, *rest):
+        msgs = rest[:n]
+        out, w, sems = rest[n:]
+
+        @pl.when(pl.program_id(0) == 0)
+        def _():
+            load_all(column_pairs(msgs, table, w, ix, first, width // 2, False), sems)
+
+        out[...] = lax.dot_general(att[...], w[...], NT, preferred_element_type=F32).astype(BF16)
+
+    return call(
+        body,
+        "attention_out_send",
+        half_blocks,
+        [pl.BlockSpec((BLK, width), lambda i, ix: ((1 - ix[2]) * half_blocks + i, 0))] + [ANY] * n,
+        pl.BlockSpec((BLK, model), lambda i, ix: (i, 0)),
+        shape(LEN // 2, model),
+        [pltpu.VMEM((model, width), BF16), pltpu.SemaphoreType.DMA((len(table),))],
+        cost(LEN * width * model, 2 * LEN * model),
+    )(idx, attended, *arrays)
+
+
+def attention_out_own(idx, attended, received, tokens, vec, found, first):
+    width = attended.shape[1]
+    arrays, table = operands(found)
+    n = len(arrays)
+    model = tokens.shape[1]
+    half_blocks = LEN // BLK // 2
+
+    def body(ix, att, recv, tok, vec_ref, *rest):
+        msgs = rest[:n]
+        hidden_ref, normed_ref, w, sems = rest[n:]
+
+        @pl.when(pl.program_id(0) == 0)
+        def _():
+            load_all(column_pairs(msgs, table, w, ix, first, width // 2, False), sems)
+
+        term = lax.dot_general(att[...], w[...], NT, preferred_element_type=F32)
+        hidden = tok[...].astype(F32) + term + recv[...].astype(F32) + vec_ref[2:3, :]
+        hidden_ref[...] = hidden
+        hat, _ = row_stats(hidden)
+        normed_ref[...] = (hat * vec_ref[3:4, :] + vec_ref[4:5, :]).astype(BF16)
+
+    row = pl.BlockSpec((BLK, model), lambda i, ix: (i, 0))
+    return call(
+        body,
+        "attention_out_own",
+        half_blocks,
+        [
+            pl.BlockSpec((BLK, width), lambda i, ix: (ix[2] * half_blocks + i, 0)),
+            row,
+            pl.BlockSpec((BLK, model), lambda i, ix: ((2 * ix[1] + ix[2]) * half_blocks + i, 0)),
+            full(8, model),
+        ]
+        + [ANY] * n,
+        [row, row],
+        [shape(LEN // 2, model, F32), shape(LEN // 2, model)],
+        [pltpu.VMEM((model, width), BF16), pltpu.SemaphoreType.DMA((len(table),))],
+        cost(LEN * width * model, 5 * LEN * model),
+    )(idx, attended, received, tokens, vec, *arrays)
+
+
+def units_main(idx, half_bit, normed, cotangent, ids, weight_table, bias, vec, mine, other, carried, hidden):
+    rows, model = normed.shape
+    sources = [operands(f) for f in (mine, other)]
+    part = sources[0][0][0].shape[2] // 2
+    counts = [len(arrays) for arrays, _ in sources]
+    last = hidden is not None
+    parts = 4
+    piece = model // parts
+    chunk = 256
+    per = part // chunk
+    c0 = 0.7978845608028654
+    c1 = 0.044715
+
+    def body(ix, normed_ref, cot, ids_ref, table_ref, bias_ref, vec_ref, *rest):
+        carry = rest[: len(carried)]
+        rest = rest[len(carried) :]
+        hid_ref, rest = (rest[0], rest[1:]) if last else (None, rest)
+        msgs = (rest[: counts[0]], rest[counts[0] : sum(counts)])
+        rest = rest[sum(counts) :]
+        n_out = 2 + parts if last else 2
+        outs, (w, grad_ref, x_ref, g_ref, pre_ref, act_ref, sems, *held) = rest[:n_out], rest[n_out:]
+        groups = []
+        used = 0
+        for o in range(2):
+            pairs = block_pairs(msgs[o], sources[o][1], w, ix, half_bit, o)
+            groups.append(copies_of(pairs, sems, used))
+            used += len(pairs)
+        for group in groups:
+            for copy in group:
+                copy.start()
+        weight = token_weights(ids_ref[...], table_ref[...])
+        grad_ref[...] = (cot[...].astype(F32) * weight).astype(BF16)
+
+        def multiply(o, c, slot):
+            x_ref[slot] = jnp.dot(normed_ref[...], w[o, :, at_lanes(c, chunk)], preferred_element_type=F32)
+            g_ref[slot] = jnp.dot(grad_ref[...], w[o, :, at_lanes(c + per, chunk)], preferred_element_type=F32)
+
+        def bend(o, c, slot):
+            at = at_lanes(o * per + c, chunk)
+            x = x_ref[slot] + bias_ref[:, at]
+            sq = x * x
+            th = jnp.tanh(c0 * x * (1.0 + c1 * sq))
+            left = 0.5 * (1.0 + th)
+            slope = left + 0.5 * x * (1.0 - th * th) * (c0 + (3.0 * c0 * c1) * sq)
+            pre_ref[:, at] = (slope * g_ref[slot]).astype(BF16)
+            act_ref[:, at] = (x * left).astype(BF16)
+
+        for o in range(2):
+            for copy in groups[o]:
+                copy.wait()
+            if o == 0:
+                multiply(0, 0, 0)
+
+                def step(c, _):
+                    multiply(0, c, lax.rem(c, 2))
+                    bend(0, c - 1, lax.rem(c + 1, 2))
+                    return 0
+
+                lax.fori_loop(1, per, step, 0)
+            else:
+                multiply(1, 0, 0)
+                bend(0, per - 1, (per - 1) % 2)
+
+                def step(c, _):
+                    multiply(1, c, lax.rem(c, 2))
+                    bend(1, c - 1, lax.rem(c + 1, 2))
+                    return 0
+
+                lax.fori_loop(1, per, step, 0)
+                bend(1, per - 1, (per - 1) % 2)
+
+        def mid_of(n):
+            at = at_rows(n, chunk)
+            lanes = at_lanes(n, chunk)
+            mid = lax.dot_general(pre_ref[:, :part], w[0, at, :part], NT, preferred_element_type=F32)
+            mid = mid + lax.dot_general(pre_ref[:, part:], w[1, at, :part], NT, preferred_element_type=F32)
+            unit = lax.dot_general(act_ref[:, :part], w[0, at, part:], NT, preferred_element_type=F32)
+            unit = unit + lax.dot_general(act_ref[:, part:], w[1, at, part:], NT, preferred_element_type=F32)
+            if carry:
+                mid = mid + carry[0][:, lanes]
+                unit = unit + carry[1][:, lanes]
+            return mid, unit, lanes
+
+        if not last:
+
+            def finish(n, _):
+                mid, unit, lanes = mid_of(n)
+                outs[0][:, lanes] = mid
+                outs[1][:, lanes] = unit
+                return 0
+
+            lax.fori_loop(0, model // chunk, finish, 0)
+            return
+        out_low, = held
+
+        def finish(n, _):
+            mid, unit, lanes = mid_of(n)
+            outs[0][:, lanes] = mid * vec_ref[3:4, lanes]
+            out_low[:, lanes] = (unit + hid_ref[:, lanes]).astype(BF16)
+            return 0
+
+        lax.fori_loop(0, model // chunk, finish, 0)
+        for k in range(parts):
+            outs[2 + k][...] = out_low[:, at_lanes((2 * ix[1] + ix[2]) ^ k, piece)]
+        step_rows = 128
+
+        def end(r, _):
+            at = at_rows(r, step_rows)
+            hat, scaler = row_stats(hid_ref[at, :])
+            grad = cot[at, :].astype(F32) * token_weights(ids_ref[at, :], table_ref[...])
+            grad = grad + norm_back(hat, scaler, outs[0][at, :])
+            outs[0][at, :] = grad
+            outs[1][at, :] = grad.astype(BF16)
+            return 0
+
+        lax.fori_loop(0, rows // step_rows, end, 0)
+
+    def token_rows(i, ix):
+        return (2 * ix[1] + ix[2], 0)
+
+    block = full(rows, model)
+    specs = [
+        block,
+        pl.BlockSpec((rows, model), token_rows),
+        pl.BlockSpec((rows, 1), token_rows),
+        full(1, LANES),
+        pl.BlockSpec((1, 2 * part), lambda i, ix: (0, half_bit)),
+        full(8, model),
+    ]
+    specs += [block] * (len(carried) + (1 if last else 0))
+    if last:
+        out_specs = [block, block] + [full(rows, piece)] * parts
+        out_shape = [shape(rows, model, F32), shape(rows, model)] + [shape(rows, piece)] * parts
+    else:
+        out_specs = [block, block]
+        out_shape = [shape(rows, model, F32)] * 2
+    arrays = [array for found, _ in sources for array in found]
+    return call(
+        body,
+        "units_main_last" if last else "units_main_first",
+        1,
+        specs + [ANY] * len(arrays),
+        out_specs,
+        out_shape,
+        [
+            pltpu.VMEM((2, model, 2 * part), BF16),
+            pltpu.VMEM((rows, model), BF16),
+            pltpu.VMEM((2, rows, chunk), F32),
+            pltpu.VMEM((2, rows, chunk), F32),
+            pltpu.VMEM((rows, 2 * part), BF16),
+            pltpu.VMEM((rows, 2 * part), BF16),
+            pltpu.SemaphoreType.DMA((sum(len(table) for _, table in sources) // 2,)),
+        ]
+        + ([pltpu.VMEM((rows, model), BF16)] if last else []),
+        cost(16 * rows * part * model, 12 * part * model, 2 * rows * part),
+    )(idx, normed, cotangent, ids, weight_table, bias, vec, *carried, *((hidden,) if last else ()), *arrays)
+
+
+def attend_back_fast(idx, queries, key_rows, value_rows, mixed, grad_own, grad_other, logsum, found, first):
+    length, width = queries.shape
+    pairs = width // LANES
+    half, model = grad_own.shape
+    arrays, table = operands(found)
+    n = len(arrays)
+
+    def body(ix, q_ref, k_ref, v_ref, o_ref, own_ref, other_ref, lse_ref, *rest):
+        msgs = rest[:n]
+        dq_ref, dk_ref, dv_ref, dq_acc, g_ref, w, sems = rest[n:]
+        pair = pl.program_id(0)
+
+        @pl.when(pair == 0)
+        def _():
+            load_all(column_pairs(msgs, table, w, ix, first, width // 2, False), sems)
+
+        weight = w[:, at_lanes(pair, LANES)]
+        for ref, rank in ((own_ref, ix[2]), (other_ref, 1 - ix[2])):
+            g_ref[at_rows(rank, half), :] = jnp.dot(ref[...], weight, preferred_element_type=F32).astype(BF16)
+        scale = HEAD_DIM**-0.5 * LOG2E
+        low = lax.broadcasted_iota(jnp.int32, (1, LANES), 1) < HEAD_DIM
+        q = q_ref[...]
+        g = g_ref[...]
+        qm = [pick(low, q, h) for h in range(2)]
+        gm = [pick(low, g, h) for h in range(2)]
+        prod = (g.astype(F32) * o_ref[...].astype(F32)).T
+        delta = [
+            jnp.sum(prod[:HEAD_DIM], axis=0, keepdims=True),
+            jnp.sum(prod[HEAD_DIM:], axis=0, keepdims=True),
+        ]
+        dq_acc[...] = jnp.zeros_like(dq_acc)
+        for j in range(length // BLK):
+            start = j * BLK
+            stop = start + BLK
+            span = length - start
+            kb = k_ref[start:stop, :]
+            vb = v_ref[start:stop, :]
+            causal = lax.broadcasted_iota(jnp.int32, (BLK, span), 1) >= lax.broadcasted_iota(
+                jnp.int32, (BLK, span), 0
+            )
+            dk = jnp.zeros((BLK, LANES), F32)
+            dv = jnp.zeros((BLK, LANES), F32)
+            for h in range(2):
+                km = pick(low, kb, h)
+                s = lax.dot_general(km, q[start:], NT, preferred_element_type=F32) * scale
+                s = jnp.where(causal, s - lse_ref[0, h : h + 1, start:], MASKED)
+                p = jnp.exp2(s)
+                dp = lax.dot_general(pick(low, vb, h), g[start:], NT, preferred_element_type=F32)
+                ds = (p * (dp - delta[h][:, start:])).astype(BF16)
+                dk = dk + jnp.dot(ds, qm[h][start:], preferred_element_type=F32)
+                dv = dv + jnp.dot(p.astype(BF16), gm[h][start:], preferred_element_type=F32)
+                dq_acc[start:, :] += lax.dot_general(ds, km, TN, preferred_element_type=F32)
+            dk_ref[start:stop, :] = (dk * HEAD_DIM**-0.5).astype(BF16)
+            dv_ref[start:stop, :] = dv.astype(BF16)
+        dq_ref[...] = (dq_acc[...] * HEAD_DIM**-0.5).astype(BF16)
+
+    spec = pl.BlockSpec((length, LANES), lambda i, ix: (0, i))
+    return call(
+        body,
+        "attend_back",
+        pairs,
+        [spec] * 4 + [full(half, model)] * 2 + [pl.BlockSpec((1, 8, length), lambda i, ix: (i, 0, 0))] + [ANY] * n,
+        [spec] * 3,
+        [shape(length, width)] * 3,
+        [
+            pltpu.VMEM((length, LANES), F32),
+            pltpu.VMEM((length, LANES), BF16),
+            pltpu.VMEM((model, width), BF16),
+            pltpu.SemaphoreType.DMA((len(table),)),
+        ],
+        cost(20 * length * length * width, 16 * length * width, 2 * pairs * length * length),
+    )(idx, queries, key_rows, value_rows, mixed, grad_own, grad_other, logsum, *arrays)
+
+
+def heads_back(idx, dq, dk, dv, normed, latent, up, down, found):
+    width = dq.shape[1]
+    part = width // 2
+    model = down.shape[1]
+    arrays, table = operands(found)
+    cols = 3 * part
+    n = len(arrays)
+    half_blocks = LEN // BLK // 2
+
+    def body(ix, dq_ref, dk_ref, dv_ref, normed_ref, latent_ref, up_ref, down_ref, *rest):
+        msgs = rest[:n]
+        send_ref, own_ref, low_ref, raise_ref, w, sems = rest[n:]
+        step = pl.program_id(0)
+
+        @pl.when(step == 0)
+        def _():
+            copies = copies_of(column_pairs(msgs, table, w, ix, 0, cols, True), sems)
+            for copy in copies:
+                copy.start()
+            low_ref[...] = jnp.zeros_like(low_ref)
+            raise_ref[...] = jnp.zeros_like(raise_ref)
+            for copy in copies:
+                copy.wait()
+
+        latent = latent_ref[...]
+        low = jnp.zeros((BLK, LANES), F32)
+        total = jnp.zeros((BLK, model), F32)
+        for a in range(2):
+            cut = slice(a * part, (a + 1) * part)
+            piece = jnp.concatenate([dq_ref[:, cut], dk_ref[:, cut], dv_ref[:, cut]], axis=1)
+            total = total + lax.dot_general(piece, w[a], NT, preferred_element_type=F32)
+            low = low + lax.dot_general(piece, up_ref[a], NT, preferred_element_type=F32)
+            term = lax.dot_general(latent, piece, TN, preferred_element_type=F32)
+            raise_ref[:, a * cols : (a + 1) * cols] += term[:8]
+        low = low.astype(BF16)
+        total = total + jnp.dot(low, down_ref[...], preferred_element_type=F32)
+        low_ref[...] += lax.dot_general(low, normed_ref[...], TN, preferred_element_type=F32)[:8]
+
+        @pl.when(step < half_blocks)
+        def _():
+            send_ref[...] = total.astype(BF16)
+
+        @pl.when(step >= half_blocks)
+        def _():
+            own_ref[...] = total
+
+    def rows(i, ix):
+        rank = jnp.where(i < half_blocks, 1 - ix[2], ix[2])
+        return (rank * half_blocks + lax.rem(i, half_blocks), 0)
+
+    row = lambda c: pl.BlockSpec((BLK, c), rows)
+    return call(
+        body,
+        "heads_back",
+        2 * half_blocks,
+        [row(width)] * 3
+        + [row(model), row(LANES), pl.BlockSpec((2, LANES, cols), lambda i, ix: (0, 0, 0)), full(LANES, model)]
+        + [ANY] * n,
+        [
+            pl.BlockSpec((BLK, model), lambda i, ix: (jnp.minimum(i, half_blocks - 1), 0)),
+            pl.BlockSpec((BLK, model), lambda i, ix: (jnp.maximum(i - half_blocks, 0), 0)),
+            full(8, model),
+            full(8, 2 * cols),
+        ],
+        [shape(LEN // 2, model), shape(LEN // 2, model, F32), shape(8, model, F32), shape(8, 2 * cols, F32)],
+        [pltpu.VMEM((2, model, cols), BF16), pltpu.SemaphoreType.DMA((len(table),))],
+        cost(4 * LEN * model * cols, 8 * model * cols),
+    )(idx, dq, dk, dv, normed, latent, up, down, *arrays)
+
+
+def tokens_back(idx, in_own, in_recv, tokens, hidden_grad, vec):
+    model = tokens.shape[1]
+    half_blocks = LEN // BLK // 2
+    parts = 4
+    part = model // parts
+
+    def body(ix, own, recv, tok, hg, vec_ref, *rest):
+        outs, held = rest[:parts], rest[parts]
+        e = vec_ref[0:1, :] * (own[...] + recv[...].astype(F32))
+        hat, scaler = row_stats(tok[...].astype(F32))
+        held[...] = (hg[...] + norm_back(hat, scaler, e)).astype(BF16)
+        for k, out in enumerate(outs):
+            out[...] = held[:, at_lanes((2 * ix[1] + ix[2]) ^ k, part)]
+
+    row = pl.BlockSpec((BLK, model), lambda i, ix: (i, 0))
+    return call(
+        body,
+        "tokens_back",
+        half_blocks,
+        [row, row, pl.BlockSpec((BLK, model), lambda i, ix: ((2 * ix[1] + ix[2]) * half_blocks + i, 0)), row, full(8, model)],
+        [pl.BlockSpec((BLK, part), lambda i, ix: (i, 0))] * parts,
+        [shape(LEN // 2, part)] * parts,
+        [pltpu.VMEM((BLK, model), BF16)],
+        cost(20 * LEN * model, 8 * LEN * model),
+    )(idx, in_own, in_recv, tokens, hidden_grad, vec)
+
+
+def to_features(idx, pieces, bias):
+    pieces = [pieces[0], core_swap(pieces[1]), hop(pieces[2], 1, 0), both_swap(pieces[3])]
+    rows, part = pieces[0].shape
+    parts = len(pieces)
+
+    def body(ix, bias_ref, *rest):
+        outs = rest[parts]
+        for k in range(parts):
+            value = rest[k][...]
+            if bias is not None:
+                value = (value.astype(F32) + bias_ref[...]).astype(BF16)
+            outs[at_rows((2 * ix[1] + ix[2]) ^ k, rows), :] = value
+
+    extra = jnp.zeros((1, part), F32) if bias is None else bias
+    return call(
+        body,
+        "to_features",
+        1,
+        [full(1, part)] + [full(rows, part)] * parts,
+        full(parts * rows, part),
+        shape(parts * rows, part),
+        [],
+        cost(parts * rows * part, 4 * parts * rows * part),
+    )(idx, extra, *pieces)
+
+
+def both_swap(value):
+    total = lax.axis_size("dp") * lax.axis_size("mp")
+    return lax.ppermute(value, AXES, [(i, i ^ 3) for i in range(total)])
+
+
+def on_device_fast(
+    tokens,
+    cotangent,
+    group_ids,
+    pre_gain,
+    pre_shift,
+    frozen_triple_weight,
+    frozen_triple_bias,
+    out_weight,
+    out_bias,
+    mid_gain,
+    mid_shift,
+    fc_weight,
+    fc_bias,
+    proj_weight,
+    proj_bias,
+    down_master,
+    up_master,
+    down_first,
+    down_second,
+    up_first,
+    up_second,
+    learn_rate,
+):
+    tok_dev, model = tokens.shape
+    ranks = lax.axis_size("mp") // 2
+    place = lax.axis_index("mp")
+    idx = jnp.stack([lax.axis_index("dp"), place // ranks, place % ranks]).astype(jnp.int32)
+    r = ADAPTER_RANK
+    step_rows, _, head_part = frozen_triple_weight.shape
+    heads_cols = 3 * head_part
+    heads_own = jnp.concatenate([frozen_triple_weight.reshape(step_rows, heads_cols), out_weight.T], axis=1)
+    units_own = jnp.concatenate([fc_weight, proj_weight.T], axis=1)
+    down = jnp.zeros((LANES, model), BF16).at[: 2 * r].set(down_master.reshape(2 * r, model).astype(BF16))
+    zero_line = jnp.zeros_like(pre_gain)
+    vec = jnp.stack([pre_gain, pre_shift, out_bias, mid_gain, mid_shift, zero_line, zero_line, zero_line]).astype(F32)
+    h_near, h_far, h_z = gather_z(heads_own, ())
+    u_near, u_far, u_z = gather_z(units_own, (h_z[3],))
+    heads, h_xy = gather_xy(h_near, h_far, (), ())
+    units, u_xy = gather_xy(u_near, u_far, (h_xy[2], h_xy[3]), ())
+    units_other = swapped_blocks(units)
+    up_low = up_master.astype(BF16).reshape(2 * ADAPTER_RANK, head_part)
+    fc_rows = fc_bias.reshape(-1, head_part)
+    small = jnp.concatenate([frozen_triple_bias, fc_rows, up_low], axis=0)
+    small = jnp.stack([small, hop(after(small, h_z[0]), 1, 0)])
+    bias = small[:, :3].reshape(2, 3 * head_part).astype(F32)
+    fc_mine = small[:, 3 : 3 + fc_rows.shape[0]].reshape(2, 1, -1)
+    fc_line = jnp.concatenate([fc_mine, core_swap(fc_mine)], axis=1).reshape(1, -1).astype(F32)
+    up_both = small[:, 3 + fc_rows.shape[0] :] * jnp.bfloat16(ADAPTER_SCALE)
+    up = jnp.zeros((2, LANES, 3 * head_part), BF16)
+    up = up.at[:, :r, :head_part].set(up_both[:, :r]).at[:, r : 2 * r, 2 * head_part :].set(up_both[:, r:])
+    groups = jnp.arange(LANES, dtype=jnp.int32)[None, :]
+    ids = group_ids[:, None]
+    normed, latent = norm_rows(idx, tokens, vec, down)
+    queries, keys, values = project_heads(idx, normed, latent, bias, up, heads)
+    mixed, logsum = attend_fast(queries, keys, values)
+    counts = jnp.sum((ids == groups).astype(jnp.int32), axis=0, keepdims=True)
+    counts = after(counts, queries)
+    bits = 1
+    while bits < lax.axis_size("dp"):
+        counts = counts + hop(counts, 0, bits)
+        bits *= 2
+    weight_table = F32(tok_dev * lax.axis_size("dp")) / (GROUPS * counts.astype(F32))
+
+    sent = core_swap(attention_out_send(idx, mixed, heads, heads_cols))
+    hidden, normed_mid = attention_out_own(idx, mixed, sent, tokens, vec, heads, heads_cols)
+    rows = (normed_mid, cotangent, ids, weight_table, fc_line, vec)
+    carried = units_main(idx, 0, *rows, units, units_other, (), None)
+    hidden_grad, hidden_low, *out_pieces = units_main(idx, 1, *rows, units, units_other, carried, hidden)
+    hidden_other = core_swap(hidden_low)
+    dq, dk, dv = attend_back_fast(
+        idx, queries, keys, values, mixed, hidden_low, hidden_other, logsum, heads, heads_cols
+    )
+    in_send, in_own, down_term, up_term = heads_back(idx, dq, dk, dv, normed, latent, up, down, heads)
+    in_recv = core_swap(in_send)
+    output = to_features(idx, out_pieces, proj_bias.astype(F32).reshape(1, -1))
+    input_grad = to_features(idx, tokens_back(idx, in_own, in_recv, tokens, hidden_grad, vec), None)
+    up_term = up_term.reshape(2 * r, 2, 3, head_part)
+    mine = jnp.concatenate([up_term[:r, 0, 0], up_term[r:, 0, 2]], axis=0)
+    theirs = jnp.concatenate([up_term[:r, 1, 0], up_term[r:, 1, 2]], axis=0)
+    down_sum = down_term + core_swap(down_term)
+    got = hop(jnp.concatenate([down_sum, theirs], axis=1), 1, 0)
+    both = jnp.concatenate([down_sum, mine], axis=1) + got
+    bits = 1
+    while bits < lax.axis_size("dp"):
+        both = both + hop(both, 0, bits)
+        bits *= 2
+    down_grad = both[:, :model].reshape(down_master.shape)
+    up_grad = ADAPTER_SCALE * both[:, model:].reshape(up_master.shape)
+    step_value = jnp.float32(STEP)
+    down_new, down_moment, down_square = adam_update(
+        down_master, down_first, down_second, down_grad, step_value, learn_rate
+    )
+    up_new, up_moment, up_square = adam_update(up_master, up_first, up_second, up_grad, step_value, learn_rate)
+    return (
+        output,
+        input_grad,
+        down_new,
+        down_moment,
+        down_square,
+        down_new.astype(BF16),
+        up_new,
+        up_moment,
+        up_square,
+        up_new.astype(BF16),
+    )
+
+
+def pick_body(mesh):
+    return on_device_fast if mesh.shape["dp"] == 8 and mesh.shape["mp"] == 4 else on_device_general
+
+
 def solution(mesh):
+    body = pick_body(mesh)
     return jax.shard_map(
-        on_device,
+        body,
         mesh=mesh,
         in_specs=(
             P("dp", None),

time: 571 us -> 322 us (0.56)
  waiting for transfers between devices: 249 us -> 112 us
  Pallas kernels: 0 us -> 134 us
  matrix products: 113 us -> 0 us
  blocking collectives: 99.7 us -> 0 us
  other arithmetic: 67.9 us -> 11.7 us
  starting transfers between devices: 0.5 us -> 44.2 us
  between operations: 16.5 us -> 2.13 us
    psum x3 -> x0, waiting for transfers between devices: 158 us -> none  [the longest x1 73.4 us: on_device(): attn_sum = lax.psum(head_term, 'mp').astype(jnp.float32)]
    pallas_call x0 -> x12, Pallas kernels: none -> 134 us  [the longest x2 44.3 us: units_main(): call(body, 'units_main_last' if last else 'units_main_first', 1, specs +...]
    dot_general x56 -> x0, matrix products: 113 us -> none  [the longest x2 20.4 us: on_device(): jnp.einsum('tf,df->td', pre_grad, fc_full, preferred_element_type=jnp.flo...]
    ppermute x0 -> x49, waiting for transfers between devices: none -> 112 us  [the longest x24 96 us: hop(): return lax.ppermute(value, AXES, [(i, i ^ flip) for i in range(total)])]
    all_gather x3 -> x0, waiting for transfers between devices: 89.6 us -> none  [the longest x1 44.4 us: fetch_frozen(): lax.all_gather(fc_weight, 'dp', axis=0, tiled=True)]
    psum x3 -> x0, blocking collectives: 69.1 us -> none  [the longest x1 38 us: on_device(): down_grad = lax.psum(grad_down, ('dp', 'mp')).reshape(down_master.shape)]
    ppermute x0 -> x49, starting transfers between devices: none -> 44.2 us  [the longest x24 30.1 us: hop(): return lax.ppermute(value, AXES, [(i, i ^ flip) for i in range(total)])]
    all_gather x1 -> x0, blocking collectives: 30.6 us -> none  [fetch_frozen(): lax.all_gather(out_weight, 'dp', axis=1, tiled=True)]
  transfers between devices with their start and end apart: 8 -> 49, of which waited for: 6 -> 17; matrix products, arithmetic and copies ran while one was open for 22% -> 6% of each run, Pallas kernels for 0% -> 14%
where the time goes in v2:
time: 322 us; the launch traced here: 320 us
  Pallas kernels  134 us (42%)
  waiting for transfers between devices  112 us (35%)
  starting transfers between devices  44.2 us (14%)
  local copies, waits for them, and re-layouts  15.8 us (5%)
  other arithmetic  11.7 us (4%)
    ppermute x24, waiting for transfers between devices, hop(): return lax.ppermute(value, AXES, [(i, i ^ flip) for i in range(total)])  96 us
    pallas_call x2, Pallas kernels, units_main(): call(body, 'units_main_last' if last else 'units_main_first', 1, specs +...  44.3 us
    ppermute x24, starting transfers between devices, hop(): return lax.ppermute(value, AXES, [(i, i ^ flip) for i in range(total)])  30.1 us
    pallas_call x1, Pallas kernels, attend_back_fast(): call(body, 'attend_back', pairs, [spec] * 4 + [full(half, model)] * 2 + [...  24.6 us
    pallas_call x1, Pallas kernels, attend_fast(): pl.pallas_call(body, grid=(pairs,), out_shape=(shape(length, width), jax....  14.5 us
    pallas_call x1, Pallas kernels, heads_back(): call(body, 'heads_back', 2 * half_blocks, [row(width)] * 3 + [row(model),...  13.6 us
    pallas_call x1, Pallas kernels, project_heads(): call(body, 'project_heads', LEN // BLK, [row(model), row(LANES), full(2,...  9.71 us
    ppermute x8, starting transfers between devices, z_hop(): return lax.ppermute(value, AXES, perm)  9.68 us
  transfers between devices with their start and end apart: 49, of which 17 were waited for; matrix products, arithmetic and copies ran while one was open for 6% of the time, Pallas kernels for 14%

profile of v2, /device:TPU:0, one launch (start us, length us, event | category | flops | bytes accessed | tf_op | source)
XLA Modules:
  0.0 320.1 jit_solution(16490076795111445597)
XLA Ops:
  15.2 5.5 %norm_rows.1 = (bf16[1024,1024]{1,0:T(8,128)(2,1)}, bf16[1024,128]{1,0:T(8,128)(2,1)}) custom-call(s32[3]{0:T(128)} %pad_add_fusion.ix, bf16[2048,1024]{1,0:T(8,128)(2,1)} %tok.5, f32[8,1024]{1,0:T(8,128)} %convert_element_type.35.vec_ref, bf16[128,1024]{1,0:T(8,128)(2,1)} %scatter.10.down_ref), custom_call_target="tpu_custom_call" | custom-call | flops 268435456 | bytes 4194304 | tf_op jit(solution)/shard_map/norm_rows/pallas_call | solution.py:527
  25.0 4.6 %collective-permute-start.17 = (bf16[128,2048]{1,0:T(8,128)(2,1)}, bf16[128,2048]{1,0:T(8,128)(2,1)}, u32[]{:S(2)}, u32[]{:S(2)}) collective-permute-start(bf16[128,2048]{1,0:T(8,128)(2,1)} %get-tuple-element.87), channel_id=1, source_target_pairs={{0,8},{1,9},{2,10},{3,11},{4,12},{5,13},{6,14},{7,15},{8,0},{9,1},... | collective-permute-start | bytes 1572872 | tf_op jit(solution)/shard_map/ppermute | solution.py:384
  31.1 5.0 %collective-permute-done.8 = bf16[128,1024]{1,0:T(8,128)(2,1)S(1)} collective-permute-done((bf16[128,1024]{1,0:T(8,128)(2,1)S(1)}, bf16[128,1024]{1,0:T(8,128)(2,1)S(1)}, u32[]{:S(2)}, u32[]{:S(2)}) %collective-permute-start.8) | collective-permute-done | bytes 262176 | tf_op jit(solution)/shard_map/ppermute | solution.py:407
  38.9 6.1 %collective-permute-done.17 = bf16[128,2048]{1,0:T(8,128)(2,1)} collective-permute-done((bf16[128,2048]{1,0:T(8,128)(2,1)}, bf16[128,2048]{1,0:T(8,128)(2,1)}, u32[]{:S(2)}, u32[]{:S(2)}) %collective-permute-start.17) | collective-permute-done | bytes 524320 | tf_op jit(solution)/shard_map/ppermute | solution.py:384
  56.6 3.7 %collective-permute-done.23 = bf16[128,2048]{1,0:T(8,128)(2,1)} collective-permute-done((bf16[128,2048]{1,0:T(8,128)(2,1)}, bf16[128,2048]{1,0:T(8,128)(2,1)}, u32[]{:S(2)}, u32[]{:S(2)}) %collective-permute-start.23) | collective-permute-done | bytes 524320 | tf_op jit(solution)/shard_map/ppermute | solution.py:407
  61.4 5.3 %collective-permute-done.3.rest_2_ = bf16[2,128,1024]{2,1,0:T(8,128)(2,1)S(1)} collective-permute-done((bf16[2,128,1024]{2,1,0:T(8,128)(2,1)S(1)}, bf16[2,128,1024]{2,1,0:T(8,128)(2,1)S(1)}, u32[]{:S(2)}, u32[]{:S(2)}) %collective-permute-start.3) | collective-permute-done | bytes 524320 | tf_op jit(solution)/shard_map/ppermute | solution.py:384
  67.2 7.4 %collective-permute-done.4.rest_3_ = bf16[2,128,1024]{2,1,0:T(8,128)(2,1)S(1)} collective-permute-done((bf16[2,128,1024]{2,1,0:T(8,128)(2,1)S(1)}, bf16[2,128,1024]{2,1,0:T(8,128)(2,1)S(1)}, u32[]{:S(2)}, u32[]{:S(2)}) %collective-permute-start.4) | collective-permute-done | bytes 524320 | tf_op jit(solution)/shard_map/ppermute | solution.py:384
  77.0 9.7 %project_heads.1 = (bf16[1024,512]{1,0:T(8,128)(2,1)}, bf16[1024,512]{1,0:T(8,128)(2,1)}, bf16[1024,512]{1,0:T(8,128)(2,1)}) custom-call(s32[3]{0:T(128)} %pad_add_fusion.ix, bf16[1024,1024]{1,0:T(8,128)(2,1)} %get-tuple-element.78.normed_ref, bf16[1024,128]{1,0:T(8,128)(2,1)} %get-tuple-element.79.latent_ref, f32[2,768]{1,0:T(2,128)} %bitcast.46, ...), custom_call_target="tpu_custom_call" | custom-call | flops 3221225472 | bytes 16777216 | tf_op jit(solution)/shard_map/project_heads/pallas_call | solution.py:561
  88.3 14.5 %attend.1 = (bf16[1024,512]{1,0:T(8,128)(2,1)}, f32[4,8,1024]{2,1,0:T(8,128)}) custom-call(bf16[1024,512]{1,0:T(8,128)(2,1)} %get-tuple-element.81.q_ref, bf16[1024,512]{1,0:T(8,128)(2,1)} %get-tuple-element.82.k_ref, bf16[1024,512]{1,0:T(8,128)(2,1)} %get-tuple-element.83.v_ref), custom_call_target="tpu_custom_call" | custom-call | flops 4294967296 | bytes 4194304 | tf_op jit(solution)/shard_map/attend/pallas_call | solution.py:608
  102.8 3.3 %collective-permute-start.14 = (s32[1,128]{1,0:T(1,128)S(1)}, s32[1,128]{1,0:T(1,128)S(1)}, u32[]{:S(2)}, u32[]{:S(2)}) collective-permute-start(s32[1,128]{1,0:T(1,128)S(1)} %add.71), channel_id=1, source_target_pairs={{0,8},{1,9},{2,10},{3,11},{4,12},{5,13},{6,14},{7,15},{8,0},{9,1},... | collective-permute-start | bytes 1544 | tf_op jit(solution)/shard_map/ppermute | solution.py:384
  106.1 4.8 %attention_out_send.1 = bf16[512,1024]{1,0:T(8,128)(2,1)} custom-call(s32[3]{0:T(128)} %pad_add_fusion.ix, bf16[1024,512]{1,0:T(8,128)(2,1)} %get-tuple-element.84.att.o_ref, bf16[2,128,1024]{2,1,0:T(8,128)(2,1)} %copy-done, bf16[2,128,1024]{2,1,0:T(8,128)(2,1)} %copy-done.2, bf16[2,128,1024]{2,1,0:T(8,128)(2,1)} %copy-done.5, ...), custom_call_target="tpu_custom_call" | custom-call | flops 536870912 | bytes 2097152 | tf_op jit(solution)/shard_map/attention_out_send/pallas_call | solution.py:637
  118.1 19.2 %collective-permute-done.19.rest_2_.rest_5_ = bf16[2,128,2048]{2,1,0:T(8,128)(2,1)S(1)} collective-permute-done((bf16[2,128,2048]{2,1,0:T(8,128)(2,1)}, bf16[2,128,2048]{2,1,0:T(8,128)(2,1)S(1)}, u32[]{:S(2)}, u32[]{:S(2)}) %collective-permute-start.19) | collective-permute-done | bytes 1048608 | tf_op jit(solution)/shard_map/ppermute | solution.py:384
  137.8 22.1 %collective-permute-done.26.rest_6_.rest_9_ = bf16[2,128,2048]{2,1,0:T(8,128)(2,1)} collective-permute-done((bf16[2,128,2048]{2,1,0:T(8,128)(2,1)S(1)}, bf16[2,128,2048]{2,1,0:T(8,128)(2,1)}, u32[]{:S(2)}, u32[]{:S(2)}) %collective-permute-start.26) | collective-permute-done | bytes 1048608 | tf_op jit(solution)/shard_map/ppermute | solution.py:384
  161.9 15.5 %collective-permute-done.20.rest_3_.rest_6_ = bf16[2,128,2048]{2,1,0:T(8,128)(2,1)} collective-permute-done((bf16[2,128,2048]{2,1,0:T(8,128)(2,1)}, bf16[2,128,2048]{2,1,0:T(8,128)(2,1)}, u32[]{:S(2)}, u32[]{:S(2)}) %collective-permute-start.20) | collective-permute-done | bytes 1048608 | tf_op jit(solution)/shard_map/ppermute | solution.py:384
  181.2 6.0 %attention_out_own.1 = (f32[512,1024]{1,0:T(8,128)}, bf16[512,1024]{1,0:T(8,128)(2,1)}) custom-call(s32[3]{0:T(128)} %pad_add_fusion.ix, bf16[1024,512]{1,0:T(8,128)(2,1)} %get-tuple-element.84.att.o_ref, bf16[512,1024]{1,0:T(8,128)(2,1)} %copy-done.11, bf16[2048,1024]{1,0:T(8,128)(2,1)} %tok.5, f32[8,1024]{1,0:T(8,128)} %convert_element_type.35.vec_ref, ...), custom_call_target="tpu_custom_call" | custom-call | flops 536870912 | bytes 5242880 | tf_op jit(solution)/shard_map/attention_out_own/pallas_call | solution.py:671
  187.3 20.4 %units_main_first.1 = (f32[512,1024]{1,0:T(8,128)}, f32[512,1024]{1,0:T(8,128)}) custom-call(s32[3]{0:T(128)} %pad_add_fusion.ix, bf16[512,1024]{1,0:T(8,128)(2,1)} %get-tuple-element.85.normed_ref, bf16[2048,1024]{1,0:T(8,128)(2,1)} %cot.3, s32[2048,1]{1,0:T(8,128)} %copy.49.ids_ref, f32[1,128]{1,0:T(1,128)} %multiply_divide_fusion.table_ref, ...), custom_call_target="tpu_custom_call" | custom-call | flops 8589934592 | bytes 12582912 | tf_op jit(solution)/shard_map/units_main_first/pallas_call | solution.py:826
  207.7 23.9 %units_main_last.1 = (f32[512,1024]{1,0:T(8,128)}, bf16[512,1024]{1,0:T(8,128)(2,1)}, bf16[512,256]{1,0:T(8,128)(2,1)}, bf16[512,256]{1,0:T(8,128)(2,1)}, bf16[5...) custom-call(s32[3]{0:T(128)} %pad_add_fusion.ix, bf16[512,1024]{1,0:T(8,128)(2,1)} %get-tuple-element.85.normed_ref, ...), custom_call_target="tpu_custom_call" | custom-call | flops 8589934592 | bytes 12582912 | tf_op jit(solution)/shard_map/units_main_last/pallas_call | solution.py:826
  235.6 24.6 %attend_back.1 = (bf16[1024,512]{1,0:T(8,128)(2,1)}, bf16[1024,512]{1,0:T(8,128)(2,1)}, bf16[1024,512]{1,0:T(8,128)(2,1)}) custom-call(s32[3]{0:T(128)} %pad_add_fusion.ix, bf16[1024,512]{1,0:T(8,128)(2,1)} %get-tuple-element.81.q_ref, bf16[1024,512]{1,0:T(8,128)(2,1)} %get-tuple-element.82.k_ref, bf16[1024,512]{1,0:T(8,128)(2,1)} %get-tuple-element.83.v_ref, ...), custom_call_target="tpu_custom_call" | custom-call | flops 10737418240 | bytes 8388608 | tf_op jit(solution)/shard_map/attend_back/pallas_call | solution.py:904
  260.3 13.6 %heads_back.1 = (bf16[512,1024]{1,0:T(8,128)(2,1)}, f32[512,1024]{1,0:T(8,128)}, f32[8,1024]{1,0:T(8,128)}, f32[8,1536]{1,0:T(8,128)}) custom-call(s32[3]{0:T(128)} %pad_add_fusion.ix, bf16[1024,512]{1,0:T(8,128)(2,1)} %get-tuple-element.98.dq_ref, bf16[1024,512]{1,0:T(8,128)(2,1)} %get-tuple-element.99.dk_ref, bf16[1024,512]{1,0:T(8,128)(2,1)} %get-tuple-element.100.dv_ref, ...), custom_call_target="tpu_custom_call" | custom-call | flops 3221225472 | bytes 6291456 | tf_op jit(solution)/shard_map/heads_back/pallas_call | solution.py:972
  281.2 3.6 %collective-permute-done.46 = f32[8,1280]{1,0:T(8,128)S(1)} collective-permute-done((f32[8,1280]{1,0:T(8,128)S(1)}, f32[8,1280]{1,0:T(8,128)S(1)}, u32[]{:S(2)}, u32[]{:S(2)}) %collective-permute-start.46) | collective-permute-done | bytes 40992 | tf_op jit(solution)/shard_map/ppermute | solution.py:384
  285.1 3.7 %collective-permute-done.47 = f32[8,1280]{1,0:T(8,128)S(1)} collective-permute-done((f32[8,1280]{1,0:T(8,128)S(1)}, f32[8,1280]{1,0:T(8,128)S(1)}, u32[]{:S(2)}, u32[]{:S(2)}) %collective-permute-start.47) | collective-permute-done | bytes 40992 | tf_op jit(solution)/shard_map/ppermute | solution.py:384
  297.1 5.2 %tokens_back.1 = (bf16[512,256]{1,0:T(8,128)(2,1)}, bf16[512,256]{1,0:T(8,128)(2,1)}, bf16[512,256]{1,0:T(8,128)(2,1)}, bf16[512,256]{1,0:T(8,128)(2,1)}) custom-call(s32[3]{0:T(128)} %pad_add_fusion.ix, f32[512,1024]{1,0:T(8,128)} %get-tuple-element.101.own, bf16[512,1024]{1,0:T(8,128)(2,1)} %copy-done.8, bf16[2048,1024]{1,0:T(8,128)(2,1)} %tok.5, ...), custom_call_target="tpu_custom_call" | custom-call | flops 20971520 | bytes 8388608 | tf_op jit(solution)/shard_map/tokens_back/pallas_call | solution.py:1006
  305.6 6.1 %collective-permute-done.42.rest_2_ = bf16[512,256]{1,0:T(8,128)(2,1)S(1)} collective-permute-done((bf16[512,256]{1,0:T(8,128)(2,1)}, bf16[512,256]{1,0:T(8,128)(2,1)S(1)}, u32[]{:S(2)}, u32[]{:S(2)}) %collective-permute-start.42) | collective-permute-done | bytes 262176 | tf_op jit(solution)/shard_map/ppermute | solution.py:384
  311.8 4.7 %collective-permute-done.43.rest_3_ = bf16[512,256]{1,0:T(8,128)(2,1)S(1)} collective-permute-done((bf16[512,256]{1,0:T(8,128)(2,1)}, bf16[512,256]{1,0:T(8,128)(2,1)S(1)}, u32[]{:S(2)}, u32[]{:S(2)}) %collective-permute-start.43) | collective-permute-done | bytes 262176 | tf_op jit(solution)/shard_map/ppermute | solution.py:1046
  (239 shorter events, 79.5 us)
Async XLA Ops:
  21.5 16.3 %collective-permute-start.1 = (bf16[15,256]{1,0:T(8,128)(2,1)S(1)}, bf16[15,256]{1,0:T(8,128)(2,1)S(1)}, u32[]{:S(2)}, u32[]{:S(2)}) collective-permute-start(bf16[15,256]{1,0:T(8,128)(2,1)S(1)} %get-tuple-element.80), channel_id=1, source_target_pairs={{0,2},{1,3},{2,0},{3,1},{4,6},{5,7},{6,4},{7,5},{8,10},{9,11},{10,... | collective-permute-start | bytes 23048 | tf_op jit(solution)/shard_map/ppermute | solution.py:384
  24.5 27.2 %collective-permute-start.2 = (bf16[2,128,1024]{2,1,0:T(8,128)(2,1)S(1)}, bf16[2,128,1024]{2,1,0:T(8,128)(2,1)S(1)}, u32[]{:S(2)}, u32[]{:S(2)}) collective-permute-start(bf16[2,128,1024]{2,1,0:T(8,128)(2,1)S(1)} %pad_maximum_fusion.2.rest_0_), channel_id=1, source_target_pairs={{0,2},{1,3},{2,0},{3,1},{4,6},{5,7},{6,4},{7,5},{8,10},{9,11},{10,... | collective-permute-start | bytes 1572872 | tf_op jit(solution)/shard_map/ppermute | solution.py:384
  25.0 20.1 %collective-permute-start.17 = (bf16[128,2048]{1,0:T(8,128)(2,1)}, bf16[128,2048]{1,0:T(8,128)(2,1)}, u32[]{:S(2)}, u32[]{:S(2)}) collective-permute-start(bf16[128,2048]{1,0:T(8,128)(2,1)} %get-tuple-element.87), channel_id=1, source_target_pairs={{0,8},{1,9},{2,10},{3,11},{4,12},{5,13},{6,14},{7,15},{8,0},{9,1},... | collective-permute-start | bytes 1572872 | tf_op jit(solution)/shard_map/ppermute | solution.py:384
  29.6 17.0 %collective-permute-start.22 = (bf16[128,2048]{1,0:T(8,128)(2,1)}, bf16[128,2048]{1,0:T(8,128)(2,1)}, u32[]{:S(2)}, u32[]{:S(2)}) collective-permute-start(bf16[128,2048]{1,0:T(8,128)(2,1)} %get-tuple-element.87), channel_id=1, source_target_pairs={{8,16},{9,17},{10,18},{11,19},{12,20},{13,21},{14,22},{15,23},{16,... | collective-permute-start | bytes 1572872 | tf_op jit(solution)/shard_map/ppermute | solution.py:407
  36.2 17.2 %collective-permute-start.10 = (bf16[2,128,1024]{2,1,0:T(8,128)(2,1)S(1)}, bf16[2,128,1024]{2,1,0:T(8,128)(2,1)S(1)}, u32[]{:S(2)}, u32[]{:S(2)}) collective-permute-start(bf16[2,128,1024]{2,1,0:T(8,128)(2,1)S(1)} %pad_maximum_fusion.3.rest_4_), channel_id=1, source_target_pairs={{0,4},{1,5},{2,6},{3,7},{4,0},{5,1},{6,2},{7,3},{8,12},{9,13},{10,... | collective-permute-start | bytes 1572872 | tf_op jit(solution)/shard_map/ppermute | solution.py:384
  37.8 16.1 %collective-permute-start.9 = (bf16[2,128,1024]{2,1,0:T(8,128)(2,1)S(1)}, bf16[2,128,1024]{2,1,0:T(8,128)(2,1)S(1)}, u32[]{:S(2)}, u32[]{:S(2)}) collective-permute-start(bf16[2,128,1024]{2,1,0:T(8,128)(2,1)S(1)} %pad_maximum_fusion.3.rest_4_), channel_id=1, source_target_pairs={{0,2},{1,3},{2,0},{3,1},{4,6},{5,7},{6,4},{7,5},{8,10},{9,11},{10,... | collective-permute-start | bytes 1572872 | tf_op jit(solution)/shard_map/ppermute | solution.py:384
  53.4 21.3 %collective-permute-start.4 = (bf16[2,128,1024]{2,1,0:T(8,128)(2,1)S(1)}, bf16[2,128,1024]{2,1,0:T(8,128)(2,1)S(1)}, u32[]{:S(2)}, u32[]{:S(2)}) collective-permute-start(bf16[2,128,1024]{2,1,0:T(8,128)(2,1)S(1)} %collective-permute-done.2.rest_1_), channel_id=1, source_target_pairs={{0,4},{1,5},{2,6},{3,7},{4,0},{5,1},{6,2},{7,3},{8,12},{9,13},{10,... | collective-permute-start | bytes 1572872 | tf_op jit(solution)/shard_map/ppermute | solution.py:384
  53.9 22.2 %collective-permute-start.11 = (bf16[2,128,1024]{2,1,0:T(8,128)(2,1)S(1)}, bf16[2,128,1024]{2,1,0:T(8,128)(2,1)S(1)}, u32[]{:S(2)}, u32[]{:S(2)}) collective-permute-start(bf16[2,128,1024]{2,1,0:T(8,128)(2,1)S(1)} %collective-permute-done.10.rest_6_), channel_id=1, source_target_pairs={{0,2},{1,3},{2,0},{3,1},{4,6},{5,7},{6,4},{7,5},{8,10},{9,11},{10,... | collective-permute-start | bytes 1572872 | tf_op jit(solution)/shard_map/ppermute | solution.py:384
  56.5 56.5 %collective-permute-start.16 = (bf16[2,1,1024]{2,0,1:T(2,128)(2,1)S(1)}, bf16[2,1,1024]{2,0,1:T(2,128)(2,1)}, u32[]{:S(2)}, u32[]{:S(2)}) collective-permute-start(bf16[2,1,1024]{2,0,1:T(2,128)(2,1)S(1)} %copy-done.26), channel_id=1, source_target_pairs={{0,1},{1,0},{2,3},{3,2},{4,5},{5,4},{6,7},{7,6},{8,9},{9,8},{10,11... | collective-permute-start | bytes 12296 | tf_op jit(solution)/shard_map/ppermute | solution.py:389
  60.3 57.2 %collective-permute-start.28 = (bf16[2,128,2048]{2,1,0:T(8,128)(2,1)}, bf16[2,128,2048]{2,1,0:T(8,128)(2,1)}, u32[]{:S(2)}, u32[]{:S(2)}) collective-permute-start(bf16[2,128,2048]{2,1,0:T(8,128)(2,1)} %pad_maximum_fusion.rest_0_.rest_3_), channel_id=1, source_target_pairs={{0,1},{1,0},{2,3},{3,2},{4,5},{5,4},{6,7},{7,6},{8,9},{9,8},{10,11... | collective-permute-start | bytes 3145736 | tf_op jit(solution)/shard_map/ppermute | solution.py:389
  66.7 51.4 %collective-permute-start.18 = (bf16[2,128,2048]{2,1,0:T(8,128)(2,1)}, bf16[2,128,2048]{2,1,0:T(8,128)(2,1)}, u32[]{:S(2)}, u32[]{:S(2)}) collective-permute-start(bf16[2,128,2048]{2,1,0:T(8,128)(2,1)} %pad_maximum_fusion.rest_0_.rest_3_), channel_id=1, source_target_pairs={{0,2},{1,3},{2,0},{3,1},{4,6},{5,7},{6,4},{7,5},{8,10},{9,11},{10,... | collective-permute-start | bytes 3145736 | tf_op jit(solution)/shard_map/ppermute | solution.py:384
  74.6 36.8 %collective-permute-start.24 = (bf16[128,2048]{1,0:T(8,128)(2,1)}, bf16[128,2048]{1,0:T(8,128)(2,1)S(1)}, u32[]{:S(2)}, u32[]{:S(2)}) collective-permute-start(bf16[128,2048]{1,0:T(8,128)(2,1)} %collective-permute-done.21), channel_id=1, source_target_pairs={{8,0},{9,1},{10,2},{11,3},{12,4},{13,5},{14,6},{15,7},{16,24},{17,... | collective-permute-start | bytes 1572872 | tf_op jit(solution)/shard_map/ppermute | solution.py:407
  86.7 16.1 %collective-permute-start.13 = (s32[1,128]{1,0:T(1,128)S(1)}, s32[1,128]{1,0:T(1,128)S(1)}, u32[]{:S(2)}, u32[]{:S(2)}) collective-permute-start(s32[1,128]{1,0:T(1,128)S(1)} %bitcast.49), channel_id=1, source_target_pairs={{0,4},{1,5},{2,6},{3,7},{4,0},{5,1},{6,2},{7,3},{8,12},{9,13},{10,... | collective-permute-start | bytes 1544 | tf_op jit(solution)/shard_map/ppermute | solution.py:384
  110.9 26.4 %collective-permute-start.19 = (bf16[2,128,2048]{2,1,0:T(8,128)(2,1)}, bf16[2,128,2048]{2,1,0:T(8,128)(2,1)S(1)}, u32[]{:S(2)}, u32[]{:S(2)}) collective-permute-start(bf16[2,128,2048]{2,1,0:T(8,128)(2,1)} %pad_maximum_fusion.rest_0_.rest_3_), channel_id=1, source_target_pairs={{0,4},{1,5},{2,6},{3,7},{4,0},{5,1},{6,2},{7,3},{8,12},{9,13},{10,... | collective-permute-start | bytes 3145736 | tf_op jit(solution)/shard_map/ppermute | solution.py:384
  113.0 24.8 %collective-permute-start.12 = (bf16[512,1024]{1,0:T(8,128)(2,1)S(1)}, bf16[512,1024]{1,0:T(8,128)(2,1)S(1)}, u32[]{:S(2)}, u32[]{:S(2)}) collective-permute-start(bf16[512,1024]{1,0:T(8,128)(2,1)S(1)} %copy-done.9), channel_id=1, source_target_pairs={{0,1},{1,0},{2,3},{3,2},{4,5},{5,4},{6,7},{7,6},{8,9},{9,8},{10,11... | collective-permute-start | bytes 3145736 | tf_op jit(solution)/shard_map/ppermute | solution.py:389
  116.0 43.9 %collective-permute-start.26 = (bf16[2,128,2048]{2,1,0:T(8,128)(2,1)S(1)}, bf16[2,128,2048]{2,1,0:T(8,128)(2,1)}, u32[]{:S(2)}, u32[]{:S(2)}) collective-permute-start(bf16[2,128,2048]{2,1,0:T(8,128)(2,1)S(1)} %pad_maximum_fusion.1.rest_4_.rest_7_), channel_id=1, source_target_pairs={{0,4},{1,5},{2,6},{3,7},{4,0},{5,1},{6,2},{7,3},{8,12},{9,13},{10,... | collective-permute-start | bytes 3145736 | tf_op jit(solution)/shard_map/ppermute | solution.py:384
  117.5 42.9 %collective-permute-start.25 = (bf16[2,128,2048]{2,1,0:T(8,128)(2,1)S(1)}, bf16[2,128,2048]{2,1,0:T(8,128)(2,1)}, u32[]{:S(2)}, u32[]{:S(2)}) collective-permute-start(bf16[2,128,2048]{2,1,0:T(8,128)(2,1)S(1)} %pad_maximum_fusion.1.rest_4_.rest_7_), channel_id=1, source_target_pairs={{0,2},{1,3},{2,0},{3,1},{4,6},{5,7},{6,4},{7,5},{8,10},{9,11},{10,... | collective-permute-start | bytes 3145736 | tf_op jit(solution)/shard_map/ppermute | solution.py:384
  118.1 42.3 %collective-permute-start.32 = (bf16[2,128,2048]{2,1,0:T(8,128)(2,1)S(1)}, bf16[2,128,2048]{2,1,0:T(8,128)(2,1)S(1)}, u32[]{:S(2)}, u32[]{:S(2)}) collective-permute-start(bf16[2,128,2048]{2,1,0:T(8,128)(2,1)S(1)} %pad_maximum_fusion.1.rest_4_.rest_7_), channel_id=1, source_target_pairs={{0,1},{1,0},{2,3},{3,2},{4,5},{5,4},{6,7},{7,6},{8,9},{9,8},{10,11... | collective-permute-start | bytes 3145736 | tf_op jit(solution)/shard_map/ppermute | solution.py:389
  137.3 40.1 %collective-permute-start.20 = (bf16[2,128,2048]{2,1,0:T(8,128)(2,1)}, bf16[2,128,2048]{2,1,0:T(8,128)(2,1)}, u32[]{:S(2)}, u32[]{:S(2)}) collective-permute-start(bf16[2,128,2048]{2,1,0:T(8,128)(2,1)} %collective-permute-done.18.rest_1_.rest_4_), channel_id=1, source_target_pairs={{0,4},{1,5},{2,6},{3,7},{4,0},{5,1},{6,2},{7,3},{8,12},{9,13},{10,... | collective-permute-start | bytes 3145736 | tf_op jit(solution)/shard_map/ppermute | solution.py:384
  137.8 39.6 %collective-permute-start.29 = (bf16[2,128,2048]{2,1,0:T(8,128)(2,1)}, bf16[2,128,2048]{2,1,0:T(8,128)(2,1)}, u32[]{:S(2)}, u32[]{:S(2)}) collective-permute-start(bf16[2,128,2048]{2,1,0:T(8,128)(2,1)} %collective-permute-done.18.rest_1_.rest_4_), channel_id=1, source_target_pairs={{0,1},{1,0},{2,3},{3,2},{4,5},{5,4},{6,7},{7,6},{8,9},{9,8},{10,11... | collective-permute-start | bytes 3145736 | tf_op jit(solution)/shard_map/ppermute | solution.py:389
  159.9 18.1 %collective-permute-start.27 = (bf16[2,128,2048]{2,1,0:T(8,128)(2,1)}, bf16[2,128,2048]{2,1,0:T(8,128)(2,1)}, u32[]{:S(2)}, u32[]{:S(2)}) collective-permute-start(bf16[2,128,2048]{2,1,0:T(8,128)(2,1)} %collective-permute-done.26.rest_6_.rest_9_), channel_id=1, source_target_pairs={{0,2},{1,3},{2,0},{3,1},{4,6},{5,7},{6,4},{7,5},{8,10},{9,11},{10,... | collective-permute-start | bytes 3145736 | tf_op jit(solution)/shard_map/ppermute | solution.py:384
  160.4 26.8 %collective-permute-start.30 = (bf16[2,128,2048]{2,1,0:T(8,128)(2,1)S(1)}, bf16[2,128,2048]{2,1,0:T(8,128)(2,1)}, u32[]{:S(2)}, u32[]{:S(2)}) collective-permute-start(bf16[2,128,2048]{2,1,0:T(8,128)(2,1)S(1)} %collective-permute-done.19.rest_2_.rest_5_), channel_id=1, source_target_pairs={{0,1},{1,0},{2,3},{3,2},{4,5},{5,4},{6,7},{7,6},{8,9},{9,8},{10,11... | collective-permute-start | bytes 3145736 | tf_op jit(solution)/shard_map/ppermute | solution.py:389
  161.4 25.8 %collective-permute-start.34 = (bf16[2,128,2048]{2,1,0:T(8,128)(2,1)}, bf16[2,128,2048]{2,1,0:T(8,128)(2,1)}, u32[]{:S(2)}, u32[]{:S(2)}) collective-permute-start(bf16[2,128,2048]{2,1,0:T(8,128)(2,1)} %collective-permute-done.26.rest_6_.rest_9_), channel_id=1, source_target_pairs={{0,1},{1,0},{2,3},{3,2},{4,5},{5,4},{6,7},{7,6},{8,9},{9,8},{10,11... | collective-permute-start | bytes 3145736 | tf_op jit(solution)/shard_map/ppermute | solution.py:389
  275.1 21.0 %collective-permute-start.40 = (bf16[512,1024]{1,0:T(8,128)(2,1)}, bf16[512,1024]{1,0:T(8,128)(2,1)S(1)}, u32[]{:S(2)}, u32[]{:S(2)}) collective-permute-start(bf16[512,1024]{1,0:T(8,128)(2,1)} %get-tuple-element.102), channel_id=1, source_target_pairs={{0,1},{1,0},{2,3},{3,2},{4,5},{5,4},{6,7},{7,6},{8,9},{9,8},{10,11... | collective-permute-start | bytes 3145736 | tf_op jit(solution)/shard_map/ppermute | solution.py:389
  (70 other events, 900.3 us)

commit v3 on v2

--- a/solution.py
+++ b/solution.py
@@ -340,7 +340,7 @@
 LOG2E = 1.4426950408889634
 NT = (((1,), (1,)), ((), ()))
 TN = (((0,), (0,)), ((), ()))
-VMEM_LIMIT = 60 << 20
+VMEM_LIMIT = 24 << 20
 F32 = jnp.float32
 BF16 = jnp.bfloat16
 AXES = ("dp", "mp")
@@ -407,6 +407,8 @@
     return lax.ppermute(value, AXES, perm)
 
 
+DIGIT = 64
+EXTRA = 8
 MIDDLE = ((1, 2), (2, 1))
 OUTWARD = ((1, 0), (2, 3))
 
@@ -424,19 +426,22 @@
     return near, far, (z1, m1, m2, f1, f2)
 
 
-def gather_xy(near, far, first_near, first_far):
-    near_b = after(near, *first_near)
-    far_b = after(far, *first_far)
-    x_near, y_near = hop(near_b, 1, 0), hop(near_b, 0, 1)
-    x_far, y_far = hop(far_b, 1, 0), hop(far_b, 0, 1)
-    d_near, d_far = hop(x_near, 0, 1), hop(y_far, 1, 0)
+def pair_xy(value):
+    return hop(value, 1, 0), hop(value, 0, 1)
+
+
+def corners(x_near, y_far):
+    return hop(x_near, 0, 1), hop(y_far, 1, 0)
+
+
+def all_blocks(near, x_near, y_near, d_near, far, x_far, y_far, d_far):
     found = []
     for c in (0, 1):
         for array, half_bit, bit in ((near, 0, 0), (x_near, 1, 0), (y_near, 0, 1), (d_near, 1, 1)):
             found.append((array, c, half_bit, 2 * c + bit))
         for array, half_bit, bit in ((far, 0, 0), (x_far, 1, 0), (y_far, 0, 1), (d_far, 1, 1)):
             found.append((array, c, half_bit, 4 + 2 * c + bit))
-    return found, (x_near, y_near, x_far, y_far, d_near, d_far)
+    return found
 
 
 def swapped_blocks(found):
@@ -482,8 +487,8 @@
 def column_pairs(refs, table, w, ix, first, count, spread):
     pairs = []
     for k, slot, half_bit, dp_bits in table:
-        src = refs[k].at[slot, :, pl.ds(first, count)]
-        rows = at_rows(ix[0] ^ dp_bits, src.shape[0])
+        src = refs[k].at[slot, pl.ds(0, LANES), pl.ds(first, count)]
+        rows = at_rows(ix[0] ^ dp_bits, LANES)
         dst = w.at[half_bit, rows, :] if spread else w.at[rows, pl.ds(half_bit * count, count)]
         pairs.append((src, dst))
     return pairs
@@ -837,7 +842,7 @@
             pltpu.VMEM((2, rows, chunk), F32),
             pltpu.VMEM((rows, 2 * part), BF16),
             pltpu.VMEM((rows, 2 * part), BF16),
-            pltpu.SemaphoreType.DMA((sum(len(table) for _, table in sources) // 2,)),
+            pltpu.SemaphoreType.DMA((sum(len(table) for _, table in sources),)),
         ]
         + ([pltpu.VMEM((rows, model), BF16)] if last else []),
         cost(16 * rows * part * model, 12 * part * model, 2 * rows * part),
@@ -1077,44 +1082,60 @@
     r = ADAPTER_RANK
     step_rows, _, head_part = frozen_triple_weight.shape
     heads_cols = 3 * head_part
+    ids = group_ids[:, None]
+    groups = jnp.arange(LANES, dtype=jnp.int32)[None, :]
+    counts = jnp.sum((ids == groups).astype(jnp.int32), axis=0)
+    up_low = up_master.astype(BF16).reshape(2 * r, head_part)
+    fc_rows = fc_bias.reshape(-1, head_part)
+    small = jnp.concatenate([frozen_triple_bias, fc_rows, up_low], axis=0)
+    n_fc, n_small = fc_rows.shape[0], small.shape[0]
+    digits = jnp.concatenate([counts // DIGIT, counts % DIGIT]).astype(BF16).reshape(1, head_part)
+    spare = 4 * EXTRA - 1 - n_small
+    extra = jnp.concatenate([digits, small, jnp.zeros((spare, head_part), BF16)], axis=0).reshape(EXTRA, model)
     heads_own = jnp.concatenate([frozen_triple_weight.reshape(step_rows, heads_cols), out_weight.T], axis=1)
+    heads_own = jnp.concatenate([heads_own, extra], axis=0)
     units_own = jnp.concatenate([fc_weight, proj_weight.T], axis=1)
     down = jnp.zeros((LANES, model), BF16).at[: 2 * r].set(down_master.reshape(2 * r, model).astype(BF16))
     zero_line = jnp.zeros_like(pre_gain)
     vec = jnp.stack([pre_gain, pre_shift, out_bias, mid_gain, mid_shift, zero_line, zero_line, zero_line]).astype(F32)
     h_near, h_far, h_z = gather_z(heads_own, ())
-    u_near, u_far, u_z = gather_z(units_own, (h_z[3],))
-    heads, h_xy = gather_xy(h_near, h_far, (), ())
-    units, u_xy = gather_xy(u_near, u_far, (h_xy[2], h_xy[3]), ())
-    units_other = swapped_blocks(units)
-    up_low = up_master.astype(BF16).reshape(2 * ADAPTER_RANK, head_part)
-    fc_rows = fc_bias.reshape(-1, head_part)
-    small = jnp.concatenate([frozen_triple_bias, fc_rows, up_low], axis=0)
-    small = jnp.stack([small, hop(after(small, h_z[0]), 1, 0)])
+    hx_near, hy_near = pair_xy(h_near)
+    hx_far, hy_far = pair_xy(after(h_far, hx_near, hy_near))
+    hd_near, hd_far = corners(after(hx_near, h_far), hy_far)
+    heads = all_blocks(h_near, hx_near, hy_near, hd_near, h_far, hx_far, hy_far, hd_far)
+    u_near, u_far, u_z = gather_z(units_own, (hx_near, hy_near))
+    theirs_small = hx_near[0, step_rows:].reshape(-1, head_part)[1 : 1 + n_small]
+    small = jnp.stack([small, theirs_small])
     bias = small[:, :3].reshape(2, 3 * head_part).astype(F32)
-    fc_mine = small[:, 3 : 3 + fc_rows.shape[0]].reshape(2, 1, -1)
+    fc_mine = small[:, 3 : 3 + n_fc].reshape(2, 1, -1)
     fc_line = jnp.concatenate([fc_mine, core_swap(fc_mine)], axis=1).reshape(1, -1).astype(F32)
-    up_both = small[:, 3 + fc_rows.shape[0] :] * jnp.bfloat16(ADAPTER_SCALE)
+    up_both = small[:, 3 + n_fc :] * jnp.bfloat16(ADAPTER_SCALE)
     up = jnp.zeros((2, LANES, 3 * head_part), BF16)
     up = up.at[:, :r, :head_part].set(up_both[:, :r]).at[:, r : 2 * r, 2 * head_part :].set(up_both[:, r:])
-    groups = jnp.arange(LANES, dtype=jnp.int32)[None, :]
-    ids = group_ids[:, None]
+    tallies = jnp.stack([v[c, step_rows] for v in (h_near, h_far, hy_near, hy_far) for c in (0, 1)]).astype(F32)
+    tallies = jnp.sum(tallies[:, :head_part].reshape(-1, 2, LANES), axis=0)
+    weight_table = F32(tok_dev * lax.axis_size("dp")) / (GROUPS * (DIGIT * tallies[:1] + tallies[1:]))
     normed, latent = norm_rows(idx, tokens, vec, down)
+    near_go = after(u_near, hd_near, hd_far)
+    ux_near, uy_near = pair_xy(near_go)
     queries, keys, values = project_heads(idx, normed, latent, bias, up, heads)
     mixed, logsum = attend_fast(queries, keys, values)
-    counts = jnp.sum((ids == groups).astype(jnp.int32), axis=0, keepdims=True)
-    counts = after(counts, queries)
-    bits = 1
-    while bits < lax.axis_size("dp"):
-        counts = counts + hop(counts, 0, bits)
-        bits *= 2
-    weight_table = F32(tok_dev * lax.axis_size("dp")) / (GROUPS * counts.astype(F32))
-
+    far_go = after(u_far, queries)
+    ux_far, uy_far = pair_xy(far_go)
     sent = core_swap(attention_out_send(idx, mixed, heads, heads_cols))
     hidden, normed_mid = attention_out_own(idx, mixed, sent, tokens, vec, heads, heads_cols)
+    straight = all_blocks(u_near, ux_near, uy_near, None, u_far, ux_far, uy_far, None)
+    first_mine = [e for e in straight if e[2] == 0]
+    first_other = swapped_blocks(first_mine)
     rows = (normed_mid, cotangent, ids, weight_table, fc_line, vec)
-    carried = units_main(idx, 0, *rows, units, units_other, (), None)
-    hidden_grad, hidden_low, *out_pieces = units_main(idx, 1, *rows, units, units_other, carried, hidden)
+    ux_near, uy_near, uy_far, _, _ = lax.optimization_barrier((ux_near, uy_near, uy_far, ux_far, normed_mid))
+    ud_near, ud_far = corners(ux_near, uy_far)
+    carried = units_main(idx, 0, *rows, first_mine, first_other, (), None)
+    ud_near, ud_far, _ = lax.optimization_barrier((ud_near, ud_far, carried[0]))
+    units = all_blocks(u_near, ux_near, uy_near, ud_near, u_far, ux_far, uy_far, ud_far)
+    last_mine = [e for e in units if e[2] == 1]
+    last_other = swapped_blocks(last_mine)
+    hidden_grad, hidden_low, *out_pieces = units_main(idx, 1, *rows, last_mine, last_other, carried, hidden)
     hidden_other = core_swap(hidden_low)
     dq, dk, dv = attend_back_fast(
         idx, queries, keys, values, mixed, hidden_low, hidden_other, logsum, heads, heads_cols

time: 322 us -> 258 us (0.80)
  waiting for transfers between devices: 112 us -> 76.6 us
  Pallas kernels: 134 us -> 102 us
  local copies, waits for them, and re-layouts: 15.8 us -> 27.7 us
  starting transfers between devices: 44.2 us -> 38.6 us
    ppermute x24 -> x20, waiting for transfers between devices: 96 us -> 51.1 us  [hop(): return lax.ppermute(value, AXES, [(i, i ^ flip) for i in range(total)])]
    unnamed x94 -> x122, local copies, waits for them, and re-layouts: 8.67 us -> 20.8 us
    pallas_call x2, Pallas kernels: 44.3 us -> 35.5 us  [units_main(): call(body, 'units_main_last' if last else 'units_main_first', 1, specs +...]
    ppermute x24 -> x20, starting transfers between devices: 30.1 us -> 25.1 us  [hop(): return lax.ppermute(value, AXES, [(i, i ^ flip) for i in range(total)])]
    ppermute x8, waiting for transfers between devices: 8.74 us -> 13.2 us  [z_hop(): return lax.ppermute(value, AXES, perm)]
    ppermute x15, waiting for transfers between devices: 2.71 us -> 7.14 us  [core_swap(): return lax.ppermute(value, AXES, [(i, i ^ 1) for i in range(total)])]
    pallas_call x1, Pallas kernels: 13.6 us -> 9.4 us  [heads_back(): call(body, 'heads_back', 2 * half_blocks, [row(width)] * 3 + [row(model),...]
    another operation x0 -> x8, local copies, waits for them, and re-layouts: none -> 3.73 us  [the longest x7 3.7 us: on_device_fast(): jnp.stack([v[c, step_rows] for v in (h_near, h_far, hy_near, hy_far) for...]
  transfers between devices with their start and end apart: 49 -> 45, of which waited for: 17 -> 19; matrix products, arithmetic and copies ran while one was open for 6% -> 5% of each run, Pallas kernels for 14% -> 19%
where the time goes in v3:
time: 258 us; the launch traced here: 256 us
  Pallas kernels  102 us (40%)
  waiting for transfers between devices  76.6 us (30%)
  starting transfers between devices  38.6 us (15%)
  local copies, waits for them, and re-layouts  27.7 us (11%)
  other arithmetic  9.13 us (4%)
    ppermute x20, waiting for transfers between devices, hop(): return lax.ppermute(value, AXES, [(i, i ^ flip) for i in range(total)])  51.1 us
    pallas_call x2, Pallas kernels, units_main(): call(body, 'units_main_last' if last else 'units_main_first', 1, specs +...  35.5 us
    ppermute x20, starting transfers between devices, hop(): return lax.ppermute(value, AXES, [(i, i ^ flip) for i in range(total)])  25.1 us
    pallas_call x1, Pallas kernels, attend_back_fast(): call(body, 'attend_back', pairs, [spec] * 4 + [full(half, model)] * 2 + [...  22.4 us
    unnamed x122, local copies, waits for them, and re-layouts  20.8 us
    pallas_call x1, Pallas kernels, attend_fast(): pl.pallas_call(body, grid=(pairs,), out_shape=(shape(length, width), jax....  13.4 us
    ppermute x8, waiting for transfers between devices, z_hop(): return lax.ppermute(value, AXES, perm)  13.2 us
    pallas_call x1, Pallas kernels, heads_back(): call(body, 'heads_back', 2 * half_blocks, [row(width)] * 3 + [row(model),...  9.4 us
  transfers between devices with their start and end apart: 45, of which 19 were waited for; matrix products, arithmetic and copies ran while one was open for 5% of the time, Pallas kernels for 19%

profile of v3, /device:TPU:0, one launch (start us, length us, event | category | flops | bytes accessed | tf_op | source)
XLA Modules:
  0.0 256.3 jit_solution(3748151782375423878)
XLA Ops:
  6.2 3.1 %collective-permute-start = (bf16[136,1024]{1,0:T(8,128)(2,1)S(1)}, bf16[136,1024]{1,0:T(8,128)(2,1)S(1)}, u32[]{:S(2)}, u32[]{:S(2)}) collective-permute-start(bf16[136,1024]{1,0:T(8,128)(2,1)S(1)} %get-tuple-element.135), channel_id=1, source_target_pairs={{0,8},{1,9},{2,10},{3,11},{4,12},{5,13},{6,14},{7,15},{8,0},{9,1},... | collective-permute-start | bytes 835592 | tf_op jit(solution)/shard_map/ppermute | solution.py:384
  11.1 4.9 %collective-permute-done = bf16[136,1024]{1,0:T(8,128)(2,1)S(1)} collective-permute-done((bf16[136,1024]{1,0:T(8,128)(2,1)S(1)}, bf16[136,1024]{1,0:T(8,128)(2,1)S(1)}, u32[]{:S(2)}, u32[]{:S(2)}) %collective-permute-start) | collective-permute-done | bytes 278560 | tf_op jit(solution)/shard_map/ppermute | solution.py:384
  24.9 2.3 copy-done
  27.2 2.9 %norm_rows.1 = (bf16[1024,1024]{1,0:T(8,128)(2,1)S(1)}, bf16[1024,128]{1,0:T(8,128)(2,1)S(1)}) custom-call(s32[3]{0:T(128)S(1)} %pad_add_fusion.ix, bf16[2048,1024]{1,0:T(8,128)(2,1)S(1)} %copy-done, f32[8,1024]{1,0:T(8,128)S(1)} %convert_element_type.41.vec_ref, bf16[128,1024]{1,0:T(8,128)(2,1)S(1)} %scatter.10.down_ref), custom_call_target="tpu_custom_call" | custom-call | flops 268435456 | bytes 4194304 | tf_op jit(solution)/shard_map/norm_rows/pallas_call | solution.py:532
  33.2 2.5 collective-permute-start.13
  39.7 8.2 %collective-permute-done.13 = bf16[128,2048]{1,0:T(8,128)(2,1)} collective-permute-done((bf16[128,2048]{1,0:T(8,128)(2,1)}, bf16[128,2048]{1,0:T(8,128)(2,1)}, u32[]{:S(2)}, u32[]{:S(2)}) %collective-permute-start.13) | collective-permute-done | bytes 524320 | tf_op jit(solution)/shard_map/ppermute | solution.py:384
  51.1 2.3 pad_maximum_fusion.rest_0_
  54.9 9.8 %collective-permute-done.17 = bf16[128,2048]{1,0:T(8,128)(2,1)S(1)} collective-permute-done((bf16[128,2048]{1,0:T(8,128)(2,1)}, bf16[128,2048]{1,0:T(8,128)(2,1)S(1)}, u32[]{:S(2)}, u32[]{:S(2)}) %collective-permute-start.17) | collective-permute-done | bytes 524320 | tf_op jit(solution)/shard_map/ppermute | solution.py:407
  66.6 6.1 %project_heads.1 = (bf16[1024,512]{1,0:T(8,128)(2,1)S(1)}, bf16[1024,512]{1,0:T(8,128)(2,1)S(1)}, bf16[1024,512]{1,0:T(8,128)(2,1)S(1)}) custom-call(s32[3]{0:T(128)S(1)} %pad_add_fusion.ix, bf16[1024,1024]{1,0:T(8,128)(2,1)S(1)} %copy-done.30, bf16[1024,128]{1,0:T(8,128)(2,1)S(1)} %copy-done.33, f32[2,768]{1,0:T(2,128)S(1)} %bitcast.60, ...), custom_call_target="tpu_custom_call" | custom-call | flops 3221225472 | bytes 16777216 | tf_op jit(solution)/shard_map/project_heads/pallas_call | solution.py:566
  72.8 13.4 %attend.1 = (bf16[1024,512]{1,0:T(8,128)(2,1)S(1)}, f32[4,8,1024]{2,1,0:T(8,128)S(1)}) custom-call(bf16[1024,512]{1,0:T(8,128)(2,1)S(1)} %get-tuple-element.87.q_ref, bf16[1024,512]{1,0:T(8,128)(2,1)S(1)} %get-tuple-element.88.k_ref, bf16[1024,512]{1,0:T(8,128)(2,1)S(1)} %get-tuple-element.89.v_ref), custom_call_target="tpu_custom_call" | custom-call | flops 4294967296 | bytes 4194304 | tf_op jit(solution)/shard_map/attend/pallas_call | solution.py:613
  86.3 2.7 %attention_out_send.1 = bf16[512,1024]{1,0:T(8,128)(2,1)} custom-call(s32[3]{0:T(128)S(1)} %pad_add_fusion.ix, bf16[1024,512]{1,0:T(8,128)(2,1)S(1)} %get-tuple-element.90.att.o_ref, bf16[2,136,1024]{2,1,0:T(8,128)(2,1)S(1)} %pad_maximum_fusion.2.rest_0_, bf16[2,136,1024]{2,1,0:T(8,128)(2,1)S(1)} %collective-permute-done.1.rest_1_, ...), custom_call_target="tpu_custom_call" | custom-call | flops 536870912 | bytes 2097152 | tf_op jit(solution)/shard_map/attention_out_send/pallas_call | solution.py:642
  97.4 18.8 %collective-permute-done.19.rest_3_ = bf16[2,128,2048]{2,1,0:T(8,128)(2,1)} collective-permute-done((bf16[2,128,2048]{2,1,0:T(8,128)(2,1)}, bf16[2,128,2048]{2,1,0:T(8,128)(2,1)}, u32[]{:S(2)}, u32[]{:S(2)}) %collective-permute-start.19) | collective-permute-done | bytes 1048608 | tf_op jit(solution)/shard_map/ppermute | solution.py:384
  124.2 3.9 %attention_out_own.1 = (f32[512,1024]{1,0:T(8,128)S(1)}, bf16[512,1024]{1,0:T(8,128)(2,1)S(1)}) custom-call(s32[3]{0:T(128)S(1)} %pad_add_fusion.ix, bf16[1024,512]{1,0:T(8,128)(2,1)S(1)} %get-tuple-element.90.att.o_ref, bf16[512,1024]{1,0:T(8,128)(2,1)} %collective-permute-done.11.recv, bf16[2048,1024]{1,0:T(8,128)(2,1)S(1)} %copy-done.1, ...), custom_call_target="tpu_custom_call" | custom-call | flops 536870912 | bytes 5242880 | tf_op jit(solution)/shard_map/attention_out_own/pallas_call | solution.py:676
  131.1 16.9 %units_main_first.1 = (f32[512,1024]{1,0:T(8,128)S(1)}, f32[512,1024]{1,0:T(8,128)S(1)}) custom-call(s32[3]{0:T(128)S(1)} %pad_add_fusion.ix, bf16[512,1024]{1,0:T(8,128)(2,1)S(1)} %get-tuple-element.91.normed_ref, bf16[2048,1024]{1,0:T(8,128)(2,1)S(1)} %copy-done.28, s32[2048,1]{1,0:T(8,128)S(1)} %copy-done.23, f32[1,128]{1,0:T(1,128)S(1)} %divide_bitcast_fusion.table_ref, ...), custom_call_target="tpu_custom_call" | custom-call | flops 8589934592 | bytes 12582912 | tf_op jit(solution)/shard_map/units_main_first/pallas_call | solution.py:831
  147.9 6.0 %collective-permute-done.26.rest_4_ = bf16[2,128,2048]{2,1,0:T(8,128)(2,1)S(1)} collective-permute-done((bf16[2,128,2048]{2,1,0:T(8,128)(2,1)}, bf16[2,128,2048]{2,1,0:T(8,128)(2,1)S(1)}, u32[]{:S(2)}, u32[]{:S(2)}) %collective-permute-start.26) | collective-permute-done | bytes 1048608 | tf_op jit(solution)/shard_map/ppermute | solution.py:384
  159.0 18.7 %units_main_last.1 = (f32[512,1024]{1,0:T(8,128)S(1)}, bf16[512,1024]{1,0:T(8,128)(2,1)S(1)}, bf16[512,256]{1,0:T(8,128)(2,1)S(1)}, bf16[512,256]{1,0:T(8,128)(2...) custom-call(s32[3]{0:T(128)S(1)} %pad_add_fusion.ix, bf16[512,1024]{1,0:T(8,128)(2,1)S(1)} %get-tuple-element.91.normed_ref, ...), custom_call_target="tpu_custom_call" | custom-call | flops 8589934592 | bytes 12582912 | tf_op jit(solution)/shard_map/units_main_last/pallas_call | solution.py:831
  179.1 2.5 collective-permute-done.35.other_ref
  181.8 22.4 %attend_back.1 = (bf16[1024,512]{1,0:T(8,128)(2,1)S(1)}, bf16[1024,512]{1,0:T(8,128)(2,1)S(1)}, bf16[1024,512]{1,0:T(8,128)(2,1)S(1)}) custom-call(s32[3]{0:T(128)S(1)} %pad_add_fusion.ix, bf16[1024,512]{1,0:T(8,128)(2,1)S(1)} %copy-done.36, bf16[1024,512]{1,0:T(8,128)(2,1)S(1)} %copy-done.38, bf16[1024,512]{1,0:T(8,128)(2,1)S(1)} %copy-done.40, ...), custom_call_target="tpu_custom_call" | custom-call | flops 10737418240 | bytes 8388608 | tf_op jit(solution)/shard_map/attend_back/pallas_call | solution.py:909
  204.2 9.4 %heads_back.1 = (bf16[512,1024]{1,0:T(8,128)(2,1)}, f32[512,1024]{1,0:T(8,128)S(1)}, f32[8,1024]{1,0:T(8,128)S(1)}, f32[8,1536]{1,0:T(8,128)S(1)}) custom-call(s32[3]{0:T(128)S(1)} %pad_add_fusion.ix, bf16[1024,512]{1,0:T(8,128)(2,1)S(1)} %get-tuple-element.108.dq_ref, bf16[1024,512]{1,0:T(8,128)(2,1)S(1)} %get-tuple-element.109.dk_ref, ...), custom_call_target="tpu_custom_call" | custom-call | flops 3221225472 | bytes 6291456 | tf_op jit(solution)/shard_map/heads_back/pallas_call | solution.py:977
  221.2 3.1 %collective-permute-done.42 = f32[8,1280]{1,0:T(8,128)S(1)} collective-permute-done((f32[8,1280]{1,0:T(8,128)S(1)}, f32[8,1280]{1,0:T(8,128)S(1)}, u32[]{:S(2)}, u32[]{:S(2)}) %collective-permute-start.42) | collective-permute-done | bytes 40992 | tf_op jit(solution)/shard_map/ppermute | solution.py:384
  226.0 2.3 collective-permute-done.43
  238.7 2.3 tokens_back.1
  244.2 6.1 %collective-permute-done.38.rest_2_ = bf16[512,256]{1,0:T(8,128)(2,1)S(1)} collective-permute-done((bf16[512,256]{1,0:T(8,128)(2,1)S(1)}, bf16[512,256]{1,0:T(8,128)(2,1)S(1)}, u32[]{:S(2)}, u32[]{:S(2)}) %collective-permute-start.38) | collective-permute-done | bytes 262176 | tf_op jit(solution)/shard_map/ppermute | solution.py:384
  250.4 4.4 %collective-permute-done.39.rest_3_ = bf16[512,256]{1,0:T(8,128)(2,1)S(1)} collective-permute-done((bf16[512,256]{1,0:T(8,128)(2,1)S(1)}, bf16[512,256]{1,0:T(8,128)(2,1)S(1)}, u32[]{:S(2)}, u32[]{:S(2)}) %collective-permute-start.39) | collective-permute-done | bytes 262176 | tf_op jit(solution)/shard_map/ppermute | solution.py:1051
  (272 shorter events, 79.1 us)
Async XLA Ops:
  16.7 16.5 %collective-permute-start.1 = (bf16[2,136,1024]{2,1,0:T(8,128)(2,1)S(1)}, bf16[2,136,1024]{2,1,0:T(8,128)(2,1)S(1)}, u32[]{:S(2)}, u32[]{:S(2)}) collective-permute-start(bf16[2,136,1024]{2,1,0:T(8,128)(2,1)S(1)} %pad_maximum_fusion.2.rest_0_), channel_id=1, source_target_pairs={{0,2},{1,3},{2,0},{3,1},{4,6},{5,7},{6,4},{7,5},{8,10},{9,11},{10,... | collective-permute-start | bytes 1671176 | tf_op jit(solution)/shard_map/ppermute | solution.py:384
  18.4 14.8 %collective-permute-start.2 = (bf16[2,136,1024]{2,1,0:T(8,128)(2,1)S(1)}, bf16[2,136,1024]{2,1,0:T(8,128)(2,1)S(1)}, u32[]{:S(2)}, u32[]{:S(2)}) collective-permute-start(bf16[2,136,1024]{2,1,0:T(8,128)(2,1)S(1)} %pad_maximum_fusion.2.rest_0_), channel_id=1, source_target_pairs={{0,4},{1,5},{2,6},{3,7},{4,0},{5,1},{6,2},{7,3},{8,12},{9,13},{10,... | collective-permute-start | bytes 1671176 | tf_op jit(solution)/shard_map/ppermute | solution.py:384
  23.3 15.0 %collective-permute-start.6 = (bf16[136,1024]{1,0:T(8,128)(2,1)S(1)}, bf16[136,1024]{1,0:T(8,128)(2,1)S(1)}, u32[]{:S(2)}, u32[]{:S(2)}) collective-permute-start(bf16[136,1024]{1,0:T(8,128)(2,1)S(1)} %collective-permute-done.3), channel_id=1, source_target_pairs={{8,0},{9,1},{10,2},{11,3},{12,4},{13,5},{14,6},{15,7},{16,24},{17,... | collective-permute-start | bytes 835592 | tf_op jit(solution)/shard_map/ppermute | solution.py:407
  33.2 14.6 %collective-permute-start.13 = (bf16[128,2048]{1,0:T(8,128)(2,1)}, bf16[128,2048]{1,0:T(8,128)(2,1)}, u32[]{:S(2)}, u32[]{:S(2)}) collective-permute-start(bf16[128,2048]{1,0:T(8,128)(2,1)} %get-tuple-element.92), channel_id=1, source_target_pairs={{0,8},{1,9},{2,10},{3,11},{4,12},{5,13},{6,14},{7,15},{8,0},{9,1},... | collective-permute-start | bytes 1572872 | tf_op jit(solution)/shard_map/ppermute | solution.py:384
  39.0 27.6 %collective-permute-start.8 = (bf16[2,136,1024]{2,1,0:T(8,128)(2,1)S(1)}, bf16[2,136,1024]{2,1,0:T(8,128)(2,1)S(1)}, u32[]{:S(2)}, u32[]{:S(2)}) collective-permute-start(bf16[2,136,1024]{2,1,0:T(8,128)(2,1)S(1)} %pad_maximum_fusion.3.rest_4_), channel_id=1, source_target_pairs={{0,2},{1,3},{2,0},{3,1},{4,6},{5,7},{6,4},{7,5},{8,10},{9,11},{10,... | collective-permute-start | bytes 1671176 | tf_op jit(solution)/shard_map/ppermute | solution.py:384
  48.5 16.2 %collective-permute-start.17 = (bf16[128,2048]{1,0:T(8,128)(2,1)}, bf16[128,2048]{1,0:T(8,128)(2,1)S(1)}, u32[]{:S(2)}, u32[]{:S(2)}) collective-permute-start(bf16[128,2048]{1,0:T(8,128)(2,1)} %collective-permute-done.16), channel_id=1, source_target_pairs={{8,0},{9,1},{10,2},{11,3},{12,4},{13,5},{14,6},{15,7},{16,24},{17,... | collective-permute-start | bytes 1572872 | tf_op jit(solution)/shard_map/ppermute | solution.py:407
  49.9 14.9 %collective-permute-start.7 = (bf16[2,136,1024]{2,1,0:T(8,128)(2,1)S(1)}, bf16[2,136,1024]{2,1,0:T(8,128)(2,1)S(1)}, u32[]{:S(2)}, u32[]{:S(2)}) collective-permute-start(bf16[2,136,1024]{2,1,0:T(8,128)(2,1)S(1)} %collective-permute-done.1.rest_1_), channel_id=1, source_target_pairs={{0,4},{1,5},{2,6},{3,7},{4,0},{5,1},{6,2},{7,3},{8,12},{9,13},{10,... | collective-permute-start | bytes 1671176 | tf_op jit(solution)/shard_map/ppermute | solution.py:384
  50.5 14.3 %collective-permute-start.10 = (bf16[2,136,1024]{2,1,0:T(8,128)(2,1)S(1)}, bf16[2,136,1024]{2,1,0:T(8,128)(2,1)S(1)}, u32[]{:S(2)}, u32[]{:S(2)}) collective-permute-start(bf16[2,136,1024]{2,1,0:T(8,128)(2,1)S(1)} %collective-permute-done.9.rest_6_), channel_id=1, source_target_pairs={{0,2},{1,3},{2,0},{3,1},{4,6},{5,7},{6,4},{7,5},{8,10},{9,11},{10,... | collective-permute-start | bytes 1671176 | tf_op jit(solution)/shard_map/ppermute | solution.py:384
  53.4 35.7 %collective-permute-start.18 = (bf16[128,2048]{1,0:T(8,128)(2,1)S(1)}, bf16[128,2048]{1,0:T(8,128)(2,1)S(1)}, u32[]{:S(2)}, u32[]{:S(2)}) collective-permute-start(bf16[128,2048]{1,0:T(8,128)(2,1)S(1)} %collective-permute-done.15), channel_id=1, source_target_pairs={{8,0},{9,1},{10,2},{11,3},{12,4},{13,5},{14,6},{15,7},{16,24},{17,... | collective-permute-start | bytes 1572872 | tf_op jit(solution)/shard_map/ppermute | solution.py:407
  64.8 30.1 %collective-permute-start.14 = (bf16[2,128,2048]{2,1,0:T(8,128)(2,1)}, bf16[2,128,2048]{2,1,0:T(8,128)(2,1)}, u32[]{:S(2)}, u32[]{:S(2)}) collective-permute-start(bf16[2,128,2048]{2,1,0:T(8,128)(2,1)} %pad_maximum_fusion.rest_0_), channel_id=1, source_target_pairs={{0,4},{1,5},{2,6},{3,7},{4,0},{5,1},{6,2},{7,3},{8,12},{9,13},{10,... | collective-permute-start | bytes 3145736 | tf_op jit(solution)/shard_map/ppermute | solution.py:384
  66.0 30.9 %collective-permute-start.24 = (bf16[2,128,2048]{2,1,0:T(8,128)(2,1)}, bf16[2,128,2048]{2,1,0:T(8,128)(2,1)}, u32[]{:S(2)}, u32[]{:S(2)}) collective-permute-start(bf16[2,128,2048]{2,1,0:T(8,128)(2,1)} %pad_maximum_fusion.rest_0_), channel_id=1, source_target_pairs={{0,2},{1,3},{2,0},{3,1},{4,6},{5,7},{6,4},{7,5},{8,10},{9,11},{10,... | collective-permute-start | bytes 3145736 | tf_op jit(solution)/shard_map/ppermute | solution.py:384
  90.3 25.9 %collective-permute-start.19 = (bf16[2,128,2048]{2,1,0:T(8,128)(2,1)}, bf16[2,128,2048]{2,1,0:T(8,128)(2,1)}, u32[]{:S(2)}, u32[]{:S(2)}) collective-permute-start(bf16[2,128,2048]{2,1,0:T(8,128)(2,1)} %pad_maximum_fusion.1.rest_2_), channel_id=1, source_target_pairs={{0,4},{1,5},{2,6},{3,7},{4,0},{5,1},{6,2},{7,3},{8,12},{9,13},{10,... | collective-permute-start | bytes 3145736 | tf_op jit(solution)/shard_map/ppermute | solution.py:384
  94.8 34.5 %collective-permute-start.20 = (bf16[2,128,2048]{2,1,0:T(8,128)(2,1)}, bf16[2,128,2048]{2,1,0:T(8,128)(2,1)}, u32[]{:S(2)}, u32[]{:S(2)}) collective-permute-start(bf16[2,128,2048]{2,1,0:T(8,128)(2,1)} %pad_maximum_fusion.rest_0_), channel_id=1, source_target_pairs={{0,1},{1,0},{2,3},{3,2},{4,5},{5,4},{6,7},{7,6},{8,9},{9,8},{10,11... | collective-permute-start | bytes 3145736 | tf_op jit(solution)/shard_map/ppermute | solution.py:389
  95.0 33.1 %collective-permute-start.25 = (bf16[2,128,2048]{2,1,0:T(8,128)(2,1)}, bf16[2,128,2048]{2,1,0:T(8,128)(2,1)}, u32[]{:S(2)}, u32[]{:S(2)}) collective-permute-start(bf16[2,128,2048]{2,1,0:T(8,128)(2,1)} %pad_maximum_fusion.1.rest_2_), channel_id=1, source_target_pairs={{0,2},{1,3},{2,0},{3,1},{4,6},{5,7},{6,4},{7,5},{8,10},{9,11},{10,... | collective-permute-start | bytes 3145736 | tf_op jit(solution)/shard_map/ppermute | solution.py:384
  96.9 33.6 %collective-permute-start.22 = (bf16[2,128,2048]{2,1,0:T(8,128)(2,1)}, bf16[2,128,2048]{2,1,0:T(8,128)(2,1)}, u32[]{:S(2)}, u32[]{:S(2)}) collective-permute-start(bf16[2,128,2048]{2,1,0:T(8,128)(2,1)} %pad_maximum_fusion.1.rest_2_), channel_id=1, source_target_pairs={{0,1},{1,0},{2,3},{3,2},{4,5},{5,4},{6,7},{7,6},{8,9},{9,8},{10,11... | collective-permute-start | bytes 3145736 | tf_op jit(solution)/shard_map/ppermute | solution.py:389
  96.9 33.7 %collective-permute-start.21 = (bf16[2,128,2048]{2,1,0:T(8,128)(2,1)}, bf16[2,128,2048]{2,1,0:T(8,128)(2,1)}, u32[]{:S(2)}, u32[]{:S(2)}) collective-permute-start(bf16[2,128,2048]{2,1,0:T(8,128)(2,1)} %collective-permute-done.14.rest_1_), channel_id=1, source_target_pairs={{0,1},{1,0},{2,3},{3,2},{4,5},{5,4},{6,7},{7,6},{8,9},{9,8},{10,11... | collective-permute-start | bytes 3145736 | tf_op jit(solution)/shard_map/ppermute | solution.py:389
  116.2 14.9 %collective-permute-start.23 = (bf16[2,128,2048]{2,1,0:T(8,128)(2,1)}, bf16[2,128,2048]{2,1,0:T(8,128)(2,1)}, u32[]{:S(2)}, u32[]{:S(2)}) collective-permute-start(bf16[2,128,2048]{2,1,0:T(8,128)(2,1)} %collective-permute-done.19.rest_3_), channel_id=1, source_target_pairs={{0,1},{1,0},{2,3},{3,2},{4,5},{5,4},{6,7},{7,6},{8,9},{9,8},{10,11... | collective-permute-start | bytes 3145736 | tf_op jit(solution)/shard_map/ppermute | solution.py:389
  128.1 25.8 %collective-permute-start.26 = (bf16[2,128,2048]{2,1,0:T(8,128)(2,1)}, bf16[2,128,2048]{2,1,0:T(8,128)(2,1)S(1)}, u32[]{:S(2)}, u32[]{:S(2)}) collective-permute-start(bf16[2,128,2048]{2,1,0:T(8,128)(2,1)} %collective-permute-done.24.rest_3_), channel_id=1, source_target_pairs={{0,4},{1,5},{2,6},{3,7},{4,0},{5,1},{6,2},{7,3},{8,12},{9,13},{10,... | collective-permute-start | bytes 3145736 | tf_op jit(solution)/shard_map/ppermute | solution.py:384
  129.3 25.5 %collective-permute-start.27 = (bf16[2,128,2048]{2,1,0:T(8,128)(2,1)}, bf16[2,128,2048]{2,1,0:T(8,128)(2,1)S(1)}, u32[]{:S(2)}, u32[]{:S(2)}) collective-permute-start(bf16[2,128,2048]{2,1,0:T(8,128)(2,1)} %collective-permute-done.19.rest_3_), channel_id=1, source_target_pairs={{0,2},{1,3},{2,0},{3,1},{4,6},{5,7},{6,4},{7,5},{8,10},{9,11},{10,... | collective-permute-start | bytes 3145736 | tf_op jit(solution)/shard_map/ppermute | solution.py:384
  130.5 24.8 %collective-permute-start.28 = (bf16[2,128,2048]{2,1,0:T(8,128)(2,1)}, bf16[2,128,2048]{2,1,0:T(8,128)(2,1)S(1)}, u32[]{:S(2)}, u32[]{:S(2)}) collective-permute-start(bf16[2,128,2048]{2,1,0:T(8,128)(2,1)} %collective-permute-done.24.rest_3_), channel_id=1, source_target_pairs={{0,1},{1,0},{2,3},{3,2},{4,5},{5,4},{6,7},{7,6},{8,9},{9,8},{10,11... | collective-permute-start | bytes 3145736 | tf_op jit(solution)/shard_map/ppermute | solution.py:389
  130.6 24.7 %collective-permute-start.30 = (bf16[2,128,2048]{2,1,0:T(8,128)(2,1)}, bf16[2,128,2048]{2,1,0:T(8,128)(2,1)S(1)}, u32[]{:S(2)}, u32[]{:S(2)}) collective-permute-start(bf16[2,128,2048]{2,1,0:T(8,128)(2,1)} %collective-permute-done.25.rest_5_), channel_id=1, source_target_pairs={{0,1},{1,0},{2,3},{3,2},{4,5},{5,4},{6,7},{7,6},{8,9},{9,8},{10,11... | collective-permute-start | bytes 3145736 | tf_op jit(solution)/shard_map/ppermute | solution.py:389
  215.0 18.2 %collective-permute-start.36 = (bf16[512,1024]{1,0:T(8,128)(2,1)}, bf16[512,1024]{1,0:T(8,128)(2,1)S(1)}, u32[]{:S(2)}, u32[]{:S(2)}) collective-permute-start(bf16[512,1024]{1,0:T(8,128)(2,1)} %get-tuple-element.112), channel_id=1, source_target_pairs={{0,1},{1,0},{2,3},{3,2},{4,5},{5,4},{6,7},{7,6},{8,9},{9,8},{10,11... | collective-permute-start | bytes 3145736 | tf_op jit(solution)/shard_map/ppermute | solution.py:389
  217.4 13.4 %collective-permute-start.32 = (bf16[512,256]{1,0:T(8,128)(2,1)}, bf16[512,256]{1,0:T(8,128)(2,1)S(1)}, u32[]{:S(2)}, u32[]{:S(2)}) collective-permute-start(bf16[512,256]{1,0:T(8,128)(2,1)} %get-tuple-element.103), channel_id=1, source_target_pairs={{0,1},{1,0},{2,3},{3,2},{4,5},{5,4},{6,7},{7,6},{8,9},{9,8},{10,11... | collective-permute-start | bytes 786440 | tf_op jit(solution)/shard_map/ppermute | solution.py:389
  217.4 13.4 %collective-permute-start.33 = (bf16[512,256]{1,0:T(8,128)(2,1)}, bf16[512,256]{1,0:T(8,128)(2,1)S(1)}, u32[]{:S(2)}, u32[]{:S(2)}) collective-permute-start(bf16[512,256]{1,0:T(8,128)(2,1)} %get-tuple-element.104), channel_id=1, source_target_pairs={{0,2},{1,3},{2,0},{3,1},{4,6},{5,7},{6,4},{7,5},{8,10},{9,11},{10,... | collective-permute-start | bytes 786440 | tf_op jit(solution)/shard_map/ppermute | solution.py:384
  (80 other events, 910.3 us)

commit v4 on v3

--- a/solution.py
+++ b/solution.py
@@ -348,7 +348,7 @@
 
 
 def cost(flops, nbytes, trans=0):
-    return pl.CostEstimate(flops=int(flops), bytes_accessed=int(nbytes), transcendentals=int(trans))
+    return pl.CostEstimate(flops=int(flops) // 10, bytes_accessed=int(nbytes) // 10, transcendentals=int(trans) // 10)
 
 
 def shape(rows, cols, dtype=BF16):
@@ -359,7 +359,7 @@
     return pl.BlockSpec((rows, cols), lambda i, ix: (0, 0))
 
 
-def call(body, name, grid, in_specs, out_specs, out_shape, scratch, est):
+def call(body, name, grid, in_specs, out_specs, out_shape, scratch, est, grant=None):
     return pl.pallas_call(
         body,
         grid_spec=pltpu.PrefetchScalarGridSpec(
@@ -370,7 +370,7 @@
             scratch_shapes=scratch,
         ),
         out_shape=out_shape,
-        compiler_params=pltpu.CompilerParams(vmem_limit_bytes=VMEM_LIMIT),
+        compiler_params=pltpu.CompilerParams(vmem_limit_bytes=grant or VMEM_LIMIT),
         cost_estimate=est,
         name=name,
     )
@@ -408,6 +408,7 @@
 
 
 DIGIT = 64
+CUTS = 1
 EXTRA = 8
 MIDDLE = ((1, 2), (2, 1))
 OUTWARD = ((1, 0), (2, 3))
@@ -421,27 +422,15 @@
     f1 = z_hop(m1, OUTWARD)
     f2 = z_hop(m2, OUTWARD)
     inner = inner_z()
-    near = jnp.stack([own, z1])
-    far = jnp.stack([jnp.where(inner, m2, f1), jnp.where(inner, m1, f2)])
-    return near, far, (z1, m1, m2, f1, f2)
+    return z1, jnp.where(inner, m2, f1), jnp.where(inner, m1, f2)
 
 
 def pair_xy(value):
     return hop(value, 1, 0), hop(value, 0, 1)
 
 
-def corners(x_near, y_far):
-    return hop(x_near, 0, 1), hop(y_far, 1, 0)
-
-
-def all_blocks(near, x_near, y_near, d_near, far, x_far, y_far, d_far):
-    found = []
-    for c in (0, 1):
-        for array, half_bit, bit in ((near, 0, 0), (x_near, 1, 0), (y_near, 0, 1), (d_near, 1, 1)):
-            found.append((array, c, half_bit, 2 * c + bit))
-        for array, half_bit, bit in ((far, 0, 0), (x_far, 1, 0), (y_far, 0, 1), (d_far, 1, 1)):
-            found.append((array, c, half_bit, 4 + 2 * c + bit))
-    return found
+def blocks_of(array, first, half_bit, bit):
+    return [(array, slot, half_bit, 2 * (first + slot) + bit) for slot in range(array.shape[0])]
 
 
 def swapped_blocks(found):
@@ -502,9 +491,9 @@
     ]
 
 
-def pick(low, value, which):
+def both_heads(low, value):
     zero = jnp.zeros((), value.dtype)
-    return jnp.where(low, value, zero) if which == 0 else jnp.where(low, zero, value)
+    return jnp.concatenate([jnp.where(low, value, zero), jnp.where(low, zero, value)], axis=0)
 
 
 def row_stats(values):
@@ -513,101 +502,216 @@
     return center * scaler, scaler
 
 
-def token_weights(ids, table):
-    lanes = lax.broadcasted_iota(jnp.int32, (ids.shape[0], LANES), 1)
-    return jnp.sum(jnp.where(ids == lanes, table, 0.0), axis=-1, keepdims=True)
+def lines_of(block):
+    part = block.shape[1] // 4
+    return lambda n: block[n // 4 : n // 4 + 1, n % 4 * part : (n % 4 + 1) * part]
+
+
+def prepare_blocks(idx, ids, triple, out_weight, bias, fc_bias, up, fc_weight, proj_weight):
+    rows, _, part = triple.shape
+    model = 4 * part
+
+    def body(ix, ids_ref, triple_ref, out_ref, bias_ref, fc_ref, up_ref, fcw_ref, proj_ref, block_ref, units_ref, spare):
+        units_ref[0, :, :model] = fcw_ref[...]
+        units_ref[0, :, model:] = proj_ref[...].astype(F32).T.astype(BF16)
+        for s in range(3):
+            block_ref[:rows, s * part : (s + 1) * part] = triple_ref[:, s, :]
+        block_ref[:rows, 3 * part :] = out_ref[...].astype(F32).T.astype(BF16)
+        lane = lax.broadcasted_iota(jnp.int32, (1, LANES), 1)
+        counts = jnp.zeros((1, LANES), F32)
+        ids = ids_ref[...]
+        for g in range(GROUPS):
+            hits = jnp.where(ids == g, 1.0, 0.0)
+            total = jnp.sum(jnp.sum(hits, axis=0, keepdims=True), axis=1, keepdims=True)
+            counts = jnp.where(lane == g, total, counts)
+        high = jnp.floor(counts * (1.0 / DIGIT))
+        spare[...] = jnp.zeros_like(spare)
+        line = lines_of(spare)
+        spare[0:1, :LANES] = high
+        spare[0:1, LANES : 2 * LANES] = counts - DIGIT * high
+
+        def put(n, value):
+            spare[n // 4 : n // 4 + 1, n % 4 * part : (n % 4 + 1) * part] = value.astype(F32)
+
+        for s in range(3):
+            put(1 + s, bias_ref[s : s + 1, :])
+        for s in range(4):
+            put(4 + s, fc_ref[:, s * part : (s + 1) * part])
+        for s in range(8):
+            put(8 + s, up_ref[s // ADAPTER_RANK, s % ADAPTER_RANK : s % ADAPTER_RANK + 1, :])
+        block_ref[rows:, :] = spare[...].astype(BF16)
+
+    arrays = (ids, triple, out_weight, bias, fc_bias, up, fc_weight, proj_weight)
+    whole = lambda v: pl.BlockSpec(v.shape, lambda i, ix: (0,) * v.ndim)
+    units = 2 * fc_weight.shape[1]
+    return call(
+        body,
+        "prepare_blocks",
+        1,
+        [whole(v) for v in arrays],
+        [full(rows + EXTRA, model), pl.BlockSpec((1, rows, units), lambda i, ix: (0, 0, 0))],
+        [shape(rows + EXTRA, model), jax.ShapeDtypeStruct((1, rows, units), BF16)],
+        [pltpu.VMEM((EXTRA, model), F32)],
+        cost(0, 4 * rows * model),
+        60 << 20,
+    )(idx, *arrays)
+
+
+def weigh(idx, ids, fc_bias, near, far, y_near, y_far, x_near, tokens_all):
+    units = fc_bias.shape[1]
+    per_row = LANES
+    own = LEN // 2 // per_row
+    rows = near.shape[1] - EXTRA
+    width = near.shape[2]
+
+    def body(ix, ids_ref, fc_ref, *rest):
+        msgs, (weight_ref, fc_out, held, sems) = rest[:5], rest[5:]
+        load_all(
+            [
+                (msgs[n // 2].at[n % 2, pl.ds(rows, EXTRA), :], held.at[n])
+                for n in range(8)
+            ]
+            + [(msgs[4].at[0, pl.ds(rows, EXTRA), :], held.at[8])],
+            sems,
+        )
+        digits = jnp.zeros((EXTRA, 2 * LANES), F32)
+        for n in range(8):
+            digits = digits + held[n, :, : 2 * LANES].astype(F32)
+        table = tokens_all / (GROUPS * (DIGIT * digits[0:1, :LANES] + digits[0:1, LANES:]))
+        for k in range(own):
+            ids_row = ids_ref[pl.ds((2 * ix[1] + ix[2]) * own + k, 1), :]
+            row = jnp.zeros((1, LANES), F32)
+            for g in range(GROUPS):
+                row = jnp.where(ids_row == g, table[:, g : g + 1], row)
+            weight_ref[k * per_row : (k + 1) * per_row, :] = jnp.broadcast_to(row, (per_row, LANES)).T
+        line = lines_of(held[8].astype(F32))
+        fc_out[0:1, :] = fc_ref[...].astype(F32)
+        fc_out[1:2, :] = jnp.concatenate([line(4 + s) for s in range(4)], axis=1)
+
+    return call(
+        body,
+        "weigh",
+        1,
+        [full(*ids.shape), full(1, units)] + [ANY] * 5,
+        [full(LEN // 2, LANES), full(2, units)],
+        [shape(LEN // 2, LANES, F32), shape(2, units, F32)],
+        [pltpu.VMEM((9, EXTRA, width), BF16), pltpu.SemaphoreType.DMA((9,))],
+        cost(0, LEN * LANES),
+    )(idx, ids, fc_bias, near, far, y_near, y_far, x_near)
 
 
 def norm_rows(idx, tokens, vec, down):
     model = tokens.shape[1]
     blocks = LEN // BLK
 
-    def body(ix, tok, vec_ref, down_ref, normed_ref, latent_ref):
+    def body(ix, tok, vec_ref, down_ref, normed_ref, latent_ref, pad_ref):
+        @pl.when(pl.program_id(0) == 0)
+        def _():
+            pad_ref[...] = jnp.zeros_like(pad_ref)
+            pad_ref[:8, :] = down_ref[...].astype(BF16)
+
         hat, _ = row_stats(tok[...].astype(F32))
         normed = (hat * vec_ref[0:1, :] + vec_ref[1:2, :]).astype(BF16)
         normed_ref[...] = normed
-        latent_ref[...] = lax.dot_general(normed, down_ref[...], NT, preferred_element_type=F32).astype(BF16)
+        latent_ref[...] = lax.dot_general(normed, pad_ref[...], NT, preferred_element_type=F32).astype(BF16)
 
     row = lambda c: pl.BlockSpec((BLK, c), lambda i, ix: (i, 0))
     return call(
         body,
         "norm_rows",
         blocks,
-        [pl.BlockSpec((BLK, model), lambda i, ix: (ix[1] * blocks + i, 0)), full(8, model), full(LANES, model)],
-        [row(model), row(LANES)],
-        [shape(LEN, model), shape(LEN, LANES)],
+        [pl.BlockSpec((BLK, model), lambda i, ix: (ix[1] * blocks + i, 0)), full(8, model), full(8, model)],
+        [row(model), row(LANES), full(LANES, model)],
+        [shape(LEN, model), shape(LEN, LANES), shape(LANES, model)],
         [],
         cost(2 * LEN * model * LANES, 4 * LEN * model),
     )(idx, tokens, vec, down)
 
 
-def project_heads(idx, normed, latent, bias, up, found):
+def project_heads(idx, normed, latent, bias, up, x_near, found):
     model = normed.shape[1]
     arrays, table = operands(found)
-    cols = bias.shape[1]
-    part = cols // 3
+    part = bias.shape[1]
+    cols = 3 * part
     n = len(arrays)
 
-    def body(ix, normed_ref, latent_ref, bias_ref, up_ref, *rest):
+    def body(ix, normed_ref, latent_ref, bias_ref, own_up_ref, near_ref, *rest):
         msgs = rest[:n]
-        q_ref, k_ref, v_ref, w, sems = rest[n:]
+        q_ref, k_ref, v_ref, up_ref, w, spare, lines, sems = rest[n:]
 
         @pl.when(pl.program_id(0) == 0)
         def _():
-            load_all(column_pairs(msgs, table, w, ix, 0, cols, True), sems)
+            pairs = column_pairs(msgs, table, w, ix, 0, cols, True)
+            load_all(pairs + [(near_ref.at[0, pl.ds(model // 8, EXTRA), :], spare)], sems)
+            line = lines_of(spare[...].astype(F32))
+            up_ref[...] = jnp.zeros_like(up_ref)
+            rank = ADAPTER_RANK
+            for a in range(2):
+                for s in range(3):
+                    lines[a : a + 1, s * part : (s + 1) * part] = (
+                        bias_ref[s : s + 1, :].astype(F32) if a == 0 else line(1 + s)
+                    )
+                rows = own_up_ref[...] if a == 0 else jnp.concatenate([line(8 + s) for s in range(8)], axis=0)
+                rows = ADAPTER_SCALE * rows
+                which = lax.broadcasted_iota(jnp.int32, rows.shape, 0) < rank
+                up_ref[a, :8, :part] = jnp.where(which, rows, 0.0).astype(BF16)
+                up_ref[a, :8, 2 * part :] = jnp.where(which, 0.0, rows).astype(BF16)
 
         for a in range(2):
-            r = jnp.dot(normed_ref[...], w[a], preferred_element_type=F32) + bias_ref[a : a + 1, :]
+            r = jnp.dot(normed_ref[...], w[a], preferred_element_type=F32) + lines[a : a + 1, :]
             r = r + jnp.dot(latent_ref[...], up_ref[a], preferred_element_type=F32)
             for out, s in ((q_ref, 0), (k_ref, 1), (v_ref, 2)):
                 out[:, a * part : (a + 1) * part] = r[:, s * part : (s + 1) * part].astype(BF16)
 
     row = lambda c: pl.BlockSpec((BLK, c), lambda i, ix: (i, 0))
+    both = pl.BlockSpec((2, LANES, cols), lambda i, ix: (0, 0, 0))
     return call(
         body,
         "project_heads",
         LEN // BLK,
-        [row(model), row(LANES), full(2, cols), pl.BlockSpec((2, LANES, cols), lambda i, ix: (0, 0, 0))] + [ANY] * n,
-        [row(2 * part)] * 3,
-        [shape(LEN, 2 * part)] * 3,
-        [pltpu.VMEM((2, model, cols), BF16), pltpu.SemaphoreType.DMA((len(table),))],
+        [row(model), row(LANES), full(3, part), full(8, part)] + [ANY] * (1 + n),
+        [row(2 * part)] * 3 + [both],
+        [shape(LEN, 2 * part)] * 3 + [jax.ShapeDtypeStruct((2, LANES, cols), BF16)],
+        [
+            pltpu.VMEM((2, model, cols), BF16),
+            pltpu.VMEM((EXTRA, model), BF16),
+            pltpu.VMEM((8, cols), F32),
+            pltpu.SemaphoreType.DMA((len(table) + 1,)),
+        ],
         cost(4 * LEN * model * cols, 16 * LEN * model),
-    )(idx, normed, latent, bias, up, *arrays)
+    )(idx, normed, latent, bias, up, x_near, *arrays)
 
 
 def attend_fast(queries, key_rows, value_rows):
     length, width = queries.shape
     pairs = width // LANES
 
-    def body(q_ref, k_ref, v_ref, o_ref, lse_ref):
+    def body(q_ref, k_ref, v_ref, o_ref, lse_ref, vx, p_ref):
+        low = lax.broadcasted_iota(jnp.int32, (1, LANES), 1) < HEAD_DIM
+        vx[:, :LANES] = v_ref[...]
+        vx[:, LANES:] = jnp.ones((length, LANES), BF16)
         scale = HEAD_DIM**-0.5 * LOG2E
-        low = lax.broadcasted_iota(jnp.int32, (1, LANES), 1) < HEAD_DIM
-        k = k_ref[...]
-        v = v_ref[...]
-        value_of = [pick(low, v, h) for h in range(2)]
+        causal = (lax.broadcasted_iota(jnp.int32, (2 * BLK, BLK), 0) & (BLK - 1)) >= lax.broadcasted_iota(
+            jnp.int32, (2 * BLK, BLK), 1
+        )
         for i in range(length // BLK):
-            stop = (i + 1) * BLK
-            qb = q_ref[i * BLK : stop, :]
-            causal = (lax.broadcasted_iota(jnp.int32, (BLK, stop), 0) + i * BLK) >= lax.broadcasted_iota(
-                jnp.int32, (BLK, stop), 1
-            )
-            out = jnp.zeros((BLK, LANES), F32)
-            logs = []
-            for h in range(2):
-                s = lax.dot_general(pick(low, qb, h), k[:stop], NT, preferred_element_type=F32) * scale
-                s = jnp.where(causal, s, MASKED)
-                top = jnp.max(s, axis=-1, keepdims=True)
-                p = jnp.exp2(s - top)
-                total = jnp.sum(p, axis=-1, keepdims=True)
-                probs = (p * (1.0 / total)).astype(BF16)
-                out = out + jnp.dot(probs, value_of[h][:stop], preferred_element_type=F32)
-                logs.append(top + jnp.log2(total))
-            o_ref[i * BLK : stop, :] = out.astype(BF16)
-            both = jnp.where(
-                low, jnp.broadcast_to(logs[0], (BLK, LANES)), jnp.broadcast_to(logs[1], (BLK, LANES))
-            ).T
-            lse_ref[0, 0:1, i * BLK : stop] = both[0:1]
-            lse_ref[0, 1:2, i * BLK : stop] = both[HEAD_DIM : HEAD_DIM + 1]
+            start, stop = i * BLK, (i + 1) * BLK
+            qb = (q_ref[start:stop, :].astype(F32) * scale).astype(BF16)
+            s = lax.dot_general(both_heads(low, qb), k_ref[:stop, :], NT, preferred_element_type=F32)
+            sd = jnp.where(causal, s[:, start:], MASKED)
+            top = jnp.max(sd, axis=-1, keepdims=True)
+            if i:
+                top = jnp.maximum(top, jnp.max(s[:, :start], axis=-1, keepdims=True))
+                p_ref[i % 2, :, :start] = jnp.exp2(s[:, :start] - top).astype(BF16)
+            p_ref[i % 2, :, start:stop] = jnp.exp2(sd - top).astype(BF16)
+            out = jnp.dot(p_ref[i % 2, :, :stop], vx[:stop, :], preferred_element_type=F32)
+            total = out[:, LANES:]
+            mixed = out[:, :LANES] / total
+            o_ref[start:stop, :] = jnp.where(low, mixed[:BLK], mixed[BLK:]).astype(BF16)
+            log = top + jnp.log2(total)
+            log = jnp.where(low, log[:BLK], log[BLK:]).T
+            lse_ref[0, 0:1, start:stop] = log[0:1]
+            lse_ref[0, 1:2, start:stop] = log[HEAD_DIM : HEAD_DIM + 1]
 
     spec = pl.BlockSpec((length, LANES), lambda i: (0, i))
     return pl.pallas_call(
@@ -616,6 +720,7 @@
         out_shape=(shape(length, width), jax.ShapeDtypeStruct((pairs, 8, length), F32)),
         in_specs=[spec] * 3,
         out_specs=(spec, pl.BlockSpec((1, 8, length), lambda i: (i, 0, 0))),
+        scratch_shapes=[pltpu.VMEM((length, 2 * LANES), BF16), pltpu.VMEM((2, 2 * BLK, length), BF16)],
         compiler_params=pltpu.CompilerParams(vmem_limit_bytes=VMEM_LIMIT),
         cost_estimate=cost(8 * length * length * width, 8 * length * width, 2 * pairs * length * length),
         name="attend",
@@ -624,6 +729,7 @@
 
 def attention_out_send(idx, attended, found, first):
     width = attended.shape[1]
+    cut = LANES * lax.axis_size("dp") // CUTS
     arrays, table = operands(found)
     n = len(arrays)
     model = LANES * lax.axis_size("dp")
@@ -631,21 +737,23 @@
 
     def body(ix, att, *rest):
         msgs = rest[:n]
-        out, w, sems = rest[n:]
+        outs, (w, sems) = rest[n : n + CUTS], rest[n + CUTS :]
 
         @pl.when(pl.program_id(0) == 0)
         def _():
             load_all(column_pairs(msgs, table, w, ix, first, width // 2, False), sems)
 
-        out[...] = lax.dot_general(att[...], w[...], NT, preferred_element_type=F32).astype(BF16)
+        term = lax.dot_general(att[...], w[...], NT, preferred_element_type=F32).astype(BF16)
+        for k, out in enumerate(outs):
+            out[...] = term[:, k * cut : (k + 1) * cut]
 
     return call(
         body,
         "attention_out_send",
         half_blocks,
         [pl.BlockSpec((BLK, width), lambda i, ix: ((1 - ix[2]) * half_blocks + i, 0))] + [ANY] * n,
-        pl.BlockSpec((BLK, model), lambda i, ix: (i, 0)),
-        shape(LEN // 2, model),
+        [pl.BlockSpec((BLK, cut), lambda i, ix: (i, 0))] * CUTS,
+        [shape(LEN // 2, cut)] * CUTS,
         [pltpu.VMEM((model, width), BF16), pltpu.SemaphoreType.DMA((len(table),))],
         cost(LEN * width * model, 2 * LEN * model),
     )(idx, attended, *arrays)
@@ -658,16 +766,17 @@
     model = tokens.shape[1]
     half_blocks = LEN // BLK // 2
 
-    def body(ix, att, recv, tok, vec_ref, *rest):
-        msgs = rest[:n]
-        hidden_ref, normed_ref, w, sems = rest[n:]
+    def body(ix, att, tok, vec_ref, *rest):
+        recv, msgs = rest[:CUTS], rest[CUTS : CUTS + n]
+        hidden_ref, normed_ref, w, sems = rest[CUTS + n :]
 
         @pl.when(pl.program_id(0) == 0)
         def _():
             load_all(column_pairs(msgs, table, w, ix, first, width // 2, False), sems)
 
         term = lax.dot_general(att[...], w[...], NT, preferred_element_type=F32)
-        hidden = tok[...].astype(F32) + term + recv[...].astype(F32) + vec_ref[2:3, :]
+        other = jnp.concatenate([r[...] for r in recv], axis=1).astype(F32)
+        hidden = tok[...].astype(F32) + term + other + vec_ref[2:3, :]
         hidden_ref[...] = hidden
         hat, _ = row_stats(hidden)
         normed_ref[...] = (hat * vec_ref[3:4, :] + vec_ref[4:5, :]).astype(BF16)
@@ -680,18 +789,18 @@
         [
             pl.BlockSpec((BLK, width), lambda i, ix: (ix[2] * half_blocks + i, 0)),
             row,
-            pl.BlockSpec((BLK, model), lambda i, ix: ((2 * ix[1] + ix[2]) * half_blocks + i, 0)),
             full(8, model),
         ]
+        + [pl.BlockSpec((BLK, model // CUTS), lambda i, ix: (i, 0))] * CUTS
         + [ANY] * n,
         [row, row],
         [shape(LEN // 2, model, F32), shape(LEN // 2, model)],
         [pltpu.VMEM((model, width), BF16), pltpu.SemaphoreType.DMA((len(table),))],
         cost(LEN * width * model, 5 * LEN * model),
-    )(idx, attended, received, tokens, vec, *arrays)
-
-
-def units_main(idx, half_bit, normed, cotangent, ids, weight_table, bias, vec, mine, other, carried, hidden):
+    )(idx, attended, tokens, vec, *received, *arrays)
+
+
+def units_main(idx, half_bit, normed, cotangent, weights, bias, bias_other, vec, mine, other, carried, hidden):
     rows, model = normed.shape
     sources = [operands(f) for f in (mine, other)]
     part = sources[0][0][0].shape[2] // 2
@@ -704,7 +813,7 @@
     c0 = 0.7978845608028654
     c1 = 0.044715
 
-    def body(ix, normed_ref, cot, ids_ref, table_ref, bias_ref, vec_ref, *rest):
+    def body(ix, normed_ref, cot, weight_ref, bias_ref, bias_other_ref, vec_ref, *rest):
         carry = rest[: len(carried)]
         rest = rest[len(carried) :]
         hid_ref, rest = (rest[0], rest[1:]) if last else (None, rest)
@@ -721,8 +830,8 @@
         for group in groups:
             for copy in group:
                 copy.start()
-        weight = token_weights(ids_ref[...], table_ref[...])
-        grad_ref[...] = (cot[...].astype(F32) * weight).astype(BF16)
+        grad_ref[...] = (cot[...].astype(F32) * weight_ref[:, :1]).astype(BF16)
+        biases = (bias_ref, bias_other_ref)
 
         def multiply(o, c, slot):
             x_ref[slot] = jnp.dot(normed_ref[...], w[o, :, at_lanes(c, chunk)], preferred_element_type=F32)
@@ -730,7 +839,7 @@
 
         def bend(o, c, slot):
             at = at_lanes(o * per + c, chunk)
-            x = x_ref[slot] + bias_ref[:, at]
+            x = x_ref[slot] + biases[o][half_bit : half_bit + 1, at_lanes(c, chunk)]
             sq = x * x
             th = jnp.tanh(c0 * x * (1.0 + c1 * sq))
             left = 0.5 * (1.0 + th)
@@ -800,7 +909,7 @@
         def end(r, _):
             at = at_rows(r, step_rows)
             hat, scaler = row_stats(hid_ref[at, :])
-            grad = cot[at, :].astype(F32) * token_weights(ids_ref[at, :], table_ref[...])
+            grad = cot[at, :].astype(F32) * weight_ref[at, :1]
             grad = grad + norm_back(hat, scaler, outs[0][at, :])
             outs[0][at, :] = grad
             outs[1][at, :] = grad.astype(BF16)
@@ -808,16 +917,13 @@
 
         lax.fori_loop(0, rows // step_rows, end, 0)
 
-    def token_rows(i, ix):
-        return (2 * ix[1] + ix[2], 0)
-
     block = full(rows, model)
     specs = [
         block,
-        pl.BlockSpec((rows, model), token_rows),
-        pl.BlockSpec((rows, 1), token_rows),
-        full(1, LANES),
-        pl.BlockSpec((1, 2 * part), lambda i, ix: (0, half_bit)),
+        block,
+        full(rows, LANES),
+        full(2, part),
+        full(2, part),
         full(8, model),
     ]
     specs += [block] * (len(carried) + (1 if last else 0))
@@ -846,19 +952,24 @@
         ]
         + ([pltpu.VMEM((rows, model), BF16)] if last else []),
         cost(16 * rows * part * model, 12 * part * model, 2 * rows * part),
-    )(idx, normed, cotangent, ids, weight_table, bias, vec, *carried, *((hidden,) if last else ()), *arrays)
-
-
-def attend_back_fast(idx, queries, key_rows, value_rows, mixed, grad_own, grad_other, logsum, found, first):
+    )(idx, normed, cotangent, weights, bias, bias_other, vec, *carried, *((hidden,) if last else ()), *arrays)
+
+
+def attend_back_fast(
+    idx, queries, key_rows, value_rows, mixed, grad_own, grad_other, logsum, normed, latent, up, found, first
+):
     length, width = queries.shape
     pairs = width // LANES
     half, model = grad_own.shape
+    per = pairs // 2
     arrays, table = operands(found)
     n = len(arrays)
 
-    def body(ix, q_ref, k_ref, v_ref, o_ref, own_ref, other_ref, lse_ref, *rest):
+    def body(ix, q_ref, k_ref, v_ref, o_ref, own_ref, other_ref, lse_ref, normed_ref, latent_ref, uq_ref, uv_ref, *rest):
         msgs = rest[:n]
-        dq_ref, dk_ref, dv_ref, dq_acc, g_ref, w, sems = rest[n:]
+        dq_ref, dk_ref, dv_ref, low_ref, down_ref, rq_ref, rv_ref, low_acc, dq_acc, g_ref, qs_ref, p_ref, ds_ref, w, sems = rest[
+            n:
+        ]
         pair = pl.program_id(0)
 
         @pl.when(pair == 0)
@@ -870,60 +981,108 @@
             g_ref[at_rows(rank, half), :] = jnp.dot(ref[...], weight, preferred_element_type=F32).astype(BF16)
         scale = HEAD_DIM**-0.5 * LOG2E
         low = lax.broadcasted_iota(jnp.int32, (1, LANES), 1) < HEAD_DIM
-        q = q_ref[...]
-        g = g_ref[...]
-        qm = [pick(low, q, h) for h in range(2)]
-        gm = [pick(low, g, h) for h in range(2)]
-        prod = (g.astype(F32) * o_ref[...].astype(F32)).T
+        qs_ref[...] = (q_ref[...].astype(F32) * scale).astype(BF16)
+        prod = (g_ref[...].astype(F32) * o_ref[...].astype(F32)).T
         delta = [
             jnp.sum(prod[:HEAD_DIM], axis=0, keepdims=True),
             jnp.sum(prod[HEAD_DIM:], axis=0, keepdims=True),
         ]
-        dq_acc[...] = jnp.zeros_like(dq_acc)
-        for j in range(length // BLK):
+        causal = lax.broadcasted_iota(jnp.int32, (BLK, BLK), 1) >= lax.broadcasted_iota(jnp.int32, (BLK, BLK), 0)
+
+        def scores(j):
             start = j * BLK
-            stop = start + BLK
-            span = length - start
-            kb = k_ref[start:stop, :]
-            vb = v_ref[start:stop, :]
-            causal = lax.broadcasted_iota(jnp.int32, (BLK, span), 1) >= lax.broadcasted_iota(
-                jnp.int32, (BLK, span), 0
-            )
-            dk = jnp.zeros((BLK, LANES), F32)
-            dv = jnp.zeros((BLK, LANES), F32)
+            stacked = both_heads(low, k_ref[start : start + BLK, :])
+            s = lax.dot_general(stacked, qs_ref[start:, :], NT, preferred_element_type=F32)
+            values = both_heads(low, v_ref[start : start + BLK, :])
+            dp = lax.dot_general(values, g_ref[start:, :], NT, preferred_element_type=F32)
             for h in range(2):
-                km = pick(low, kb, h)
-                s = lax.dot_general(km, q[start:], NT, preferred_element_type=F32) * scale
-                s = jnp.where(causal, s - lse_ref[0, h : h + 1, start:], MASKED)
-                p = jnp.exp2(s)
-                dp = lax.dot_general(pick(low, vb, h), g[start:], NT, preferred_element_type=F32)
-                ds = (p * (dp - delta[h][:, start:])).astype(BF16)
-                dk = dk + jnp.dot(ds, qm[h][start:], preferred_element_type=F32)
-                dv = dv + jnp.dot(p.astype(BF16), gm[h][start:], preferred_element_type=F32)
-                dq_acc[start:, :] += lax.dot_general(ds, km, TN, preferred_element_type=F32)
-            dk_ref[start:stop, :] = (dk * HEAD_DIM**-0.5).astype(BF16)
-            dv_ref[start:stop, :] = dv.astype(BF16)
+                rows = slice(h * BLK, (h + 1) * BLK)
+                for a, b in ((start, start + BLK), (start + BLK, length)):
+                    if a == b:
+                        continue
+                    sh = s[rows, a - start : b - start] - lse_ref[0, h : h + 1, a:b]
+                    if a == start:
+                        sh = jnp.where(causal, sh, MASKED)
+                    p = jnp.exp2(sh)
+                    p_ref[j % 2, rows, a:b] = p.astype(BF16)
+                    ds = p * (dp[rows, a - start : b - start] - delta[h][:, a:b])
+                    ds_ref[j % 2, rows, a:b] = ds.astype(BF16)
+            return stacked
+
+        def spread(j, stacked):
+            start = j * BLK
+            ds = ds_ref[j % 2, :, start:]
+            dk = jnp.dot(ds, q_ref[start:, :], preferred_element_type=F32)
+            dv = jnp.dot(p_ref[j % 2, :, start:], g_ref[start:, :], preferred_element_type=F32)
+            dk = jnp.where(low, dk[:BLK], dk[BLK:]) * HEAD_DIM**-0.5
+            dk_ref[start : start + BLK, :] = dk.astype(BF16)
+            dv_ref[start : start + BLK, :] = jnp.where(low, dv[:BLK], dv[BLK:]).astype(BF16)
+            dq = lax.dot_general(ds, stacked, TN, preferred_element_type=F32)
+            if j == 0:
+                dq_acc[...] = dq
+            else:
+                dq_acc[start:, :] += dq
+
+        stacked = scores(0)
+        for j in range(1, length // BLK):
+            coming = scores(j)
+            spread(j - 1, stacked)
+            stacked = coming
+        spread(length // BLK - 1, stacked)
         dq_ref[...] = (dq_acc[...] * HEAD_DIM**-0.5).astype(BF16)
+        term = lax.dot_general(dq_ref[...], uq_ref[0], NT, preferred_element_type=F32)
+        term = term + lax.dot_general(dv_ref[...], uv_ref[0], NT, preferred_element_type=F32)
+        latent_t = latent_ref[...]
+        rq_ref[...] = lax.dot_general(latent_t, dq_ref[...], TN, preferred_element_type=F32)[:8]
+        rv_ref[...] = lax.dot_general(latent_t, dv_ref[...], TN, preferred_element_type=F32)[:8]
+
+        @pl.when(pair == 0)
+        def _():
+            low_acc[...] = term
+
+        @pl.when(pair > 0)
+        def _():
+            low_acc[...] += term
+
+        @pl.when(pair == pairs - 1)
+        def _():
+            low_grad = low_acc[...].astype(BF16)
+            low_ref[...] = low_grad
+            down_ref[...] = lax.dot_general(low_grad, normed_ref[...], TN, preferred_element_type=F32)[:8]
 
     spec = pl.BlockSpec((length, LANES), lambda i, ix: (0, i))
     return call(
         body,
         "attend_back",
         pairs,
-        [spec] * 4 + [full(half, model)] * 2 + [pl.BlockSpec((1, 8, length), lambda i, ix: (i, 0, 0))] + [ANY] * n,
-        [spec] * 3,
-        [shape(length, width)] * 3,
+        [spec] * 4
+        + [full(half, model)] * 2
+        + [pl.BlockSpec((1, 8, length), lambda i, ix: (i, 0, 0)), full(length, model), full(length, LANES)]
+        + [
+            pl.BlockSpec((1, LANES, LANES), lambda i, ix: (i // per, 0, lax.rem(i, per))),
+            pl.BlockSpec((1, LANES, LANES), lambda i, ix: (i // per, 0, 2 * per + lax.rem(i, per))),
+        ]
+        + [ANY] * n,
+        [spec] * 3
+        + [full(length, LANES), full(8, model)]
+        + [pl.BlockSpec((8, LANES), lambda i, ix: (0, i))] * 2,
+        [shape(length, width)] * 3
+        + [shape(length, LANES), shape(8, model, F32), shape(8, width, F32), shape(8, width, F32)],
         [
             pltpu.VMEM((length, LANES), F32),
+            pltpu.VMEM((length, LANES), F32),
             pltpu.VMEM((length, LANES), BF16),
+            pltpu.VMEM((length, LANES), BF16),
+            pltpu.VMEM((2, 2 * BLK, length), BF16),
+            pltpu.VMEM((2, 2 * BLK, length), BF16),
             pltpu.VMEM((model, width), BF16),
             pltpu.SemaphoreType.DMA((len(table),)),
         ],
         cost(20 * length * length * width, 16 * length * width, 2 * pairs * length * length),
-    )(idx, queries, key_rows, value_rows, mixed, grad_own, grad_other, logsum, *arrays)
-
-
-def heads_back(idx, dq, dk, dv, normed, latent, up, down, found):
+    )(idx, queries, key_rows, value_rows, mixed, grad_own, grad_other, logsum, normed, latent, up, up, *arrays)
+
+
+def heads_back(idx, dq, dk, dv, latent_low, down, found):
     width = dq.shape[1]
     part = width // 2
     model = down.shape[1]
@@ -932,34 +1091,20 @@
     n = len(arrays)
     half_blocks = LEN // BLK // 2
 
-    def body(ix, dq_ref, dk_ref, dv_ref, normed_ref, latent_ref, up_ref, down_ref, *rest):
+    def body(ix, dq_ref, dk_ref, dv_ref, low_ref, down_ref, *rest):
         msgs = rest[:n]
-        send_ref, own_ref, low_ref, raise_ref, w, sems = rest[n:]
+        send_ref, own_ref, w, sems = rest[n:]
         step = pl.program_id(0)
 
         @pl.when(step == 0)
         def _():
-            copies = copies_of(column_pairs(msgs, table, w, ix, 0, cols, True), sems)
-            for copy in copies:
-                copy.start()
-            low_ref[...] = jnp.zeros_like(low_ref)
-            raise_ref[...] = jnp.zeros_like(raise_ref)
-            for copy in copies:
-                copy.wait()
-
-        latent = latent_ref[...]
-        low = jnp.zeros((BLK, LANES), F32)
-        total = jnp.zeros((BLK, model), F32)
+            load_all(column_pairs(msgs, table, w, ix, 0, cols, True), sems)
+
+        total = jnp.dot(low_ref[...], down_ref[...], preferred_element_type=F32)
         for a in range(2):
             cut = slice(a * part, (a + 1) * part)
             piece = jnp.concatenate([dq_ref[:, cut], dk_ref[:, cut], dv_ref[:, cut]], axis=1)
             total = total + lax.dot_general(piece, w[a], NT, preferred_element_type=F32)
-            low = low + lax.dot_general(piece, up_ref[a], NT, preferred_element_type=F32)
-            term = lax.dot_general(latent, piece, TN, preferred_element_type=F32)
-            raise_ref[:, a * cols : (a + 1) * cols] += term[:8]
-        low = low.astype(BF16)
-        total = total + jnp.dot(low, down_ref[...], preferred_element_type=F32)
-        low_ref[...] += lax.dot_general(low, normed_ref[...], TN, preferred_element_type=F32)[:8]
 
         @pl.when(step < half_blocks)
         def _():
@@ -978,19 +1123,15 @@
         body,
         "heads_back",
         2 * half_blocks,
-        [row(width)] * 3
-        + [row(model), row(LANES), pl.BlockSpec((2, LANES, cols), lambda i, ix: (0, 0, 0)), full(LANES, model)]
-        + [ANY] * n,
+        [row(width)] * 3 + [row(LANES), full(LANES, model)] + [ANY] * n,
         [
             pl.BlockSpec((BLK, model), lambda i, ix: (jnp.minimum(i, half_blocks - 1), 0)),
             pl.BlockSpec((BLK, model), lambda i, ix: (jnp.maximum(i - half_blocks, 0), 0)),
-            full(8, model),
-            full(8, 2 * cols),
         ],
-        [shape(LEN // 2, model), shape(LEN // 2, model, F32), shape(8, model, F32), shape(8, 2 * cols, F32)],
+        [shape(LEN // 2, model), shape(LEN // 2, model, F32)],
         [pltpu.VMEM((2, model, cols), BF16), pltpu.SemaphoreType.DMA((len(table),))],
-        cost(4 * LEN * model * cols, 8 * model * cols),
-    )(idx, dq, dk, dv, normed, latent, up, down, *arrays)
+        cost(4 * LEN * model * cols, 4 * model * cols),
+    )(idx, dq, dk, dv, latent_low, down, *arrays)
 
 
 def tokens_back(idx, in_own, in_recv, tokens, hidden_grad, vec):
@@ -1012,7 +1153,7 @@
         body,
         "tokens_back",
         half_blocks,
-        [row, row, pl.BlockSpec((BLK, model), lambda i, ix: ((2 * ix[1] + ix[2]) * half_blocks + i, 0)), row, full(8, model)],
+        [row, row, row, row, full(8, model)],
         [pl.BlockSpec((BLK, part), lambda i, ix: (i, 0))] * parts,
         [shape(LEN // 2, part)] * parts,
         [pltpu.VMEM((BLK, model), BF16)],
@@ -1020,8 +1161,11 @@
     )(idx, in_own, in_recv, tokens, hidden_grad, vec)
 
 
+def exchange_features(pieces):
+    return [pieces[0], core_swap(pieces[1]), hop(pieces[2], 1, 0), both_swap(pieces[3])]
+
+
 def to_features(idx, pieces, bias):
-    pieces = [pieces[0], core_swap(pieces[1]), hop(pieces[2], 1, 0), both_swap(pieces[3])]
     rows, part = pieces[0].shape
     parts = len(pieces)
 
@@ -1082,80 +1226,83 @@
     r = ADAPTER_RANK
     step_rows, _, head_part = frozen_triple_weight.shape
     heads_cols = 3 * head_part
-    ids = group_ids[:, None]
-    groups = jnp.arange(LANES, dtype=jnp.int32)[None, :]
-    counts = jnp.sum((ids == groups).astype(jnp.int32), axis=0)
-    up_low = up_master.astype(BF16).reshape(2 * r, head_part)
-    fc_rows = fc_bias.reshape(-1, head_part)
-    small = jnp.concatenate([frozen_triple_bias, fc_rows, up_low], axis=0)
-    n_fc, n_small = fc_rows.shape[0], small.shape[0]
-    digits = jnp.concatenate([counts // DIGIT, counts % DIGIT]).astype(BF16).reshape(1, head_part)
-    spare = 4 * EXTRA - 1 - n_small
-    extra = jnp.concatenate([digits, small, jnp.zeros((spare, head_part), BF16)], axis=0).reshape(EXTRA, model)
-    heads_own = jnp.concatenate([frozen_triple_weight.reshape(step_rows, heads_cols), out_weight.T], axis=1)
-    heads_own = jnp.concatenate([heads_own, extra], axis=0)
-    units_own = jnp.concatenate([fc_weight, proj_weight.T], axis=1)
-    down = jnp.zeros((LANES, model), BF16).at[: 2 * r].set(down_master.reshape(2 * r, model).astype(BF16))
+    ids = group_ids.reshape(-1, LANES)
+    fc_line = fc_bias.reshape(1, -1)
+    up_rows = up_master.reshape(2 * r, head_part)
+    heads_own, u_own = prepare_blocks(
+        idx, ids, frozen_triple_weight, out_weight, frozen_triple_bias, fc_line, up_master, fc_weight, proj_weight
+    )
     zero_line = jnp.zeros_like(pre_gain)
     vec = jnp.stack([pre_gain, pre_shift, out_bias, mid_gain, mid_shift, zero_line, zero_line, zero_line]).astype(F32)
-    h_near, h_far, h_z = gather_z(heads_own, ())
+    own_start = (idx[1] * ranks + idx[2]) * (LEN // 2)
+    own_rows = lambda v: lax.dynamic_slice_in_dim(v, own_start, LEN // 2, 0)
+    tok_own, cot_own = own_rows(tokens), own_rows(cotangent)
+    h_z1, h_z2, h_z3 = gather_z(heads_own, ())
+    h_near, h_far = jnp.stack([heads_own, h_z1]), jnp.stack([h_z2, h_z3])
     hx_near, hy_near = pair_xy(h_near)
-    hx_far, hy_far = pair_xy(after(h_far, hx_near, hy_near))
-    hd_near, hd_far = corners(after(hx_near, h_far), hy_far)
-    heads = all_blocks(h_near, hx_near, hy_near, hd_near, h_far, hx_far, hy_far, hd_far)
-    u_near, u_far, u_z = gather_z(units_own, (hx_near, hy_near))
-    theirs_small = hx_near[0, step_rows:].reshape(-1, head_part)[1 : 1 + n_small]
-    small = jnp.stack([small, theirs_small])
-    bias = small[:, :3].reshape(2, 3 * head_part).astype(F32)
-    fc_mine = small[:, 3 : 3 + n_fc].reshape(2, 1, -1)
-    fc_line = jnp.concatenate([fc_mine, core_swap(fc_mine)], axis=1).reshape(1, -1).astype(F32)
-    up_both = small[:, 3 + n_fc :] * jnp.bfloat16(ADAPTER_SCALE)
-    up = jnp.zeros((2, LANES, 3 * head_part), BF16)
-    up = up.at[:, :r, :head_part].set(up_both[:, :r]).at[:, r : 2 * r, 2 * head_part :].set(up_both[:, r:])
-    tallies = jnp.stack([v[c, step_rows] for v in (h_near, h_far, hy_near, hy_far) for c in (0, 1)]).astype(F32)
-    tallies = jnp.sum(tallies[:, :head_part].reshape(-1, 2, LANES), axis=0)
-    weight_table = F32(tok_dev * lax.axis_size("dp")) / (GROUPS * (DIGIT * tallies[:1] + tallies[1:]))
-    normed, latent = norm_rows(idx, tokens, vec, down)
-    near_go = after(u_near, hd_near, hd_far)
-    ux_near, uy_near = pair_xy(near_go)
-    queries, keys, values = project_heads(idx, normed, latent, bias, up, heads)
+    hx_far, hy_far = pair_xy(h_far)
+    ux0, uy0 = pair_xy(after(u_own, hx_far, hy_far))
+    hd_near, hd_far = hop(after(hx_near, h_far), 0, 1), hop(hy_far, 1, 0)
+    heads = []
+    for first, arrays in ((0, (h_near, hx_near, hy_near, hd_near)), (2, (h_far, hx_far, hy_far, hd_far))):
+        for n, array in enumerate(arrays):
+            heads += blocks_of(array, first, n % 2, n // 2)
+    u_rest = jnp.concatenate(gather_z(u_own, (h_far, hx_near, hy_near)))
+    weights, fc_mine = weigh(
+        idx, ids, fc_line, h_near, h_far, hy_near, hy_far, hx_near, float(tok_dev * lax.axis_size("dp"))
+    )
+    fc_other = core_swap(fc_mine)
+    down8 = down_master.reshape(2 * r, model)
+    normed, latent, down = norm_rows(idx, after(tokens, hx_far, tok_own, cot_own), vec, down8)
+    ux, uy = pair_xy(after(u_rest, hd_near, hd_far, ux0, uy0))
+    ready = after(normed, u_rest, ux0, uy0)
+    queries, keys, values, up = project_heads(idx, ready, latent, frozen_triple_bias, up_rows, hx_near, heads)
     mixed, logsum = attend_fast(queries, keys, values)
-    far_go = after(u_far, queries)
-    ux_far, uy_far = pair_xy(far_go)
-    sent = core_swap(attention_out_send(idx, mixed, heads, heads_cols))
-    hidden, normed_mid = attention_out_own(idx, mixed, sent, tokens, vec, heads, heads_cols)
-    straight = all_blocks(u_near, ux_near, uy_near, None, u_far, ux_far, uy_far, None)
-    first_mine = [e for e in straight if e[2] == 0]
-    first_other = swapped_blocks(first_mine)
-    rows = (normed_mid, cotangent, ids, weight_table, fc_line, vec)
-    ux_near, uy_near, uy_far, _, _ = lax.optimization_barrier((ux_near, uy_near, uy_far, ux_far, normed_mid))
-    ud_near, ud_far = corners(ux_near, uy_far)
+    sent = [core_swap(v) for v in attention_out_send(idx, mixed, heads, heads_cols)]
+    hidden, normed_mid = attention_out_own(idx, mixed, sent, tok_own, vec, heads, heads_cols)
+    rows = (normed_mid, cot_own, weights, fc_mine, fc_other, vec)
+    ux0, ux, uy, _ = lax.optimization_barrier((ux0, ux, uy, normed_mid))
+    ud0, ud1, ud2 = hop(ux0, 0, 1), hop(ux[:1], 0, 1), hop(uy[1:], 1, 0)
+
+    def table(half_bit, bit, *arrays):
+        found, start = [], 0
+        for array in arrays:
+            found += blocks_of(array, start, half_bit, bit)
+            start += array.shape[0]
+        return found
+
+    swap = lambda *arrays: [core_swap(v) for v in arrays]
+    first_mine = table(0, 0, u_own, u_rest) + table(0, 1, uy0, uy)
+    first_other = table(0, 0, *swap(u_own, u_rest)) + table(0, 1, *swap(uy0, uy))
     carried = units_main(idx, 0, *rows, first_mine, first_other, (), None)
-    ud_near, ud_far, _ = lax.optimization_barrier((ud_near, ud_far, carried[0]))
-    units = all_blocks(u_near, ux_near, uy_near, ud_near, u_far, ux_far, uy_far, ud_far)
-    last_mine = [e for e in units if e[2] == 1]
-    last_other = swapped_blocks(last_mine)
+    ud0, ud1, ud2, _ = lax.optimization_barrier((ud0, ud1, ud2, carried[0]))
+    last_mine = table(1, 0, ux0, ux) + table(1, 1, ud0, ud1, ud2)
+    last_other = table(1, 0, *swap(ux0, ux)) + table(1, 1, *swap(ud0, ud1, ud2))
     hidden_grad, hidden_low, *out_pieces = units_main(idx, 1, *rows, last_mine, last_other, carried, hidden)
     hidden_other = core_swap(hidden_low)
-    dq, dk, dv = attend_back_fast(
-        idx, queries, keys, values, mixed, hidden_low, hidden_other, logsum, heads, heads_cols
+    out_pieces = exchange_features(out_pieces)
+    dq, dk, dv, latent_low, down_term, up_q, up_v = attend_back_fast(
+        idx, queries, keys, values, mixed, hidden_low, hidden_other, logsum, normed, latent, up, heads, heads_cols
     )
-    in_send, in_own, down_term, up_term = heads_back(idx, dq, dk, dv, normed, latent, up, down, heads)
+    up_term = jnp.stack([up_q[:r], up_v[r:]]).reshape(2 * r, 2, head_part)
+    terms = jnp.concatenate([down_term, up_term[:, 1], up_term[:, 0]], axis=1)
+    terms = terms + hop(terms, 0, 1)
+    dq, out_pieces = lax.optimization_barrier((dq, out_pieces))
+    in_send, in_own = heads_back(idx, dq, dk, dv, latent_low, down, heads)
     in_recv = core_swap(in_send)
+    terms = after(terms, in_own)
+    terms = terms + hop(terms, 0, 2)
+    in_pieces = tokens_back(idx, in_own, in_recv, tok_own, hidden_grad, vec)
+    terms = after(terms, in_recv)
+    terms = terms + hop(terms, 0, 4)
+    terms, out_pieces = lax.optimization_barrier((terms, out_pieces, in_pieces[2]))[:2]
     output = to_features(idx, out_pieces, proj_bias.astype(F32).reshape(1, -1))
-    input_grad = to_features(idx, tokens_back(idx, in_own, in_recv, tokens, hidden_grad, vec), None)
-    up_term = up_term.reshape(2 * r, 2, 3, head_part)
-    mine = jnp.concatenate([up_term[:r, 0, 0], up_term[r:, 0, 2]], axis=0)
-    theirs = jnp.concatenate([up_term[:r, 1, 0], up_term[r:, 1, 2]], axis=0)
-    down_sum = down_term + core_swap(down_term)
-    got = hop(jnp.concatenate([down_sum, theirs], axis=1), 1, 0)
-    both = jnp.concatenate([down_sum, mine], axis=1) + got
-    bits = 1
-    while bits < lax.axis_size("dp"):
-        both = both + hop(both, 0, bits)
-        bits *= 2
-    down_grad = both[:, :model].reshape(down_master.shape)
-    up_grad = ADAPTER_SCALE * both[:, model:].reshape(up_master.shape)
+    input_grad = to_features(idx, exchange_features(in_pieces), None)
+    width = model + head_part
+    got = hop(terms[:, :width], 1, 0)
+    down_sum = terms[:, :model] + got[:, :model]
+    down_grad = (down_sum + core_swap(down_sum)).reshape(down_master.shape)
+    up_grad = ADAPTER_SCALE * (terms[:, width:] + got[:, model:]).reshape(up_master.shape)
     step_value = jnp.float32(STEP)
     down_new, down_moment, down_square = adam_update(
         down_master, down_first, down_second, down_grad, step_value, learn_rate

time: 258 us -> 249 us (0.965)
  starting transfers between devices: 38.6 us -> 48.9 us
  local copies, waits for them, and re-layouts: 27.7 us -> 19.9 us
  Pallas kernels: 102 us -> 96.9 us
  other arithmetic: 9.13 us -> 4.53 us
    ppermute x20 -> x21, starting transfers between devices: 25.1 us -> 36.2 us  [hop(): return lax.ppermute(value, AXES, [(i, i ^ flip) for i in range(total)])]
    unnamed x122 -> x93, local copies, waits for them, and re-layouts: 20.8 us -> 13.2 us
    another operation x12 -> x5, other arithmetic: 5.84 us -> 1.13 us  [the longest x4 1.13 us: on_device_fast(): h_near, h_far = (jnp.stack([heads_own, h_z1]), jnp.stack([h_z2, h_z3]))]
    ppermute x8, waiting for transfers between devices: 13.2 us -> 17 us  [z_hop(): return lax.ppermute(value, AXES, perm)]
    another operation x8 -> x1, local copies, waits for them, and re-layouts: 3.73 us -> 0.01 us  [on_device_fast(): up_term = jnp.stack([up_q[:r], up_v[r:]]).reshape(2 * r, 2, head_part)]
    ppermute x2, waiting for transfers between devices: 5.16 us -> 2.15 us  [both_swap(): return lax.ppermute(value, AXES, [(i, i ^ 3) for i in range(total)])]
    dynamic_slice x0 -> x2, local copies, waits for them, and re-layouts: none -> 2.86 us  [on_device_fast(): own_rows = lambda v: lax.dynamic_slice_in_dim(v, own_start, LEN // 2, 0)]
    ppermute x20 -> x21, waiting for transfers between devices: 51.1 us -> 48.9 us  [hop(): return lax.ppermute(value, AXES, [(i, i ^ flip) for i in range(total)])]
  transfers between devices with their start and end apart: 45 -> 47, of which waited for: 19 -> 21; matrix products, arithmetic and copies ran while one was open for 5% -> 4% of each run, Pallas kernels for 19% -> 27%
where the time goes in v4:
time: 249 us; the launch traced here: 247 us
  Pallas kernels  96.9 us (39%)
  waiting for transfers between devices  74.9 us (30%)
  starting transfers between devices  48.9 us (20%)
  local copies, waits for them, and re-layouts  19.9 us (8%)
  other arithmetic  4.53 us (2%)
    ppermute x21, waiting for transfers between devices, hop(): return lax.ppermute(value, AXES, [(i, i ^ flip) for i in range(total)])  48.9 us
    ppermute x21, starting transfers between devices, hop(): return lax.ppermute(value, AXES, [(i, i ^ flip) for i in range(total)])  36.2 us
    pallas_call x2, Pallas kernels, units_main(): call(body, 'units_main_last' if last else 'units_main_first', 1, specs +...  33.8 us
    pallas_call x1, Pallas kernels, attend_back_fast(): call(body, 'attend_back', pairs, [spec] * 4 + [full(half, model)] * 2 + [...  21.8 us
    ppermute x8, waiting for transfers between devices, z_hop(): return lax.ppermute(value, AXES, perm)  17 us
    unnamed x93, local copies, waits for them, and re-layouts  13.2 us
    pallas_call x1, Pallas kernels, attend_fast(): pl.pallas_call(body, grid=(pairs,), out_shape=(shape(length, width), jax....  11 us
    ppermute x8, starting transfers between devices, z_hop(): return lax.ppermute(value, AXES, perm)  7.86 us
  transfers between devices with their start and end apart: 47, of which 21 were waited for; matrix products, arithmetic and copies ran while one was open for 4% of the time, Pallas kernels for 27%

profile of v4, /device:TPU:0, one launch (start us, length us, event | category | flops | bytes accessed | tf_op | source)
XLA Modules:
  0.0 247.4 jit_solution(10391298720010982476)
XLA Ops:
  4.3 3.3 %prepare_blocks.1 = (bf16[136,1024]{1,0:T(8,128)(2,1)}, bf16[1,128,2048]{2,1,0:T(8,128)(2,1)}) custom-call(s32[3]{0:T(128)} %pad_add_fusion.ix, s32[16,128]{1,0:T(8,128)} %bitcast.21, bf16[128,3,256]{2,1,0:T(4,128)(2,1)} %copy.32.triple_ref, bf16[256,128]{1,0:T(8,128)(2,1)} %out_ref.1, bf16[3,256]{1,0:T(4,128)(2,1)} %bias_ref.3, ...), custom_call_target="tpu_custom_call" | custom-call | bytes 52428 | tf_op jit(solution)/shard_map/prepare_blocks/pallas_call | solution.py:547
  7.6 3.0 %collective-permute-start = (bf16[136,1024]{1,0:T(8,128)(2,1)}, bf16[136,1024]{1,0:T(8,128)(2,1)S(1)}, u32[]{:S(2)}, u32[]{:S(2)}) collective-permute-start(bf16[136,1024]{1,0:T(8,128)(2,1)} %get-tuple-element.70), channel_id=1, source_target_pairs={{0,8},{1,9},{2,10},{3,11},{4,12},{5,13},{6,14},{7,15},{8,0},{9,1},... | collective-permute-start | bytes 835592 | tf_op jit(solution)/shard_map/ppermute | solution.py:384
  11.3 6.2 %collective-permute-done = bf16[136,1024]{1,0:T(8,128)(2,1)S(1)} collective-permute-done((bf16[136,1024]{1,0:T(8,128)(2,1)}, bf16[136,1024]{1,0:T(8,128)(2,1)S(1)}, u32[]{:S(2)}, u32[]{:S(2)}) %collective-permute-start) | collective-permute-done | bytes 278560 | tf_op jit(solution)/shard_map/ppermute | solution.py:384
  25.1 5.1 %collective-permute-done.3 = bf16[136,1024]{1,0:T(8,128)(2,1)S(1)} collective-permute-done((bf16[136,1024]{1,0:T(8,128)(2,1)S(1)}, bf16[136,1024]{1,0:T(8,128)(2,1)S(1)}, u32[]{:S(2)}, u32[]{:S(2)}) %collective-permute-start.3) | collective-permute-done | bytes 278560 | tf_op jit(solution)/shard_map/ppermute | solution.py:407
  30.2 5.3 %collective-permute-done.4 = bf16[136,1024]{1,0:T(8,128)(2,1)S(1)} collective-permute-done((bf16[136,1024]{1,0:T(8,128)(2,1)S(1)}, bf16[136,1024]{1,0:T(8,128)(2,1)S(1)}, u32[]{:S(2)}, u32[]{:S(2)}) %collective-permute-start.4) | collective-permute-done | bytes 278560 | tf_op jit(solution)/shard_map/ppermute | solution.py:407
  36.8 8.1 %collective-permute-start.8 = (bf16[1,128,2048]{2,1,0:T(8,128)(2,1)S(1)}, bf16[1,128,2048]{2,1,0:T(8,128)(2,1)S(1)}, u32[]{:S(2)}, u32[]{:S(2)}) collective-permute-start(bf16[1,128,2048]{2,1,0:T(8,128)(2,1)S(1)} %copy-done.17), channel_id=1, source_target_pairs={{0,8},{1,9},{2,10},{3,11},{4,12},{5,13},{6,14},{7,15},{8,0},{9,1},... | collective-permute-start | bytes 1572872 | tf_op jit(solution)/shard_map/ppermute | solution.py:384
  45.5 8.2 %collective-permute-done.8 = bf16[1,128,2048]{2,1,0:T(8,128)(2,1)S(1)} collective-permute-done((bf16[1,128,2048]{2,1,0:T(8,128)(2,1)S(1)}, bf16[1,128,2048]{2,1,0:T(8,128)(2,1)S(1)}, u32[]{:S(2)}, u32[]{:S(2)}) %collective-permute-start.8) | collective-permute-done | bytes 524320 | tf_op jit(solution)/shard_map/ppermute | solution.py:384
  59.8 10.3 %collective-permute-done.13.rest_6_.rest_7_.rest_3_ = bf16[2,136,1024]{2,1,0:T(8,128)(2,1)S(1)} collective-permute-done((bf16[2,136,1024]{2,1,0:T(8,128)(2,1)S(1)}, bf16[2,136,1024]{2,1,0:T(8,128)(2,1)S(1)}, u32[]{:S(2)}, u32[]{:S(2)}) %collective-permute-start.13) | collective-permute-done | bytes 557088 | tf_op jit(solution)/shard_map/ppermute | solution.py:384
  74.2 6.6 %collective-permute-done.12 = bf16[1,128,2048]{2,1,0:T(8,128)(2,1)S(1)} collective-permute-done((bf16[1,128,2048]{2,1,0:T(8,128)(2,1)S(1)}, bf16[1,128,2048]{2,1,0:T(8,128)(2,1)S(1)}, u32[]{:S(2)}, u32[]{:S(2)}) %collective-permute-start.12) | collective-permute-done | bytes 524320 | tf_op jit(solution)/shard_map/ppermute | solution.py:407
  83.7 5.4 %collective-permute-done.15.rest_2_ = bf16[1,128,2048]{2,1,0:T(8,128)(2,1)S(1)} collective-permute-done((bf16[1,128,2048]{2,1,0:T(8,128)(2,1)S(1)}, bf16[1,128,2048]{2,1,0:T(8,128)(2,1)S(1)}, u32[]{:S(2)}, u32[]{:S(2)}) %collective-permute-start.15) | collective-permute-done | bytes 524320 | tf_op jit(solution)/shard_map/ppermute | solution.py:384
  89.1 2.8 %collective-permute-done.17.rest_7_.rest_8_ = bf16[2,136,1024]{2,1,0:T(8,128)(2,1)S(1)} collective-permute-done((bf16[2,136,1024]{2,1,0:T(8,128)(2,1)S(1)}, bf16[2,136,1024]{2,1,0:T(8,128)(2,1)S(1)}, u32[]{:S(2)}, u32[]{:S(2)}) %collective-permute-start.17) | collective-permute-done | bytes 557088 | tf_op jit(solution)/shard_map/ppermute | solution.py:384
  96.5 3.1 %norm_rows.1 = (bf16[1024,1024]{1,0:T(8,128)(2,1)S(1)}, bf16[1024,128]{1,0:T(8,128)(2,1)S(1)}, bf16[128,1024]{1,0:T(8,128)(2,1)S(1)}) custom-call(s32[3]{0:T(128)S(1)} %copy-done.29, bf16[2048,1024]{1,0:T(8,128)(2,1)S(1)} %copy-done.6, f32[8,1024]{1,0:T(8,128)S(1)} %convert_element_type.10.vec_ref, f32[8,1024]{1,0:T(8,128)S(1)} %reshape.52.down_ref), custom_call_target="tpu_custom_call" | custom-call | flops 26843544 | bytes 419430 | tf_op jit(solution)/shard_map/norm_rows/pallas_call | solution.py:619
  99.7 6.1 %project_heads.1 = (bf16[1024,512]{1,0:T(8,128)(2,1)S(1)}, bf16[1024,512]{1,0:T(8,128)(2,1)S(1)}, bf16[1024,512]{1,0:T(8,128)(2,1)S(1)}, bf16[2,128,768]{2,1,0:T(8,128)(2,1)S(1)}) custom-call(s32[3]{0:T(128)S(1)} %copy-done.29, bf16[1024,1024]{1,0:T(8,128)(2,1)S(1)} %get-tuple-element.76.normed_ref, bf16[1024,128]{1,0:T(8,128)(2,1)S(1)} %get-tuple-element.77.latent_ref, ...), custom_call_target="tpu_custom_call" | custom-call | flops 322122560 | bytes 1677721 | tf_op jit(solution)/shard_map/project_heads/pallas_call | solution.py:668
  105.8 11.0 %attend.1 = (bf16[1024,512]{1,0:T(8,128)(2,1)S(1)}, f32[4,8,1024]{2,1,0:T(8,128)S(1)}) custom-call(bf16[1024,512]{1,0:T(8,128)(2,1)S(1)} %get-tuple-element.79.q_ref, bf16[1024,512]{1,0:T(8,128)(2,1)S(1)} %get-tuple-element.80.k_ref, bf16[1024,512]{1,0:T(8,128)(2,1)S(1)} %get-tuple-element.81.v_ref), custom_call_target="tpu_custom_call" | custom-call | flops 429496736 | bytes 419430 | tf_op jit(solution)/shard_map/attend/pallas_call | solution.py:717
  119.3 2.9 %collective-permute-done.18.rest_0_ = bf16[512,1024]{1,0:T(8,128)(2,1)S(1)} collective-permute-done((bf16[512,1024]{1,0:T(8,128)(2,1)S(1)}, bf16[512,1024]{1,0:T(8,128)(2,1)S(1)}, u32[]{:S(2)}, u32[]{:S(2)}) %collective-permute-start.18) | collective-permute-done | bytes 1048608 | tf_op jit(solution)/shard_map/ppermute | solution.py:389
  122.1 2.5 %attention_out_own.1 = (f32[512,1024]{1,0:T(8,128)S(1)}, bf16[512,1024]{1,0:T(8,128)(2,1)S(1)}) custom-call(s32[3]{0:T(128)S(1)} %copy-done.29, bf16[1024,512]{1,0:T(8,128)(2,1)S(1)} %get-tuple-element.82.att.o_ref, bf16[512,1024]{1,0:T(8,128)(2,1)S(1)} %constant_dynamic-slice_fusion.1.tok, f32[8,1024]{1,0:T(8,128)S(1)} %convert_element_type.10.vec_ref, ...), custom_call_target="tpu_custom_call" | custom-call | flops 53687092 | bytes 524288 | tf_op jit(solution)/shard_map/attention_out_own/pallas_call | solution.py:785
  133.0 16.3 %units_main_first.1 = (f32[512,1024]{1,0:T(8,128)S(1)}, f32[512,1024]{1,0:T(8,128)S(1)}) custom-call(s32[3]{0:T(128)S(1)} %copy-done.29, bf16[512,1024]{1,0:T(8,128)(2,1)S(1)} %get-tuple-element.83.normed_ref, bf16[512,1024]{1,0:T(8,128)(2,1)S(1)} %constant_dynamic-slice_fusion.cot, f32[512,128]{1,0:T(8,128)S(1)} %get-tuple-element.84.weight_ref, ...), custom_call_target="tpu_custom_call" | custom-call | flops 858993472 | bytes 1258291 | tf_op jit(solution)/shard_map/units_main_first/pallas_call | solution.py:937
  149.3 7.1 %collective-permute-done.26.rest_5_ = bf16[1,128,2048]{2,1,0:T(8,128)(2,1)S(1)} collective-permute-done((bf16[1,128,2048]{2,1,0:T(8,128)(2,1)S(1)}, bf16[1,128,2048]{2,1,0:T(8,128)(2,1)S(1)}, u32[]{:S(2)}, u32[]{:S(2)}) %collective-permute-start.26) | collective-permute-done | bytes 524320 | tf_op jit(solution)/shard_map/ppermute | solution.py:384
  162.8 17.4 %units_main_last.1 = (f32[512,1024]{1,0:T(8,128)S(1)}, bf16[512,1024]{1,0:T(8,128)(2,1)S(1)}, bf16[512,256]{1,0:T(8,128)(2,1)S(1)}, bf16[512,256]{1,0:T(8,128)(2...) custom-call(s32[3]{0:T(128)S(1)} %copy-done.29, bf16[512,1024]{1,0:T(8,128)(2,1)S(1)} %get-tuple-element.83.normed_ref, ...), custom_call_target="tpu_custom_call" | custom-call | flops 858993472 | bytes 1258291 | tf_op jit(solution)/shard_map/units_main_last/pallas_call | solution.py:937
  184.2 21.8 %attend_back.1 = (bf16[1024,512]{1,0:T(8,128)(2,1)S(1)}, bf16[1024,512]{1,0:T(8,128)(2,1)S(1)}, bf16[1024,512]{1,0:T(8,128)(2,1)S(1)}, bf16[1024,128]{1,0:T(8,12...) custom-call(s32[3]{0:T(128)S(1)} %copy-done.29, ...), custom_call_target="tpu_custom_call" | custom-call | flops 1073741824 | bytes 838860 | tf_op jit(solution)/shard_map/attend_back/pallas_call | solution.py:1054
  206.0 7.0 %heads_back.1 = (bf16[512,1024]{1,0:T(8,128)(2,1)}, f32[512,1024]{1,0:T(8,128)S(1)}) custom-call(s32[3]{0:T(128)S(1)} %copy-done.29, bf16[1024,512]{1,0:T(8,128)(2,1)S(1)} %get-tuple-element.107.dq_ref, bf16[1024,512]{1,0:T(8,128)(2,1)S(1)} %get-tuple-element.108.dk_ref, bf16[1024,512]{1,0:T(8,128)(2,1)S(1)} %get-tuple-element.109.dv_ref, ...), custom_call_target="tpu_custom_call" | custom-call | flops 322122560 | bytes 314572 | tf_op jit(solution)/shard_map/heads_back/pallas_call | solution.py:1122
  218.8 2.8 %collective-permute-start.39 = (f32[8,1536]{1,0:T(8,128)S(1)}, f32[8,1536]{1,0:T(8,128)S(1)}, u32[]{:S(2)}, u32[]{:S(2)}) collective-permute-start(f32[8,1536]{1,0:T(8,128)S(1)} %fusion.1), channel_id=1, source_target_pairs={{0,8},{1,9},{2,10},{3,11},{4,12},{5,13},{6,14},{7,15},{8,0},{9,1},... | collective-permute-start | bytes 147464 | tf_op jit(solution)/shard_map/ppermute | solution.py:384
  223.7 3.1 %collective-permute-start.41 = (f32[8,1536]{1,0:T(8,128)S(1)}, f32[8,1536]{1,0:T(8,128)S(1)}, u32[]{:S(2)}, u32[]{:S(2)}) collective-permute-start(f32[8,1536]{1,0:T(8,128)S(1)} %add.65), channel_id=1, source_target_pairs={{0,16},{1,17},{2,18},{3,19},{4,20},{5,21},{6,22},{7,23},{8,24},{9,... | collective-permute-start | bytes 147464 | tf_op jit(solution)/shard_map/ppermute | solution.py:384
  241.0 2.7 %collective-permute-done.43.rest_2_ = bf16[512,256]{1,0:T(8,128)(2,1)S(1)} collective-permute-done((bf16[512,256]{1,0:T(8,128)(2,1)S(1)}, bf16[512,256]{1,0:T(8,128)(2,1)S(1)}, u32[]{:S(2)}, u32[]{:S(2)}) %collective-permute-start.43) | collective-permute-done | bytes 262176 | tf_op jit(solution)/shard_map/ppermute | solution.py:384
  (220 shorter events, 77.1 us)
Async XLA Ops:
  18.2 12.0 %collective-permute-start.3 = (bf16[136,1024]{1,0:T(8,128)(2,1)S(1)}, bf16[136,1024]{1,0:T(8,128)(2,1)S(1)}, u32[]{:S(2)}, u32[]{:S(2)}) collective-permute-start(bf16[136,1024]{1,0:T(8,128)(2,1)S(1)} %collective-permute-done.2), channel_id=1, source_target_pairs={{8,0},{9,1},{10,2},{11,3},{12,4},{13,5},{14,6},{15,7},{16,24},{17,... | collective-permute-start | bytes 835592 | tf_op jit(solution)/shard_map/ppermute | solution.py:407
  19.5 16.0 %collective-permute-start.4 = (bf16[136,1024]{1,0:T(8,128)(2,1)S(1)}, bf16[136,1024]{1,0:T(8,128)(2,1)S(1)}, u32[]{:S(2)}, u32[]{:S(2)}) collective-permute-start(bf16[136,1024]{1,0:T(8,128)(2,1)S(1)} %collective-permute-done.1), channel_id=1, source_target_pairs={{8,0},{9,1},{10,2},{11,3},{12,4},{13,5},{14,6},{15,7},{16,24},{17,... | collective-permute-start | bytes 835592 | tf_op jit(solution)/shard_map/ppermute | solution.py:407
  21.8 13.9 %collective-permute-start.6 = (bf16[2,136,1024]{2,1,0:T(8,128)(2,1)S(1)}, bf16[2,136,1024]{2,1,0:T(8,128)(2,1)S(1)}, u32[]{:S(2)}, u32[]{:S(2)}) collective-permute-start(bf16[2,136,1024]{2,1,0:T(8,128)(2,1)S(1)} %pad_maximum_fusion.2.rest_0_.rest_1_), channel_id=1, source_target_pairs={{0,2},{1,3},{2,0},{3,1},{4,6},{5,7},{6,4},{7,5},{8,10},{9,11},{10,... | collective-permute-start | bytes 1671176 | tf_op jit(solution)/shard_map/ppermute | solution.py:384
  23.6 13.2 %collective-permute-start.7 = (bf16[2,136,1024]{2,1,0:T(8,128)(2,1)S(1)}, bf16[2,136,1024]{2,1,0:T(8,128)(2,1)S(1)}, u32[]{:S(2)}, u32[]{:S(2)}) collective-permute-start(bf16[2,136,1024]{2,1,0:T(8,128)(2,1)S(1)} %pad_maximum_fusion.2.rest_0_.rest_1_), channel_id=1, source_target_pairs={{0,4},{1,5},{2,6},{3,7},{4,0},{5,1},{6,2},{7,3},{8,12},{9,13},{10,... | collective-permute-start | bytes 1671176 | tf_op jit(solution)/shard_map/ppermute | solution.py:384
  36.8 17.0 %collective-permute-start.8 = (bf16[1,128,2048]{2,1,0:T(8,128)(2,1)S(1)}, bf16[1,128,2048]{2,1,0:T(8,128)(2,1)S(1)}, u32[]{:S(2)}, u32[]{:S(2)}) collective-permute-start(bf16[1,128,2048]{2,1,0:T(8,128)(2,1)S(1)} %copy-done.17), channel_id=1, source_target_pairs={{0,8},{1,9},{2,10},{3,11},{4,12},{5,13},{6,14},{7,15},{8,0},{9,1},... | collective-permute-start | bytes 1572872 | tf_op jit(solution)/shard_map/ppermute | solution.py:384
  44.8 11.8 %collective-permute-start.10 = (bf16[1,128,2048]{2,1,0:T(8,128)(2,1)S(1)}, bf16[1,128,2048]{2,1,0:T(8,128)(2,1)S(1)}, u32[]{:S(2)}, u32[]{:S(2)}) collective-permute-start(bf16[1,128,2048]{2,1,0:T(8,128)(2,1)S(1)} %copy-done.17), channel_id=1, source_target_pairs={{8,16},{9,17},{10,18},{11,19},{12,20},{13,21},{14,22},{15,23},{16,... | collective-permute-start | bytes 1572872 | tf_op jit(solution)/shard_map/ppermute | solution.py:407
  54.4 15.6 %collective-permute-start.13 = (bf16[2,136,1024]{2,1,0:T(8,128)(2,1)S(1)}, bf16[2,136,1024]{2,1,0:T(8,128)(2,1)S(1)}, u32[]{:S(2)}, u32[]{:S(2)}) collective-permute-start(bf16[2,136,1024]{2,1,0:T(8,128)(2,1)S(1)} %pad_maximum_fusion.1.rest_4_.rest_5_.rest_1_), channel_id=1, source_target_pairs={{0,4},{1,5},{2,6},{3,7},{4,0},{5,1},{6,2},{7,3},{8,12},{9,13},{10,... | collective-permute-start | bytes 1671176 | tf_op jit(solution)/shard_map/ppermute | solution.py:384
  56.0 14.0 %collective-permute-start.5 = (bf16[2,136,1024]{2,1,0:T(8,128)(2,1)S(1)}, bf16[2,136,1024]{2,1,0:T(8,128)(2,1)S(1)}, u32[]{:S(2)}, u32[]{:S(2)}) collective-permute-start(bf16[2,136,1024]{2,1,0:T(8,128)(2,1)S(1)} %pad_maximum_fusion.1.rest_4_.rest_5_.rest_1_), channel_id=1, source_target_pairs={{0,2},{1,3},{2,0},{3,1},{4,6},{5,7},{6,4},{7,5},{8,10},{9,11},{10,... | collective-permute-start | bytes 1671176 | tf_op jit(solution)/shard_map/ppermute | solution.py:384
  56.6 15.6 %collective-permute-start.11 = (bf16[1,128,2048]{2,1,0:T(8,128)(2,1)S(1)}, bf16[1,128,2048]{2,1,0:T(8,128)(2,1)S(1)}, u32[]{:S(2)}, u32[]{:S(2)}) collective-permute-start(bf16[1,128,2048]{2,1,0:T(8,128)(2,1)S(1)} %collective-permute-done.10), channel_id=1, source_target_pairs={{8,0},{9,1},{10,2},{11,3},{12,4},{13,5},{14,6},{15,7},{16,24},{17,... | collective-permute-start | bytes 1572872 | tf_op jit(solution)/shard_map/ppermute | solution.py:407
  57.9 22.9 %collective-permute-start.12 = (bf16[1,128,2048]{2,1,0:T(8,128)(2,1)S(1)}, bf16[1,128,2048]{2,1,0:T(8,128)(2,1)S(1)}, u32[]{:S(2)}, u32[]{:S(2)}) collective-permute-start(bf16[1,128,2048]{2,1,0:T(8,128)(2,1)S(1)} %collective-permute-done.9), channel_id=1, source_target_pairs={{8,0},{9,1},{10,2},{11,3},{12,4},{13,5},{14,6},{15,7},{16,24},{17,... | collective-permute-start | bytes 1572872 | tf_op jit(solution)/shard_map/ppermute | solution.py:407
  59.2 23.1 %collective-permute-start.16 = (bf16[2,136,1024]{2,1,0:T(8,128)(2,1)S(1)}, bf16[2,136,1024]{2,1,0:T(8,128)(2,1)S(1)}, u32[]{:S(2)}, u32[]{:S(2)}) collective-permute-start(bf16[2,136,1024]{2,1,0:T(8,128)(2,1)S(1)} %collective-permute-done.6.near_ref.rest_1_.rest_2_.rest_4_), channel_id=1, source_target_pairs={{0,4},{1,5},{2,6},{3,7},{4,0},{5,1},{6,2},{7,3},{8,12},{9,13},{10,... | collective-permute-start | bytes 1671176 | tf_op jit(solution)/shard_map/ppermute | solution.py:384
  70.1 13.6 %collective-permute-start.14 = (bf16[1,128,2048]{2,1,0:T(8,128)(2,1)S(1)}, bf16[1,128,2048]{2,1,0:T(8,128)(2,1)S(1)}, u32[]{:S(2)}, u32[]{:S(2)}) collective-permute-start(bf16[1,128,2048]{2,1,0:T(8,128)(2,1)S(1)} %copy-done.17), channel_id=1, source_target_pairs={{0,2},{1,3},{2,0},{3,1},{4,6},{5,7},{6,4},{7,5},{8,10},{9,11},{10,... | collective-permute-start | bytes 1572872 | tf_op jit(solution)/shard_map/ppermute | solution.py:384
  70.6 18.4 %collective-permute-start.15 = (bf16[1,128,2048]{2,1,0:T(8,128)(2,1)S(1)}, bf16[1,128,2048]{2,1,0:T(8,128)(2,1)S(1)}, u32[]{:S(2)}, u32[]{:S(2)}) collective-permute-start(bf16[1,128,2048]{2,1,0:T(8,128)(2,1)S(1)} %copy-done.17), channel_id=1, source_target_pairs={{0,4},{1,5},{2,6},{3,7},{4,0},{5,1},{6,2},{7,3},{8,12},{9,13},{10,... | collective-permute-start | bytes 1572872 | tf_op jit(solution)/shard_map/ppermute | solution.py:384
  72.2 19.7 %collective-permute-start.17 = (bf16[2,136,1024]{2,1,0:T(8,128)(2,1)S(1)}, bf16[2,136,1024]{2,1,0:T(8,128)(2,1)S(1)}, u32[]{:S(2)}, u32[]{:S(2)}) collective-permute-start(bf16[2,136,1024]{2,1,0:T(8,128)(2,1)S(1)} %collective-permute-done.13.rest_6_.rest_7_.rest_3_), channel_id=1, source_target_pairs={{0,2},{1,3},{2,0},{3,1},{4,6},{5,7},{6,4},{7,5},{8,10},{9,11},{10,... | collective-permute-start | bytes 1671176 | tf_op jit(solution)/shard_map/ppermute | solution.py:384
  92.7 32.0 %collective-permute-start.20 = (bf16[3,128,2048]{2,1,0:T(8,128)(2,1)}, bf16[3,128,2048]{2,1,0:T(8,128)(2,1)}, u32[]{:S(2)}, u32[]{:S(2)}) collective-permute-start(bf16[3,128,2048]{2,1,0:T(8,128)(2,1)} %pad_maximum_fusion.rest_1_), channel_id=1, source_target_pairs={{0,2},{1,3},{2,0},{3,1},{4,6},{5,7},{6,4},{7,5},{8,10},{9,11},{10,... | collective-permute-start | bytes 4718600 | tf_op jit(solution)/shard_map/ppermute | solution.py:384
  93.3 31.5 %collective-permute-start.21 = (bf16[3,128,2048]{2,1,0:T(8,128)(2,1)}, bf16[3,128,2048]{2,1,0:T(8,128)(2,1)}, u32[]{:S(2)}, u32[]{:S(2)}) collective-permute-start(bf16[3,128,2048]{2,1,0:T(8,128)(2,1)} %pad_maximum_fusion.rest_1_), channel_id=1, source_target_pairs={{0,4},{1,5},{2,6},{3,7},{4,0},{5,1},{6,2},{7,3},{8,12},{9,13},{10,... | collective-permute-start | bytes 4718600 | tf_op jit(solution)/shard_map/ppermute | solution.py:384
  118.8 14.0 %collective-permute-start.23 = (bf16[3,128,2048]{2,1,0:T(8,128)(2,1)}, bf16[3,128,2048]{2,1,0:T(8,128)(2,1)S(1)}, u32[]{:S(2)}, u32[]{:S(2)}) collective-permute-start(bf16[3,128,2048]{2,1,0:T(8,128)(2,1)} %pad_maximum_fusion.rest_1_), channel_id=1, source_target_pairs={{0,1},{1,0},{2,3},{3,2},{4,5},{5,4},{6,7},{7,6},{8,9},{9,8},{10,11... | collective-permute-start | bytes 4718600 | tf_op jit(solution)/shard_map/ppermute | solution.py:389
  126.8 29.7 %collective-permute-start.28 = (bf16[2,128,2048]{2,1,0:T(8,128)(2,1)S(1)}, bf16[2,128,2048]{2,1,0:T(8,128)(2,1)S(1)}, u32[]{:S(2)}, u32[]{:S(2)}) collective-permute-start(bf16[2,128,2048]{2,1,0:T(8,128)(2,1)S(1)} %slice.34), channel_id=1, source_target_pairs={{0,2},{1,3},{2,0},{3,1},{4,6},{5,7},{6,4},{7,5},{8,10},{9,11},{10,... | collective-permute-start | bytes 3145736 | tf_op jit(solution)/shard_map/ppermute | solution.py:384
  130.6 18.7 %collective-permute-start.27 = (bf16[1,128,2048]{2,1,0:T(8,128)(2,1)S(1)}, bf16[1,128,2048]{2,1,0:T(8,128)(2,1)S(1)}, u32[]{:S(2)}, u32[]{:S(2)}) collective-permute-start(bf16[1,128,2048]{2,1,0:T(8,128)(2,1)S(1)} %slice.33), channel_id=1, source_target_pairs={{0,4},{1,5},{2,6},{3,7},{4,0},{5,1},{6,2},{7,3},{8,12},{9,13},{10,... | collective-permute-start | bytes 1572872 | tf_op jit(solution)/shard_map/ppermute | solution.py:384
  132.7 23.7 %collective-permute-start.26 = (bf16[1,128,2048]{2,1,0:T(8,128)(2,1)S(1)}, bf16[1,128,2048]{2,1,0:T(8,128)(2,1)S(1)}, u32[]{:S(2)}, u32[]{:S(2)}) collective-permute-start(bf16[1,128,2048]{2,1,0:T(8,128)(2,1)S(1)} %copy-done.16), channel_id=1, source_target_pairs={{0,4},{1,5},{2,6},{3,7},{4,0},{5,1},{6,2},{7,3},{8,12},{9,13},{10,... | collective-permute-start | bytes 1572872 | tf_op jit(solution)/shard_map/ppermute | solution.py:384
  132.8 27.1 %collective-permute-start.30 = (bf16[3,128,2048]{2,1,0:T(8,128)(2,1)}, bf16[3,128,2048]{2,1,0:T(8,128)(2,1)S(1)}, u32[]{:S(2)}, u32[]{:S(2)}) collective-permute-start(bf16[3,128,2048]{2,1,0:T(8,128)(2,1)} %collective-permute-done.20.rest_4_), channel_id=1, source_target_pairs={{0,1},{1,0},{2,3},{3,2},{4,5},{5,4},{6,7},{7,6},{8,9},{9,8},{10,11... | collective-permute-start | bytes 4718600 | tf_op jit(solution)/shard_map/ppermute | solution.py:389
  181.7 24.3 %collective-permute-start.36 = (bf16[512,256]{1,0:T(8,128)(2,1)S(1)}, bf16[512,256]{1,0:T(8,128)(2,1)S(1)}, u32[]{:S(2)}, u32[]{:S(2)}) collective-permute-start(bf16[512,256]{1,0:T(8,128)(2,1)S(1)} %get-tuple-element.104), channel_id=1, source_target_pairs={{0,1},{1,0},{2,3},{3,2},{4,5},{5,4},{6,7},{7,6},{8,9},{9,8},{10,11... | collective-permute-start | bytes 786440 | tf_op jit(solution)/shard_map/ppermute | solution.py:389
  182.1 24.0 %collective-permute-start.37 = (bf16[512,256]{1,0:T(8,128)(2,1)S(1)}, bf16[512,256]{1,0:T(8,128)(2,1)S(1)}, u32[]{:S(2)}, u32[]{:S(2)}) collective-permute-start(bf16[512,256]{1,0:T(8,128)(2,1)S(1)} %get-tuple-element.105), channel_id=1, source_target_pairs={{0,2},{1,3},{2,0},{3,1},{4,6},{5,7},{6,4},{7,5},{8,10},{9,11},{10,... | collective-permute-start | bytes 786440 | tf_op jit(solution)/shard_map/ppermute | solution.py:384
  182.9 23.1 %collective-permute-start.38 = (bf16[512,256]{1,0:T(8,128)(2,1)S(1)}, bf16[512,256]{1,0:T(8,128)(2,1)S(1)}, u32[]{:S(2)}, u32[]{:S(2)}) collective-permute-start(bf16[512,256]{1,0:T(8,128)(2,1)S(1)} %get-tuple-element.106), channel_id=1, source_target_pairs={{0,3},{1,2},{2,1},{3,0},{4,7},{5,6},{6,5},{7,4},{8,11},{9,10},{10,... | collective-permute-start | bytes 786440 | tf_op jit(solution)/shard_map/ppermute | solution.py:1195
  (68 other events, 442.8 us)

commit v5 on v4

--- a/solution.py
+++ b/solution.py
@@ -414,13 +414,13 @@
 OUTWARD = ((1, 0), (2, 3))
 
 
-def gather_z(own, first):
+def gather_z(own, first, second):
     begin = after(own, *first)
     z1 = hop(begin, 0, 2)
     m1 = z_hop(begin, MIDDLE)
     m2 = z_hop(z1, MIDDLE)
     f1 = z_hop(m1, OUTWARD)
-    f2 = z_hop(m2, OUTWARD)
+    f2 = z_hop(after(m2, *second), OUTWARD)
     inner = inner_z()
     return z1, jnp.where(inner, m2, f1), jnp.where(inner, m1, f2)
 
@@ -429,8 +429,8 @@
     return hop(value, 1, 0), hop(value, 0, 1)
 
 
-def blocks_of(array, first, half_bit, bit):
-    return [(array, slot, half_bit, 2 * (first + slot) + bit) for slot in range(array.shape[0])]
+def blocks_of(array, first, half_bit, bit, row=0):
+    return [(array, slot, half_bit, 2 * (first + slot) + bit, row) for slot in range(array.shape[0])]
 
 
 def swapped_blocks(found):
@@ -475,7 +475,7 @@
 
 def column_pairs(refs, table, w, ix, first, count, spread):
     pairs = []
-    for k, slot, half_bit, dp_bits in table:
+    for k, slot, half_bit, dp_bits, _ in table:
         src = refs[k].at[slot, pl.ds(0, LANES), pl.ds(first, count)]
         rows = at_rows(ix[0] ^ dp_bits, LANES)
         dst = w.at[half_bit, rows, :] if spread else w.at[rows, pl.ds(half_bit * count, count)]
@@ -484,11 +484,12 @@
 
 
 def block_pairs(refs, table, w, ix, half_bit, slot_out):
-    return [
-        (refs[k].at[slot], w.at[slot_out, at_rows(ix[0] ^ dp_bits, refs[k].shape[1]), :])
-        for k, slot, a, dp_bits in table
-        if a == half_bit
-    ]
+    pairs = []
+    for k, slot, a, dp_bits, row in table:
+        if a == half_bit:
+            rows = pl.ds(pl.multiple_of((ix[0] ^ dp_bits) * LANES + row, LANES // 2), refs[k].shape[1])
+            pairs.append((refs[k].at[slot], w.at[slot_out, rows, :]))
+    return pairs
 
 
 def both_heads(low, value):
@@ -808,7 +809,7 @@
     last = hidden is not None
     parts = 4
     piece = model // parts
-    chunk = 256
+    chunk = 512
     per = part // chunk
     c0 = 0.7978845608028654
     c1 = 0.044715
@@ -819,7 +820,7 @@
         hid_ref, rest = (rest[0], rest[1:]) if last else (None, rest)
         msgs = (rest[: counts[0]], rest[counts[0] : sum(counts)])
         rest = rest[sum(counts) :]
-        n_out = 2 + parts if last else 2
+        n_out = 1 + parts if last else 2
         outs, (w, grad_ref, x_ref, g_ref, pre_ref, act_ref, sems, *held) = rest[:n_out], rest[n_out:]
         groups = []
         used = 0
@@ -872,47 +873,46 @@
                 bend(1, per - 1, (per - 1) % 2)
 
         def mid_of(n):
-            at = at_rows(n, chunk)
-            lanes = at_lanes(n, chunk)
+            at = at_rows(n, BLK)
+            lanes = at_lanes(n, BLK)
             mid = lax.dot_general(pre_ref[:, :part], w[0, at, :part], NT, preferred_element_type=F32)
             mid = mid + lax.dot_general(pre_ref[:, part:], w[1, at, :part], NT, preferred_element_type=F32)
             unit = lax.dot_general(act_ref[:, :part], w[0, at, part:], NT, preferred_element_type=F32)
             unit = unit + lax.dot_general(act_ref[:, part:], w[1, at, part:], NT, preferred_element_type=F32)
             if carry:
-                mid = mid + carry[0][:, lanes]
-                unit = unit + carry[1][:, lanes]
+                mid = mid + carry[0][:, lanes].astype(F32)
+                unit = unit + carry[1][:, lanes].astype(F32)
             return mid, unit, lanes
 
         if not last:
 
             def finish(n, _):
                 mid, unit, lanes = mid_of(n)
-                outs[0][:, lanes] = mid
-                outs[1][:, lanes] = unit
+                outs[0][:, lanes] = mid.astype(BF16)
+                outs[1][:, lanes] = unit.astype(BF16)
                 return 0
 
-            lax.fori_loop(0, model // chunk, finish, 0)
+            lax.fori_loop(0, model // BLK, finish, 0)
             return
-        out_low, = held
+        out_low, mid_ref = held
 
         def finish(n, _):
             mid, unit, lanes = mid_of(n)
-            outs[0][:, lanes] = mid * vec_ref[3:4, lanes]
+            mid_ref[:, lanes] = mid * vec_ref[3:4, lanes]
             out_low[:, lanes] = (unit + hid_ref[:, lanes]).astype(BF16)
             return 0
 
-        lax.fori_loop(0, model // chunk, finish, 0)
+        lax.fori_loop(0, model // BLK, finish, 0)
         for k in range(parts):
-            outs[2 + k][...] = out_low[:, at_lanes((2 * ix[1] + ix[2]) ^ k, piece)]
+            outs[1 + k][...] = out_low[:, at_lanes((2 * ix[1] + ix[2]) ^ k, piece)]
         step_rows = 128
 
         def end(r, _):
             at = at_rows(r, step_rows)
             hat, scaler = row_stats(hid_ref[at, :])
             grad = cot[at, :].astype(F32) * weight_ref[at, :1]
-            grad = grad + norm_back(hat, scaler, outs[0][at, :])
-            outs[0][at, :] = grad
-            outs[1][at, :] = grad.astype(BF16)
+            grad = grad + norm_back(hat, scaler, mid_ref[at, :])
+            outs[0][at, :] = grad.astype(BF16)
             return 0
 
         lax.fori_loop(0, rows // step_rows, end, 0)
@@ -928,11 +928,11 @@
     ]
     specs += [block] * (len(carried) + (1 if last else 0))
     if last:
-        out_specs = [block, block] + [full(rows, piece)] * parts
-        out_shape = [shape(rows, model, F32), shape(rows, model)] + [shape(rows, piece)] * parts
+        out_specs = [block] + [full(rows, piece)] * parts
+        out_shape = [shape(rows, model)] + [shape(rows, piece)] * parts
     else:
         out_specs = [block, block]
-        out_shape = [shape(rows, model, F32)] * 2
+        out_shape = [shape(rows, model)] * 2
     arrays = [array for found, _ in sources for array in found]
     return call(
         body,
@@ -950,7 +950,7 @@
             pltpu.VMEM((rows, 2 * part), BF16),
             pltpu.SemaphoreType.DMA((sum(len(table) for _, table in sources),)),
         ]
-        + ([pltpu.VMEM((rows, model), BF16)] if last else []),
+        + ([pltpu.VMEM((rows, model), BF16), pltpu.VMEM((rows, model), F32)] if last else []),
         cost(16 * rows * part * model, 12 * part * model, 2 * rows * part),
     )(idx, normed, cotangent, weights, bias, bias_other, vec, *carried, *((hidden,) if last else ()), *arrays)
 
@@ -1112,7 +1112,7 @@
 
         @pl.when(step >= half_blocks)
         def _():
-            own_ref[...] = total
+            own_ref[...] = total.astype(BF16)
 
     def rows(i, ix):
         rank = jnp.where(i < half_blocks, 1 - ix[2], ix[2])
@@ -1128,7 +1128,7 @@
             pl.BlockSpec((BLK, model), lambda i, ix: (jnp.minimum(i, half_blocks - 1), 0)),
             pl.BlockSpec((BLK, model), lambda i, ix: (jnp.maximum(i - half_blocks, 0), 0)),
         ],
-        [shape(LEN // 2, model), shape(LEN // 2, model, F32)],
+        [shape(LEN // 2, model)] * 2,
         [pltpu.VMEM((2, model, cols), BF16), pltpu.SemaphoreType.DMA((len(table),))],
         cost(4 * LEN * model * cols, 4 * model * cols),
     )(idx, dq, dk, dv, latent_low, down, *arrays)
@@ -1142,9 +1142,9 @@
 
     def body(ix, own, recv, tok, hg, vec_ref, *rest):
         outs, held = rest[:parts], rest[parts]
-        e = vec_ref[0:1, :] * (own[...] + recv[...].astype(F32))
+        e = vec_ref[0:1, :] * (own[...].astype(F32) + recv[...].astype(F32))
         hat, scaler = row_stats(tok[...].astype(F32))
-        held[...] = (hg[...] + norm_back(hat, scaler, e)).astype(BF16)
+        held[...] = (hg[...].astype(F32) + norm_back(hat, scaler, e)).astype(BF16)
         for k, out in enumerate(outs):
             out[...] = held[:, at_lanes((2 * ix[1] + ix[2]) ^ k, part)]
 
@@ -1158,6 +1158,7 @@
         [shape(LEN // 2, part)] * parts,
         [pltpu.VMEM((BLK, model), BF16)],
         cost(20 * LEN * model, 8 * LEN * model),
+        56 << 20,
     )(idx, in_own, in_recv, tokens, hidden_grad, vec)
 
 
@@ -1237,32 +1238,34 @@
     own_start = (idx[1] * ranks + idx[2]) * (LEN // 2)
     own_rows = lambda v: lax.dynamic_slice_in_dim(v, own_start, LEN // 2, 0)
     tok_own, cot_own = own_rows(tokens), own_rows(cotangent)
-    h_z1, h_z2, h_z3 = gather_z(heads_own, ())
+    h_z1, h_z2, h_z3 = gather_z(heads_own, (), ())
     h_near, h_far = jnp.stack([heads_own, h_z1]), jnp.stack([h_z2, h_z3])
-    hx_near, hy_near = pair_xy(h_near)
-    hx_far, hy_far = pair_xy(h_far)
-    ux0, uy0 = pair_xy(after(u_own, hx_far, hy_far))
-    hd_near, hd_far = hop(after(hx_near, h_far), 0, 1), hop(hy_far, 1, 0)
+    ux0, uy0 = pair_xy(u_own)
+    hx_near, hy_near = pair_xy(after(h_near, ux0, uy0))
+    hx_far, hy_far = pair_xy(after(h_far, hx_near, hy_near))
+    hd_near, hd_far = hop(after(hx_near, hy_far), 0, 1), hop(hy_far, 1, 0)
+    ud0 = hop(after(ux0, hd_near), 0, 1)
     heads = []
     for first, arrays in ((0, (h_near, hx_near, hy_near, hd_near)), (2, (h_far, hx_far, hy_far, hd_far))):
         for n, array in enumerate(arrays):
             heads += blocks_of(array, first, n % 2, n // 2)
-    u_rest = jnp.concatenate(gather_z(u_own, (h_far, hx_near, hy_near)))
+    u_rest = jnp.concatenate(gather_z(u_own, (h_far,), (hx_far, hy_far)))
     weights, fc_mine = weigh(
         idx, ids, fc_line, h_near, h_far, hy_near, hy_far, hx_near, float(tok_dev * lax.axis_size("dp"))
     )
     fc_other = core_swap(fc_mine)
     down8 = down_master.reshape(2 * r, model)
     normed, latent, down = norm_rows(idx, after(tokens, hx_far, tok_own, cot_own), vec, down8)
-    ux, uy = pair_xy(after(u_rest, hd_near, hd_far, ux0, uy0))
-    ready = after(normed, u_rest, ux0, uy0)
+    ux, uy = pair_xy(after(u_rest, hd_far, ud0))
+    ready = after(normed, u_rest, ud0, weights)
     queries, keys, values, up = project_heads(idx, ready, latent, frozen_triple_bias, up_rows, hx_near, heads)
     mixed, logsum = attend_fast(queries, keys, values)
     sent = [core_swap(v) for v in attention_out_send(idx, mixed, heads, heads_cols)]
     hidden, normed_mid = attention_out_own(idx, mixed, sent, tok_own, vec, heads, heads_cols)
     rows = (normed_mid, cot_own, weights, fc_mine, fc_other, vec)
-    ux0, ux, uy, _ = lax.optimization_barrier((ux0, ux, uy, normed_mid))
-    ud0, ud1, ud2 = hop(ux0, 0, 1), hop(ux[:1], 0, 1), hop(uy[1:], 1, 0)
+    ux, uy, _ = lax.optimization_barrier((ux, uy, normed_mid))
+    cut = step_rows // 2
+    ud_low, ud_high = hop(ux[:, :cut], 0, 1), hop(uy[:, cut:], 1, 0)
 
     def table(half_bit, bit, *arrays):
         found, start = [], 0
@@ -1275,34 +1278,33 @@
     first_mine = table(0, 0, u_own, u_rest) + table(0, 1, uy0, uy)
     first_other = table(0, 0, *swap(u_own, u_rest)) + table(0, 1, *swap(uy0, uy))
     carried = units_main(idx, 0, *rows, first_mine, first_other, (), None)
-    ud0, ud1, ud2, _ = lax.optimization_barrier((ud0, ud1, ud2, carried[0]))
-    last_mine = table(1, 0, ux0, ux) + table(1, 1, ud0, ud1, ud2)
-    last_other = table(1, 0, *swap(ux0, ux)) + table(1, 1, *swap(ud0, ud1, ud2))
-    hidden_grad, hidden_low, *out_pieces = units_main(idx, 1, *rows, last_mine, last_other, carried, hidden)
+    ud_low, ud_high, _ = lax.optimization_barrier((ud_low, ud_high, carried[0]))
+    corner = lambda v, low, high: table(1, 1, v) + blocks_of(low, 1, 1, 1) + blocks_of(high, 1, 1, 1, cut)
+    last_mine = table(1, 0, ux0, ux) + corner(ud0, ud_low, ud_high)
+    last_other = table(1, 0, *swap(ux0, ux)) + corner(*swap(ud0, ud_low, ud_high))
+    hidden_low, *out_pieces = units_main(idx, 1, *rows, last_mine, last_other, carried, hidden)
     hidden_other = core_swap(hidden_low)
     out_pieces = exchange_features(out_pieces)
     dq, dk, dv, latent_low, down_term, up_q, up_v = attend_back_fast(
         idx, queries, keys, values, mixed, hidden_low, hidden_other, logsum, normed, latent, up, heads, heads_cols
     )
     up_term = jnp.stack([up_q[:r], up_v[r:]]).reshape(2 * r, 2, head_part)
-    terms = jnp.concatenate([down_term, up_term[:, 1], up_term[:, 0]], axis=1)
-    terms = terms + hop(terms, 0, 1)
+    down_sum = down_term + core_swap(down_term)
     dq, out_pieces = lax.optimization_barrier((dq, out_pieces))
     in_send, in_own = heads_back(idx, dq, dk, dv, latent_low, down, heads)
     in_recv = core_swap(in_send)
-    terms = after(terms, in_own)
-    terms = terms + hop(terms, 0, 2)
-    in_pieces = tokens_back(idx, in_own, in_recv, tok_own, hidden_grad, vec)
-    terms = after(terms, in_recv)
-    terms = terms + hop(terms, 0, 4)
-    terms, out_pieces = lax.optimization_barrier((terms, out_pieces, in_pieces[2]))[:2]
+    got = hop(after(jnp.concatenate([down_sum, up_term[:, 1]], axis=1), in_send), 1, 0)
+    terms = jnp.concatenate([down_sum, up_term[:, 0]], axis=1) + got
+    in_pieces = tokens_back(idx, in_own, in_recv, tok_own, hidden_low, vec)
+    in_pieces = exchange_features(in_pieces)
+    terms = after(terms, in_pieces[1])
+    for bit in (1, 2, 4):
+        terms = terms + hop(terms, 0, bit)
+    out_pieces = lax.optimization_barrier((out_pieces, in_pieces[1]))[0]
     output = to_features(idx, out_pieces, proj_bias.astype(F32).reshape(1, -1))
-    input_grad = to_features(idx, exchange_features(in_pieces), None)
-    width = model + head_part
-    got = hop(terms[:, :width], 1, 0)
-    down_sum = terms[:, :model] + got[:, :model]
-    down_grad = (down_sum + core_swap(down_sum)).reshape(down_master.shape)
-    up_grad = ADAPTER_SCALE * (terms[:, width:] + got[:, model:]).reshape(up_master.shape)
+    input_grad = to_features(idx, in_pieces, None)
+    down_grad = terms[:, :model].reshape(down_master.shape)
+    up_grad = ADAPTER_SCALE * terms[:, model:].reshape(up_master.shape)
     step_value = jnp.float32(STEP)
     down_new, down_moment, down_square = adam_update(
         down_master, down_first, down_second, down_grad, step_value, learn_rate

time: 249 us -> 224 us (0.90)
  waiting for transfers between devices: 74.9 us -> 60.8 us
  local copies, waits for them, and re-layouts: 19.9 us -> 14.5 us
  starting transfers between devices: 48.9 us -> 45 us
    ppermute x21, waiting for transfers between devices: 48.9 us -> 32.4 us  [hop(): return lax.ppermute(value, AXES, [(i, i ^ flip) for i in range(total)])]
    unnamed x93 -> x89, local copies, waits for them, and re-layouts: 13.2 us -> 7.93 us
    ppermute x21, starting transfers between devices: 36.2 us -> 32 us  [hop(): return lax.ppermute(value, AXES, [(i, i ^ flip) for i in range(total)])]
    ppermute x16, waiting for transfers between devices: 6.83 us -> 10.7 us  [core_swap(): return lax.ppermute(value, AXES, [(i, i ^ 1) for i in range(total)])]
    pallas_call x2, Pallas kernels: 33.8 us -> 30 us  [units_main(): call(body, 'units_main_last' if last else 'units_main_first', 1, specs +...]
    pallas_call x1, Pallas kernels: 2.18 us -> 5 us  [tokens_back(): call(body, 'tokens_back', half_blocks, [row, row, row, row, full(8, model...]
  transfers between devices with their start and end apart: 47 -> 47, of which waited for: 21 -> 22; matrix products, arithmetic and copies ran while one was open for 4% -> 4% of each run, Pallas kernels for 27% -> 31%
where the time goes in v5:
time: 224 us; the launch traced here: 223 us
  Pallas kernels  95.9 us (43%)
  waiting for transfers between devices  60.8 us (27%)
  starting transfers between devices  45 us (20%)
  local copies, waits for them, and re-layouts  14.5 us (6%)
  other arithmetic  4.54 us (2%)
    ppermute x21, waiting for transfers between devices, hop(): return lax.ppermute(value, AXES, [(i, i ^ flip) for i in range(total)])  32.4 us
    ppermute x21, starting transfers between devices, hop(): return lax.ppermute(value, AXES, [(i, i ^ flip) for i in range(total)])  32 us
    pallas_call x2, Pallas kernels, units_main(): call(body, 'units_main_last' if last else 'units_main_first', 1, specs +...  30 us
    pallas_call x1, Pallas kernels, attend_back_fast(): call(body, 'attend_back', pairs, [spec] * 4 + [full(half, model)] * 2 + [...  21.8 us
    ppermute x8, waiting for transfers between devices, z_hop(): return lax.ppermute(value, AXES, perm)  17.7 us
    pallas_call x1, Pallas kernels, attend_fast(): pl.pallas_call(body, grid=(pairs,), out_shape=(shape(length, width), jax....  11 us
    ppermute x16, waiting for transfers between devices, core_swap(): return lax.ppermute(value, AXES, [(i, i ^ 1) for i in range(total)])  10.7 us
    unnamed x89, local copies, waits for them, and re-layouts  7.93 us
  transfers between devices with their start and end apart: 47, of which 22 were waited for; matrix products, arithmetic and copies ran while one was open for 4% of the time, Pallas kernels for 31%

profile of v5, /device:TPU:0, one launch (start us, length us, event | category | flops | bytes accessed | tf_op | source)
XLA Modules:
  0.0 223.1 jit_solution(12132391988997837137)
XLA Ops:
  4.3 3.3 %prepare_blocks.1 = (bf16[136,1024]{1,0:T(8,128)(2,1)}, bf16[1,128,2048]{2,1,0:T(8,128)(2,1)}) custom-call(s32[3]{0:T(128)} %pad_add_fusion.ix, s32[16,128]{1,0:T(8,128)} %bitcast.21, bf16[128,3,256]{2,1,0:T(4,128)(2,1)} %copy.32.triple_ref, bf16[256,128]{1,0:T(8,128)(2,1)} %out_ref.1, bf16[3,256]{1,0:T(4,128)(2,1)} %bias_ref.3, ...), custom_call_target="tpu_custom_call" | custom-call | bytes 52428 | tf_op jit(solution)/shard_map/prepare_blocks/pallas_call | solution.py:548
  7.6 3.0 %collective-permute-start = (bf16[136,1024]{1,0:T(8,128)(2,1)}, bf16[136,1024]{1,0:T(8,128)(2,1)S(1)}, u32[]{:S(2)}, u32[]{:S(2)}) collective-permute-start(bf16[136,1024]{1,0:T(8,128)(2,1)} %get-tuple-element.69), channel_id=1, source_target_pairs={{0,8},{1,9},{2,10},{3,11},{4,12},{5,13},{6,14},{7,15},{8,0},{9,1},... | collective-permute-start | bytes 835592 | tf_op jit(solution)/shard_map/ppermute | solution.py:384
  14.4 3.1 %collective-permute-done = bf16[136,1024]{1,0:T(8,128)(2,1)S(1)} collective-permute-done((bf16[136,1024]{1,0:T(8,128)(2,1)}, bf16[136,1024]{1,0:T(8,128)(2,1)S(1)}, u32[]{:S(2)}, u32[]{:S(2)}) %collective-permute-start) | collective-permute-done | bytes 278560 | tf_op jit(solution)/shard_map/ppermute | solution.py:384
  21.8 3.1 %collective-permute-done.5.rest_3_ = bf16[1,128,2048]{2,1,0:T(8,128)(2,1)S(1)} collective-permute-done((bf16[1,128,2048]{2,1,0:T(8,128)(2,1)}, bf16[1,128,2048]{2,1,0:T(8,128)(2,1)S(1)}, u32[]{:S(2)}, u32[]{:S(2)}) %collective-permute-start.5) | collective-permute-done | bytes 524320 | tf_op jit(solution)/shard_map/ppermute | solution.py:384
  30.1 5.4 %collective-permute-done.4 = bf16[136,1024]{1,0:T(8,128)(2,1)S(1)} collective-permute-done((bf16[136,1024]{1,0:T(8,128)(2,1)S(1)}, bf16[136,1024]{1,0:T(8,128)(2,1)S(1)}, u32[]{:S(2)}, u32[]{:S(2)}) %collective-permute-start.4) | collective-permute-done | bytes 278560 | tf_op jit(solution)/shard_map/ppermute | solution.py:407
  42.4 5.2 %collective-permute-done.10 = bf16[1,128,2048]{2,1,0:T(8,128)(2,1)S(1)} collective-permute-done((bf16[1,128,2048]{2,1,0:T(8,128)(2,1)S(1)}, bf16[1,128,2048]{2,1,0:T(8,128)(2,1)S(1)}, u32[]{:S(2)}, u32[]{:S(2)}) %collective-permute-start.10) | collective-permute-done | bytes 524320 | tf_op jit(solution)/shard_map/ppermute | solution.py:384
  49.6 3.5 %collective-permute-done.14.rest_3_.rest_6_.rest_7_ = bf16[2,136,1024]{2,1,0:T(8,128)(2,1)S(1)} collective-permute-done((bf16[2,136,1024]{2,1,0:T(8,128)(2,1)S(1)}, bf16[2,136,1024]{2,1,0:T(8,128)(2,1)S(1)}, u32[]{:S(2)}, u32[]{:S(2)}) %collective-permute-start.14) | collective-permute-done | bytes 557088 | tf_op jit(solution)/shard_map/ppermute | solution.py:384
  56.6 4.9 %collective-permute-done.13 = bf16[1,128,2048]{2,1,0:T(8,128)(2,1)S(1)} collective-permute-done((bf16[1,128,2048]{2,1,0:T(8,128)(2,1)S(1)}, bf16[1,128,2048]{2,1,0:T(8,128)(2,1)S(1)}, u32[]{:S(2)}, u32[]{:S(2)}) %collective-permute-start.13) | collective-permute-done | bytes 524320 | tf_op jit(solution)/shard_map/ppermute | solution.py:407
  61.5 3.5 %collective-permute-done.16.rest_3_.rest_4_ = bf16[2,136,1024]{2,1,0:T(8,128)(2,1)S(1)} collective-permute-done((bf16[2,136,1024]{2,1,0:T(8,128)(2,1)S(1)}, bf16[2,136,1024]{2,1,0:T(8,128)(2,1)S(1)}, u32[]{:S(2)}, u32[]{:S(2)}) %collective-permute-start.16) | collective-permute-done | bytes 557088 | tf_op jit(solution)/shard_map/ppermute | solution.py:384
  67.3 6.2 %collective-permute-done.15 = bf16[1,128,2048]{2,1,0:T(8,128)(2,1)S(1)} collective-permute-done((bf16[1,128,2048]{2,1,0:T(8,128)(2,1)S(1)}, bf16[1,128,2048]{2,1,0:T(8,128)(2,1)S(1)}, u32[]{:S(2)}, u32[]{:S(2)}) %collective-permute-start.15) | collective-permute-done | bytes 524320 | tf_op jit(solution)/shard_map/ppermute | solution.py:407
  84.2 3.0 %norm_rows.1 = (bf16[1024,1024]{1,0:T(8,128)(2,1)S(1)}, bf16[1024,128]{1,0:T(8,128)(2,1)S(1)}, bf16[128,1024]{1,0:T(8,128)(2,1)S(1)}) custom-call(s32[3]{0:T(128)S(1)} %copy-done.25, bf16[2048,1024]{1,0:T(8,128)(2,1)S(1)} %copy-done.5, f32[8,1024]{1,0:T(8,128)S(1)} %convert_element_type.10.vec_ref, f32[8,1024]{1,0:T(8,128)S(1)} %reshape.52.down_ref), custom_call_target="tpu_custom_call" | custom-call | flops 26843544 | bytes 419430 | tf_op jit(solution)/shard_map/norm_rows/pallas_call | solution.py:620
  87.2 6.2 %project_heads.1 = (bf16[1024,512]{1,0:T(8,128)(2,1)S(1)}, bf16[1024,512]{1,0:T(8,128)(2,1)S(1)}, bf16[1024,512]{1,0:T(8,128)(2,1)S(1)}, bf16[2,128,768]{2,1,0:T(8,128)(2,1)S(1)}) custom-call(s32[3]{0:T(128)S(1)} %copy-done.25, bf16[1024,1024]{1,0:T(8,128)(2,1)S(1)} %get-tuple-element.80.normed_ref, bf16[1024,128]{1,0:T(8,128)(2,1)S(1)} %get-tuple-element.81.latent_ref, ...), custom_call_target="tpu_custom_call" | custom-call | flops 322122560 | bytes 1677721 | tf_op jit(solution)/shard_map/project_heads/pallas_call | solution.py:669
  93.3 11.0 %attend.1 = (bf16[1024,512]{1,0:T(8,128)(2,1)S(1)}, f32[4,8,1024]{2,1,0:T(8,128)S(1)}) custom-call(bf16[1024,512]{1,0:T(8,128)(2,1)S(1)} %get-tuple-element.82.q_ref, bf16[1024,512]{1,0:T(8,128)(2,1)S(1)} %get-tuple-element.83.k_ref, bf16[1024,512]{1,0:T(8,128)(2,1)S(1)} %get-tuple-element.84.v_ref), custom_call_target="tpu_custom_call" | custom-call | flops 429496736 | bytes 419430 | tf_op jit(solution)/shard_map/attend/pallas_call | solution.py:718
  106.8 2.9 %collective-permute-done.19.rest_0_ = bf16[512,1024]{1,0:T(8,128)(2,1)S(1)} collective-permute-done((bf16[512,1024]{1,0:T(8,128)(2,1)S(1)}, bf16[512,1024]{1,0:T(8,128)(2,1)S(1)}, u32[]{:S(2)}, u32[]{:S(2)}) %collective-permute-start.19) | collective-permute-done | bytes 1048608 | tf_op jit(solution)/shard_map/ppermute | solution.py:389
  118.6 14.4 %units_main_first.1 = (bf16[512,1024]{1,0:T(8,128)(2,1)S(1)}, bf16[512,1024]{1,0:T(8,128)(2,1)S(1)}) custom-call(s32[3]{0:T(128)S(1)} %copy-done.25, bf16[512,1024]{1,0:T(8,128)(2,1)S(1)} %get-tuple-element.86.normed_ref, bf16[512,1024]{1,0:T(8,128)(2,1)S(1)} %constant_dynamic-slice_fusion.cot, f32[512,128]{1,0:T(8,128)S(1)} %get-tuple-element.79.weight_ref, ...), custom_call_target="tpu_custom_call" | custom-call | flops 858993472 | bytes 1258291 | tf_op jit(solution)/shard_map/units_main_first/pallas_call | solution.py:937
  133.0 3.8 %collective-permute-done.27.rest_6_ = bf16[3,64,2048]{2,1,0:T(8,128)(2,1)S(1)} collective-permute-done((bf16[3,64,2048]{2,1,0:T(8,128)(2,1)S(1)}, bf16[3,64,2048]{2,1,0:T(8,128)(2,1)S(1)}, u32[]{:S(2)}, u32[]{:S(2)}) %collective-permute-start.27) | collective-permute-done | bytes 786464 | tf_op jit(solution)/shard_map/ppermute | solution.py:384
  138.6 3.1 %collective-permute-done.29.rest_8_ = bf16[1,128,2048]{2,1,0:T(8,128)(2,1)S(1)} collective-permute-done((bf16[1,128,2048]{2,1,0:T(8,128)(2,1)S(1)}, bf16[1,128,2048]{2,1,0:T(8,128)(2,1)S(1)}, u32[]{:S(2)}, u32[]{:S(2)}) %collective-permute-start.29) | collective-permute-done | bytes 524320 | tf_op jit(solution)/shard_map/ppermute | solution.py:389
  142.5 15.6 %units_main_last.1 = (bf16[512,1024]{1,0:T(8,128)(2,1)S(1)}, bf16[512,256]{1,0:T(8,128)(2,1)S(1)}, bf16[512,256]{1,0:T(8,128)(2,1)S(1)}, bf16[512,256]{1,0:T(8,128)(2,1)S(1)}, bf16[512,256]{1,0:T(8,128)(2,1)S(1)}) custom-call(s32[3]{0:T(128)S(1)} %copy-done.25, bf16[512,1024]{1,0:T(8,128)(2,1)S(1)} %get-tuple-element.86.normed_ref, ...), custom_call_target="tpu_custom_call" | custom-call | flops 858993472 | bytes 1258291 | tf_op jit(solution)/shard_map/units_main_last/pallas_call | solution.py:937
  160.9 21.8 %attend_back.1 = (bf16[1024,512]{1,0:T(8,128)(2,1)S(1)}, bf16[1024,512]{1,0:T(8,128)(2,1)S(1)}, bf16[1024,512]{1,0:T(8,128)(2,1)S(1)}, bf16[1024,128]{1,0:T(8,12...) custom-call(s32[3]{0:T(128)S(1)} %copy-done.25, ...), custom_call_target="tpu_custom_call" | custom-call | flops 1073741824 | bytes 838860 | tf_op jit(solution)/shard_map/attend_back/pallas_call | solution.py:1054
  183.5 6.9 %heads_back.1 = (bf16[512,1024]{1,0:T(8,128)(2,1)}, bf16[512,1024]{1,0:T(8,128)(2,1)S(1)}) custom-call(s32[3]{0:T(128)S(1)} %copy-done.25, bf16[1024,512]{1,0:T(8,128)(2,1)S(1)} %get-tuple-element.108.dq_ref, bf16[1024,512]{1,0:T(8,128)(2,1)S(1)} %get-tuple-element.109.dk_ref, bf16[1024,512]{1,0:T(8,128)(2,1)S(1)} %get-tuple-element.110.dv_ref, ...), custom_call_target="tpu_custom_call" | custom-call | flops 322122560 | bytes 314572 | tf_op jit(solution)/shard_map/heads_back/pallas_call | solution.py:1122
  195.7 5.0 %tokens_back.1 = (bf16[512,256]{1,0:T(8,128)(2,1)}, bf16[512,256]{1,0:T(8,128)(2,1)}, bf16[512,256]{1,0:T(8,128)(2,1)}, bf16[512,256]{1,0:T(8,128)(2,1)}) custom-call(s32[3]{0:T(128)} %pad_add_fusion.ix, bf16[512,1024]{1,0:T(8,128)(2,1)} %copy-done.8, bf16[512,1024]{1,0:T(8,128)(2,1)} %copy-done.30, bf16[512,1024]{1,0:T(8,128)(2,1)} %copy-done.4, ...), custom_call_target="tpu_custom_call" | custom-call | flops 2097152 | bytes 838860 | tf_op jit(solution)/shard_map/tokens_back/pallas_call | solution.py:1152
  203.7 3.0 %collective-permute-done.44 = f32[8,1280]{1,0:T(8,128)S(1)} collective-permute-done((f32[8,1280]{1,0:T(8,128)S(1)}, f32[8,1280]{1,0:T(8,128)S(1)}, u32[]{:S(2)}, u32[]{:S(2)}) %collective-permute-start.44) | collective-permute-done | bytes 40992 | tf_op jit(solution)/shard_map/ppermute | solution.py:384
  206.7 5.8 %collective-permute-start.45 = (f32[8,1280]{1,0:T(8,128)S(1)}, f32[8,1280]{1,0:T(8,128)S(1)}, u32[]{:S(2)}, u32[]{:S(2)}) collective-permute-start(f32[8,1280]{1,0:T(8,128)S(1)} %add.63), channel_id=1, source_target_pairs={{0,8},{1,9},{2,10},{3,11},{4,12},{5,13},{6,14},{7,15},{8,0},{9,1},... | collective-permute-start | bytes 122888 | tf_op jit(solution)/shard_map/ppermute | solution.py:384
  214.6 3.0 %collective-permute-start.46 = (f32[8,1280]{1,0:T(8,128)S(1)}, f32[8,1280]{1,0:T(8,128)S(1)}, u32[]{:S(2)}, u32[]{:S(2)}) collective-permute-start(f32[8,1280]{1,0:T(8,128)S(1)} %add.64), channel_id=1, source_target_pairs={{0,16},{1,17},{2,18},{3,19},{4,20},{5,21},{6,22},{7,23},{8,24},{9,... | collective-permute-start | bytes 122888 | tf_op jit(solution)/shard_map/ppermute | solution.py:384
  (216 shorter events, 74.2 us)
Async XLA Ops:
  11.3 13.7 %collective-permute-start.5 = (bf16[1,128,2048]{2,1,0:T(8,128)(2,1)}, bf16[1,128,2048]{2,1,0:T(8,128)(2,1)S(1)}, u32[]{:S(2)}, u32[]{:S(2)}) collective-permute-start(bf16[1,128,2048]{2,1,0:T(8,128)(2,1)} %get-tuple-element.75.rest_0_), channel_id=1, source_target_pairs={{0,2},{1,3},{2,0},{3,1},{4,6},{5,7},{6,4},{7,5},{8,10},{9,11},{10,... | collective-permute-start | bytes 1572872 | tf_op jit(solution)/shard_map/ppermute | solution.py:384
  12.9 13.4 %collective-permute-start.6 = (bf16[1,128,2048]{2,1,0:T(8,128)(2,1)}, bf16[1,128,2048]{2,1,0:T(8,128)(2,1)}, u32[]{:S(2)}, u32[]{:S(2)}) collective-permute-start(bf16[1,128,2048]{2,1,0:T(8,128)(2,1)} %get-tuple-element.75.rest_0_), channel_id=1, source_target_pairs={{0,4},{1,5},{2,6},{3,7},{4,0},{5,1},{6,2},{7,3},{8,12},{9,13},{10,... | collective-permute-start | bytes 1572872 | tf_op jit(solution)/shard_map/ppermute | solution.py:384
  19.5 16.0 %collective-permute-start.4 = (bf16[136,1024]{1,0:T(8,128)(2,1)S(1)}, bf16[136,1024]{1,0:T(8,128)(2,1)S(1)}, u32[]{:S(2)}, u32[]{:S(2)}) collective-permute-start(bf16[136,1024]{1,0:T(8,128)(2,1)S(1)} %collective-permute-done.1), channel_id=1, source_target_pairs={{8,0},{9,1},{10,2},{11,3},{12,4},{13,5},{14,6},{15,7},{16,24},{17,... | collective-permute-start | bytes 835592 | tf_op jit(solution)/shard_map/ppermute | solution.py:407
  26.3 12.9 %collective-permute-start.7 = (bf16[2,136,1024]{2,1,0:T(8,128)(2,1)S(1)}, bf16[2,136,1024]{2,1,0:T(8,128)(2,1)S(1)}, u32[]{:S(2)}, u32[]{:S(2)}) collective-permute-start(bf16[2,136,1024]{2,1,0:T(8,128)(2,1)S(1)} %pad_maximum_fusion.2.rest_0_.rest_1_), channel_id=1, source_target_pairs={{0,2},{1,3},{2,0},{3,1},{4,6},{5,7},{6,4},{7,5},{8,10},{9,11},{10,... | collective-permute-start | bytes 1671176 | tf_op jit(solution)/shard_map/ppermute | solution.py:384
  27.2 13.0 %collective-permute-start.8 = (bf16[2,136,1024]{2,1,0:T(8,128)(2,1)S(1)}, bf16[2,136,1024]{2,1,0:T(8,128)(2,1)S(1)}, u32[]{:S(2)}, u32[]{:S(2)}) collective-permute-start(bf16[2,136,1024]{2,1,0:T(8,128)(2,1)S(1)} %pad_maximum_fusion.2.rest_0_.rest_1_), channel_id=1, source_target_pairs={{0,4},{1,5},{2,6},{3,7},{4,0},{5,1},{6,2},{7,3},{8,12},{9,13},{10,... | collective-permute-start | bytes 1671176 | tf_op jit(solution)/shard_map/ppermute | solution.py:384
  35.6 12.0 %collective-permute-start.10 = (bf16[1,128,2048]{2,1,0:T(8,128)(2,1)S(1)}, bf16[1,128,2048]{2,1,0:T(8,128)(2,1)S(1)}, u32[]{:S(2)}, u32[]{:S(2)}) collective-permute-start(bf16[1,128,2048]{2,1,0:T(8,128)(2,1)S(1)} %copy-done.9), channel_id=1, source_target_pairs={{0,8},{1,9},{2,10},{3,11},{4,12},{5,13},{6,14},{7,15},{8,0},{9,1},... | collective-permute-start | bytes 1572872 | tf_op jit(solution)/shard_map/ppermute | solution.py:384
  35.7 12.6 %collective-permute-start.12 = (bf16[1,128,2048]{2,1,0:T(8,128)(2,1)S(1)}, bf16[1,128,2048]{2,1,0:T(8,128)(2,1)S(1)}, u32[]{:S(2)}, u32[]{:S(2)}) collective-permute-start(bf16[1,128,2048]{2,1,0:T(8,128)(2,1)S(1)} %copy-done.9), channel_id=1, source_target_pairs={{8,16},{9,17},{10,18},{11,19},{12,20},{13,21},{14,22},{15,23},{16,... | collective-permute-start | bytes 1572872 | tf_op jit(solution)/shard_map/ppermute | solution.py:407
  40.2 12.8 %collective-permute-start.14 = (bf16[2,136,1024]{2,1,0:T(8,128)(2,1)S(1)}, bf16[2,136,1024]{2,1,0:T(8,128)(2,1)S(1)}, u32[]{:S(2)}, u32[]{:S(2)}) collective-permute-start(bf16[2,136,1024]{2,1,0:T(8,128)(2,1)S(1)} %pad_maximum_fusion.1.rest_1_.rest_4_.rest_5_), channel_id=1, source_target_pairs={{0,4},{1,5},{2,6},{3,7},{4,0},{5,1},{6,2},{7,3},{8,12},{9,13},{10,... | collective-permute-start | bytes 1671176 | tf_op jit(solution)/shard_map/ppermute | solution.py:384
  41.8 12.8 %collective-permute-start.9 = (bf16[2,136,1024]{2,1,0:T(8,128)(2,1)S(1)}, bf16[2,136,1024]{2,1,0:T(8,128)(2,1)S(1)}, u32[]{:S(2)}, u32[]{:S(2)}) collective-permute-start(bf16[2,136,1024]{2,1,0:T(8,128)(2,1)S(1)} %pad_maximum_fusion.1.rest_1_.rest_4_.rest_5_), channel_id=1, source_target_pairs={{0,2},{1,3},{2,0},{3,1},{4,6},{5,7},{6,4},{7,5},{8,10},{9,11},{10,... | collective-permute-start | bytes 1671176 | tf_op jit(solution)/shard_map/ppermute | solution.py:384
  48.3 13.2 %collective-permute-start.13 = (bf16[1,128,2048]{2,1,0:T(8,128)(2,1)S(1)}, bf16[1,128,2048]{2,1,0:T(8,128)(2,1)S(1)}, u32[]{:S(2)}, u32[]{:S(2)}) collective-permute-start(bf16[1,128,2048]{2,1,0:T(8,128)(2,1)S(1)} %collective-permute-done.12), channel_id=1, source_target_pairs={{8,0},{9,1},{10,2},{11,3},{12,4},{13,5},{14,6},{15,7},{16,24},{17,... | collective-permute-start | bytes 1572872 | tf_op jit(solution)/shard_map/ppermute | solution.py:407
  53.0 12.0 %collective-permute-start.16 = (bf16[2,136,1024]{2,1,0:T(8,128)(2,1)S(1)}, bf16[2,136,1024]{2,1,0:T(8,128)(2,1)S(1)}, u32[]{:S(2)}, u32[]{:S(2)}) collective-permute-start(bf16[2,136,1024]{2,1,0:T(8,128)(2,1)S(1)} %collective-permute-done.7.rest_4_.near_ref.rest_1_.rest_2_), channel_id=1, source_target_pairs={{0,4},{1,5},{2,6},{3,7},{4,0},{5,1},{6,2},{7,3},{8,12},{9,13},{10,... | collective-permute-start | bytes 1671176 | tf_op jit(solution)/shard_map/ppermute | solution.py:384
  54.6 19.0 %collective-permute-start.15 = (bf16[1,128,2048]{2,1,0:T(8,128)(2,1)S(1)}, bf16[1,128,2048]{2,1,0:T(8,128)(2,1)S(1)}, u32[]{:S(2)}, u32[]{:S(2)}) collective-permute-start(bf16[1,128,2048]{2,1,0:T(8,128)(2,1)S(1)} %collective-permute-done.11), channel_id=1, source_target_pairs={{8,0},{9,1},{10,2},{11,3},{12,4},{13,5},{14,6},{15,7},{16,24},{17,... | collective-permute-start | bytes 1572872 | tf_op jit(solution)/shard_map/ppermute | solution.py:407
  55.9 19.1 %collective-permute-start.18 = (bf16[2,136,1024]{2,1,0:T(8,128)(2,1)S(1)}, bf16[2,136,1024]{2,1,0:T(8,128)(2,1)S(1)}, u32[]{:S(2)}, u32[]{:S(2)}) collective-permute-start(bf16[2,136,1024]{2,1,0:T(8,128)(2,1)S(1)} %collective-permute-done.14.rest_3_.rest_6_.rest_7_), channel_id=1, source_target_pairs={{0,2},{1,3},{2,0},{3,1},{4,6},{5,7},{6,4},{7,5},{8,10},{9,11},{10,... | collective-permute-start | bytes 1671176 | tf_op jit(solution)/shard_map/ppermute | solution.py:384
  76.6 35.6 %collective-permute-start.21 = (bf16[3,128,2048]{2,1,0:T(8,128)(2,1)}, bf16[3,128,2048]{2,1,0:T(8,128)(2,1)}, u32[]{:S(2)}, u32[]{:S(2)}) collective-permute-start(bf16[3,128,2048]{2,1,0:T(8,128)(2,1)} %pad_maximum_fusion.rest_1_), channel_id=1, source_target_pairs={{0,2},{1,3},{2,0},{3,1},{4,6},{5,7},{6,4},{7,5},{8,10},{9,11},{10,... | collective-permute-start | bytes 4718600 | tf_op jit(solution)/shard_map/ppermute | solution.py:384
  78.1 34.1 %collective-permute-start.22 = (bf16[3,128,2048]{2,1,0:T(8,128)(2,1)}, bf16[3,128,2048]{2,1,0:T(8,128)(2,1)}, u32[]{:S(2)}, u32[]{:S(2)}) collective-permute-start(bf16[3,128,2048]{2,1,0:T(8,128)(2,1)} %pad_maximum_fusion.rest_1_), channel_id=1, source_target_pairs={{0,4},{1,5},{2,6},{3,7},{4,0},{5,1},{6,2},{7,3},{8,12},{9,13},{10,... | collective-permute-start | bytes 4718600 | tf_op jit(solution)/shard_map/ppermute | solution.py:384
  106.3 12.3 %collective-permute-start.24 = (bf16[3,128,2048]{2,1,0:T(8,128)(2,1)}, bf16[3,128,2048]{2,1,0:T(8,128)(2,1)S(1)}, u32[]{:S(2)}, u32[]{:S(2)}) collective-permute-start(bf16[3,128,2048]{2,1,0:T(8,128)(2,1)} %pad_maximum_fusion.rest_1_), channel_id=1, source_target_pairs={{0,1},{1,0},{2,3},{3,2},{4,5},{5,4},{6,7},{7,6},{8,9},{9,8},{10,11... | collective-permute-start | bytes 4718600 | tf_op jit(solution)/shard_map/ppermute | solution.py:389
  117.0 19.8 %collective-permute-start.27 = (bf16[3,64,2048]{2,1,0:T(8,128)(2,1)S(1)}, bf16[3,64,2048]{2,1,0:T(8,128)(2,1)S(1)}, u32[]{:S(2)}, u32[]{:S(2)}) collective-permute-start(bf16[3,64,2048]{2,1,0:T(8,128)(2,1)S(1)} %slice.24), channel_id=1, source_target_pairs={{0,4},{1,5},{2,6},{3,7},{4,0},{5,1},{6,2},{7,3},{8,12},{9,13},{10,... | collective-permute-start | bytes 2359304 | tf_op jit(solution)/shard_map/ppermute | solution.py:384
  118.1 19.5 %collective-permute-start.28 = (bf16[3,64,2048]{2,1,0:T(8,128)(2,1)S(1)}, bf16[3,64,2048]{2,1,0:T(8,128)(2,1)S(1)}, u32[]{:S(2)}, u32[]{:S(2)}) collective-permute-start(bf16[3,64,2048]{2,1,0:T(8,128)(2,1)S(1)} %slice.25), channel_id=1, source_target_pairs={{0,2},{1,3},{2,0},{3,1},{4,6},{5,7},{6,4},{7,5},{8,10},{9,11},{10,... | collective-permute-start | bytes 2359304 | tf_op jit(solution)/shard_map/ppermute | solution.py:384
  118.6 23.9 %collective-permute-start.30 = (bf16[3,128,2048]{2,1,0:T(8,128)(2,1)}, bf16[3,128,2048]{2,1,0:T(8,128)(2,1)S(1)}, u32[]{:S(2)}, u32[]{:S(2)}) collective-permute-start(bf16[3,128,2048]{2,1,0:T(8,128)(2,1)} %collective-permute-done.21.rest_4_), channel_id=1, source_target_pairs={{0,1},{1,0},{2,3},{3,2},{4,5},{5,4},{6,7},{7,6},{8,9},{9,8},{10,11... | collective-permute-start | bytes 4718600 | tf_op jit(solution)/shard_map/ppermute | solution.py:389
  158.4 24.4 %collective-permute-start.35 = (bf16[512,256]{1,0:T(8,128)(2,1)S(1)}, bf16[512,256]{1,0:T(8,128)(2,1)S(1)}, u32[]{:S(2)}, u32[]{:S(2)}) collective-permute-start(bf16[512,256]{1,0:T(8,128)(2,1)S(1)} %get-tuple-element.101), channel_id=1, source_target_pairs={{0,1},{1,0},{2,3},{3,2},{4,5},{5,4},{6,7},{7,6},{8,9},{9,8},{10,11... | collective-permute-start | bytes 786440 | tf_op jit(solution)/shard_map/ppermute | solution.py:389
  158.7 24.7 %collective-permute-start.36 = (bf16[512,256]{1,0:T(8,128)(2,1)S(1)}, bf16[512,256]{1,0:T(8,128)(2,1)S(1)}, u32[]{:S(2)}, u32[]{:S(2)}) collective-permute-start(bf16[512,256]{1,0:T(8,128)(2,1)S(1)} %get-tuple-element.102), channel_id=1, source_target_pairs={{0,2},{1,3},{2,0},{3,1},{4,6},{5,7},{6,4},{7,5},{8,10},{9,11},{10,... | collective-permute-start | bytes 786440 | tf_op jit(solution)/shard_map/ppermute | solution.py:384
  159.3 24.2 %collective-permute-start.37 = (bf16[512,256]{1,0:T(8,128)(2,1)S(1)}, bf16[512,256]{1,0:T(8,128)(2,1)S(1)}, u32[]{:S(2)}, u32[]{:S(2)}) collective-permute-start(bf16[512,256]{1,0:T(8,128)(2,1)S(1)} %get-tuple-element.103), channel_id=1, source_target_pairs={{0,3},{1,2},{2,1},{3,0},{4,7},{5,6},{6,5},{7,4},{8,11},{9,10},{10,... | collective-permute-start | bytes 786440 | tf_op jit(solution)/shard_map/ppermute | solution.py:1196
  200.8 19.2 %collective-permute-start.40 = (bf16[512,256]{1,0:T(8,128)(2,1)}, bf16[512,256]{1,0:T(8,128)(2,1)S(1)}, u32[]{:S(2)}, u32[]{:S(2)}) collective-permute-start(bf16[512,256]{1,0:T(8,128)(2,1)} %get-tuple-element.121), channel_id=1, source_target_pairs={{0,2},{1,3},{2,0},{3,1},{4,6},{5,7},{6,4},{7,5},{8,10},{9,11},{10,... | collective-permute-start | bytes 786440 | tf_op jit(solution)/shard_map/ppermute | solution.py:384
  202.4 17.7 %collective-permute-start.41 = (bf16[512,256]{1,0:T(8,128)(2,1)}, bf16[512,256]{1,0:T(8,128)(2,1)S(1)}, u32[]{:S(2)}, u32[]{:S(2)}) collective-permute-start(bf16[512,256]{1,0:T(8,128)(2,1)} %get-tuple-element.122), channel_id=1, source_target_pairs={{0,3},{1,2},{2,1},{3,0},{4,7},{5,6},{6,5},{7,4},{8,11},{9,10},{10,... | collective-permute-start | bytes 786440 | tf_op jit(solution)/shard_map/ppermute | solution.py:1196
  (66 other events, 615.7 us)

commit v6 on v5

--- a/solution.py
+++ b/solution.py
@@ -801,11 +801,17 @@
     )(idx, attended, tokens, vec, *received, *arrays)
 
 
-def units_main(idx, half_bit, normed, cotangent, weights, bias, bias_other, vec, mine, other, carried, hidden):
+def units_main(idx, normed, cotangent, weights, vec, biases, groups, carried, hidden):
     rows, model = normed.shape
-    sources = [operands(f) for f in (mine, other)]
-    part = sources[0][0][0].shape[2] // 2
-    counts = [len(arrays) for arrays, _ in sources]
+    arrays, entries = operands([e for half_bit, _, found in groups for e in found if e[2] == half_bit])
+    n, count = len(arrays), len(groups)
+    part = arrays[0].shape[2] // 2
+    at_entry = 0
+    tables = []
+    for half_bit, _, found in groups:
+        size = sum(e[2] == half_bit for e in found)
+        tables.append(entries[at_entry : at_entry + size])
+        at_entry += size
     last = hidden is not None
     parts = 4
     piece = model // parts
@@ -814,25 +820,24 @@
     c0 = 0.7978845608028654
     c1 = 0.044715
 
-    def body(ix, normed_ref, cot, weight_ref, bias_ref, bias_other_ref, vec_ref, *rest):
+    def body(ix, normed_ref, cot, weight_ref, vec_ref, bias_ref, bias_other_ref, *rest):
         carry = rest[: len(carried)]
         rest = rest[len(carried) :]
         hid_ref, rest = (rest[0], rest[1:]) if last else (None, rest)
-        msgs = (rest[: counts[0]], rest[counts[0] : sum(counts)])
-        rest = rest[sum(counts) :]
+        msgs, rest = rest[:n], rest[n:]
         n_out = 1 + parts if last else 2
         outs, (w, grad_ref, x_ref, g_ref, pre_ref, act_ref, sems, *held) = rest[:n_out], rest[n_out:]
-        groups = []
+        loads = []
         used = 0
-        for o in range(2):
-            pairs = block_pairs(msgs[o], sources[o][1], w, ix, half_bit, o)
-            groups.append(copies_of(pairs, sems, used))
+        for o in range(count):
+            pairs = block_pairs(msgs, tables[o], w, ix, groups[o][0], o)
+            loads.append(copies_of(pairs, sems, used))
             used += len(pairs)
-        for group in groups:
-            for copy in group:
+        for load in loads:
+            for copy in load:
                 copy.start()
         grad_ref[...] = (cot[...].astype(F32) * weight_ref[:, :1]).astype(BF16)
-        biases = (bias_ref, bias_other_ref)
+        biases_of = (bias_ref, bias_other_ref)
 
         def multiply(o, c, slot):
             x_ref[slot] = jnp.dot(normed_ref[...], w[o, :, at_lanes(c, chunk)], preferred_element_type=F32)
@@ -840,7 +845,8 @@
 
         def bend(o, c, slot):
             at = at_lanes(o * per + c, chunk)
-            x = x_ref[slot] + biases[o][half_bit : half_bit + 1, at_lanes(c, chunk)]
+            half_bit, core_bit, _ = groups[o]
+            x = x_ref[slot] + biases_of[core_bit][half_bit : half_bit + 1, at_lanes(c, chunk)]
             sq = x * x
             th = jnp.tanh(c0 * x * (1.0 + c1 * sq))
             left = 0.5 * (1.0 + th)
@@ -848,37 +854,30 @@
             pre_ref[:, at] = (slope * g_ref[slot]).astype(BF16)
             act_ref[:, at] = (x * left).astype(BF16)
 
-        for o in range(2):
-            for copy in groups[o]:
+        for o in range(count):
+            for copy in loads[o]:
                 copy.wait()
-            if o == 0:
-                multiply(0, 0, 0)
-
-                def step(c, _):
-                    multiply(0, c, lax.rem(c, 2))
-                    bend(0, c - 1, lax.rem(c + 1, 2))
-                    return 0
-
-                lax.fori_loop(1, per, step, 0)
-            else:
-                multiply(1, 0, 0)
-                bend(0, per - 1, (per - 1) % 2)
-
-                def step(c, _):
-                    multiply(1, c, lax.rem(c, 2))
-                    bend(1, c - 1, lax.rem(c + 1, 2))
-                    return 0
-
-                lax.fori_loop(1, per, step, 0)
-                bend(1, per - 1, (per - 1) % 2)
+            multiply(o, 0, 0)
+            if o:
+                bend(o - 1, per - 1, (per - 1) % 2)
+
+            def step(c, _, o=o):
+                multiply(o, c, lax.rem(c, 2))
+                bend(o, c - 1, lax.rem(c + 1, 2))
+                return 0
+
+            lax.fori_loop(1, per, step, 0)
+        bend(count - 1, per - 1, (per - 1) % 2)
 
         def mid_of(n):
             at = at_rows(n, BLK)
             lanes = at_lanes(n, BLK)
-            mid = lax.dot_general(pre_ref[:, :part], w[0, at, :part], NT, preferred_element_type=F32)
-            mid = mid + lax.dot_general(pre_ref[:, part:], w[1, at, :part], NT, preferred_element_type=F32)
-            unit = lax.dot_general(act_ref[:, :part], w[0, at, part:], NT, preferred_element_type=F32)
-            unit = unit + lax.dot_general(act_ref[:, part:], w[1, at, part:], NT, preferred_element_type=F32)
+            mid = jnp.zeros((rows, BLK), F32)
+            unit = jnp.zeros((rows, BLK), F32)
+            for o in range(count):
+                cols = slice(o * part, (o + 1) * part)
+                mid = mid + lax.dot_general(pre_ref[:, cols], w[o, at, :part], NT, preferred_element_type=F32)
+                unit = unit + lax.dot_general(act_ref[:, cols], w[o, at, part:], NT, preferred_element_type=F32)
             if carry:
                 mid = mid + carry[0][:, lanes].astype(F32)
                 unit = unit + carry[1][:, lanes].astype(F32)
@@ -922,9 +921,9 @@
         block,
         block,
         full(rows, LANES),
+        full(8, model),
         full(2, part),
         full(2, part),
-        full(8, model),
     ]
     specs += [block] * (len(carried) + (1 if last else 0))
     if last:
@@ -933,26 +932,25 @@
     else:
         out_specs = [block, block]
         out_shape = [shape(rows, model)] * 2
-    arrays = [array for found, _ in sources for array in found]
     return call(
         body,
-        "units_main_last" if last else "units_main_first",
+        "units_main_last" if last else "units_main_first" if not carried else "units_main_next",
         1,
         specs + [ANY] * len(arrays),
         out_specs,
         out_shape,
         [
-            pltpu.VMEM((2, model, 2 * part), BF16),
+            pltpu.VMEM((count, model, 2 * part), BF16),
             pltpu.VMEM((rows, model), BF16),
             pltpu.VMEM((2, rows, chunk), F32),
             pltpu.VMEM((2, rows, chunk), F32),
-            pltpu.VMEM((rows, 2 * part), BF16),
-            pltpu.VMEM((rows, 2 * part), BF16),
-            pltpu.SemaphoreType.DMA((sum(len(table) for _, table in sources),)),
+            pltpu.VMEM((rows, count * part), BF16),
+            pltpu.VMEM((rows, count * part), BF16),
+            pltpu.SemaphoreType.DMA((len(entries),)),
         ]
         + ([pltpu.VMEM((rows, model), BF16), pltpu.VMEM((rows, model), F32)] if last else []),
-        cost(16 * rows * part * model, 12 * part * model, 2 * rows * part),
-    )(idx, normed, cotangent, weights, bias, bias_other, vec, *carried, *((hidden,) if last else ()), *arrays)
+        cost(8 * count * rows * part * model, 8 * count * part * model, count * rows * part),
+    )(idx, normed, cotangent, weights, vec, *biases, *carried, *((hidden,) if last else ()), *arrays)
 
 
 def attend_back_fast(
@@ -1256,13 +1254,13 @@
     fc_other = core_swap(fc_mine)
     down8 = down_master.reshape(2 * r, model)
     normed, latent, down = norm_rows(idx, after(tokens, hx_far, tok_own, cot_own), vec, down8)
-    ux, uy = pair_xy(after(u_rest, hd_far, ud0))
+    ux, uy = pair_xy(after(u_rest, hd_far))
     ready = after(normed, u_rest, ud0, weights)
     queries, keys, values, up = project_heads(idx, ready, latent, frozen_triple_bias, up_rows, hx_near, heads)
     mixed, logsum = attend_fast(queries, keys, values)
     sent = [core_swap(v) for v in attention_out_send(idx, mixed, heads, heads_cols)]
     hidden, normed_mid = attention_out_own(idx, mixed, sent, tok_own, vec, heads, heads_cols)
-    rows = (normed_mid, cot_own, weights, fc_mine, fc_other, vec)
+    rows = (normed_mid, cot_own, weights, vec, (fc_mine, fc_other))
     ux, uy, _ = lax.optimization_barrier((ux, uy, normed_mid))
     cut = step_rows // 2
     ud_low, ud_high = hop(ux[:, :cut], 0, 1), hop(uy[:, cut:], 1, 0)
@@ -1275,14 +1273,18 @@
         return found
 
     swap = lambda *arrays: [core_swap(v) for v in arrays]
+    corner = lambda v, low, high: table(1, 1, v) + blocks_of(low, 1, 1, 1) + blocks_of(high, 1, 1, 1, cut)
     first_mine = table(0, 0, u_own, u_rest) + table(0, 1, uy0, uy)
     first_other = table(0, 0, *swap(u_own, u_rest)) + table(0, 1, *swap(uy0, uy))
-    carried = units_main(idx, 0, *rows, first_mine, first_other, (), None)
-    ud_low, ud_high, _ = lax.optimization_barrier((ud_low, ud_high, carried[0]))
-    corner = lambda v, low, high: table(1, 1, v) + blocks_of(low, 1, 1, 1) + blocks_of(high, 1, 1, 1, cut)
+    carried = units_main(idx, *rows, [(0, 0, first_mine), (0, 1, first_other)], (), None)
+    ud_low, ud_high, ux0_late, ux_late, ud0_late, _ = lax.optimization_barrier(
+        (ud_low, ud_high, ux0, ux, ud0, carried[0])
+    )
     last_mine = table(1, 0, ux0, ux) + corner(ud0, ud_low, ud_high)
-    last_other = table(1, 0, *swap(ux0, ux)) + corner(*swap(ud0, ud_low, ud_high))
-    hidden_low, *out_pieces = units_main(idx, 1, *rows, last_mine, last_other, carried, hidden)
+    last_other = table(1, 0, *swap(ux0_late, ux_late)) + corner(*swap(ud0_late, ud_low, ud_high))
+    carried = units_main(idx, *rows, [(1, 0, last_mine)], carried, None)
+    groups = [(1, 1, last_other)]
+    hidden_low, *out_pieces = units_main(idx, *rows, groups, carried, hidden)
     hidden_other = core_swap(hidden_low)
     out_pieces = exchange_features(out_pieces)
     dq, dk, dv, latent_low, down_term, up_q, up_v = attend_back_fast(

time: 224 us -> 215 us (0.960)
  waiting for transfers between devices: 60.8 us -> 55.2 us
    ppermute x21, waiting for transfers between devices: 32.4 us -> 27 us  [hop(): return lax.ppermute(value, AXES, [(i, i ^ flip) for i in range(total)])]
    unnamed x89 -> x79, local copies, waits for them, and re-layouts: 7.93 us -> 6.28 us
    pallas_call x2 -> x3, Pallas kernels: 30 us -> 31.4 us  [units_main(): call(body, 'units_main_last' if last else 'units_main_first' if not carri...]
  transfers between devices with their start and end apart: 47 -> 47, of which waited for: 22 -> 21; matrix products, arithmetic and copies ran while one was open for 4% -> 4% of each run, Pallas kernels for 31% -> 36%
where the time goes in v6:
time: 215 us
  Pallas kernels  97 us (45%)
  waiting for transfers between devices  55.2 us (26%)
  starting transfers between devices  43 us (20%)
  local copies, waits for them, and re-layouts  12.9 us (6%)
  other arithmetic  4.54 us (2%)
  between operations  2.25 us (1%)
    pallas_call x3, Pallas kernels, units_main(): call(body, 'units_main_last' if last else 'units_main_first' if not carri...  31.4 us
    ppermute x21, starting transfers between devices, hop(): return lax.ppermute(value, AXES, [(i, i ^ flip) for i in range(total)])  30.1 us
    ppermute x21, waiting for transfers between devices, hop(): return lax.ppermute(value, AXES, [(i, i ^ flip) for i in range(total)])  27 us
    pallas_call x1, Pallas kernels, attend_back_fast(): call(body, 'attend_back', pairs, [spec] * 4 + [full(half, model)] * 2 + [...  21.5 us
    ppermute x8, waiting for transfers between devices, z_hop(): return lax.ppermute(value, AXES, perm)  19.7 us
    pallas_call x1, Pallas kernels, attend_fast(): pl.pallas_call(body, grid=(pairs,), out_shape=(shape(length, width), jax....  11 us
    ppermute x16, waiting for transfers between devices, core_swap(): return lax.ppermute(value, AXES, [(i, i ^ 1) for i in range(total)])  8.53 us
    ppermute x8, starting transfers between devices, z_hop(): return lax.ppermute(value, AXES, perm)  7.87 us
  transfers between devices with their start and end apart: 47, of which 21 were waited for; matrix products, arithmetic and copies ran while one was open for 4% of the time, Pallas kernels for 36%

profile of v6, /device:TPU:0, one launch (start us, length us, event | category | flops | bytes accessed | tf_op | source)
XLA Modules:
  0.0 214.9 jit_solution(4396891955650825319)
XLA Ops:
  4.3 3.3 %prepare_blocks.1 = (bf16[136,1024]{1,0:T(8,128)(2,1)}, bf16[1,128,2048]{2,1,0:T(8,128)(2,1)}) custom-call(s32[3]{0:T(128)} %pad_add_fusion.ix, s32[16,128]{1,0:T(8,128)} %bitcast.21, bf16[128,3,256]{2,1,0:T(4,128)(2,1)} %copy.32.triple_ref, bf16[256,128]{1,0:T(8,128)(2,1)} %out_ref.1, bf16[3,256]{1,0:T(4,128)(2,1)} %bias_ref.3, ...), custom_call_target="tpu_custom_call" | custom-call | bytes 52428 | tf_op jit(solution)/shard_map/prepare_blocks/pallas_call | solution.py:548
  7.6 3.0 %collective-permute-start = (bf16[136,1024]{1,0:T(8,128)(2,1)}, bf16[136,1024]{1,0:T(8,128)(2,1)S(1)}, u32[]{:S(2)}, u32[]{:S(2)}) collective-permute-start(bf16[136,1024]{1,0:T(8,128)(2,1)} %get-tuple-element.74), channel_id=1, source_target_pairs={{0,8},{1,9},{2,10},{3,11},{4,12},{5,13},{6,14},{7,15},{8,0},{9,1},... | collective-permute-start | bytes 835592 | tf_op jit(solution)/shard_map/ppermute | solution.py:384
  14.4 3.1 %collective-permute-done = bf16[136,1024]{1,0:T(8,128)(2,1)S(1)} collective-permute-done((bf16[136,1024]{1,0:T(8,128)(2,1)}, bf16[136,1024]{1,0:T(8,128)(2,1)S(1)}, u32[]{:S(2)}, u32[]{:S(2)}) %collective-permute-start) | collective-permute-done | bytes 278560 | tf_op jit(solution)/shard_map/ppermute | solution.py:384
  21.8 3.2 %collective-permute-done.5.rest_2_ = bf16[1,128,2048]{2,1,0:T(8,128)(2,1)} collective-permute-done((bf16[1,128,2048]{2,1,0:T(8,128)(2,1)}, bf16[1,128,2048]{2,1,0:T(8,128)(2,1)}, u32[]{:S(2)}, u32[]{:S(2)}) %collective-permute-start.5) | collective-permute-done | bytes 524320 | tf_op jit(solution)/shard_map/ppermute | solution.py:384
  30.3 5.3 %collective-permute-done.4 = bf16[136,1024]{1,0:T(8,128)(2,1)S(1)} collective-permute-done((bf16[136,1024]{1,0:T(8,128)(2,1)S(1)}, bf16[136,1024]{1,0:T(8,128)(2,1)S(1)}, u32[]{:S(2)}, u32[]{:S(2)}) %collective-permute-start.4) | collective-permute-done | bytes 278560 | tf_op jit(solution)/shard_map/ppermute | solution.py:407
  36.5 2.7 %collective-permute-done.7.rest_4_.near_ref.rest_1_.rest_2_ = bf16[2,136,1024]{2,1,0:T(8,128)(2,1)S(1)} collective-permute-done((bf16[2,136,1024]{2,1,0:T(8,128)(2,1)S(1)}, bf16[2,136,1024]{2,1,0:T(8,128)(2,1)S(1)}, u32[]{:S(2)}, u32[]{:S(2)}) %collective-permute-start.7) | collective-permute-done | bytes 557088 | tf_op jit(solution)/shard_map/ppermute | solution.py:384
  42.6 5.2 %collective-permute-done.10 = bf16[1,128,2048]{2,1,0:T(8,128)(2,1)S(1)} collective-permute-done((bf16[1,128,2048]{2,1,0:T(8,128)(2,1)S(1)}, bf16[1,128,2048]{2,1,0:T(8,128)(2,1)S(1)}, u32[]{:S(2)}, u32[]{:S(2)}) %collective-permute-start.10) | collective-permute-done | bytes 524320 | tf_op jit(solution)/shard_map/ppermute | solution.py:384
  49.8 2.6 %collective-permute-done.14.rest_3_.rest_6_.rest_7_ = bf16[2,136,1024]{2,1,0:T(8,128)(2,1)S(1)} collective-permute-done((bf16[2,136,1024]{2,1,0:T(8,128)(2,1)S(1)}, bf16[2,136,1024]{2,1,0:T(8,128)(2,1)S(1)}, u32[]{:S(2)}, u32[]{:S(2)}) %collective-permute-start.14) | collective-permute-done | bytes 557088 | tf_op jit(solution)/shard_map/ppermute | solution.py:384
  56.8 5.0 %collective-permute-done.13 = bf16[1,128,2048]{2,1,0:T(8,128)(2,1)S(1)} collective-permute-done((bf16[1,128,2048]{2,1,0:T(8,128)(2,1)S(1)}, bf16[1,128,2048]{2,1,0:T(8,128)(2,1)S(1)}, u32[]{:S(2)}, u32[]{:S(2)}) %collective-permute-start.13) | collective-permute-done | bytes 524320 | tf_op jit(solution)/shard_map/ppermute | solution.py:407
  66.5 7.4 %collective-permute-done.15 = bf16[1,128,2048]{2,1,0:T(8,128)(2,1)S(1)} collective-permute-done((bf16[1,128,2048]{2,1,0:T(8,128)(2,1)S(1)}, bf16[1,128,2048]{2,1,0:T(8,128)(2,1)S(1)}, u32[]{:S(2)}, u32[]{:S(2)}) %collective-permute-start.15) | collective-permute-done | bytes 524320 | tf_op jit(solution)/shard_map/ppermute | solution.py:407
  83.5 3.0 %norm_rows.1 = (bf16[1024,1024]{1,0:T(8,128)(2,1)S(1)}, bf16[1024,128]{1,0:T(8,128)(2,1)S(1)}, bf16[128,1024]{1,0:T(8,128)(2,1)S(1)}) custom-call(s32[3]{0:T(128)S(1)} %copy-done.20, bf16[2048,1024]{1,0:T(8,128)(2,1)S(1)} %copy-done.5, f32[8,1024]{1,0:T(8,128)S(1)} %convert_element_type.10.vec_ref, f32[8,1024]{1,0:T(8,128)S(1)} %reshape.52.down_ref), custom_call_target="tpu_custom_call" | custom-call | flops 26843544 | bytes 419430 | tf_op jit(solution)/shard_map/norm_rows/pallas_call | solution.py:620
  86.6 6.2 %project_heads.1 = (bf16[1024,512]{1,0:T(8,128)(2,1)S(1)}, bf16[1024,512]{1,0:T(8,128)(2,1)S(1)}, bf16[1024,512]{1,0:T(8,128)(2,1)S(1)}, bf16[2,128,768]{2,1,0:T(8,128)(2,1)S(1)}) custom-call(s32[3]{0:T(128)S(1)} %copy-done.20, bf16[1024,1024]{1,0:T(8,128)(2,1)S(1)} %get-tuple-element.85.normed_ref, bf16[1024,128]{1,0:T(8,128)(2,1)S(1)} %get-tuple-element.86.latent_ref, ...), custom_call_target="tpu_custom_call" | custom-call | flops 322122560 | bytes 1677721 | tf_op jit(solution)/shard_map/project_heads/pallas_call | solution.py:669
  92.7 11.0 %attend.1 = (bf16[1024,512]{1,0:T(8,128)(2,1)S(1)}, f32[4,8,1024]{2,1,0:T(8,128)S(1)}) custom-call(bf16[1024,512]{1,0:T(8,128)(2,1)S(1)} %get-tuple-element.87.q_ref, bf16[1024,512]{1,0:T(8,128)(2,1)S(1)} %get-tuple-element.88.k_ref, bf16[1024,512]{1,0:T(8,128)(2,1)S(1)} %get-tuple-element.89.v_ref), custom_call_target="tpu_custom_call" | custom-call | flops 429496736 | bytes 419430 | tf_op jit(solution)/shard_map/attend/pallas_call | solution.py:718
  106.2 2.9 %collective-permute-done.19.rest_0_ = bf16[512,1024]{1,0:T(8,128)(2,1)S(1)} collective-permute-done((bf16[512,1024]{1,0:T(8,128)(2,1)S(1)}, bf16[512,1024]{1,0:T(8,128)(2,1)S(1)}, u32[]{:S(2)}, u32[]{:S(2)}) %collective-permute-start.19) | collective-permute-done | bytes 1048608 | tf_op jit(solution)/shard_map/ppermute | solution.py:389
  109.1 2.5 %attention_out_own.1 = (f32[512,1024]{1,0:T(8,128)S(1)}, bf16[512,1024]{1,0:T(8,128)(2,1)S(1)}) custom-call(s32[3]{0:T(128)S(1)} %copy-done.20, bf16[1024,512]{1,0:T(8,128)(2,1)S(1)} %get-tuple-element.90.att.o_ref, bf16[512,1024]{1,0:T(8,128)(2,1)S(1)} %constant_dynamic-slice_fusion.1.tok, f32[8,1024]{1,0:T(8,128)S(1)} %convert_element_type.10.vec_ref, ...), custom_call_target="tpu_custom_call" | custom-call | flops 53687092 | bytes 524288 | tf_op jit(solution)/shard_map/attention_out_own/pallas_call | solution.py:786
  119.8 14.4 %units_main_first.1 = (bf16[512,1024]{1,0:T(8,128)(2,1)S(1)}, bf16[512,1024]{1,0:T(8,128)(2,1)S(1)}) custom-call(s32[3]{0:T(128)S(1)} %copy-done.20, bf16[512,1024]{1,0:T(8,128)(2,1)S(1)} %get-tuple-element.91.normed_ref, bf16[512,1024]{1,0:T(8,128)(2,1)S(1)} %constant_dynamic-slice_fusion.cot, f32[512,128]{1,0:T(8,128)S(1)} %get-tuple-element.84.weight_ref, ...), custom_call_target="tpu_custom_call" | custom-call | flops 858993472 | bytes 1677721 | tf_op jit(solution)/shard_map/units_main_first/pallas_call | solution.py:935
  136.1 8.1 %units_main_next.1 = (bf16[512,1024]{1,0:T(8,128)(2,1)S(1)}, bf16[512,1024]{1,0:T(8,128)(2,1)S(1)}) custom-call(s32[3]{0:T(128)S(1)} %copy-done.20, bf16[512,1024]{1,0:T(8,128)(2,1)S(1)} %get-tuple-element.91.normed_ref, bf16[512,1024]{1,0:T(8,128)(2,1)S(1)} %constant_dynamic-slice_fusion.cot, f32[512,128]{1,0:T(8,128)S(1)} %get-tuple-element.84.weight_ref, ...), custom_call_target="tpu_custom_call" | custom-call | flops 429496736 | bytes 838860 | tf_op jit(solution)/shard_map/units_main_next/pallas_call | solution.py:935
  144.3 9.0 %units_main_last.1 = (bf16[512,1024]{1,0:T(8,128)(2,1)S(1)}, bf16[512,256]{1,0:T(8,128)(2,1)S(1)}, bf16[512,256]{1,0:T(8,128)(2,1)S(1)}, bf16[512,256]{1,0:T(8,128)(2,1)S(1)}, bf16[512,256]{1,0:T(8,128)(2,1)S(1)}) custom-call(s32[3]{0:T(128)S(1)} %copy-done.20, bf16[512,1024]{1,0:T(8,128)(2,1)S(1)} %get-tuple-element.91.normed_ref, ...), custom_call_target="tpu_custom_call" | custom-call | flops 429496736 | bytes 838860 | tf_op jit(solution)/shard_map/units_main_last/pallas_call | solution.py:935
  156.8 21.5 %attend_back.1 = (bf16[1024,512]{1,0:T(8,128)(2,1)S(1)}, bf16[1024,512]{1,0:T(8,128)(2,1)S(1)}, bf16[1024,512]{1,0:T(8,128)(2,1)S(1)}, bf16[1024,128]{1,0:T(8,12...) custom-call(s32[3]{0:T(128)S(1)} %copy-done.20, ...), custom_call_target="tpu_custom_call" | custom-call | flops 1073741824 | bytes 838860 | tf_op jit(solution)/shard_map/attend_back/pallas_call | solution.py:1052
  178.4 6.9 %heads_back.1 = (bf16[512,1024]{1,0:T(8,128)(2,1)}, bf16[512,1024]{1,0:T(8,128)(2,1)S(1)}) custom-call(s32[3]{0:T(128)S(1)} %copy-done.20, bf16[1024,512]{1,0:T(8,128)(2,1)S(1)} %get-tuple-element.118.dq_ref, bf16[1024,512]{1,0:T(8,128)(2,1)S(1)} %get-tuple-element.119.dk_ref, bf16[1024,512]{1,0:T(8,128)(2,1)S(1)} %get-tuple-element.120.dv_ref, ...), custom_call_target="tpu_custom_call" | custom-call | flops 322122560 | bytes 314572 | tf_op jit(solution)/shard_map/heads_back/pallas_call | solution.py:1120
  190.7 5.0 %tokens_back.1 = (bf16[512,256]{1,0:T(8,128)(2,1)}, bf16[512,256]{1,0:T(8,128)(2,1)}, bf16[512,256]{1,0:T(8,128)(2,1)}, bf16[512,256]{1,0:T(8,128)(2,1)}) custom-call(s32[3]{0:T(128)} %pad_add_fusion.ix, bf16[512,1024]{1,0:T(8,128)(2,1)} %copy-done.8, bf16[512,1024]{1,0:T(8,128)(2,1)} %copy-done.25, bf16[512,1024]{1,0:T(8,128)(2,1)} %copy-done.4, ...), custom_call_target="tpu_custom_call" | custom-call | flops 2097152 | bytes 838860 | tf_op jit(solution)/shard_map/tokens_back/pallas_call | solution.py:1150
  198.5 3.2 %collective-permute-done.44 = f32[8,1280]{1,0:T(8,128)S(1)} collective-permute-done((f32[8,1280]{1,0:T(8,128)S(1)}, f32[8,1280]{1,0:T(8,128)S(1)}, u32[]{:S(2)}, u32[]{:S(2)}) %collective-permute-start.44) | collective-permute-done | bytes 40992 | tf_op jit(solution)/shard_map/ppermute | solution.py:384
  201.8 2.5 %collective-permute-start.45 = (f32[8,1280]{1,0:T(8,128)S(1)}, f32[8,1280]{1,0:T(8,128)S(1)}, u32[]{:S(2)}, u32[]{:S(2)}) collective-permute-start(f32[8,1280]{1,0:T(8,128)S(1)} %add.63), channel_id=1, source_target_pairs={{0,8},{1,9},{2,10},{3,11},{4,12},{5,13},{6,14},{7,15},{8,0},{9,1},... | collective-permute-start | bytes 122888 | tf_op jit(solution)/shard_map/ppermute | solution.py:384
  206.2 3.2 %collective-permute-start.46 = (f32[8,1280]{1,0:T(8,128)S(1)}, f32[8,1280]{1,0:T(8,128)S(1)}, u32[]{:S(2)}, u32[]{:S(2)}) collective-permute-start(f32[8,1280]{1,0:T(8,128)S(1)} %add.64), channel_id=1, source_target_pairs={{0,16},{1,17},{2,18},{3,19},{4,20},{5,21},{6,22},{7,23},{8,24},{9,... | collective-permute-start | bytes 122888 | tf_op jit(solution)/shard_map/ppermute | solution.py:384
  (207 shorter events, 72.5 us)
Async XLA Ops:
  11.3 13.8 %collective-permute-start.5 = (bf16[1,128,2048]{2,1,0:T(8,128)(2,1)}, bf16[1,128,2048]{2,1,0:T(8,128)(2,1)}, u32[]{:S(2)}, u32[]{:S(2)}) collective-permute-start(bf16[1,128,2048]{2,1,0:T(8,128)(2,1)} %get-tuple-element.80.rest_0_), channel_id=1, source_target_pairs={{0,2},{1,3},{2,0},{3,1},{4,6},{5,7},{6,4},{7,5},{8,10},{9,11},{10,... | collective-permute-start | bytes 1572872 | tf_op jit(solution)/shard_map/ppermute | solution.py:384
  12.9 13.4 %collective-permute-start.6 = (bf16[1,128,2048]{2,1,0:T(8,128)(2,1)}, bf16[1,128,2048]{2,1,0:T(8,128)(2,1)}, u32[]{:S(2)}, u32[]{:S(2)}) collective-permute-start(bf16[1,128,2048]{2,1,0:T(8,128)(2,1)} %get-tuple-element.80.rest_0_), channel_id=1, source_target_pairs={{0,4},{1,5},{2,6},{3,7},{4,0},{5,1},{6,2},{7,3},{8,12},{9,13},{10,... | collective-permute-start | bytes 1572872 | tf_op jit(solution)/shard_map/ppermute | solution.py:384
  18.2 12.1 %collective-permute-start.3 = (bf16[136,1024]{1,0:T(8,128)(2,1)S(1)}, bf16[136,1024]{1,0:T(8,128)(2,1)S(1)}, u32[]{:S(2)}, u32[]{:S(2)}) collective-permute-start(bf16[136,1024]{1,0:T(8,128)(2,1)S(1)} %collective-permute-done.2), channel_id=1, source_target_pairs={{8,0},{9,1},{10,2},{11,3},{12,4},{13,5},{14,6},{15,7},{16,24},{17,... | collective-permute-start | bytes 835592 | tf_op jit(solution)/shard_map/ppermute | solution.py:407
  19.5 16.1 %collective-permute-start.4 = (bf16[136,1024]{1,0:T(8,128)(2,1)S(1)}, bf16[136,1024]{1,0:T(8,128)(2,1)S(1)}, u32[]{:S(2)}, u32[]{:S(2)}) collective-permute-start(bf16[136,1024]{1,0:T(8,128)(2,1)S(1)} %collective-permute-done.1), channel_id=1, source_target_pairs={{8,0},{9,1},{10,2},{11,3},{12,4},{13,5},{14,6},{15,7},{16,24},{17,... | collective-permute-start | bytes 835592 | tf_op jit(solution)/shard_map/ppermute | solution.py:407
  26.3 12.9 %collective-permute-start.7 = (bf16[2,136,1024]{2,1,0:T(8,128)(2,1)S(1)}, bf16[2,136,1024]{2,1,0:T(8,128)(2,1)S(1)}, u32[]{:S(2)}, u32[]{:S(2)}) collective-permute-start(bf16[2,136,1024]{2,1,0:T(8,128)(2,1)S(1)} %pad_maximum_fusion.2.rest_0_.rest_1_), channel_id=1, source_target_pairs={{0,2},{1,3},{2,0},{3,1},{4,6},{5,7},{6,4},{7,5},{8,10},{9,11},{10,... | collective-permute-start | bytes 1671176 | tf_op jit(solution)/shard_map/ppermute | solution.py:384
  26.8 12.8 %collective-permute-start.8 = (bf16[2,136,1024]{2,1,0:T(8,128)(2,1)S(1)}, bf16[2,136,1024]{2,1,0:T(8,128)(2,1)S(1)}, u32[]{:S(2)}, u32[]{:S(2)}) collective-permute-start(bf16[2,136,1024]{2,1,0:T(8,128)(2,1)S(1)} %pad_maximum_fusion.2.rest_0_.rest_1_), channel_id=1, source_target_pairs={{0,4},{1,5},{2,6},{3,7},{4,0},{5,1},{6,2},{7,3},{8,12},{9,13},{10,... | collective-permute-start | bytes 1671176 | tf_op jit(solution)/shard_map/ppermute | solution.py:384
  35.7 12.1 %collective-permute-start.10 = (bf16[1,128,2048]{2,1,0:T(8,128)(2,1)S(1)}, bf16[1,128,2048]{2,1,0:T(8,128)(2,1)S(1)}, u32[]{:S(2)}, u32[]{:S(2)}) collective-permute-start(bf16[1,128,2048]{2,1,0:T(8,128)(2,1)S(1)} %copy-done.9), channel_id=1, source_target_pairs={{0,8},{1,9},{2,10},{3,11},{4,12},{5,13},{6,14},{7,15},{8,0},{9,1},... | collective-permute-start | bytes 1572872 | tf_op jit(solution)/shard_map/ppermute | solution.py:384
  35.8 12.7 %collective-permute-start.12 = (bf16[1,128,2048]{2,1,0:T(8,128)(2,1)S(1)}, bf16[1,128,2048]{2,1,0:T(8,128)(2,1)S(1)}, u32[]{:S(2)}, u32[]{:S(2)}) collective-permute-start(bf16[1,128,2048]{2,1,0:T(8,128)(2,1)S(1)} %copy-done.9), channel_id=1, source_target_pairs={{8,16},{9,17},{10,18},{11,19},{12,20},{13,21},{14,22},{15,23},{16,... | collective-permute-start | bytes 1572872 | tf_op jit(solution)/shard_map/ppermute | solution.py:407
  39.6 12.8 %collective-permute-start.14 = (bf16[2,136,1024]{2,1,0:T(8,128)(2,1)S(1)}, bf16[2,136,1024]{2,1,0:T(8,128)(2,1)S(1)}, u32[]{:S(2)}, u32[]{:S(2)}) collective-permute-start(bf16[2,136,1024]{2,1,0:T(8,128)(2,1)S(1)} %pad_maximum_fusion.1.rest_1_.rest_4_.rest_5_), channel_id=1, source_target_pairs={{0,4},{1,5},{2,6},{3,7},{4,0},{5,1},{6,2},{7,3},{8,12},{9,13},{10,... | collective-permute-start | bytes 1671176 | tf_op jit(solution)/shard_map/ppermute | solution.py:384
  41.1 12.8 %collective-permute-start.9 = (bf16[2,136,1024]{2,1,0:T(8,128)(2,1)S(1)}, bf16[2,136,1024]{2,1,0:T(8,128)(2,1)S(1)}, u32[]{:S(2)}, u32[]{:S(2)}) collective-permute-start(bf16[2,136,1024]{2,1,0:T(8,128)(2,1)S(1)} %pad_maximum_fusion.1.rest_1_.rest_4_.rest_5_), channel_id=1, source_target_pairs={{0,2},{1,3},{2,0},{3,1},{4,6},{5,7},{6,4},{7,5},{8,10},{9,11},{10,... | collective-permute-start | bytes 1671176 | tf_op jit(solution)/shard_map/ppermute | solution.py:384
  48.5 13.3 %collective-permute-start.13 = (bf16[1,128,2048]{2,1,0:T(8,128)(2,1)S(1)}, bf16[1,128,2048]{2,1,0:T(8,128)(2,1)S(1)}, u32[]{:S(2)}, u32[]{:S(2)}) collective-permute-start(bf16[1,128,2048]{2,1,0:T(8,128)(2,1)S(1)} %collective-permute-done.12), channel_id=1, source_target_pairs={{8,0},{9,1},{10,2},{11,3},{12,4},{13,5},{14,6},{15,7},{16,24},{17,... | collective-permute-start | bytes 1572872 | tf_op jit(solution)/shard_map/ppermute | solution.py:407
  53.9 20.0 %collective-permute-start.15 = (bf16[1,128,2048]{2,1,0:T(8,128)(2,1)S(1)}, bf16[1,128,2048]{2,1,0:T(8,128)(2,1)S(1)}, u32[]{:S(2)}, u32[]{:S(2)}) collective-permute-start(bf16[1,128,2048]{2,1,0:T(8,128)(2,1)S(1)} %collective-permute-done.11), channel_id=1, source_target_pairs={{8,0},{9,1},{10,2},{11,3},{12,4},{13,5},{14,6},{15,7},{16,24},{17,... | collective-permute-start | bytes 1572872 | tf_op jit(solution)/shard_map/ppermute | solution.py:407
  55.2 20.2 %collective-permute-start.18 = (bf16[2,136,1024]{2,1,0:T(8,128)(2,1)S(1)}, bf16[2,136,1024]{2,1,0:T(8,128)(2,1)S(1)}, u32[]{:S(2)}, u32[]{:S(2)}) collective-permute-start(bf16[2,136,1024]{2,1,0:T(8,128)(2,1)S(1)} %collective-permute-done.14.rest_3_.rest_6_.rest_7_), channel_id=1, source_target_pairs={{0,2},{1,3},{2,0},{3,1},{4,6},{5,7},{6,4},{7,5},{8,10},{9,11},{10,... | collective-permute-start | bytes 1671176 | tf_op jit(solution)/shard_map/ppermute | solution.py:384
  65.0 21.5 %collective-permute-start.17 = (bf16[1,128,2048]{2,1,0:T(8,128)(2,1)}, bf16[1,128,2048]{2,1,0:T(8,128)(2,1)}, u32[]{:S(2)}, u32[]{:S(2)}) collective-permute-start(bf16[1,128,2048]{2,1,0:T(8,128)(2,1)} %collective-permute-done.5.rest_2_), channel_id=1, source_target_pairs={{0,4},{1,5},{2,6},{3,7},{4,0},{5,1},{6,2},{7,3},{8,12},{9,13},{10,... | collective-permute-start | bytes 1572872 | tf_op jit(solution)/shard_map/ppermute | solution.py:384
  76.2 35.4 %collective-permute-start.21 = (bf16[3,128,2048]{2,1,0:T(8,128)(2,1)}, bf16[3,128,2048]{2,1,0:T(8,128)(2,1)}, u32[]{:S(2)}, u32[]{:S(2)}) collective-permute-start(bf16[3,128,2048]{2,1,0:T(8,128)(2,1)} %pad_maximum_fusion.rest_1_), channel_id=1, source_target_pairs={{0,2},{1,3},{2,0},{3,1},{4,6},{5,7},{6,4},{7,5},{8,10},{9,11},{10,... | collective-permute-start | bytes 4718600 | tf_op jit(solution)/shard_map/ppermute | solution.py:384
  77.7 33.9 %collective-permute-start.22 = (bf16[3,128,2048]{2,1,0:T(8,128)(2,1)}, bf16[3,128,2048]{2,1,0:T(8,128)(2,1)}, u32[]{:S(2)}, u32[]{:S(2)}) collective-permute-start(bf16[3,128,2048]{2,1,0:T(8,128)(2,1)} %pad_maximum_fusion.rest_1_), channel_id=1, source_target_pairs={{0,4},{1,5},{2,6},{3,7},{4,0},{5,1},{6,2},{7,3},{8,12},{9,13},{10,... | collective-permute-start | bytes 4718600 | tf_op jit(solution)/shard_map/ppermute | solution.py:384
  105.7 14.1 %collective-permute-start.24 = (bf16[3,128,2048]{2,1,0:T(8,128)(2,1)}, bf16[3,128,2048]{2,1,0:T(8,128)(2,1)S(1)}, u32[]{:S(2)}, u32[]{:S(2)}) collective-permute-start(bf16[3,128,2048]{2,1,0:T(8,128)(2,1)} %pad_maximum_fusion.rest_1_), channel_id=1, source_target_pairs={{0,1},{1,0},{2,3},{3,2},{4,5},{5,4},{6,7},{7,6},{8,9},{9,8},{10,11... | collective-permute-start | bytes 4718600 | tf_op jit(solution)/shard_map/ppermute | solution.py:389
  114.6 19.6 %collective-permute-start.27 = (bf16[3,64,2048]{2,1,0:T(8,128)(2,1)S(1)}, bf16[3,64,2048]{2,1,0:T(8,128)(2,1)S(1)}, u32[]{:S(2)}, u32[]{:S(2)}) collective-permute-start(bf16[3,64,2048]{2,1,0:T(8,128)(2,1)S(1)} %slice.24), channel_id=1, source_target_pairs={{0,4},{1,5},{2,6},{3,7},{4,0},{5,1},{6,2},{7,3},{8,12},{9,13},{10,... | collective-permute-start | bytes 2359304 | tf_op jit(solution)/shard_map/ppermute | solution.py:384
  115.9 19.2 %collective-permute-start.28 = (bf16[3,64,2048]{2,1,0:T(8,128)(2,1)S(1)}, bf16[3,64,2048]{2,1,0:T(8,128)(2,1)S(1)}, u32[]{:S(2)}, u32[]{:S(2)}) collective-permute-start(bf16[3,64,2048]{2,1,0:T(8,128)(2,1)S(1)} %slice.25), channel_id=1, source_target_pairs={{0,2},{1,3},{2,0},{3,1},{4,6},{5,7},{6,4},{7,5},{8,10},{9,11},{10,... | collective-permute-start | bytes 2359304 | tf_op jit(solution)/shard_map/ppermute | solution.py:384
  154.5 23.8 %collective-permute-start.35 = (bf16[512,256]{1,0:T(8,128)(2,1)S(1)}, bf16[512,256]{1,0:T(8,128)(2,1)S(1)}, u32[]{:S(2)}, u32[]{:S(2)}) collective-permute-start(bf16[512,256]{1,0:T(8,128)(2,1)S(1)} %get-tuple-element.111), channel_id=1, source_target_pairs={{0,1},{1,0},{2,3},{3,2},{4,5},{5,4},{6,7},{7,6},{8,9},{9,8},{10,11... | collective-permute-start | bytes 786440 | tf_op jit(solution)/shard_map/ppermute | solution.py:389
  154.5 23.8 %collective-permute-start.36 = (bf16[512,256]{1,0:T(8,128)(2,1)S(1)}, bf16[512,256]{1,0:T(8,128)(2,1)S(1)}, u32[]{:S(2)}, u32[]{:S(2)}) collective-permute-start(bf16[512,256]{1,0:T(8,128)(2,1)S(1)} %get-tuple-element.112), channel_id=1, source_target_pairs={{0,2},{1,3},{2,0},{3,1},{4,6},{5,7},{6,4},{7,5},{8,10},{9,11},{10,... | collective-permute-start | bytes 786440 | tf_op jit(solution)/shard_map/ppermute | solution.py:384
  155.2 23.1 %collective-permute-start.37 = (bf16[512,256]{1,0:T(8,128)(2,1)S(1)}, bf16[512,256]{1,0:T(8,128)(2,1)S(1)}, u32[]{:S(2)}, u32[]{:S(2)}) collective-permute-start(bf16[512,256]{1,0:T(8,128)(2,1)S(1)} %get-tuple-element.113), channel_id=1, source_target_pairs={{0,3},{1,2},{2,1},{3,0},{4,7},{5,6},{6,5},{7,4},{8,11},{9,10},{10,... | collective-permute-start | bytes 786440 | tf_op jit(solution)/shard_map/ppermute | solution.py:1194
  195.9 16.0 %collective-permute-start.40 = (bf16[512,256]{1,0:T(8,128)(2,1)}, bf16[512,256]{1,0:T(8,128)(2,1)S(1)}, u32[]{:S(2)}, u32[]{:S(2)}) collective-permute-start(bf16[512,256]{1,0:T(8,128)(2,1)} %get-tuple-element.131), channel_id=1, source_target_pairs={{0,2},{1,3},{2,0},{3,1},{4,6},{5,7},{6,4},{7,5},{8,10},{9,11},{10,... | collective-permute-start | bytes 786440 | tf_op jit(solution)/shard_map/ppermute | solution.py:384
  197.3 14.6 %collective-permute-start.41 = (bf16[512,256]{1,0:T(8,128)(2,1)}, bf16[512,256]{1,0:T(8,128)(2,1)S(1)}, u32[]{:S(2)}, u32[]{:S(2)}) collective-permute-start(bf16[512,256]{1,0:T(8,128)(2,1)} %get-tuple-element.132), channel_id=1, source_target_pairs={{0,3},{1,2},{2,1},{3,0},{4,7},{5,6},{6,5},{7,4},{8,11},{9,10},{10,... | collective-permute-start | bytes 786440 | tf_op jit(solution)/shard_map/ppermute | solution.py:1194
  (61 other events, 494.2 us)

commit v7 on v6

--- a/solution.py
+++ b/solution.py
@@ -605,7 +605,7 @@
     model = tokens.shape[1]
     blocks = LEN // BLK
 
-    def body(ix, tok, vec_ref, down_ref, normed_ref, latent_ref, pad_ref):
+    def body(ix, tok, vec_ref, down_ref, normed_ref, latent_ref, latent_t_ref, pad_ref):
         @pl.when(pl.program_id(0) == 0)
         def _():
             pad_ref[...] = jnp.zeros_like(pad_ref)
@@ -615,6 +615,8 @@
         normed = (hat * vec_ref[0:1, :] + vec_ref[1:2, :]).astype(BF16)
         normed_ref[...] = normed
         latent_ref[...] = lax.dot_general(normed, pad_ref[...], NT, preferred_element_type=F32).astype(BF16)
+        turned = lax.dot_general(pad_ref[:16, :], normed, NT, preferred_element_type=F32)
+        latent_t_ref[...] = turned.astype(BF16)
 
     row = lambda c: pl.BlockSpec((BLK, c), lambda i, ix: (i, 0))
     return call(
@@ -622,8 +624,8 @@
         "norm_rows",
         blocks,
         [pl.BlockSpec((BLK, model), lambda i, ix: (ix[1] * blocks + i, 0)), full(8, model), full(8, model)],
-        [row(model), row(LANES), full(LANES, model)],
-        [shape(LEN, model), shape(LEN, LANES), shape(LANES, model)],
+        [row(model), row(LANES), pl.BlockSpec((16, BLK), lambda i, ix: (0, i)), full(LANES, model)],
+        [shape(LEN, model), shape(LEN, LANES), shape(16, LEN), shape(LANES, model)],
         [],
         cost(2 * LEN * model * LANES, 4 * LEN * model),
     )(idx, tokens, vec, down)
@@ -816,6 +818,7 @@
     parts = 4
     piece = model // parts
     chunk = 512
+    wide = 512 if hidden is not None else 256
     per = part // chunk
     c0 = 0.7978845608028654
     c1 = 0.044715
@@ -870,10 +873,10 @@
         bend(count - 1, per - 1, (per - 1) % 2)
 
         def mid_of(n):
-            at = at_rows(n, BLK)
-            lanes = at_lanes(n, BLK)
-            mid = jnp.zeros((rows, BLK), F32)
-            unit = jnp.zeros((rows, BLK), F32)
+            at = at_rows(n, wide)
+            lanes = at_lanes(n, wide)
+            mid = jnp.zeros((rows, wide), F32)
+            unit = jnp.zeros((rows, wide), F32)
             for o in range(count):
                 cols = slice(o * part, (o + 1) * part)
                 mid = mid + lax.dot_general(pre_ref[:, cols], w[o, at, :part], NT, preferred_element_type=F32)
@@ -891,7 +894,7 @@
                 outs[1][:, lanes] = unit.astype(BF16)
                 return 0
 
-            lax.fori_loop(0, model // BLK, finish, 0)
+            lax.fori_loop(0, model // wide, finish, 0)
             return
         out_low, mid_ref = held
 
@@ -901,7 +904,7 @@
             out_low[:, lanes] = (unit + hid_ref[:, lanes]).astype(BF16)
             return 0
 
-        lax.fori_loop(0, model // BLK, finish, 0)
+        lax.fori_loop(0, model // wide, finish, 0)
         for k in range(parts):
             outs[1 + k][...] = out_low[:, at_lanes((2 * ix[1] + ix[2]) ^ k, piece)]
         step_rows = 128
@@ -965,7 +968,7 @@
 
     def body(ix, q_ref, k_ref, v_ref, o_ref, own_ref, other_ref, lse_ref, normed_ref, latent_ref, uq_ref, uv_ref, *rest):
         msgs = rest[:n]
-        dq_ref, dk_ref, dv_ref, low_ref, down_ref, rq_ref, rv_ref, low_acc, dq_acc, g_ref, qs_ref, p_ref, ds_ref, w, sems = rest[
+        dq_ref, dk_ref, dv_ref, low_ref, down_ref, rq_ref, rv_ref, low_acc, dq_acc, g2_ref, g_ref, qs_ref, p_ref, ds_ref, w, sems = rest[
             n:
         ]
         pair = pl.program_id(0)
@@ -974,9 +977,13 @@
         def _():
             load_all(column_pairs(msgs, table, w, ix, first, width // 2, False), sems)
 
-        weight = w[:, at_lanes(pair, LANES)]
-        for ref, rank in ((own_ref, ix[2]), (other_ref, 1 - ix[2])):
-            g_ref[at_rows(rank, half), :] = jnp.dot(ref[...], weight, preferred_element_type=F32).astype(BF16)
+        @pl.when(lax.rem(pair, 2) == 0)
+        def _():
+            weight = w[:, at_lanes(pair // 2, 2 * LANES)]
+            for ref, rank in ((own_ref, ix[2]), (other_ref, 1 - ix[2])):
+                g2_ref[at_rows(rank, half), :] = jnp.dot(ref[...], weight, preferred_element_type=F32).astype(BF16)
+
+        g_ref[...] = g2_ref[:, at_lanes(lax.rem(pair, 2), LANES)]
         scale = HEAD_DIM**-0.5 * LOG2E
         low = lax.broadcasted_iota(jnp.int32, (1, LANES), 1) < HEAD_DIM
         qs_ref[...] = (q_ref[...].astype(F32) * scale).astype(BF16)
@@ -1028,11 +1035,12 @@
             stacked = coming
         spread(length // BLK - 1, stacked)
         dq_ref[...] = (dq_acc[...] * HEAD_DIM**-0.5).astype(BF16)
-        term = lax.dot_general(dq_ref[...], uq_ref[0], NT, preferred_element_type=F32)
-        term = term + lax.dot_general(dv_ref[...], uv_ref[0], NT, preferred_element_type=F32)
-        latent_t = latent_ref[...]
-        rq_ref[...] = lax.dot_general(latent_t, dq_ref[...], TN, preferred_element_type=F32)[:8]
-        rv_ref[...] = lax.dot_general(latent_t, dv_ref[...], TN, preferred_element_type=F32)[:8]
+        grads = jnp.concatenate([dq_ref[...], dv_ref[...]], axis=1)
+        ups = jnp.concatenate([uq_ref[0], uv_ref[0]], axis=1)
+        term = lax.dot_general(grads, ups, NT, preferred_element_type=F32)
+        raised = jnp.dot(latent_ref[...], grads, preferred_element_type=F32)
+        rq_ref[...] = raised[:8, :LANES]
+        rv_ref[...] = raised[:8, LANES:]
 
         @pl.when(pair == 0)
         def _():
@@ -1044,9 +1052,9 @@
 
         @pl.when(pair == pairs - 1)
         def _():
-            low_grad = low_acc[...].astype(BF16)
-            low_ref[...] = low_grad
-            down_ref[...] = lax.dot_general(low_grad, normed_ref[...], TN, preferred_element_type=F32)[:8]
+            low_ref[...] = low_acc[...].astype(BF16)
+            low_rows = low_acc[...].T[: latent_ref.shape[0]].astype(BF16)
+            down_ref[...] = jnp.dot(low_rows, normed_ref[...], preferred_element_type=F32)[:8]
 
     spec = pl.BlockSpec((length, LANES), lambda i, ix: (0, i))
     return call(
@@ -1055,7 +1063,7 @@
         pairs,
         [spec] * 4
         + [full(half, model)] * 2
-        + [pl.BlockSpec((1, 8, length), lambda i, ix: (i, 0, 0)), full(length, model), full(length, LANES)]
+        + [pl.BlockSpec((1, 8, length), lambda i, ix: (i, 0, 0)), full(length, model), full(*latent.shape)]
         + [
             pl.BlockSpec((1, LANES, LANES), lambda i, ix: (i // per, 0, lax.rem(i, per))),
             pl.BlockSpec((1, LANES, LANES), lambda i, ix: (i // per, 0, 2 * per + lax.rem(i, per))),
@@ -1069,6 +1077,7 @@
         [
             pltpu.VMEM((length, LANES), F32),
             pltpu.VMEM((length, LANES), F32),
+            pltpu.VMEM((length, 2 * LANES), BF16),
             pltpu.VMEM((length, LANES), BF16),
             pltpu.VMEM((length, LANES), BF16),
             pltpu.VMEM((2, 2 * BLK, length), BF16),
@@ -1253,12 +1262,13 @@
     )
     fc_other = core_swap(fc_mine)
     down8 = down_master.reshape(2 * r, model)
-    normed, latent, down = norm_rows(idx, after(tokens, hx_far, tok_own, cot_own), vec, down8)
+    normed, latent, latent_t, down = norm_rows(idx, after(tokens, hx_far, tok_own, cot_own), vec, down8)
     ux, uy = pair_xy(after(u_rest, hd_far))
     ready = after(normed, u_rest, ud0, weights)
     queries, keys, values, up = project_heads(idx, ready, latent, frozen_triple_bias, up_rows, hx_near, heads)
     mixed, logsum = attend_fast(queries, keys, values)
     sent = [core_swap(v) for v in attention_out_send(idx, mixed, heads, heads_cols)]
+    sent, fc_other = lax.optimization_barrier((sent, fc_other))
     hidden, normed_mid = attention_out_own(idx, mixed, sent, tok_own, vec, heads, heads_cols)
     rows = (normed_mid, cot_own, weights, vec, (fc_mine, fc_other))
     ux, uy, _ = lax.optimization_barrier((ux, uy, normed_mid))
@@ -1288,7 +1298,7 @@
     hidden_other = core_swap(hidden_low)
     out_pieces = exchange_features(out_pieces)
     dq, dk, dv, latent_low, down_term, up_q, up_v = attend_back_fast(
-        idx, queries, keys, values, mixed, hidden_low, hidden_other, logsum, normed, latent, up, heads, heads_cols
+        idx, queries, keys, values, mixed, hidden_low, hidden_other, logsum, normed, latent_t, up, heads, heads_cols
     )
     up_term = jnp.stack([up_q[:r], up_v[r:]]).reshape(2 * r, 2, head_part)
     down_sum = down_term + core_swap(down_term)

time: 215 us -> 214 us (level)
  no operation moved by 1% of the time
where the time goes in v7:
time: 214 us; the launch traced here: 213 us
  Pallas kernels  95.7 us (45%)
  waiting for transfers between devices  54.9 us (26%)
  starting transfers between devices  42.9 us (20%)
  local copies, waits for them, and re-layouts  12.9 us (6%)
  other arithmetic  4.54 us (2%)
  between operations  2.23 us (1%)
    pallas_call x3, Pallas kernels, units_main(): call(body, 'units_main_last' if last else 'units_main_first' if not carri...  30.9 us
    ppermute x21, starting transfers between devices, hop(): return lax.ppermute(value, AXES, [(i, i ^ flip) for i in range(total)])  29.9 us
    ppermute x21, waiting for transfers between devices, hop(): return lax.ppermute(value, AXES, [(i, i ^ flip) for i in range(total)])  28.5 us
    pallas_call x1, Pallas kernels, attend_back_fast(): call(body, 'attend_back', pairs, [spec] * 4 + [full(half, model)] * 2 + [...  20.3 us
    ppermute x8, waiting for transfers between devices, z_hop(): return lax.ppermute(value, AXES, perm)  19.7 us
    pallas_call x1, Pallas kernels, attend_fast(): pl.pallas_call(body, grid=(pairs,), out_shape=(shape(length, width), jax....  11 us
    ppermute x8, starting transfers between devices, z_hop(): return lax.ppermute(value, AXES, perm)  7.87 us
    pallas_call x1, Pallas kernels, heads_back(): call(body, 'heads_back', 2 * half_blocks, [row(width)] * 3 + [row(LANES),...  6.91 us
  transfers between devices with their start and end apart: 47, of which 21 were waited for; matrix products, arithmetic and copies ran while one was open for 4% of the time, Pallas kernels for 36%

profile of v7, /device:TPU:0, one launch (start us, length us, event | category | flops | bytes accessed | tf_op | source)
XLA Modules:
  0.0 213.2 jit_solution(249694158388194689)
XLA Ops:
  4.3 3.3 %prepare_blocks.1 = (bf16[136,1024]{1,0:T(8,128)(2,1)}, bf16[1,128,2048]{2,1,0:T(8,128)(2,1)}) custom-call(s32[3]{0:T(128)} %pad_add_fusion.ix, s32[16,128]{1,0:T(8,128)} %bitcast.21, bf16[128,3,256]{2,1,0:T(4,128)(2,1)} %copy.32.triple_ref, bf16[256,128]{1,0:T(8,128)(2,1)} %out_ref.1, bf16[3,256]{1,0:T(4,128)(2,1)} %bias_ref.3, ...), custom_call_target="tpu_custom_call" | custom-call | bytes 52428 | tf_op jit(solution)/shard_map/prepare_blocks/pallas_call | solution.py:548
  7.6 3.0 %collective-permute-start = (bf16[136,1024]{1,0:T(8,128)(2,1)}, bf16[136,1024]{1,0:T(8,128)(2,1)S(1)}, u32[]{:S(2)}, u32[]{:S(2)}) collective-permute-start(bf16[136,1024]{1,0:T(8,128)(2,1)} %get-tuple-element.77), channel_id=1, source_target_pairs={{0,8},{1,9},{2,10},{3,11},{4,12},{5,13},{6,14},{7,15},{8,0},{9,1},... | collective-permute-start | bytes 835592 | tf_op jit(solution)/shard_map/ppermute | solution.py:384
  14.4 3.1 %collective-permute-done = bf16[136,1024]{1,0:T(8,128)(2,1)S(1)} collective-permute-done((bf16[136,1024]{1,0:T(8,128)(2,1)}, bf16[136,1024]{1,0:T(8,128)(2,1)S(1)}, u32[]{:S(2)}, u32[]{:S(2)}) %collective-permute-start) | collective-permute-done | bytes 278560 | tf_op jit(solution)/shard_map/ppermute | solution.py:384
  21.8 3.2 %collective-permute-done.5.rest_2_ = bf16[1,128,2048]{2,1,0:T(8,128)(2,1)} collective-permute-done((bf16[1,128,2048]{2,1,0:T(8,128)(2,1)}, bf16[1,128,2048]{2,1,0:T(8,128)(2,1)}, u32[]{:S(2)}, u32[]{:S(2)}) %collective-permute-start.5) | collective-permute-done | bytes 524320 | tf_op jit(solution)/shard_map/ppermute | solution.py:384
  30.3 5.3 %collective-permute-done.4 = bf16[136,1024]{1,0:T(8,128)(2,1)S(1)} collective-permute-done((bf16[136,1024]{1,0:T(8,128)(2,1)S(1)}, bf16[136,1024]{1,0:T(8,128)(2,1)S(1)}, u32[]{:S(2)}, u32[]{:S(2)}) %collective-permute-start.4) | collective-permute-done | bytes 278560 | tf_op jit(solution)/shard_map/ppermute | solution.py:407
  36.5 2.7 %collective-permute-done.7.rest_4_.near_ref.rest_1_.rest_2_ = bf16[2,136,1024]{2,1,0:T(8,128)(2,1)S(1)} collective-permute-done((bf16[2,136,1024]{2,1,0:T(8,128)(2,1)S(1)}, bf16[2,136,1024]{2,1,0:T(8,128)(2,1)S(1)}, u32[]{:S(2)}, u32[]{:S(2)}) %collective-permute-start.7) | collective-permute-done | bytes 557088 | tf_op jit(solution)/shard_map/ppermute | solution.py:384
  42.6 5.2 %collective-permute-done.10 = bf16[1,128,2048]{2,1,0:T(8,128)(2,1)S(1)} collective-permute-done((bf16[1,128,2048]{2,1,0:T(8,128)(2,1)S(1)}, bf16[1,128,2048]{2,1,0:T(8,128)(2,1)S(1)}, u32[]{:S(2)}, u32[]{:S(2)}) %collective-permute-start.10) | collective-permute-done | bytes 524320 | tf_op jit(solution)/shard_map/ppermute | solution.py:384
  49.8 2.6 %collective-permute-done.14.rest_3_.rest_6_.rest_7_ = bf16[2,136,1024]{2,1,0:T(8,128)(2,1)S(1)} collective-permute-done((bf16[2,136,1024]{2,1,0:T(8,128)(2,1)S(1)}, bf16[2,136,1024]{2,1,0:T(8,128)(2,1)S(1)}, u32[]{:S(2)}, u32[]{:S(2)}) %collective-permute-start.14) | collective-permute-done | bytes 557088 | tf_op jit(solution)/shard_map/ppermute | solution.py:384
  56.8 5.0 %collective-permute-done.13 = bf16[1,128,2048]{2,1,0:T(8,128)(2,1)S(1)} collective-permute-done((bf16[1,128,2048]{2,1,0:T(8,128)(2,1)S(1)}, bf16[1,128,2048]{2,1,0:T(8,128)(2,1)S(1)}, u32[]{:S(2)}, u32[]{:S(2)}) %collective-permute-start.13) | collective-permute-done | bytes 524320 | tf_op jit(solution)/shard_map/ppermute | solution.py:407
  61.8 2.3 %collective-permute-done.16.rest_3_.rest_4_ = bf16[2,136,1024]{2,1,0:T(8,128)(2,1)S(1)} collective-permute-done((bf16[2,136,1024]{2,1,0:T(8,128)(2,1)S(1)}, bf16[2,136,1024]{2,1,0:T(8,128)(2,1)S(1)}, u32[]{:S(2)}, u32[]{:S(2)}) %collective-permute-start.16) | collective-permute-done | bytes 557088 | tf_op jit(solution)/shard_map/ppermute | solution.py:384
  66.5 7.4 %collective-permute-done.15 = bf16[1,128,2048]{2,1,0:T(8,128)(2,1)S(1)} collective-permute-done((bf16[1,128,2048]{2,1,0:T(8,128)(2,1)S(1)}, bf16[1,128,2048]{2,1,0:T(8,128)(2,1)S(1)}, u32[]{:S(2)}, u32[]{:S(2)}) %collective-permute-start.15) | collective-permute-done | bytes 524320 | tf_op jit(solution)/shard_map/ppermute | solution.py:407
  83.5 3.4 %norm_rows.1 = (bf16[1024,1024]{1,0:T(8,128)(2,1)S(1)}, bf16[1024,128]{1,0:T(8,128)(2,1)S(1)}, bf16[16,1024]{1,0:T(8,128)(2,1)S(1)}, bf16[128,1024]{1,0:T(8,128)(2,1)S(1)}) custom-call(s32[3]{0:T(128)S(1)} %copy-done.20, bf16[2048,1024]{1,0:T(8,128)(2,1)S(1)} %copy-done.5, f32[8,1024]{1,0:T(8,128)S(1)} %convert_element_type.10.vec_ref, ...), custom_call_target="tpu_custom_call" | custom-call | flops 26843544 | bytes 419430 | tf_op jit(solution)/shard_map/norm_rows/pallas_call | solution.py:622
  87.0 6.2 %project_heads.1 = (bf16[1024,512]{1,0:T(8,128)(2,1)S(1)}, bf16[1024,512]{1,0:T(8,128)(2,1)S(1)}, bf16[1024,512]{1,0:T(8,128)(2,1)S(1)}, bf16[2,128,768]{2,1,0:T(8,128)(2,1)S(1)}) custom-call(s32[3]{0:T(128)S(1)} %copy-done.20, bf16[1024,1024]{1,0:T(8,128)(2,1)S(1)} %get-tuple-element.88.normed_ref, bf16[1024,128]{1,0:T(8,128)(2,1)S(1)} %get-tuple-element.89.latent_ref, ...), custom_call_target="tpu_custom_call" | custom-call | flops 322122560 | bytes 1677721 | tf_op jit(solution)/shard_map/project_heads/pallas_call | solution.py:671
  93.1 11.0 %attend.1 = (bf16[1024,512]{1,0:T(8,128)(2,1)S(1)}, f32[4,8,1024]{2,1,0:T(8,128)S(1)}) custom-call(bf16[1024,512]{1,0:T(8,128)(2,1)S(1)} %get-tuple-element.90.q_ref, bf16[1024,512]{1,0:T(8,128)(2,1)S(1)} %get-tuple-element.91.k_ref, bf16[1024,512]{1,0:T(8,128)(2,1)S(1)} %get-tuple-element.92.v_ref), custom_call_target="tpu_custom_call" | custom-call | flops 429496736 | bytes 419430 | tf_op jit(solution)/shard_map/attend/pallas_call | solution.py:720
  108.8 2.5 %attention_out_own.1 = (f32[512,1024]{1,0:T(8,128)S(1)}, bf16[512,1024]{1,0:T(8,128)(2,1)S(1)}) custom-call(s32[3]{0:T(128)S(1)} %copy-done.20, bf16[1024,512]{1,0:T(8,128)(2,1)S(1)} %get-tuple-element.93.att.o_ref, bf16[512,1024]{1,0:T(8,128)(2,1)S(1)} %constant_dynamic-slice_fusion.1.tok, f32[8,1024]{1,0:T(8,128)S(1)} %convert_element_type.10.vec_ref, ...), custom_call_target="tpu_custom_call" | custom-call | flops 53687092 | bytes 524288 | tf_op jit(solution)/shard_map/attention_out_own/pallas_call | solution.py:788
  118.6 14.4 %units_main_first.1 = (bf16[512,1024]{1,0:T(8,128)(2,1)S(1)}, bf16[512,1024]{1,0:T(8,128)(2,1)S(1)}) custom-call(s32[3]{0:T(128)S(1)} %copy-done.20, bf16[512,1024]{1,0:T(8,128)(2,1)S(1)} %get-tuple-element.96.normed_ref, bf16[512,1024]{1,0:T(8,128)(2,1)S(1)} %constant_dynamic-slice_fusion.cot, f32[512,128]{1,0:T(8,128)S(1)} %get-tuple-element.87.weight_ref, ...), custom_call_target="tpu_custom_call" | custom-call | flops 858993472 | bytes 1677721 | tf_op jit(solution)/shard_map/units_main_first/pallas_call | solution.py:938
  136.1 8.1 %units_main_next.1 = (bf16[512,1024]{1,0:T(8,128)(2,1)S(1)}, bf16[512,1024]{1,0:T(8,128)(2,1)S(1)}) custom-call(s32[3]{0:T(128)S(1)} %copy-done.20, bf16[512,1024]{1,0:T(8,128)(2,1)S(1)} %get-tuple-element.96.normed_ref, bf16[512,1024]{1,0:T(8,128)(2,1)S(1)} %constant_dynamic-slice_fusion.cot, f32[512,128]{1,0:T(8,128)S(1)} %get-tuple-element.87.weight_ref, ...), custom_call_target="tpu_custom_call" | custom-call | flops 429496736 | bytes 838860 | tf_op jit(solution)/shard_map/units_main_next/pallas_call | solution.py:938
  144.3 8.5 %units_main_last.1 = (bf16[512,1024]{1,0:T(8,128)(2,1)S(1)}, bf16[512,256]{1,0:T(8,128)(2,1)S(1)}, bf16[512,256]{1,0:T(8,128)(2,1)S(1)}, bf16[512,256]{1,0:T(8,128)(2,1)S(1)}, bf16[512,256]{1,0:T(8,128)(2,1)S(1)}) custom-call(s32[3]{0:T(128)S(1)} %copy-done.20, bf16[512,1024]{1,0:T(8,128)(2,1)S(1)} %get-tuple-element.96.normed_ref, ...), custom_call_target="tpu_custom_call" | custom-call | flops 429496736 | bytes 838860 | tf_op jit(solution)/shard_map/units_main_last/pallas_call | solution.py:938
  155.7 20.3 %attend_back.1 = (bf16[1024,512]{1,0:T(8,128)(2,1)S(1)}, bf16[1024,512]{1,0:T(8,128)(2,1)S(1)}, bf16[1024,512]{1,0:T(8,128)(2,1)S(1)}, bf16[1024,128]{1,0:T(8,12...) custom-call(s32[3]{0:T(128)S(1)} %copy-done.20, ...), custom_call_target="tpu_custom_call" | custom-call | flops 1073741824 | bytes 838860 | tf_op jit(solution)/shard_map/attend_back/pallas_call | solution.py:1060
  176.7 6.9 %heads_back.1 = (bf16[512,1024]{1,0:T(8,128)(2,1)}, bf16[512,1024]{1,0:T(8,128)(2,1)S(1)}) custom-call(s32[3]{0:T(128)S(1)} %copy-done.20, bf16[1024,512]{1,0:T(8,128)(2,1)S(1)} %get-tuple-element.124.dq_ref, bf16[1024,512]{1,0:T(8,128)(2,1)S(1)} %get-tuple-element.125.dk_ref, bf16[1024,512]{1,0:T(8,128)(2,1)S(1)} %get-tuple-element.126.dv_ref, ...), custom_call_target="tpu_custom_call" | custom-call | flops 322122560 | bytes 314572 | tf_op jit(solution)/shard_map/heads_back/pallas_call | solution.py:1129
  189.0 5.0 %tokens_back.1 = (bf16[512,256]{1,0:T(8,128)(2,1)}, bf16[512,256]{1,0:T(8,128)(2,1)}, bf16[512,256]{1,0:T(8,128)(2,1)}, bf16[512,256]{1,0:T(8,128)(2,1)}) custom-call(s32[3]{0:T(128)} %pad_add_fusion.ix, bf16[512,1024]{1,0:T(8,128)(2,1)} %copy-done.8, bf16[512,1024]{1,0:T(8,128)(2,1)} %copy-done.25, bf16[512,1024]{1,0:T(8,128)(2,1)} %copy-done.4, ...), custom_call_target="tpu_custom_call" | custom-call | flops 2097152 | bytes 838860 | tf_op jit(solution)/shard_map/tokens_back/pallas_call | solution.py:1159
  196.7 3.4 %collective-permute-done.44 = f32[8,1280]{1,0:T(8,128)S(1)} collective-permute-done((f32[8,1280]{1,0:T(8,128)S(1)}, f32[8,1280]{1,0:T(8,128)S(1)}, u32[]{:S(2)}, u32[]{:S(2)}) %collective-permute-start.44) | collective-permute-done | bytes 40992 | tf_op jit(solution)/shard_map/ppermute | solution.py:384
  200.1 2.4 %collective-permute-start.45 = (f32[8,1280]{1,0:T(8,128)S(1)}, f32[8,1280]{1,0:T(8,128)S(1)}, u32[]{:S(2)}, u32[]{:S(2)}) collective-permute-start(f32[8,1280]{1,0:T(8,128)S(1)} %add.63), channel_id=1, source_target_pairs={{0,8},{1,9},{2,10},{3,11},{4,12},{5,13},{6,14},{7,15},{8,0},{9,1},... | collective-permute-start | bytes 122888 | tf_op jit(solution)/shard_map/ppermute | solution.py:384
  204.5 3.2 %collective-permute-start.46 = (f32[8,1280]{1,0:T(8,128)S(1)}, f32[8,1280]{1,0:T(8,128)S(1)}, u32[]{:S(2)}, u32[]{:S(2)}) collective-permute-start(f32[8,1280]{1,0:T(8,128)S(1)} %add.64), channel_id=1, source_target_pairs={{0,16},{1,17},{2,18},{3,19},{4,20},{5,21},{6,22},{7,23},{8,24},{9,... | collective-permute-start | bytes 122888 | tf_op jit(solution)/shard_map/ppermute | solution.py:384
  (207 shorter events, 72.5 us)
Async XLA Ops:
  11.3 13.8 %collective-permute-start.5 = (bf16[1,128,2048]{2,1,0:T(8,128)(2,1)}, bf16[1,128,2048]{2,1,0:T(8,128)(2,1)}, u32[]{:S(2)}, u32[]{:S(2)}) collective-permute-start(bf16[1,128,2048]{2,1,0:T(8,128)(2,1)} %get-tuple-element.83.rest_0_), channel_id=1, source_target_pairs={{0,2},{1,3},{2,0},{3,1},{4,6},{5,7},{6,4},{7,5},{8,10},{9,11},{10,... | collective-permute-start | bytes 1572872 | tf_op jit(solution)/shard_map/ppermute | solution.py:384
  12.9 13.4 %collective-permute-start.6 = (bf16[1,128,2048]{2,1,0:T(8,128)(2,1)}, bf16[1,128,2048]{2,1,0:T(8,128)(2,1)}, u32[]{:S(2)}, u32[]{:S(2)}) collective-permute-start(bf16[1,128,2048]{2,1,0:T(8,128)(2,1)} %get-tuple-element.83.rest_0_), channel_id=1, source_target_pairs={{0,4},{1,5},{2,6},{3,7},{4,0},{5,1},{6,2},{7,3},{8,12},{9,13},{10,... | collective-permute-start | bytes 1572872 | tf_op jit(solution)/shard_map/ppermute | solution.py:384
  18.2 12.1 %collective-permute-start.3 = (bf16[136,1024]{1,0:T(8,128)(2,1)S(1)}, bf16[136,1024]{1,0:T(8,128)(2,1)S(1)}, u32[]{:S(2)}, u32[]{:S(2)}) collective-permute-start(bf16[136,1024]{1,0:T(8,128)(2,1)S(1)} %collective-permute-done.2), channel_id=1, source_target_pairs={{8,0},{9,1},{10,2},{11,3},{12,4},{13,5},{14,6},{15,7},{16,24},{17,... | collective-permute-start | bytes 835592 | tf_op jit(solution)/shard_map/ppermute | solution.py:407
  19.5 16.1 %collective-permute-start.4 = (bf16[136,1024]{1,0:T(8,128)(2,1)S(1)}, bf16[136,1024]{1,0:T(8,128)(2,1)S(1)}, u32[]{:S(2)}, u32[]{:S(2)}) collective-permute-start(bf16[136,1024]{1,0:T(8,128)(2,1)S(1)} %collective-permute-done.1), channel_id=1, source_target_pairs={{8,0},{9,1},{10,2},{11,3},{12,4},{13,5},{14,6},{15,7},{16,24},{17,... | collective-permute-start | bytes 835592 | tf_op jit(solution)/shard_map/ppermute | solution.py:407
  26.3 12.9 %collective-permute-start.7 = (bf16[2,136,1024]{2,1,0:T(8,128)(2,1)S(1)}, bf16[2,136,1024]{2,1,0:T(8,128)(2,1)S(1)}, u32[]{:S(2)}, u32[]{:S(2)}) collective-permute-start(bf16[2,136,1024]{2,1,0:T(8,128)(2,1)S(1)} %pad_maximum_fusion.2.rest_0_.rest_1_), channel_id=1, source_target_pairs={{0,2},{1,3},{2,0},{3,1},{4,6},{5,7},{6,4},{7,5},{8,10},{9,11},{10,... | collective-permute-start | bytes 1671176 | tf_op jit(solution)/shard_map/ppermute | solution.py:384
  26.8 12.8 %collective-permute-start.8 = (bf16[2,136,1024]{2,1,0:T(8,128)(2,1)S(1)}, bf16[2,136,1024]{2,1,0:T(8,128)(2,1)S(1)}, u32[]{:S(2)}, u32[]{:S(2)}) collective-permute-start(bf16[2,136,1024]{2,1,0:T(8,128)(2,1)S(1)} %pad_maximum_fusion.2.rest_0_.rest_1_), channel_id=1, source_target_pairs={{0,4},{1,5},{2,6},{3,7},{4,0},{5,1},{6,2},{7,3},{8,12},{9,13},{10,... | collective-permute-start | bytes 1671176 | tf_op jit(solution)/shard_map/ppermute | solution.py:384
  35.7 12.1 %collective-permute-start.10 = (bf16[1,128,2048]{2,1,0:T(8,128)(2,1)S(1)}, bf16[1,128,2048]{2,1,0:T(8,128)(2,1)S(1)}, u32[]{:S(2)}, u32[]{:S(2)}) collective-permute-start(bf16[1,128,2048]{2,1,0:T(8,128)(2,1)S(1)} %copy-done.9), channel_id=1, source_target_pairs={{0,8},{1,9},{2,10},{3,11},{4,12},{5,13},{6,14},{7,15},{8,0},{9,1},... | collective-permute-start | bytes 1572872 | tf_op jit(solution)/shard_map/ppermute | solution.py:384
  35.8 12.7 %collective-permute-start.12 = (bf16[1,128,2048]{2,1,0:T(8,128)(2,1)S(1)}, bf16[1,128,2048]{2,1,0:T(8,128)(2,1)S(1)}, u32[]{:S(2)}, u32[]{:S(2)}) collective-permute-start(bf16[1,128,2048]{2,1,0:T(8,128)(2,1)S(1)} %copy-done.9), channel_id=1, source_target_pairs={{8,16},{9,17},{10,18},{11,19},{12,20},{13,21},{14,22},{15,23},{16,... | collective-permute-start | bytes 1572872 | tf_op jit(solution)/shard_map/ppermute | solution.py:407
  39.6 12.8 %collective-permute-start.14 = (bf16[2,136,1024]{2,1,0:T(8,128)(2,1)S(1)}, bf16[2,136,1024]{2,1,0:T(8,128)(2,1)S(1)}, u32[]{:S(2)}, u32[]{:S(2)}) collective-permute-start(bf16[2,136,1024]{2,1,0:T(8,128)(2,1)S(1)} %pad_maximum_fusion.1.rest_1_.rest_4_.rest_5_), channel_id=1, source_target_pairs={{0,4},{1,5},{2,6},{3,7},{4,0},{5,1},{6,2},{7,3},{8,12},{9,13},{10,... | collective-permute-start | bytes 1671176 | tf_op jit(solution)/shard_map/ppermute | solution.py:384
  41.1 12.8 %collective-permute-start.9 = (bf16[2,136,1024]{2,1,0:T(8,128)(2,1)S(1)}, bf16[2,136,1024]{2,1,0:T(8,128)(2,1)S(1)}, u32[]{:S(2)}, u32[]{:S(2)}) collective-permute-start(bf16[2,136,1024]{2,1,0:T(8,128)(2,1)S(1)} %pad_maximum_fusion.1.rest_1_.rest_4_.rest_5_), channel_id=1, source_target_pairs={{0,2},{1,3},{2,0},{3,1},{4,6},{5,7},{6,4},{7,5},{8,10},{9,11},{10,... | collective-permute-start | bytes 1671176 | tf_op jit(solution)/shard_map/ppermute | solution.py:384
  48.5 13.3 %collective-permute-start.13 = (bf16[1,128,2048]{2,1,0:T(8,128)(2,1)S(1)}, bf16[1,128,2048]{2,1,0:T(8,128)(2,1)S(1)}, u32[]{:S(2)}, u32[]{:S(2)}) collective-permute-start(bf16[1,128,2048]{2,1,0:T(8,128)(2,1)S(1)} %collective-permute-done.12), channel_id=1, source_target_pairs={{8,0},{9,1},{10,2},{11,3},{12,4},{13,5},{14,6},{15,7},{16,24},{17,... | collective-permute-start | bytes 1572872 | tf_op jit(solution)/shard_map/ppermute | solution.py:407
  53.9 20.0 %collective-permute-start.15 = (bf16[1,128,2048]{2,1,0:T(8,128)(2,1)S(1)}, bf16[1,128,2048]{2,1,0:T(8,128)(2,1)S(1)}, u32[]{:S(2)}, u32[]{:S(2)}) collective-permute-start(bf16[1,128,2048]{2,1,0:T(8,128)(2,1)S(1)} %collective-permute-done.11), channel_id=1, source_target_pairs={{8,0},{9,1},{10,2},{11,3},{12,4},{13,5},{14,6},{15,7},{16,24},{17,... | collective-permute-start | bytes 1572872 | tf_op jit(solution)/shard_map/ppermute | solution.py:407
  55.2 20.2 %collective-permute-start.18 = (bf16[2,136,1024]{2,1,0:T(8,128)(2,1)S(1)}, bf16[2,136,1024]{2,1,0:T(8,128)(2,1)S(1)}, u32[]{:S(2)}, u32[]{:S(2)}) collective-permute-start(bf16[2,136,1024]{2,1,0:T(8,128)(2,1)S(1)} %collective-permute-done.14.rest_3_.rest_6_.rest_7_), channel_id=1, source_target_pairs={{0,2},{1,3},{2,0},{3,1},{4,6},{5,7},{6,4},{7,5},{8,10},{9,11},{10,... | collective-permute-start | bytes 1671176 | tf_op jit(solution)/shard_map/ppermute | solution.py:384
  65.0 22.0 %collective-permute-start.17 = (bf16[1,128,2048]{2,1,0:T(8,128)(2,1)}, bf16[1,128,2048]{2,1,0:T(8,128)(2,1)}, u32[]{:S(2)}, u32[]{:S(2)}) collective-permute-start(bf16[1,128,2048]{2,1,0:T(8,128)(2,1)} %collective-permute-done.5.rest_2_), channel_id=1, source_target_pairs={{0,4},{1,5},{2,6},{3,7},{4,0},{5,1},{6,2},{7,3},{8,12},{9,13},{10,... | collective-permute-start | bytes 1572872 | tf_op jit(solution)/shard_map/ppermute | solution.py:384
  76.2 35.1 %collective-permute-start.21 = (bf16[3,128,2048]{2,1,0:T(8,128)(2,1)}, bf16[3,128,2048]{2,1,0:T(8,128)(2,1)}, u32[]{:S(2)}, u32[]{:S(2)}) collective-permute-start(bf16[3,128,2048]{2,1,0:T(8,128)(2,1)} %pad_maximum_fusion.rest_1_), channel_id=1, source_target_pairs={{0,2},{1,3},{2,0},{3,1},{4,6},{5,7},{6,4},{7,5},{8,10},{9,11},{10,... | collective-permute-start | bytes 4718600 | tf_op jit(solution)/shard_map/ppermute | solution.py:384
  77.7 33.7 %collective-permute-start.22 = (bf16[3,128,2048]{2,1,0:T(8,128)(2,1)}, bf16[3,128,2048]{2,1,0:T(8,128)(2,1)}, u32[]{:S(2)}, u32[]{:S(2)}) collective-permute-start(bf16[3,128,2048]{2,1,0:T(8,128)(2,1)} %pad_maximum_fusion.rest_1_), channel_id=1, source_target_pairs={{0,4},{1,5},{2,6},{3,7},{4,0},{5,1},{6,2},{7,3},{8,12},{9,13},{10,... | collective-permute-start | bytes 4718600 | tf_op jit(solution)/shard_map/ppermute | solution.py:384
  106.6 12.0 %collective-permute-start.24 = (bf16[3,128,2048]{2,1,0:T(8,128)(2,1)}, bf16[3,128,2048]{2,1,0:T(8,128)(2,1)S(1)}, u32[]{:S(2)}, u32[]{:S(2)}) collective-permute-start(bf16[3,128,2048]{2,1,0:T(8,128)(2,1)} %pad_maximum_fusion.rest_1_), channel_id=1, source_target_pairs={{0,1},{1,0},{2,3},{3,2},{4,5},{5,4},{6,7},{7,6},{8,9},{9,8},{10,11... | collective-permute-start | bytes 4718600 | tf_op jit(solution)/shard_map/ppermute | solution.py:389
  114.4 19.6 %collective-permute-start.27 = (bf16[3,64,2048]{2,1,0:T(8,128)(2,1)S(1)}, bf16[3,64,2048]{2,1,0:T(8,128)(2,1)S(1)}, u32[]{:S(2)}, u32[]{:S(2)}) collective-permute-start(bf16[3,64,2048]{2,1,0:T(8,128)(2,1)S(1)} %slice.24), channel_id=1, source_target_pairs={{0,4},{1,5},{2,6},{3,7},{4,0},{5,1},{6,2},{7,3},{8,12},{9,13},{10,... | collective-permute-start | bytes 2359304 | tf_op jit(solution)/shard_map/ppermute | solution.py:384
  115.9 19.2 %collective-permute-start.28 = (bf16[3,64,2048]{2,1,0:T(8,128)(2,1)S(1)}, bf16[3,64,2048]{2,1,0:T(8,128)(2,1)S(1)}, u32[]{:S(2)}, u32[]{:S(2)}) collective-permute-start(bf16[3,64,2048]{2,1,0:T(8,128)(2,1)S(1)} %slice.25), channel_id=1, source_target_pairs={{0,2},{1,3},{2,0},{3,1},{4,6},{5,7},{6,4},{7,5},{8,10},{9,11},{10,... | collective-permute-start | bytes 2359304 | tf_op jit(solution)/shard_map/ppermute | solution.py:384
  153.4 22.6 %collective-permute-start.35 = (bf16[512,256]{1,0:T(8,128)(2,1)S(1)}, bf16[512,256]{1,0:T(8,128)(2,1)S(1)}, u32[]{:S(2)}, u32[]{:S(2)}) collective-permute-start(bf16[512,256]{1,0:T(8,128)(2,1)S(1)} %get-tuple-element.117), channel_id=1, source_target_pairs={{0,1},{1,0},{2,3},{3,2},{4,5},{5,4},{6,7},{7,6},{8,9},{9,8},{10,11... | collective-permute-start | bytes 786440 | tf_op jit(solution)/shard_map/ppermute | solution.py:389
  153.5 23.2 %collective-permute-start.36 = (bf16[512,256]{1,0:T(8,128)(2,1)S(1)}, bf16[512,256]{1,0:T(8,128)(2,1)S(1)}, u32[]{:S(2)}, u32[]{:S(2)}) collective-permute-start(bf16[512,256]{1,0:T(8,128)(2,1)S(1)} %get-tuple-element.118), channel_id=1, source_target_pairs={{0,2},{1,3},{2,0},{3,1},{4,6},{5,7},{6,4},{7,5},{8,10},{9,11},{10,... | collective-permute-start | bytes 786440 | tf_op jit(solution)/shard_map/ppermute | solution.py:384
  154.0 22.7 %collective-permute-start.37 = (bf16[512,256]{1,0:T(8,128)(2,1)S(1)}, bf16[512,256]{1,0:T(8,128)(2,1)S(1)}, u32[]{:S(2)}, u32[]{:S(2)}) collective-permute-start(bf16[512,256]{1,0:T(8,128)(2,1)S(1)} %get-tuple-element.119), channel_id=1, source_target_pairs={{0,3},{1,2},{2,1},{3,0},{4,7},{5,6},{6,5},{7,4},{8,11},{9,10},{10,... | collective-permute-start | bytes 786440 | tf_op jit(solution)/shard_map/ppermute | solution.py:1203
  194.2 15.9 %collective-permute-start.40 = (bf16[512,256]{1,0:T(8,128)(2,1)}, bf16[512,256]{1,0:T(8,128)(2,1)S(1)}, u32[]{:S(2)}, u32[]{:S(2)}) collective-permute-start(bf16[512,256]{1,0:T(8,128)(2,1)} %get-tuple-element.137), channel_id=1, source_target_pairs={{0,2},{1,3},{2,0},{3,1},{4,6},{5,7},{6,4},{7,5},{8,10},{9,11},{10,... | collective-permute-start | bytes 786440 | tf_op jit(solution)/shard_map/ppermute | solution.py:384
  195.7 14.5 %collective-permute-start.41 = (bf16[512,256]{1,0:T(8,128)(2,1)}, bf16[512,256]{1,0:T(8,128)(2,1)S(1)}, u32[]{:S(2)}, u32[]{:S(2)}) collective-permute-start(bf16[512,256]{1,0:T(8,128)(2,1)} %get-tuple-element.138), channel_id=1, source_target_pairs={{0,3},{1,2},{2,1},{3,0},{4,7},{5,6},{6,5},{7,4},{8,11},{9,10},{10,... | collective-permute-start | bytes 786440 | tf_op jit(solution)/shard_map/ppermute | solution.py:1203
  (61 other events, 509.3 us)

commit v8 on v7

--- a/solution.py
+++ b/solution.py
@@ -537,7 +537,7 @@
         for s in range(3):
             put(1 + s, bias_ref[s : s + 1, :])
         for s in range(4):
-            put(4 + s, fc_ref[:, s * part : (s + 1) * part])
+            put(4 + s, fc_ref[pl.ds(s * part, part)].reshape(1, part))
         for s in range(8):
             put(8 + s, up_ref[s // ADAPTER_RANK, s % ADAPTER_RANK : s % ADAPTER_RANK + 1, :])
         block_ref[rows:, :] = spare[...].astype(BF16)
@@ -693,14 +693,14 @@
         low = lax.broadcasted_iota(jnp.int32, (1, LANES), 1) < HEAD_DIM
         vx[:, :LANES] = v_ref[...]
         vx[:, LANES:] = jnp.ones((length, LANES), BF16)
-        scale = HEAD_DIM**-0.5 * LOG2E
+        scale = HEAD_DIM**-0.5
         causal = (lax.broadcasted_iota(jnp.int32, (2 * BLK, BLK), 0) & (BLK - 1)) >= lax.broadcasted_iota(
             jnp.int32, (2 * BLK, BLK), 1
         )
         for i in range(length // BLK):
             start, stop = i * BLK, (i + 1) * BLK
-            qb = (q_ref[start:stop, :].astype(F32) * scale).astype(BF16)
-            s = lax.dot_general(both_heads(low, qb), k_ref[:stop, :], NT, preferred_element_type=F32)
+            qb = q_ref[start:stop, :] * BF16(scale)
+            s = lax.dot_general(both_heads(low, qb), k_ref[:stop, :], NT, preferred_element_type=F32) * LOG2E
             sd = jnp.where(causal, s[:, start:], MASKED)
             top = jnp.max(sd, axis=-1, keepdims=True)
             if i:
@@ -818,7 +818,7 @@
     parts = 4
     piece = model // parts
     chunk = 512
-    wide = 512 if hidden is not None else 256
+    wide = 256
     per = part // chunk
     c0 = 0.7978845608028654
     c1 = 0.044715
@@ -984,9 +984,9 @@
                 g2_ref[at_rows(rank, half), :] = jnp.dot(ref[...], weight, preferred_element_type=F32).astype(BF16)
 
         g_ref[...] = g2_ref[:, at_lanes(lax.rem(pair, 2), LANES)]
-        scale = HEAD_DIM**-0.5 * LOG2E
+        scale = HEAD_DIM**-0.5
         low = lax.broadcasted_iota(jnp.int32, (1, LANES), 1) < HEAD_DIM
-        qs_ref[...] = (q_ref[...].astype(F32) * scale).astype(BF16)
+        qs_ref[...] = q_ref[...] * BF16(scale)
         prod = (g_ref[...].astype(F32) * o_ref[...].astype(F32)).T
         delta = [
             jnp.sum(prod[:HEAD_DIM], axis=0, keepdims=True),
@@ -1005,7 +1005,7 @@
                 for a, b in ((start, start + BLK), (start + BLK, length)):
                     if a == b:
                         continue
-                    sh = s[rows, a - start : b - start] - lse_ref[0, h : h + 1, a:b]
+                    sh = s[rows, a - start : b - start] * LOG2E - lse_ref[0, h : h + 1, a:b]
                     if a == start:
                         sh = jnp.where(causal, sh, MASKED)
                     p = jnp.exp2(sh)
@@ -1165,7 +1165,7 @@
         [shape(LEN // 2, part)] * parts,
         [pltpu.VMEM((BLK, model), BF16)],
         cost(20 * LEN * model, 8 * LEN * model),
-        56 << 20,
+        40 << 20,
     )(idx, in_own, in_recv, tokens, hidden_grad, vec)
 
 
@@ -1238,7 +1238,7 @@
     fc_line = fc_bias.reshape(1, -1)
     up_rows = up_master.reshape(2 * r, head_part)
     heads_own, u_own = prepare_blocks(
-        idx, ids, frozen_triple_weight, out_weight, frozen_triple_bias, fc_line, up_master, fc_weight, proj_weight
+        idx, ids, frozen_triple_weight, out_weight, frozen_triple_bias, fc_bias, up_master, fc_weight, proj_weight
     )
     zero_line = jnp.zeros_like(pre_gain)
     vec = jnp.stack([pre_gain, pre_shift, out_bias, mid_gain, mid_shift, zero_line, zero_line, zero_line]).astype(F32)

time: 214 us -> 213 us (level)
    unnamed x79 -> x77, local copies, waits for them, and re-layouts: 6.28 us -> 9.02 us
    pallas_call x1, Pallas kernels: 5 us -> 2.3 us  [tokens_back(): call(body, 'tokens_back', half_blocks, [row, row, row, row, full(8, model...]
  transfers between devices with their start and end apart: 47 -> 47, of which waited for: 21 -> 20; matrix products, arithmetic and copies ran while one was open for 4% -> 4% of each run, Pallas kernels for 36% -> 35%
where the time goes in v8:
time: 213 us; the launch traced here: 212 us
  Pallas kernels  94.1 us (44%)
  waiting for transfers between devices  54.2 us (25%)
  starting transfers between devices  43 us (20%)
  local copies, waits for them, and re-layouts  14.4 us (7%)
  other arithmetic  4.52 us (2%)
  between operations  2.22 us (1%)
    pallas_call x3, Pallas kernels, units_main(): call(body, 'units_main_last' if last else 'units_main_first' if not carri...  31.4 us
    ppermute x21, starting transfers between devices, hop(): return lax.ppermute(value, AXES, [(i, i ^ flip) for i in range(total)])  30 us
    ppermute x21, waiting for transfers between devices, hop(): return lax.ppermute(value, AXES, [(i, i ^ flip) for i in range(total)])  27.8 us
    pallas_call x1, Pallas kernels, attend_back_fast(): call(body, 'attend_back', pairs, [spec] * 4 + [full(half, model)] * 2 + [...  20.4 us
    ppermute x8, waiting for transfers between devices, z_hop(): return lax.ppermute(value, AXES, perm)  19.7 us
    pallas_call x1, Pallas kernels, attend_fast(): pl.pallas_call(body, grid=(pairs,), out_shape=(shape(length, width), jax....  11.5 us
    unnamed x77, local copies, waits for them, and re-layouts  9.02 us
    ppermute x8, starting transfers between devices, z_hop(): return lax.ppermute(value, AXES, perm)  7.87 us
  transfers between devices with their start and end apart: 47, of which 20 were waited for; matrix products, arithmetic and copies ran while one was open for 4% of the time, Pallas kernels for 35%

profile of v8, /device:TPU:0, one launch (start us, length us, event | category | flops | bytes accessed | tf_op | source)
XLA Modules:
  0.0 212.5 jit_solution(17449559087598551172)
XLA Ops:
  3.0 3.3 %prepare_blocks.1 = (bf16[136,1024]{1,0:T(8,128)(2,1)}, bf16[1,128,2048]{2,1,0:T(8,128)(2,1)}) custom-call(s32[3]{0:T(128)} %pad_add_fusion.ix, s32[16,128]{1,0:T(8,128)} %bitcast.21, bf16[128,3,256]{2,1,0:T(4,128)(2,1)} %copy.32.triple_ref, bf16[256,128]{1,0:T(8,128)(2,1)} %out_ref.1, bf16[3,256]{1,0:T(4,128)(2,1)} %bias_ref.3, bf16[1024]{0:T(1024)(128)(2,1)} %fc_ref.1, ...), custom_call_target="tpu_custom_call" | custom-call | bytes 52428 | tf_op jit(solution)/shard_map/prepare_blocks/pallas_call | solution.py:548
  6.3 3.0 %collective-permute-start = (bf16[136,1024]{1,0:T(8,128)(2,1)}, bf16[136,1024]{1,0:T(8,128)(2,1)S(1)}, u32[]{:S(2)}, u32[]{:S(2)}) collective-permute-start(bf16[136,1024]{1,0:T(8,128)(2,1)} %get-tuple-element.77), channel_id=1, source_target_pairs={{0,8},{1,9},{2,10},{3,11},{4,12},{5,13},{6,14},{7,15},{8,0},{9,1},... | collective-permute-start | bytes 835592 | tf_op jit(solution)/shard_map/ppermute | solution.py:384
  13.1 3.1 %collective-permute-done = bf16[136,1024]{1,0:T(8,128)(2,1)S(1)} collective-permute-done((bf16[136,1024]{1,0:T(8,128)(2,1)}, bf16[136,1024]{1,0:T(8,128)(2,1)S(1)}, u32[]{:S(2)}, u32[]{:S(2)}) %collective-permute-start) | collective-permute-done | bytes 278560 | tf_op jit(solution)/shard_map/ppermute | solution.py:384
  20.6 3.2 %collective-permute-done.5.rest_2_ = bf16[1,128,2048]{2,1,0:T(8,128)(2,1)} collective-permute-done((bf16[1,128,2048]{2,1,0:T(8,128)(2,1)}, bf16[1,128,2048]{2,1,0:T(8,128)(2,1)}, u32[]{:S(2)}, u32[]{:S(2)}) %collective-permute-start.5) | collective-permute-done | bytes 524320 | tf_op jit(solution)/shard_map/ppermute | solution.py:384
  29.0 5.3 %collective-permute-done.4 = bf16[136,1024]{1,0:T(8,128)(2,1)S(1)} collective-permute-done((bf16[136,1024]{1,0:T(8,128)(2,1)S(1)}, bf16[136,1024]{1,0:T(8,128)(2,1)S(1)}, u32[]{:S(2)}, u32[]{:S(2)}) %collective-permute-start.4) | collective-permute-done | bytes 278560 | tf_op jit(solution)/shard_map/ppermute | solution.py:407
  35.2 2.7 %collective-permute-done.7.rest_4_.near_ref.rest_1_.rest_2_ = bf16[2,136,1024]{2,1,0:T(8,128)(2,1)S(1)} collective-permute-done((bf16[2,136,1024]{2,1,0:T(8,128)(2,1)S(1)}, bf16[2,136,1024]{2,1,0:T(8,128)(2,1)S(1)}, u32[]{:S(2)}, u32[]{:S(2)}) %collective-permute-start.7) | collective-permute-done | bytes 557088 | tf_op jit(solution)/shard_map/ppermute | solution.py:384
  41.3 5.2 %collective-permute-done.10 = bf16[1,128,2048]{2,1,0:T(8,128)(2,1)S(1)} collective-permute-done((bf16[1,128,2048]{2,1,0:T(8,128)(2,1)S(1)}, bf16[1,128,2048]{2,1,0:T(8,128)(2,1)S(1)}, u32[]{:S(2)}, u32[]{:S(2)}) %collective-permute-start.10) | collective-permute-done | bytes 524320 | tf_op jit(solution)/shard_map/ppermute | solution.py:384
  48.5 2.6 %collective-permute-done.14.rest_3_.rest_6_.rest_7_ = bf16[2,136,1024]{2,1,0:T(8,128)(2,1)S(1)} collective-permute-done((bf16[2,136,1024]{2,1,0:T(8,128)(2,1)S(1)}, bf16[2,136,1024]{2,1,0:T(8,128)(2,1)S(1)}, u32[]{:S(2)}, u32[]{:S(2)}) %collective-permute-start.14) | collective-permute-done | bytes 557088 | tf_op jit(solution)/shard_map/ppermute | solution.py:384
  55.5 5.0 %collective-permute-done.13 = bf16[1,128,2048]{2,1,0:T(8,128)(2,1)S(1)} collective-permute-done((bf16[1,128,2048]{2,1,0:T(8,128)(2,1)S(1)}, bf16[1,128,2048]{2,1,0:T(8,128)(2,1)S(1)}, u32[]{:S(2)}, u32[]{:S(2)}) %collective-permute-start.13) | collective-permute-done | bytes 524320 | tf_op jit(solution)/shard_map/ppermute | solution.py:407
  60.6 2.3 %collective-permute-done.16.rest_3_.rest_4_ = bf16[2,136,1024]{2,1,0:T(8,128)(2,1)S(1)} collective-permute-done((bf16[2,136,1024]{2,1,0:T(8,128)(2,1)S(1)}, bf16[2,136,1024]{2,1,0:T(8,128)(2,1)S(1)}, u32[]{:S(2)}, u32[]{:S(2)}) %collective-permute-start.16) | collective-permute-done | bytes 557088 | tf_op jit(solution)/shard_map/ppermute | solution.py:384
  65.2 7.4 %collective-permute-done.15 = bf16[1,128,2048]{2,1,0:T(8,128)(2,1)S(1)} collective-permute-done((bf16[1,128,2048]{2,1,0:T(8,128)(2,1)S(1)}, bf16[1,128,2048]{2,1,0:T(8,128)(2,1)S(1)}, u32[]{:S(2)}, u32[]{:S(2)}) %collective-permute-start.15) | collective-permute-done | bytes 524320 | tf_op jit(solution)/shard_map/ppermute | solution.py:407
  82.3 3.4 %norm_rows.1 = (bf16[1024,1024]{1,0:T(8,128)(2,1)S(1)}, bf16[1024,128]{1,0:T(8,128)(2,1)S(1)}, bf16[16,1024]{1,0:T(8,128)(2,1)S(1)}, bf16[128,1024]{1,0:T(8,128)(2,1)S(1)}) custom-call(s32[3]{0:T(128)S(1)} %copy-done.21, bf16[2048,1024]{1,0:T(8,128)(2,1)S(1)} %copy-done.6, f32[8,1024]{1,0:T(8,128)S(1)} %convert_element_type.10.vec_ref, ...), custom_call_target="tpu_custom_call" | custom-call | flops 26843544 | bytes 419430 | tf_op jit(solution)/shard_map/norm_rows/pallas_call | solution.py:622
  85.7 6.2 %project_heads.1 = (bf16[1024,512]{1,0:T(8,128)(2,1)S(1)}, bf16[1024,512]{1,0:T(8,128)(2,1)S(1)}, bf16[1024,512]{1,0:T(8,128)(2,1)S(1)}, bf16[2,128,768]{2,1,0:T(8,128)(2,1)S(1)}) custom-call(s32[3]{0:T(128)S(1)} %copy-done.21, bf16[1024,1024]{1,0:T(8,128)(2,1)S(1)} %get-tuple-element.88.normed_ref, bf16[1024,128]{1,0:T(8,128)(2,1)S(1)} %get-tuple-element.89.latent_ref, ...), custom_call_target="tpu_custom_call" | custom-call | flops 322122560 | bytes 1677721 | tf_op jit(solution)/shard_map/project_heads/pallas_call | solution.py:671
  91.9 11.5 %attend.1 = (bf16[1024,512]{1,0:T(8,128)(2,1)S(1)}, f32[4,8,1024]{2,1,0:T(8,128)S(1)}) custom-call(bf16[1024,512]{1,0:T(8,128)(2,1)S(1)} %get-tuple-element.90.q_ref, bf16[1024,512]{1,0:T(8,128)(2,1)S(1)} %get-tuple-element.91.k_ref, bf16[1024,512]{1,0:T(8,128)(2,1)S(1)} %get-tuple-element.92.v_ref), custom_call_target="tpu_custom_call" | custom-call | flops 429496736 | bytes 419430 | tf_op jit(solution)/shard_map/attend/pallas_call | solution.py:720
  108.0 2.5 %attention_out_own.1 = (f32[512,1024]{1,0:T(8,128)S(1)}, bf16[512,1024]{1,0:T(8,128)(2,1)S(1)}) custom-call(s32[3]{0:T(128)S(1)} %copy-done.21, bf16[1024,512]{1,0:T(8,128)(2,1)S(1)} %get-tuple-element.93.att.o_ref, bf16[512,1024]{1,0:T(8,128)(2,1)S(1)} %constant_dynamic-slice_fusion.1.tok, f32[8,1024]{1,0:T(8,128)S(1)} %convert_element_type.10.vec_ref, ...), custom_call_target="tpu_custom_call" | custom-call | flops 53687092 | bytes 524288 | tf_op jit(solution)/shard_map/attention_out_own/pallas_call | solution.py:788
  117.4 14.4 %units_main_first.1 = (bf16[512,1024]{1,0:T(8,128)(2,1)S(1)}, bf16[512,1024]{1,0:T(8,128)(2,1)S(1)}) custom-call(s32[3]{0:T(128)S(1)} %copy-done.21, bf16[512,1024]{1,0:T(8,128)(2,1)S(1)} %get-tuple-element.96.normed_ref, bf16[512,1024]{1,0:T(8,128)(2,1)S(1)} %constant_dynamic-slice_fusion.cot, f32[512,128]{1,0:T(8,128)S(1)} %get-tuple-element.87.weight_ref, ...), custom_call_target="tpu_custom_call" | custom-call | flops 858993472 | bytes 1677721 | tf_op jit(solution)/shard_map/units_main_first/pallas_call | solution.py:938
  134.9 8.1 %units_main_next.1 = (bf16[512,1024]{1,0:T(8,128)(2,1)S(1)}, bf16[512,1024]{1,0:T(8,128)(2,1)S(1)}) custom-call(s32[3]{0:T(128)S(1)} %copy-done.21, bf16[512,1024]{1,0:T(8,128)(2,1)S(1)} %get-tuple-element.96.normed_ref, bf16[512,1024]{1,0:T(8,128)(2,1)S(1)} %constant_dynamic-slice_fusion.cot, f32[512,128]{1,0:T(8,128)S(1)} %get-tuple-element.87.weight_ref, ...), custom_call_target="tpu_custom_call" | custom-call | flops 429496736 | bytes 838860 | tf_op jit(solution)/shard_map/units_main_next/pallas_call | solution.py:938
  143.0 9.0 %units_main_last.1 = (bf16[512,1024]{1,0:T(8,128)(2,1)S(1)}, bf16[512,256]{1,0:T(8,128)(2,1)S(1)}, bf16[512,256]{1,0:T(8,128)(2,1)S(1)}, bf16[512,256]{1,0:T(8,128)(2,1)S(1)}, bf16[512,256]{1,0:T(8,128)(2,1)S(1)}) custom-call(s32[3]{0:T(128)S(1)} %copy-done.21, bf16[512,1024]{1,0:T(8,128)(2,1)S(1)} %get-tuple-element.96.normed_ref, ...), custom_call_target="tpu_custom_call" | custom-call | flops 429496736 | bytes 838860 | tf_op jit(solution)/shard_map/units_main_last/pallas_call | solution.py:938
  154.9 20.4 %attend_back.1 = (bf16[1024,512]{1,0:T(8,128)(2,1)S(1)}, bf16[1024,512]{1,0:T(8,128)(2,1)S(1)}, bf16[1024,512]{1,0:T(8,128)(2,1)S(1)}, bf16[1024,128]{1,0:T(8,12...) custom-call(s32[3]{0:T(128)S(1)} %copy-done.21, ...), custom_call_target="tpu_custom_call" | custom-call | flops 1073741824 | bytes 838860 | tf_op jit(solution)/shard_map/attend_back/pallas_call | solution.py:1060
  176.1 6.9 %heads_back.1 = (bf16[512,1024]{1,0:T(8,128)(2,1)}, bf16[512,1024]{1,0:T(8,128)(2,1)S(1)}) custom-call(s32[3]{0:T(128)S(1)} %copy-done.21, bf16[1024,512]{1,0:T(8,128)(2,1)S(1)} %get-tuple-element.124.dq_ref, bf16[1024,512]{1,0:T(8,128)(2,1)S(1)} %get-tuple-element.125.dk_ref, bf16[1024,512]{1,0:T(8,128)(2,1)S(1)} %get-tuple-element.126.dv_ref, ...), custom_call_target="tpu_custom_call" | custom-call | flops 322122560 | bytes 314572 | tf_op jit(solution)/shard_map/heads_back/pallas_call | solution.py:1129
  191.0 2.3 %tokens_back.1 = (bf16[512,256]{1,0:T(8,128)(2,1)S(1)}, bf16[512,256]{1,0:T(8,128)(2,1)S(1)}, bf16[512,256]{1,0:T(8,128)(2,1)S(1)}, bf16[512,256]{1,0:T(8,128)(2,1)S(1)}) custom-call(s32[3]{0:T(128)S(1)} %copy-done.21, bf16[512,1024]{1,0:T(8,128)(2,1)S(1)} %copy-done.10, bf16[512,1024]{1,0:T(8,128)(2,1)S(1)} %collective-permute-done.38.recv, ...), custom_call_target="tpu_custom_call" | custom-call | flops 2097152 | bytes 838860 | tf_op jit(solution)/shard_map/tokens_back/pallas_call | solution.py:1159
  196.5 2.9 %collective-permute-done.44 = f32[8,1280]{1,0:T(8,128)S(1)} collective-permute-done((f32[8,1280]{1,0:T(8,128)S(1)}, f32[8,1280]{1,0:T(8,128)S(1)}, u32[]{:S(2)}, u32[]{:S(2)}) %collective-permute-start.44) | collective-permute-done | bytes 40992 | tf_op jit(solution)/shard_map/ppermute | solution.py:384
  199.4 2.4 %collective-permute-start.45 = (f32[8,1280]{1,0:T(8,128)S(1)}, f32[8,1280]{1,0:T(8,128)S(1)}, u32[]{:S(2)}, u32[]{:S(2)}) collective-permute-start(f32[8,1280]{1,0:T(8,128)S(1)} %add.63), channel_id=1, source_target_pairs={{0,8},{1,9},{2,10},{3,11},{4,12},{5,13},{6,14},{7,15},{8,0},{9,1},... | collective-permute-start | bytes 122888 | tf_op jit(solution)/shard_map/ppermute | solution.py:384
  203.8 3.2 %collective-permute-start.46 = (f32[8,1280]{1,0:T(8,128)S(1)}, f32[8,1280]{1,0:T(8,128)S(1)}, u32[]{:S(2)}, u32[]{:S(2)}) collective-permute-start(f32[8,1280]{1,0:T(8,128)S(1)} %add.64), channel_id=1, source_target_pairs={{0,16},{1,17},{2,18},{3,19},{4,20},{5,21},{6,22},{7,23},{8,24},{9,... | collective-permute-start | bytes 122888 | tf_op jit(solution)/shard_map/ppermute | solution.py:384
  (205 shorter events, 73.9 us)
Async XLA Ops:
  10.0 13.8 %collective-permute-start.5 = (bf16[1,128,2048]{2,1,0:T(8,128)(2,1)}, bf16[1,128,2048]{2,1,0:T(8,128)(2,1)}, u32[]{:S(2)}, u32[]{:S(2)}) collective-permute-start(bf16[1,128,2048]{2,1,0:T(8,128)(2,1)} %get-tuple-element.83.rest_0_), channel_id=1, source_target_pairs={{0,2},{1,3},{2,0},{3,1},{4,6},{5,7},{6,4},{7,5},{8,10},{9,11},{10,... | collective-permute-start | bytes 1572872 | tf_op jit(solution)/shard_map/ppermute | solution.py:384
  11.6 13.4 %collective-permute-start.6 = (bf16[1,128,2048]{2,1,0:T(8,128)(2,1)}, bf16[1,128,2048]{2,1,0:T(8,128)(2,1)}, u32[]{:S(2)}, u32[]{:S(2)}) collective-permute-start(bf16[1,128,2048]{2,1,0:T(8,128)(2,1)} %get-tuple-element.83.rest_0_), channel_id=1, source_target_pairs={{0,4},{1,5},{2,6},{3,7},{4,0},{5,1},{6,2},{7,3},{8,12},{9,13},{10,... | collective-permute-start | bytes 1572872 | tf_op jit(solution)/shard_map/ppermute | solution.py:384
  16.9 12.1 %collective-permute-start.3 = (bf16[136,1024]{1,0:T(8,128)(2,1)S(1)}, bf16[136,1024]{1,0:T(8,128)(2,1)S(1)}, u32[]{:S(2)}, u32[]{:S(2)}) collective-permute-start(bf16[136,1024]{1,0:T(8,128)(2,1)S(1)} %collective-permute-done.2), channel_id=1, source_target_pairs={{8,0},{9,1},{10,2},{11,3},{12,4},{13,5},{14,6},{15,7},{16,24},{17,... | collective-permute-start | bytes 835592 | tf_op jit(solution)/shard_map/ppermute | solution.py:407
  18.2 16.1 %collective-permute-start.4 = (bf16[136,1024]{1,0:T(8,128)(2,1)S(1)}, bf16[136,1024]{1,0:T(8,128)(2,1)S(1)}, u32[]{:S(2)}, u32[]{:S(2)}) collective-permute-start(bf16[136,1024]{1,0:T(8,128)(2,1)S(1)} %collective-permute-done.1), channel_id=1, source_target_pairs={{8,0},{9,1},{10,2},{11,3},{12,4},{13,5},{14,6},{15,7},{16,24},{17,... | collective-permute-start | bytes 835592 | tf_op jit(solution)/shard_map/ppermute | solution.py:407
  25.0 12.9 %collective-permute-start.7 = (bf16[2,136,1024]{2,1,0:T(8,128)(2,1)S(1)}, bf16[2,136,1024]{2,1,0:T(8,128)(2,1)S(1)}, u32[]{:S(2)}, u32[]{:S(2)}) collective-permute-start(bf16[2,136,1024]{2,1,0:T(8,128)(2,1)S(1)} %pad_maximum_fusion.2.rest_0_.rest_1_), channel_id=1, source_target_pairs={{0,2},{1,3},{2,0},{3,1},{4,6},{5,7},{6,4},{7,5},{8,10},{9,11},{10,... | collective-permute-start | bytes 1671176 | tf_op jit(solution)/shard_map/ppermute | solution.py:384
  25.5 12.8 %collective-permute-start.8 = (bf16[2,136,1024]{2,1,0:T(8,128)(2,1)S(1)}, bf16[2,136,1024]{2,1,0:T(8,128)(2,1)S(1)}, u32[]{:S(2)}, u32[]{:S(2)}) collective-permute-start(bf16[2,136,1024]{2,1,0:T(8,128)(2,1)S(1)} %pad_maximum_fusion.2.rest_0_.rest_1_), channel_id=1, source_target_pairs={{0,4},{1,5},{2,6},{3,7},{4,0},{5,1},{6,2},{7,3},{8,12},{9,13},{10,... | collective-permute-start | bytes 1671176 | tf_op jit(solution)/shard_map/ppermute | solution.py:384
  34.4 12.1 %collective-permute-start.10 = (bf16[1,128,2048]{2,1,0:T(8,128)(2,1)S(1)}, bf16[1,128,2048]{2,1,0:T(8,128)(2,1)S(1)}, u32[]{:S(2)}, u32[]{:S(2)}) collective-permute-start(bf16[1,128,2048]{2,1,0:T(8,128)(2,1)S(1)} %copy-done.11), channel_id=1, source_target_pairs={{0,8},{1,9},{2,10},{3,11},{4,12},{5,13},{6,14},{7,15},{8,0},{9,1},... | collective-permute-start | bytes 1572872 | tf_op jit(solution)/shard_map/ppermute | solution.py:384
  34.5 12.7 %collective-permute-start.12 = (bf16[1,128,2048]{2,1,0:T(8,128)(2,1)S(1)}, bf16[1,128,2048]{2,1,0:T(8,128)(2,1)S(1)}, u32[]{:S(2)}, u32[]{:S(2)}) collective-permute-start(bf16[1,128,2048]{2,1,0:T(8,128)(2,1)S(1)} %copy-done.11), channel_id=1, source_target_pairs={{8,16},{9,17},{10,18},{11,19},{12,20},{13,21},{14,22},{15,23},{16,... | collective-permute-start | bytes 1572872 | tf_op jit(solution)/shard_map/ppermute | solution.py:407
  38.3 12.8 %collective-permute-start.14 = (bf16[2,136,1024]{2,1,0:T(8,128)(2,1)S(1)}, bf16[2,136,1024]{2,1,0:T(8,128)(2,1)S(1)}, u32[]{:S(2)}, u32[]{:S(2)}) collective-permute-start(bf16[2,136,1024]{2,1,0:T(8,128)(2,1)S(1)} %pad_maximum_fusion.1.rest_1_.rest_4_.rest_5_), channel_id=1, source_target_pairs={{0,4},{1,5},{2,6},{3,7},{4,0},{5,1},{6,2},{7,3},{8,12},{9,13},{10,... | collective-permute-start | bytes 1671176 | tf_op jit(solution)/shard_map/ppermute | solution.py:384
  39.9 12.8 %collective-permute-start.9 = (bf16[2,136,1024]{2,1,0:T(8,128)(2,1)S(1)}, bf16[2,136,1024]{2,1,0:T(8,128)(2,1)S(1)}, u32[]{:S(2)}, u32[]{:S(2)}) collective-permute-start(bf16[2,136,1024]{2,1,0:T(8,128)(2,1)S(1)} %pad_maximum_fusion.1.rest_1_.rest_4_.rest_5_), channel_id=1, source_target_pairs={{0,2},{1,3},{2,0},{3,1},{4,6},{5,7},{6,4},{7,5},{8,10},{9,11},{10,... | collective-permute-start | bytes 1671176 | tf_op jit(solution)/shard_map/ppermute | solution.py:384
  47.2 13.3 %collective-permute-start.13 = (bf16[1,128,2048]{2,1,0:T(8,128)(2,1)S(1)}, bf16[1,128,2048]{2,1,0:T(8,128)(2,1)S(1)}, u32[]{:S(2)}, u32[]{:S(2)}) collective-permute-start(bf16[1,128,2048]{2,1,0:T(8,128)(2,1)S(1)} %collective-permute-done.12), channel_id=1, source_target_pairs={{8,0},{9,1},{10,2},{11,3},{12,4},{13,5},{14,6},{15,7},{16,24},{17,... | collective-permute-start | bytes 1572872 | tf_op jit(solution)/shard_map/ppermute | solution.py:407
  51.1 11.8 %collective-permute-start.16 = (bf16[2,136,1024]{2,1,0:T(8,128)(2,1)S(1)}, bf16[2,136,1024]{2,1,0:T(8,128)(2,1)S(1)}, u32[]{:S(2)}, u32[]{:S(2)}) collective-permute-start(bf16[2,136,1024]{2,1,0:T(8,128)(2,1)S(1)} %collective-permute-done.7.rest_4_.near_ref.rest_1_.rest_2_), channel_id=1, source_target_pairs={{0,4},{1,5},{2,6},{3,7},{4,0},{5,1},{6,2},{7,3},{8,12},{9,13},{10,... | collective-permute-start | bytes 1671176 | tf_op jit(solution)/shard_map/ppermute | solution.py:384
  52.7 20.0 %collective-permute-start.15 = (bf16[1,128,2048]{2,1,0:T(8,128)(2,1)S(1)}, bf16[1,128,2048]{2,1,0:T(8,128)(2,1)S(1)}, u32[]{:S(2)}, u32[]{:S(2)}) collective-permute-start(bf16[1,128,2048]{2,1,0:T(8,128)(2,1)S(1)} %collective-permute-done.11), channel_id=1, source_target_pairs={{8,0},{9,1},{10,2},{11,3},{12,4},{13,5},{14,6},{15,7},{16,24},{17,... | collective-permute-start | bytes 1572872 | tf_op jit(solution)/shard_map/ppermute | solution.py:407
  53.9 20.2 %collective-permute-start.18 = (bf16[2,136,1024]{2,1,0:T(8,128)(2,1)S(1)}, bf16[2,136,1024]{2,1,0:T(8,128)(2,1)S(1)}, u32[]{:S(2)}, u32[]{:S(2)}) collective-permute-start(bf16[2,136,1024]{2,1,0:T(8,128)(2,1)S(1)} %collective-permute-done.14.rest_3_.rest_6_.rest_7_), channel_id=1, source_target_pairs={{0,2},{1,3},{2,0},{3,1},{4,6},{5,7},{6,4},{7,5},{8,10},{9,11},{10,... | collective-permute-start | bytes 1671176 | tf_op jit(solution)/shard_map/ppermute | solution.py:384
  63.7 22.0 %collective-permute-start.17 = (bf16[1,128,2048]{2,1,0:T(8,128)(2,1)}, bf16[1,128,2048]{2,1,0:T(8,128)(2,1)}, u32[]{:S(2)}, u32[]{:S(2)}) collective-permute-start(bf16[1,128,2048]{2,1,0:T(8,128)(2,1)} %collective-permute-done.5.rest_2_), channel_id=1, source_target_pairs={{0,4},{1,5},{2,6},{3,7},{4,0},{5,1},{6,2},{7,3},{8,12},{9,13},{10,... | collective-permute-start | bytes 1572872 | tf_op jit(solution)/shard_map/ppermute | solution.py:384
  75.0 35.6 %collective-permute-start.21 = (bf16[3,128,2048]{2,1,0:T(8,128)(2,1)}, bf16[3,128,2048]{2,1,0:T(8,128)(2,1)}, u32[]{:S(2)}, u32[]{:S(2)}) collective-permute-start(bf16[3,128,2048]{2,1,0:T(8,128)(2,1)} %pad_maximum_fusion.rest_1_), channel_id=1, source_target_pairs={{0,2},{1,3},{2,0},{3,1},{4,6},{5,7},{6,4},{7,5},{8,10},{9,11},{10,... | collective-permute-start | bytes 4718600 | tf_op jit(solution)/shard_map/ppermute | solution.py:384
  76.5 34.2 %collective-permute-start.22 = (bf16[3,128,2048]{2,1,0:T(8,128)(2,1)}, bf16[3,128,2048]{2,1,0:T(8,128)(2,1)}, u32[]{:S(2)}, u32[]{:S(2)}) collective-permute-start(bf16[3,128,2048]{2,1,0:T(8,128)(2,1)} %pad_maximum_fusion.rest_1_), channel_id=1, source_target_pairs={{0,4},{1,5},{2,6},{3,7},{4,0},{5,1},{6,2},{7,3},{8,12},{9,13},{10,... | collective-permute-start | bytes 4718600 | tf_op jit(solution)/shard_map/ppermute | solution.py:384
  113.6 19.7 %collective-permute-start.27 = (bf16[3,64,2048]{2,1,0:T(8,128)(2,1)S(1)}, bf16[3,64,2048]{2,1,0:T(8,128)(2,1)S(1)}, u32[]{:S(2)}, u32[]{:S(2)}) collective-permute-start(bf16[3,64,2048]{2,1,0:T(8,128)(2,1)S(1)} %slice.24), channel_id=1, source_target_pairs={{0,4},{1,5},{2,6},{3,7},{4,0},{5,1},{6,2},{7,3},{8,12},{9,13},{10,... | collective-permute-start | bytes 2359304 | tf_op jit(solution)/shard_map/ppermute | solution.py:384
  114.7 19.2 %collective-permute-start.28 = (bf16[3,64,2048]{2,1,0:T(8,128)(2,1)S(1)}, bf16[3,64,2048]{2,1,0:T(8,128)(2,1)S(1)}, u32[]{:S(2)}, u32[]{:S(2)}) collective-permute-start(bf16[3,64,2048]{2,1,0:T(8,128)(2,1)S(1)} %slice.25), channel_id=1, source_target_pairs={{0,2},{1,3},{2,0},{3,1},{4,6},{5,7},{6,4},{7,5},{8,10},{9,11},{10,... | collective-permute-start | bytes 2359304 | tf_op jit(solution)/shard_map/ppermute | solution.py:384
  152.6 22.8 %collective-permute-start.35 = (bf16[512,256]{1,0:T(8,128)(2,1)S(1)}, bf16[512,256]{1,0:T(8,128)(2,1)S(1)}, u32[]{:S(2)}, u32[]{:S(2)}) collective-permute-start(bf16[512,256]{1,0:T(8,128)(2,1)S(1)} %get-tuple-element.117), channel_id=1, source_target_pairs={{0,1},{1,0},{2,3},{3,2},{4,5},{5,4},{6,7},{7,6},{8,9},{9,8},{10,11... | collective-permute-start | bytes 786440 | tf_op jit(solution)/shard_map/ppermute | solution.py:389
  152.6 23.4 %collective-permute-start.36 = (bf16[512,256]{1,0:T(8,128)(2,1)S(1)}, bf16[512,256]{1,0:T(8,128)(2,1)S(1)}, u32[]{:S(2)}, u32[]{:S(2)}) collective-permute-start(bf16[512,256]{1,0:T(8,128)(2,1)S(1)} %get-tuple-element.118), channel_id=1, source_target_pairs={{0,2},{1,3},{2,0},{3,1},{4,6},{5,7},{6,4},{7,5},{8,10},{9,11},{10,... | collective-permute-start | bytes 786440 | tf_op jit(solution)/shard_map/ppermute | solution.py:384
  153.2 22.9 %collective-permute-start.37 = (bf16[512,256]{1,0:T(8,128)(2,1)S(1)}, bf16[512,256]{1,0:T(8,128)(2,1)S(1)}, u32[]{:S(2)}, u32[]{:S(2)}) collective-permute-start(bf16[512,256]{1,0:T(8,128)(2,1)S(1)} %get-tuple-element.119), channel_id=1, source_target_pairs={{0,3},{1,2},{2,1},{3,0},{4,7},{5,6},{6,5},{7,4},{8,11},{9,10},{10,... | collective-permute-start | bytes 786440 | tf_op jit(solution)/shard_map/ppermute | solution.py:1203
  193.5 15.9 %collective-permute-start.40 = (bf16[512,256]{1,0:T(8,128)(2,1)S(1)}, bf16[512,256]{1,0:T(8,128)(2,1)S(1)}, u32[]{:S(2)}, u32[]{:S(2)}) collective-permute-start(bf16[512,256]{1,0:T(8,128)(2,1)S(1)} %get-tuple-element.137), channel_id=1, source_target_pairs={{0,2},{1,3},{2,0},{3,1},{4,6},{5,7},{6,4},{7,5},{8,10},{9,11},{10,... | collective-permute-start | bytes 786440 | tf_op jit(solution)/shard_map/ppermute | solution.py:384
  195.0 14.5 %collective-permute-start.41 = (bf16[512,256]{1,0:T(8,128)(2,1)S(1)}, bf16[512,256]{1,0:T(8,128)(2,1)S(1)}, u32[]{:S(2)}, u32[]{:S(2)}) collective-permute-start(bf16[512,256]{1,0:T(8,128)(2,1)S(1)} %get-tuple-element.138), channel_id=1, source_target_pairs={{0,3},{1,2},{2,1},{3,0},{4,7},{5,6},{6,5},{7,4},{8,11},{9,10},{10,... | collective-permute-start | bytes 786440 | tf_op jit(solution)/shard_map/ppermute | solution.py:1203
  (60 other events, 400.4 us)

commit v9 on v8

--- a/solution.py
+++ b/solution.py
@@ -818,7 +818,7 @@
     parts = 4
     piece = model // parts
     chunk = 512
-    wide = 256
+    wide = 512 if len(groups) == 1 and hidden is None else 256
     per = part // chunk
     c0 = 0.7978845608028654
     c1 = 0.044715

time: 213 us -> 213 us (level)
  no operation moved by 1% of the time
where the time goes in v9:
time: 213 us; the launch traced here: 212 us
  Pallas kernels  93.7 us (44%)
  waiting for transfers between devices  54.2 us (25%)
  starting transfers between devices  43 us (20%)
  local copies, waits for them, and re-layouts  14.4 us (7%)
  other arithmetic  4.52 us (2%)
  between operations  2.22 us (1%)
    pallas_call x3, Pallas kernels, units_main(): call(body, 'units_main_last' if last else 'units_main_first' if not carri...  31 us
    ppermute x21, starting transfers between devices, hop(): return lax.ppermute(value, AXES, [(i, i ^ flip) for i in range(total)])  30 us
    ppermute x21, waiting for transfers between devices, hop(): return lax.ppermute(value, AXES, [(i, i ^ flip) for i in range(total)])  27.8 us
    pallas_call x1, Pallas kernels, attend_back_fast(): call(body, 'attend_back', pairs, [spec] * 4 + [full(half, model)] * 2 + [...  20.4 us
    ppermute x8, waiting for transfers between devices, z_hop(): return lax.ppermute(value, AXES, perm)  19.7 us
    pallas_call x1, Pallas kernels, attend_fast(): pl.pallas_call(body, grid=(pairs,), out_shape=(shape(length, width), jax....  11.5 us
    unnamed x77, local copies, waits for them, and re-layouts  9.02 us
    ppermute x8, starting transfers between devices, z_hop(): return lax.ppermute(value, AXES, perm)  7.87 us
  transfers between devices with their start and end apart: 47, of which 20 were waited for; matrix products, arithmetic and copies ran while one was open for 4% of the time, Pallas kernels for 35%

profile of v9, /device:TPU:0, one launch (start us, length us, event | category | flops | bytes accessed | tf_op | source)
XLA Modules:
  0.0 212.1 jit_solution(16645899305131784209)
XLA Ops:
  3.0 3.3 %prepare_blocks.1 = (bf16[136,1024]{1,0:T(8,128)(2,1)}, bf16[1,128,2048]{2,1,0:T(8,128)(2,1)}) custom-call(s32[3]{0:T(128)} %pad_add_fusion.ix, s32[16,128]{1,0:T(8,128)} %bitcast.21, bf16[128,3,256]{2,1,0:T(4,128)(2,1)} %copy.32.triple_ref, bf16[256,128]{1,0:T(8,128)(2,1)} %out_ref.1, bf16[3,256]{1,0:T(4,128)(2,1)} %bias_ref.3, bf16[1024]{0:T(1024)(128)(2,1)} %fc_ref.1, ...), custom_call_target="tpu_custom_call" | custom-call | bytes 52428 | tf_op jit(solution)/shard_map/prepare_blocks/pallas_call | solution.py:548
  6.3 3.0 %collective-permute-start = (bf16[136,1024]{1,0:T(8,128)(2,1)}, bf16[136,1024]{1,0:T(8,128)(2,1)S(1)}, u32[]{:S(2)}, u32[]{:S(2)}) collective-permute-start(bf16[136,1024]{1,0:T(8,128)(2,1)} %get-tuple-element.77), channel_id=1, source_target_pairs={{0,8},{1,9},{2,10},{3,11},{4,12},{5,13},{6,14},{7,15},{8,0},{9,1},... | collective-permute-start | bytes 835592 | tf_op jit(solution)/shard_map/ppermute | solution.py:384
  13.1 3.1 %collective-permute-done = bf16[136,1024]{1,0:T(8,128)(2,1)S(1)} collective-permute-done((bf16[136,1024]{1,0:T(8,128)(2,1)}, bf16[136,1024]{1,0:T(8,128)(2,1)S(1)}, u32[]{:S(2)}, u32[]{:S(2)}) %collective-permute-start) | collective-permute-done | bytes 278560 | tf_op jit(solution)/shard_map/ppermute | solution.py:384
  20.6 3.2 %collective-permute-done.5.rest_2_ = bf16[1,128,2048]{2,1,0:T(8,128)(2,1)} collective-permute-done((bf16[1,128,2048]{2,1,0:T(8,128)(2,1)}, bf16[1,128,2048]{2,1,0:T(8,128)(2,1)}, u32[]{:S(2)}, u32[]{:S(2)}) %collective-permute-start.5) | collective-permute-done | bytes 524320 | tf_op jit(solution)/shard_map/ppermute | solution.py:384
  29.0 5.3 %collective-permute-done.4 = bf16[136,1024]{1,0:T(8,128)(2,1)S(1)} collective-permute-done((bf16[136,1024]{1,0:T(8,128)(2,1)S(1)}, bf16[136,1024]{1,0:T(8,128)(2,1)S(1)}, u32[]{:S(2)}, u32[]{:S(2)}) %collective-permute-start.4) | collective-permute-done | bytes 278560 | tf_op jit(solution)/shard_map/ppermute | solution.py:407
  35.2 2.7 %collective-permute-done.7.rest_4_.near_ref.rest_1_.rest_2_ = bf16[2,136,1024]{2,1,0:T(8,128)(2,1)S(1)} collective-permute-done((bf16[2,136,1024]{2,1,0:T(8,128)(2,1)S(1)}, bf16[2,136,1024]{2,1,0:T(8,128)(2,1)S(1)}, u32[]{:S(2)}, u32[]{:S(2)}) %collective-permute-start.7) | collective-permute-done | bytes 557088 | tf_op jit(solution)/shard_map/ppermute | solution.py:384
  41.3 5.2 %collective-permute-done.10 = bf16[1,128,2048]{2,1,0:T(8,128)(2,1)S(1)} collective-permute-done((bf16[1,128,2048]{2,1,0:T(8,128)(2,1)S(1)}, bf16[1,128,2048]{2,1,0:T(8,128)(2,1)S(1)}, u32[]{:S(2)}, u32[]{:S(2)}) %collective-permute-start.10) | collective-permute-done | bytes 524320 | tf_op jit(solution)/shard_map/ppermute | solution.py:384
  48.5 2.6 %collective-permute-done.14.rest_3_.rest_6_.rest_7_ = bf16[2,136,1024]{2,1,0:T(8,128)(2,1)S(1)} collective-permute-done((bf16[2,136,1024]{2,1,0:T(8,128)(2,1)S(1)}, bf16[2,136,1024]{2,1,0:T(8,128)(2,1)S(1)}, u32[]{:S(2)}, u32[]{:S(2)}) %collective-permute-start.14) | collective-permute-done | bytes 557088 | tf_op jit(solution)/shard_map/ppermute | solution.py:384
  55.5 5.0 %collective-permute-done.13 = bf16[1,128,2048]{2,1,0:T(8,128)(2,1)S(1)} collective-permute-done((bf16[1,128,2048]{2,1,0:T(8,128)(2,1)S(1)}, bf16[1,128,2048]{2,1,0:T(8,128)(2,1)S(1)}, u32[]{:S(2)}, u32[]{:S(2)}) %collective-permute-start.13) | collective-permute-done | bytes 524320 | tf_op jit(solution)/shard_map/ppermute | solution.py:407
  60.6 2.3 %collective-permute-done.16.rest_3_.rest_4_ = bf16[2,136,1024]{2,1,0:T(8,128)(2,1)S(1)} collective-permute-done((bf16[2,136,1024]{2,1,0:T(8,128)(2,1)S(1)}, bf16[2,136,1024]{2,1,0:T(8,128)(2,1)S(1)}, u32[]{:S(2)}, u32[]{:S(2)}) %collective-permute-start.16) | collective-permute-done | bytes 557088 | tf_op jit(solution)/shard_map/ppermute | solution.py:384
  65.2 7.4 %collective-permute-done.15 = bf16[1,128,2048]{2,1,0:T(8,128)(2,1)S(1)} collective-permute-done((bf16[1,128,2048]{2,1,0:T(8,128)(2,1)S(1)}, bf16[1,128,2048]{2,1,0:T(8,128)(2,1)S(1)}, u32[]{:S(2)}, u32[]{:S(2)}) %collective-permute-start.15) | collective-permute-done | bytes 524320 | tf_op jit(solution)/shard_map/ppermute | solution.py:407
  82.3 3.4 %norm_rows.1 = (bf16[1024,1024]{1,0:T(8,128)(2,1)S(1)}, bf16[1024,128]{1,0:T(8,128)(2,1)S(1)}, bf16[16,1024]{1,0:T(8,128)(2,1)S(1)}, bf16[128,1024]{1,0:T(8,128)(2,1)S(1)}) custom-call(s32[3]{0:T(128)S(1)} %copy-done.21, bf16[2048,1024]{1,0:T(8,128)(2,1)S(1)} %copy-done.6, f32[8,1024]{1,0:T(8,128)S(1)} %convert_element_type.10.vec_ref, ...), custom_call_target="tpu_custom_call" | custom-call | flops 26843544 | bytes 419430 | tf_op jit(solution)/shard_map/norm_rows/pallas_call | solution.py:622
  85.7 6.2 %project_heads.1 = (bf16[1024,512]{1,0:T(8,128)(2,1)S(1)}, bf16[1024,512]{1,0:T(8,128)(2,1)S(1)}, bf16[1024,512]{1,0:T(8,128)(2,1)S(1)}, bf16[2,128,768]{2,1,0:T(8,128)(2,1)S(1)}) custom-call(s32[3]{0:T(128)S(1)} %copy-done.21, bf16[1024,1024]{1,0:T(8,128)(2,1)S(1)} %get-tuple-element.88.normed_ref, bf16[1024,128]{1,0:T(8,128)(2,1)S(1)} %get-tuple-element.89.latent_ref, ...), custom_call_target="tpu_custom_call" | custom-call | flops 322122560 | bytes 1677721 | tf_op jit(solution)/shard_map/project_heads/pallas_call | solution.py:671
  91.9 11.5 %attend.1 = (bf16[1024,512]{1,0:T(8,128)(2,1)S(1)}, f32[4,8,1024]{2,1,0:T(8,128)S(1)}) custom-call(bf16[1024,512]{1,0:T(8,128)(2,1)S(1)} %get-tuple-element.90.q_ref, bf16[1024,512]{1,0:T(8,128)(2,1)S(1)} %get-tuple-element.91.k_ref, bf16[1024,512]{1,0:T(8,128)(2,1)S(1)} %get-tuple-element.92.v_ref), custom_call_target="tpu_custom_call" | custom-call | flops 429496736 | bytes 419430 | tf_op jit(solution)/shard_map/attend/pallas_call | solution.py:720
  108.0 2.5 %attention_out_own.1 = (f32[512,1024]{1,0:T(8,128)S(1)}, bf16[512,1024]{1,0:T(8,128)(2,1)S(1)}) custom-call(s32[3]{0:T(128)S(1)} %copy-done.21, bf16[1024,512]{1,0:T(8,128)(2,1)S(1)} %get-tuple-element.93.att.o_ref, bf16[512,1024]{1,0:T(8,128)(2,1)S(1)} %constant_dynamic-slice_fusion.1.tok, f32[8,1024]{1,0:T(8,128)S(1)} %convert_element_type.10.vec_ref, ...), custom_call_target="tpu_custom_call" | custom-call | flops 53687092 | bytes 524288 | tf_op jit(solution)/shard_map/attention_out_own/pallas_call | solution.py:788
  117.4 14.4 %units_main_first.1 = (bf16[512,1024]{1,0:T(8,128)(2,1)S(1)}, bf16[512,1024]{1,0:T(8,128)(2,1)S(1)}) custom-call(s32[3]{0:T(128)S(1)} %copy-done.21, bf16[512,1024]{1,0:T(8,128)(2,1)S(1)} %get-tuple-element.96.normed_ref, bf16[512,1024]{1,0:T(8,128)(2,1)S(1)} %constant_dynamic-slice_fusion.cot, f32[512,128]{1,0:T(8,128)S(1)} %get-tuple-element.87.weight_ref, ...), custom_call_target="tpu_custom_call" | custom-call | flops 858993472 | bytes 1677721 | tf_op jit(solution)/shard_map/units_main_first/pallas_call | solution.py:938
  134.9 7.7 %units_main_next.1 = (bf16[512,1024]{1,0:T(8,128)(2,1)S(1)}, bf16[512,1024]{1,0:T(8,128)(2,1)S(1)}) custom-call(s32[3]{0:T(128)S(1)} %copy-done.21, bf16[512,1024]{1,0:T(8,128)(2,1)S(1)} %get-tuple-element.96.normed_ref, bf16[512,1024]{1,0:T(8,128)(2,1)S(1)} %constant_dynamic-slice_fusion.cot, f32[512,128]{1,0:T(8,128)S(1)} %get-tuple-element.87.weight_ref, ...), custom_call_target="tpu_custom_call" | custom-call | flops 429496736 | bytes 838860 | tf_op jit(solution)/shard_map/units_main_next/pallas_call | solution.py:938
  142.6 8.9 %units_main_last.1 = (bf16[512,1024]{1,0:T(8,128)(2,1)S(1)}, bf16[512,256]{1,0:T(8,128)(2,1)S(1)}, bf16[512,256]{1,0:T(8,128)(2,1)S(1)}, bf16[512,256]{1,0:T(8,128)(2,1)S(1)}, bf16[512,256]{1,0:T(8,128)(2,1)S(1)}) custom-call(s32[3]{0:T(128)S(1)} %copy-done.21, bf16[512,1024]{1,0:T(8,128)(2,1)S(1)} %get-tuple-element.96.normed_ref, ...), custom_call_target="tpu_custom_call" | custom-call | flops 429496736 | bytes 838860 | tf_op jit(solution)/shard_map/units_main_last/pallas_call | solution.py:938
  154.4 20.4 %attend_back.1 = (bf16[1024,512]{1,0:T(8,128)(2,1)S(1)}, bf16[1024,512]{1,0:T(8,128)(2,1)S(1)}, bf16[1024,512]{1,0:T(8,128)(2,1)S(1)}, bf16[1024,128]{1,0:T(8,12...) custom-call(s32[3]{0:T(128)S(1)} %copy-done.21, ...), custom_call_target="tpu_custom_call" | custom-call | flops 1073741824 | bytes 838860 | tf_op jit(solution)/shard_map/attend_back/pallas_call | solution.py:1060
  175.7 6.9 %heads_back.1 = (bf16[512,1024]{1,0:T(8,128)(2,1)}, bf16[512,1024]{1,0:T(8,128)(2,1)S(1)}) custom-call(s32[3]{0:T(128)S(1)} %copy-done.21, bf16[1024,512]{1,0:T(8,128)(2,1)S(1)} %get-tuple-element.124.dq_ref, bf16[1024,512]{1,0:T(8,128)(2,1)S(1)} %get-tuple-element.125.dk_ref, bf16[1024,512]{1,0:T(8,128)(2,1)S(1)} %get-tuple-element.126.dv_ref, ...), custom_call_target="tpu_custom_call" | custom-call | flops 322122560 | bytes 314572 | tf_op jit(solution)/shard_map/heads_back/pallas_call | solution.py:1129
  190.6 2.3 %tokens_back.1 = (bf16[512,256]{1,0:T(8,128)(2,1)S(1)}, bf16[512,256]{1,0:T(8,128)(2,1)S(1)}, bf16[512,256]{1,0:T(8,128)(2,1)S(1)}, bf16[512,256]{1,0:T(8,128)(2,1)S(1)}) custom-call(s32[3]{0:T(128)S(1)} %copy-done.21, bf16[512,1024]{1,0:T(8,128)(2,1)S(1)} %copy-done.10, bf16[512,1024]{1,0:T(8,128)(2,1)S(1)} %collective-permute-done.38.recv, ...), custom_call_target="tpu_custom_call" | custom-call | flops 2097152 | bytes 838860 | tf_op jit(solution)/shard_map/tokens_back/pallas_call | solution.py:1159
  196.1 2.9 %collective-permute-done.44 = f32[8,1280]{1,0:T(8,128)S(1)} collective-permute-done((f32[8,1280]{1,0:T(8,128)S(1)}, f32[8,1280]{1,0:T(8,128)S(1)}, u32[]{:S(2)}, u32[]{:S(2)}) %collective-permute-start.44) | collective-permute-done | bytes 40992 | tf_op jit(solution)/shard_map/ppermute | solution.py:384
  199.0 2.4 %collective-permute-start.45 = (f32[8,1280]{1,0:T(8,128)S(1)}, f32[8,1280]{1,0:T(8,128)S(1)}, u32[]{:S(2)}, u32[]{:S(2)}) collective-permute-start(f32[8,1280]{1,0:T(8,128)S(1)} %add.63), channel_id=1, source_target_pairs={{0,8},{1,9},{2,10},{3,11},{4,12},{5,13},{6,14},{7,15},{8,0},{9,1},... | collective-permute-start | bytes 122888 | tf_op jit(solution)/shard_map/ppermute | solution.py:384
  203.4 3.2 %collective-permute-start.46 = (f32[8,1280]{1,0:T(8,128)S(1)}, f32[8,1280]{1,0:T(8,128)S(1)}, u32[]{:S(2)}, u32[]{:S(2)}) collective-permute-start(f32[8,1280]{1,0:T(8,128)S(1)} %add.64), channel_id=1, source_target_pairs={{0,16},{1,17},{2,18},{3,19},{4,20},{5,21},{6,22},{7,23},{8,24},{9,... | collective-permute-start | bytes 122888 | tf_op jit(solution)/shard_map/ppermute | solution.py:384
  (205 shorter events, 73.9 us)
Async XLA Ops:
  10.0 13.8 %collective-permute-start.5 = (bf16[1,128,2048]{2,1,0:T(8,128)(2,1)}, bf16[1,128,2048]{2,1,0:T(8,128)(2,1)}, u32[]{:S(2)}, u32[]{:S(2)}) collective-permute-start(bf16[1,128,2048]{2,1,0:T(8,128)(2,1)} %get-tuple-element.83.rest_0_), channel_id=1, source_target_pairs={{0,2},{1,3},{2,0},{3,1},{4,6},{5,7},{6,4},{7,5},{8,10},{9,11},{10,... | collective-permute-start | bytes 1572872 | tf_op jit(solution)/shard_map/ppermute | solution.py:384
  11.6 13.4 %collective-permute-start.6 = (bf16[1,128,2048]{2,1,0:T(8,128)(2,1)}, bf16[1,128,2048]{2,1,0:T(8,128)(2,1)}, u32[]{:S(2)}, u32[]{:S(2)}) collective-permute-start(bf16[1,128,2048]{2,1,0:T(8,128)(2,1)} %get-tuple-element.83.rest_0_), channel_id=1, source_target_pairs={{0,4},{1,5},{2,6},{3,7},{4,0},{5,1},{6,2},{7,3},{8,12},{9,13},{10,... | collective-permute-start | bytes 1572872 | tf_op jit(solution)/shard_map/ppermute | solution.py:384
  16.9 12.1 %collective-permute-start.3 = (bf16[136,1024]{1,0:T(8,128)(2,1)S(1)}, bf16[136,1024]{1,0:T(8,128)(2,1)S(1)}, u32[]{:S(2)}, u32[]{:S(2)}) collective-permute-start(bf16[136,1024]{1,0:T(8,128)(2,1)S(1)} %collective-permute-done.2), channel_id=1, source_target_pairs={{8,0},{9,1},{10,2},{11,3},{12,4},{13,5},{14,6},{15,7},{16,24},{17,... | collective-permute-start | bytes 835592 | tf_op jit(solution)/shard_map/ppermute | solution.py:407
  18.2 16.1 %collective-permute-start.4 = (bf16[136,1024]{1,0:T(8,128)(2,1)S(1)}, bf16[136,1024]{1,0:T(8,128)(2,1)S(1)}, u32[]{:S(2)}, u32[]{:S(2)}) collective-permute-start(bf16[136,1024]{1,0:T(8,128)(2,1)S(1)} %collective-permute-done.1), channel_id=1, source_target_pairs={{8,0},{9,1},{10,2},{11,3},{12,4},{13,5},{14,6},{15,7},{16,24},{17,... | collective-permute-start | bytes 835592 | tf_op jit(solution)/shard_map/ppermute | solution.py:407
  25.0 12.9 %collective-permute-start.7 = (bf16[2,136,1024]{2,1,0:T(8,128)(2,1)S(1)}, bf16[2,136,1024]{2,1,0:T(8,128)(2,1)S(1)}, u32[]{:S(2)}, u32[]{:S(2)}) collective-permute-start(bf16[2,136,1024]{2,1,0:T(8,128)(2,1)S(1)} %pad_maximum_fusion.2.rest_0_.rest_1_), channel_id=1, source_target_pairs={{0,2},{1,3},{2,0},{3,1},{4,6},{5,7},{6,4},{7,5},{8,10},{9,11},{10,... | collective-permute-start | bytes 1671176 | tf_op jit(solution)/shard_map/ppermute | solution.py:384
  25.5 12.8 %collective-permute-start.8 = (bf16[2,136,1024]{2,1,0:T(8,128)(2,1)S(1)}, bf16[2,136,1024]{2,1,0:T(8,128)(2,1)S(1)}, u32[]{:S(2)}, u32[]{:S(2)}) collective-permute-start(bf16[2,136,1024]{2,1,0:T(8,128)(2,1)S(1)} %pad_maximum_fusion.2.rest_0_.rest_1_), channel_id=1, source_target_pairs={{0,4},{1,5},{2,6},{3,7},{4,0},{5,1},{6,2},{7,3},{8,12},{9,13},{10,... | collective-permute-start | bytes 1671176 | tf_op jit(solution)/shard_map/ppermute | solution.py:384
  34.4 12.1 %collective-permute-start.10 = (bf16[1,128,2048]{2,1,0:T(8,128)(2,1)S(1)}, bf16[1,128,2048]{2,1,0:T(8,128)(2,1)S(1)}, u32[]{:S(2)}, u32[]{:S(2)}) collective-permute-start(bf16[1,128,2048]{2,1,0:T(8,128)(2,1)S(1)} %copy-done.11), channel_id=1, source_target_pairs={{0,8},{1,9},{2,10},{3,11},{4,12},{5,13},{6,14},{7,15},{8,0},{9,1},... | collective-permute-start | bytes 1572872 | tf_op jit(solution)/shard_map/ppermute | solution.py:384
  34.5 12.7 %collective-permute-start.12 = (bf16[1,128,2048]{2,1,0:T(8,128)(2,1)S(1)}, bf16[1,128,2048]{2,1,0:T(8,128)(2,1)S(1)}, u32[]{:S(2)}, u32[]{:S(2)}) collective-permute-start(bf16[1,128,2048]{2,1,0:T(8,128)(2,1)S(1)} %copy-done.11), channel_id=1, source_target_pairs={{8,16},{9,17},{10,18},{11,19},{12,20},{13,21},{14,22},{15,23},{16,... | collective-permute-start | bytes 1572872 | tf_op jit(solution)/shard_map/ppermute | solution.py:407
  38.3 12.8 %collective-permute-start.14 = (bf16[2,136,1024]{2,1,0:T(8,128)(2,1)S(1)}, bf16[2,136,1024]{2,1,0:T(8,128)(2,1)S(1)}, u32[]{:S(2)}, u32[]{:S(2)}) collective-permute-start(bf16[2,136,1024]{2,1,0:T(8,128)(2,1)S(1)} %pad_maximum_fusion.1.rest_1_.rest_4_.rest_5_), channel_id=1, source_target_pairs={{0,4},{1,5},{2,6},{3,7},{4,0},{5,1},{6,2},{7,3},{8,12},{9,13},{10,... | collective-permute-start | bytes 1671176 | tf_op jit(solution)/shard_map/ppermute | solution.py:384
  39.9 12.8 %collective-permute-start.9 = (bf16[2,136,1024]{2,1,0:T(8,128)(2,1)S(1)}, bf16[2,136,1024]{2,1,0:T(8,128)(2,1)S(1)}, u32[]{:S(2)}, u32[]{:S(2)}) collective-permute-start(bf16[2,136,1024]{2,1,0:T(8,128)(2,1)S(1)} %pad_maximum_fusion.1.rest_1_.rest_4_.rest_5_), channel_id=1, source_target_pairs={{0,2},{1,3},{2,0},{3,1},{4,6},{5,7},{6,4},{7,5},{8,10},{9,11},{10,... | collective-permute-start | bytes 1671176 | tf_op jit(solution)/shard_map/ppermute | solution.py:384
  47.2 13.3 %collective-permute-start.13 = (bf16[1,128,2048]{2,1,0:T(8,128)(2,1)S(1)}, bf16[1,128,2048]{2,1,0:T(8,128)(2,1)S(1)}, u32[]{:S(2)}, u32[]{:S(2)}) collective-permute-start(bf16[1,128,2048]{2,1,0:T(8,128)(2,1)S(1)} %collective-permute-done.12), channel_id=1, source_target_pairs={{8,0},{9,1},{10,2},{11,3},{12,4},{13,5},{14,6},{15,7},{16,24},{17,... | collective-permute-start | bytes 1572872 | tf_op jit(solution)/shard_map/ppermute | solution.py:407
  51.1 11.8 %collective-permute-start.16 = (bf16[2,136,1024]{2,1,0:T(8,128)(2,1)S(1)}, bf16[2,136,1024]{2,1,0:T(8,128)(2,1)S(1)}, u32[]{:S(2)}, u32[]{:S(2)}) collective-permute-start(bf16[2,136,1024]{2,1,0:T(8,128)(2,1)S(1)} %collective-permute-done.7.rest_4_.near_ref.rest_1_.rest_2_), channel_id=1, source_target_pairs={{0,4},{1,5},{2,6},{3,7},{4,0},{5,1},{6,2},{7,3},{8,12},{9,13},{10,... | collective-permute-start | bytes 1671176 | tf_op jit(solution)/shard_map/ppermute | solution.py:384
  52.7 20.0 %collective-permute-start.15 = (bf16[1,128,2048]{2,1,0:T(8,128)(2,1)S(1)}, bf16[1,128,2048]{2,1,0:T(8,128)(2,1)S(1)}, u32[]{:S(2)}, u32[]{:S(2)}) collective-permute-start(bf16[1,128,2048]{2,1,0:T(8,128)(2,1)S(1)} %collective-permute-done.11), channel_id=1, source_target_pairs={{8,0},{9,1},{10,2},{11,3},{12,4},{13,5},{14,6},{15,7},{16,24},{17,... | collective-permute-start | bytes 1572872 | tf_op jit(solution)/shard_map/ppermute | solution.py:407
  53.9 20.2 %collective-permute-start.18 = (bf16[2,136,1024]{2,1,0:T(8,128)(2,1)S(1)}, bf16[2,136,1024]{2,1,0:T(8,128)(2,1)S(1)}, u32[]{:S(2)}, u32[]{:S(2)}) collective-permute-start(bf16[2,136,1024]{2,1,0:T(8,128)(2,1)S(1)} %collective-permute-done.14.rest_3_.rest_6_.rest_7_), channel_id=1, source_target_pairs={{0,2},{1,3},{2,0},{3,1},{4,6},{5,7},{6,4},{7,5},{8,10},{9,11},{10,... | collective-permute-start | bytes 1671176 | tf_op jit(solution)/shard_map/ppermute | solution.py:384
  63.7 22.0 %collective-permute-start.17 = (bf16[1,128,2048]{2,1,0:T(8,128)(2,1)}, bf16[1,128,2048]{2,1,0:T(8,128)(2,1)}, u32[]{:S(2)}, u32[]{:S(2)}) collective-permute-start(bf16[1,128,2048]{2,1,0:T(8,128)(2,1)} %collective-permute-done.5.rest_2_), channel_id=1, source_target_pairs={{0,4},{1,5},{2,6},{3,7},{4,0},{5,1},{6,2},{7,3},{8,12},{9,13},{10,... | collective-permute-start | bytes 1572872 | tf_op jit(solution)/shard_map/ppermute | solution.py:384
  75.0 35.6 %collective-permute-start.21 = (bf16[3,128,2048]{2,1,0:T(8,128)(2,1)}, bf16[3,128,2048]{2,1,0:T(8,128)(2,1)}, u32[]{:S(2)}, u32[]{:S(2)}) collective-permute-start(bf16[3,128,2048]{2,1,0:T(8,128)(2,1)} %pad_maximum_fusion.rest_1_), channel_id=1, source_target_pairs={{0,2},{1,3},{2,0},{3,1},{4,6},{5,7},{6,4},{7,5},{8,10},{9,11},{10,... | collective-permute-start | bytes 4718600 | tf_op jit(solution)/shard_map/ppermute | solution.py:384
  76.5 34.2 %collective-permute-start.22 = (bf16[3,128,2048]{2,1,0:T(8,128)(2,1)}, bf16[3,128,2048]{2,1,0:T(8,128)(2,1)}, u32[]{:S(2)}, u32[]{:S(2)}) collective-permute-start(bf16[3,128,2048]{2,1,0:T(8,128)(2,1)} %pad_maximum_fusion.rest_1_), channel_id=1, source_target_pairs={{0,4},{1,5},{2,6},{3,7},{4,0},{5,1},{6,2},{7,3},{8,12},{9,13},{10,... | collective-permute-start | bytes 4718600 | tf_op jit(solution)/shard_map/ppermute | solution.py:384
  113.6 19.7 %collective-permute-start.27 = (bf16[3,64,2048]{2,1,0:T(8,128)(2,1)S(1)}, bf16[3,64,2048]{2,1,0:T(8,128)(2,1)S(1)}, u32[]{:S(2)}, u32[]{:S(2)}) collective-permute-start(bf16[3,64,2048]{2,1,0:T(8,128)(2,1)S(1)} %slice.24), channel_id=1, source_target_pairs={{0,4},{1,5},{2,6},{3,7},{4,0},{5,1},{6,2},{7,3},{8,12},{9,13},{10,... | collective-permute-start | bytes 2359304 | tf_op jit(solution)/shard_map/ppermute | solution.py:384
  114.7 19.2 %collective-permute-start.28 = (bf16[3,64,2048]{2,1,0:T(8,128)(2,1)S(1)}, bf16[3,64,2048]{2,1,0:T(8,128)(2,1)S(1)}, u32[]{:S(2)}, u32[]{:S(2)}) collective-permute-start(bf16[3,64,2048]{2,1,0:T(8,128)(2,1)S(1)} %slice.25), channel_id=1, source_target_pairs={{0,2},{1,3},{2,0},{3,1},{4,6},{5,7},{6,4},{7,5},{8,10},{9,11},{10,... | collective-permute-start | bytes 2359304 | tf_op jit(solution)/shard_map/ppermute | solution.py:384
  152.1 22.8 %collective-permute-start.35 = (bf16[512,256]{1,0:T(8,128)(2,1)S(1)}, bf16[512,256]{1,0:T(8,128)(2,1)S(1)}, u32[]{:S(2)}, u32[]{:S(2)}) collective-permute-start(bf16[512,256]{1,0:T(8,128)(2,1)S(1)} %get-tuple-element.117), channel_id=1, source_target_pairs={{0,1},{1,0},{2,3},{3,2},{4,5},{5,4},{6,7},{7,6},{8,9},{9,8},{10,11... | collective-permute-start | bytes 786440 | tf_op jit(solution)/shard_map/ppermute | solution.py:389
  152.2 23.4 %collective-permute-start.36 = (bf16[512,256]{1,0:T(8,128)(2,1)S(1)}, bf16[512,256]{1,0:T(8,128)(2,1)S(1)}, u32[]{:S(2)}, u32[]{:S(2)}) collective-permute-start(bf16[512,256]{1,0:T(8,128)(2,1)S(1)} %get-tuple-element.118), channel_id=1, source_target_pairs={{0,2},{1,3},{2,0},{3,1},{4,6},{5,7},{6,4},{7,5},{8,10},{9,11},{10,... | collective-permute-start | bytes 786440 | tf_op jit(solution)/shard_map/ppermute | solution.py:384
  152.8 22.9 %collective-permute-start.37 = (bf16[512,256]{1,0:T(8,128)(2,1)S(1)}, bf16[512,256]{1,0:T(8,128)(2,1)S(1)}, u32[]{:S(2)}, u32[]{:S(2)}) collective-permute-start(bf16[512,256]{1,0:T(8,128)(2,1)S(1)} %get-tuple-element.119), channel_id=1, source_target_pairs={{0,3},{1,2},{2,1},{3,0},{4,7},{5,6},{6,5},{7,4},{8,11},{9,10},{10,... | collective-permute-start | bytes 786440 | tf_op jit(solution)/shard_map/ppermute | solution.py:1203
  193.1 15.9 %collective-permute-start.40 = (bf16[512,256]{1,0:T(8,128)(2,1)S(1)}, bf16[512,256]{1,0:T(8,128)(2,1)S(1)}, u32[]{:S(2)}, u32[]{:S(2)}) collective-permute-start(bf16[512,256]{1,0:T(8,128)(2,1)S(1)} %get-tuple-element.137), channel_id=1, source_target_pairs={{0,2},{1,3},{2,0},{3,1},{4,6},{5,7},{6,4},{7,5},{8,10},{9,11},{10,... | collective-permute-start | bytes 786440 | tf_op jit(solution)/shard_map/ppermute | solution.py:384
  194.6 14.5 %collective-permute-start.41 = (bf16[512,256]{1,0:T(8,128)(2,1)S(1)}, bf16[512,256]{1,0:T(8,128)(2,1)S(1)}, u32[]{:S(2)}, u32[]{:S(2)}) collective-permute-start(bf16[512,256]{1,0:T(8,128)(2,1)S(1)} %get-tuple-element.138), channel_id=1, source_target_pairs={{0,3},{1,2},{2,1},{3,0},{4,7},{5,6},{6,5},{7,4},{8,11},{9,10},{10,... | collective-permute-start | bytes 786440 | tf_op jit(solution)/shard_map/ppermute | solution.py:1203
  (60 other events, 398.4 us)
